TPU v7x, 32 devices: a whole 2x2x4 slice. The times are simulated.
32 devices in a mesh: section: 2 (over core), dp: 16 (over z, y, x).
Axes of the slice: x: 2, y: 2, z: 4, core: 2. Of those that a mesh axis runs over, the one named last changes fastest.
Arguments:
- inputs: bfloat16 [9728, 256], P('dp'), may hold values from -6 to 6
- cotangent: bfloat16 [9728, 256], P('dp'), may hold values from -6 to 6
- vectors: float32 [2, 3328], P('section'), as said below
- kernels: float32 [2, 9, 256], P('section'), may hold values from -2 to 2
- w_qkv: float32 [2, 256, 768], P('section'), may hold values from -0.375 to 0.375
- w_proj: float32 [2, 256, 256], P('section'), may hold values from -0.75 to 0.75
- w_fc1: float32 [2, 256, 1024], P('section'), may hold values from -0.375 to 0.375
- w_fc2: float32 [2, 1024, 256], P('section'), may hold values from -0.1875 to 0.1875
- momentum_vectors: float32 [2, 3328], P('section'), may hold values from -0.09375 to 0.09375
- momentum_kernels: float32 [2, 9, 256], P('section'), may hold values from -0.046875 to 0.046875
- momentum_qkv: float32 [2, 256, 768], P('section'), may hold values from -0.02734375 to 0.02734375
- momentum_proj: float32 [2, 256, 256], P('section'), may hold values from -0.02734375 to 0.02734375
- momentum_fc1: float32 [2, 256, 1024], P('section'), may hold values from -0.02734375 to 0.02734375
- momentum_fc2: float32 [2, 1024, 256], P('section'), may hold values from -0.02734375 to 0.02734375
- average_vectors: float32 [2, 3328], P('section'), as said below
- average_kernels: float32 [2, 9, 256], P('section'), may hold values from -2 to 2
- average_qkv: float32 [2, 256, 768], P('section'), may hold values from -0.375 to 0.375
- average_proj: float32 [2, 256, 256], P('section'), may hold values from -0.75 to 0.75
- average_fc1: float32 [2, 256, 1024], P('section'), may hold values from -0.375 to 0.375
- average_fc2: float32 [2, 1024, 256], P('section'), may hold values from -0.1875 to 0.1875
Outputs:
- block_outputs: float32 [2, 9728, 256], P('section', 'dp')
- input_grads: float32 [2, 9728, 256], P('section', 'dp')
- grad_vectors: float32 [2, 3328], P('section')
- grad_kernels: float32 [2, 9, 256], P('section')
- grad_qkv: float32 [2, 256, 768], P('section')
- grad_proj: float32 [2, 256, 256], P('section')
- grad_fc1: float32 [2, 256, 1024], P('section')
- grad_fc2: float32 [2, 1024, 256], P('section')
- grad_norm: float32 [], replicated
- new_momentum_vectors: float32 [2, 3328], P('section')
- new_momentum_kernels: float32 [2, 9, 256], P('section')
- new_momentum_qkv: float32 [2, 256, 768], P('section')
- new_momentum_proj: float32 [2, 256, 256], P('section')
- new_momentum_fc1: float32 [2, 256, 1024], P('section')
- new_momentum_fc2: float32 [2, 1024, 256], P('section')
- new_vectors: float32 [2, 3328], P('section')
- new_kernels: float32 [2, 9, 256], P('section')
- new_w_qkv: float32 [2, 256, 768], P('section')
- new_w_proj: float32 [2, 256, 256], P('section')
- new_w_fc1: float32 [2, 256, 1024], P('section')
- new_w_fc2: float32 [2, 1024, 256], P('section')
- new_average_vectors: float32 [2, 3328], P('section')
- new_average_kernels: float32 [2, 9, 256], P('section')
- new_average_qkv: float32 [2, 256, 768], P('section')
- new_average_proj: float32 [2, 256, 256], P('section')
- new_average_fc1: float32 [2, 256, 1024], P('section')
- new_average_fc2: float32 [2, 1024, 256], P('section')
- copy_qkv: bfloat16 [2, 256, 768], P('section')
- copy_proj: bfloat16 [2, 256, 256], P('section')
- copy_fc1: bfloat16 [2, 256, 1024], P('section')
- copy_fc2: bfloat16 [2, 1024, 256], P('section')
Inputs may be any that keep to these rules, and one draw needn't show every extreme that they name: `vectors`: gains are positive. `average_vectors`: gains are positive.
All inputs are finite; a program needn't handle non-finite values.
Results may differ from a plain program's by a relative error of at most 0.022.
The roundings to bfloat16 on the way count: a program that leaves them out, or rounds other values in their place, can miss the bound.
Values may be sent and summed in bfloat16 or wider, within the bound.
No kernel may reach another device: no remote copies, remote signals or barrier semaphores. Data moves between devices by JAX's collectives and lax.ppermute only.
A program may use at most 128 MiB of HBM per device.

v0:
```python
import jax
import jax.numpy as jnp
import numpy as np
from jax import lax
from jax.experimental import pallas as pl
from jax.experimental.pallas import tpu as pltpu
from jax.sharding import PartitionSpec as P

D = 256
HALF = 128
HEADS = 8
HEAD = 32
FF = 1024
BIG_SIDE = 14
SMALL_SIDE = 6
BIG_MB = 1
SMALL_MB = 3
STEP = 8
MB_TOK = 304
VEC = 3328

NORM_EPS = 1e-05
CLIP_LIMIT = 5.0
LEARN_RATE = 4.0
MOMENTUM_DECAY = 0.9
WEIGHT_DECAY = 5e-05

F32 = jnp.float32
BF16 = jnp.bfloat16

GROUP = 128
GROUPS = ((0, 112), (112, 84), (196, 108))
KINDS = (0, 0, 1)
NGROUP = len(GROUPS)
ATT = NGROUP * GROUP
SCALE = HEAD ** -0.5
LOG2E = 1.4426950408889634
EXP_SCALE = SCALE * LOG2E
OFF = -1e30
ROWS = ((0, 80), (80, 80), (160, 80), (240, 64))
GRAD_ROWS = 3328
SMALL_ROW = 3072


def placement_tables():
    plain = np.zeros((ATT, MB_TOK), np.float32)
    turned = np.zeros((ATT, MB_TOK), np.float32)
    transposed = []
    base = 0
    for side, count in ((BIG_SIDE, BIG_MB), (SMALL_SIDE, SMALL_MB)):
        for _ in range(count):
            for row in range(side):
                for col in range(side):
                    transposed.append(base + col * side + row)
            base += side * side
    for group, (first, size) in enumerate(GROUPS):
        for at in range(size):
            plain[group * GROUP + at, first + at] = 1.0
            turned[group * GROUP + at, transposed[first + at]] = 1.0
    return plain, turned


def stripe_tables():
    shifts = np.zeros((2, 5 * GROUP, GROUP), np.float32)
    fence = np.full((2, GROUP, GROUP), OFF, np.float32)
    lower = np.zeros((2, GROUP, HALF), np.float32)
    for kind, (side, sizes) in enumerate(((BIG_SIDE, 112), (SMALL_SIDE, 108))):
        stripe = 2 * side
        for at in range(GROUP):
            own = at // stripe
            fence[kind, at, own * stripe : (own + 1) * stripe] = 0.0
        for at in range(sizes):
            own, inner = divmod(at, stripe)
            row, col = divmod(inner, side)
            lower[kind, at, :] = float(row)
            moves = ((row, col - 1), (row, col + 1), (1 - row, col - 1), (1 - row, col), (1 - row, col + 1))
            for move, (to_row, to_col) in enumerate(moves):
                if 0 <= to_col < side:
                    shifts[kind, move * GROUP + at, own * stripe + to_row * side + to_col] = 1.0
    return shifts, fence, lower


def dot(a, b):
    return jnp.dot(a, b, preferred_element_type=F32)


def dot_nt(a, b):
    return lax.dot_general(a, b, (((1,), (1,)), ((), ())), preferred_element_type=F32)


def dot_tn(a, b):
    return lax.dot_general(a, b, (((0,), (0,)), ((), ())), preferred_element_type=F32)


def head_masks():
    lane = lax.broadcasted_iota(jnp.int32, (1, HALF), 1) // HEAD
    return [(lane == head).astype(BF16) for head in range(HEADS // 2)]


def stacked_heads(rows, masks):
    return jnp.concatenate([rows * mask for mask in masks], axis=0)


def picked_heads(product):
    return jnp.concatenate(
        [
            product[HEAD * head : HEAD * (head + 1), GROUP * head : GROUP * (head + 1)]
            for head in range(HEADS // 2)
        ],
        axis=0,
    )


def turned_taps(taps):
    first = [taps[index : index + 1, :HALF] for index in range(9)]
    second = [taps[3 * (index % 3) + index // 3 :, HALF:][:1] for index in range(9)]
    return [jnp.concatenate([a, b], axis=1) for a, b in zip(first, second)]


def norm_forward(x, gain, offset):
    centre = x - jnp.mean(x, axis=-1, keepdims=True)
    spread = jnp.mean(centre * centre, axis=-1, keepdims=True)
    scale = lax.rsqrt(spread + NORM_EPS)
    hat = centre * scale
    return hat, scale, hat * gain + offset


def norm_backward(grad, hat, scale, gain):
    inner = grad * gain
    mean_inner = jnp.mean(inner, axis=-1, keepdims=True)
    mean_cross = jnp.mean(inner * hat, axis=-1, keepdims=True)
    return scale * (inner - mean_inner - hat * mean_cross)


def column_sum(x):
    return jnp.sum(x.astype(F32), axis=0, keepdims=True)


def vec_at(vec, index, width=1):
    return vec[:, index * D : (index + width) * D]


def forward_block(x_ref, out_ref, vec, taps, w, saved, tables, work):
    wq, wp, w1, w2 = w
    (hat1, scale1, normed, qkv, probs, mixed, hat2, scale2, normed2, slope, activ) = saved
    plain, turned, plain_t, turned_t, shifts, fence, lower = tables
    normed_nat, mixed_att, middle, hidden = work
    for start, size in ROWS:
        rows = pl.ds(start, size)
        hat, scale, y = norm_forward(x_ref[rows, :].astype(F32), vec_at(vec, 0), vec_at(vec, 2))
        hat1[rows, :] = hat
        scale1[rows, :] = jnp.broadcast_to(scale, (size, HALF))
        normed_nat[rows, :] = y.astype(BF16)
    base = normed_nat[...]
    biases = (vec_at(vec, 4), None, vec_at(vec, 5))
    for half, table in enumerate((plain, turned)):
        placed = dot(table[...], base).astype(BF16)
        normed[half] = placed
        lanes = slice(half * HALF, (half + 1) * HALF)
        for part in range(3):
            got = dot(placed, wq[:, part * D + half * HALF : part * D + (half + 1) * HALF])
            if biases[part] is not None:
                got = got + biases[part][:, lanes]
            qkv[part, :, lanes] = got.astype(BF16)
    masks = head_masks()
    taps9 = turned_taps(taps)
    bias = vec_at(vec, 7)
    for group in range(NGROUP):
        kind = KINDS[group]
        rows = pl.ds(group * GROUP, GROUP)
        v = qkv[2, rows, :]
        moved = dot(shifts[kind], v)
        low_row = lower[kind] > 0.5
        low_row = jnp.concatenate([low_row, low_row], axis=1)
        lepe = bias + taps9[4] * v.astype(F32)
        lepe = lepe + taps9[3] * moved[0:GROUP] + taps9[5] * moved[GROUP : 2 * GROUP]
        for step in range(3):
            tap = jnp.where(low_row, taps9[step], taps9[6 + step])
            lepe = lepe + tap * moved[(2 + step) * GROUP : (3 + step) * GROUP]
        fenced = fence[kind]
        for half in range(2):
            lanes = slice(half * HALF, (half + 1) * HALF)
            q_stack = stacked_heads(qkv[0, rows, lanes], masks)
            scores = dot_nt(qkv[1, rows, lanes], q_stack)
            low = []
            for head in range(HEADS // 2):
                s = scores[:, head * GROUP : (head + 1) * GROUP] + fenced
                p = jnp.exp2((s - jnp.max(s, axis=0, keepdims=True)) * EXP_SCALE)
                p = p * (1.0 / jnp.sum(p, axis=0, keepdims=True))
                probs[group * 2 + half, :, head * GROUP : (head + 1) * GROUP] = p
                low.append(p.astype(BF16))
            attended = picked_heads(dot(v[:, lanes].T, jnp.concatenate(low, axis=1))).T
            mixed_att[rows, lanes] = (attended + lepe[:, lanes]).astype(BF16)
    mixed[:, :HALF] = dot(plain_t[...], mixed_att[:, :HALF]).astype(BF16)
    mixed[:, HALF:] = dot(turned_t[...], mixed_att[:, HALF:]).astype(BF16)
    middle[...] = dot(mixed[...], wp[...])
    for start, size in ROWS:
        rows = pl.ds(start, size)
        mid = x_ref[rows, :].astype(F32) + middle[rows, :] + vec_at(vec, 6)
        middle[rows, :] = mid
        hat, scale, y = norm_forward(mid, vec_at(vec, 1), vec_at(vec, 3))
        hat2[rows, :] = hat
        scale2[rows, :] = jnp.broadcast_to(scale, (size, HALF))
        normed2[rows, :] = y.astype(BF16)
    hidden[...] = dot(normed2[...], w1[...])
    for start, size in ROWS:
        rows = pl.ds(start, size)
        for part in range(4):
            cols = slice(part * D, (part + 1) * D)
            h = hidden[rows, cols] + vec_at(vec, 9 + part)
            cdf = 0.5 * (1.0 + lax.erf(h * 0.7071067811865476))
            pdf = 0.3989422804014327 * jnp.exp(-0.5 * h * h)
            activ[rows, cols] = (h * cdf).astype(BF16)
            slope[rows, cols] = cdf + h * pdf
    out_ref[...] = dot(activ[...], w2[...])
    for start, size in ROWS:
        rows = pl.ds(start, size)
        out_ref[rows, :] = out_ref[rows, :] + middle[rows, :] + vec_at(vec, 8)


def backward_block(up_ref, grad_ref, vec, taps, w, saved, tables, work, gbuf, small):
    wq, wp, w1, w2 = w
    (hat1, scale1, normed, qkv, probs, mixed, hat2, scale2, normed2, slope, activ) = saved
    plain, turned, plain_t, turned_t, shifts, fence, lower = tables
    branch, gact, ghid, gmid, gmix, dqkv, dnat, gnorm = work
    branch[...] = up_ref[...].astype(BF16)
    gbuf[2048:3072, :] = dot_tn(activ[...], branch[...]).astype(BF16)
    sums = column_sum(branch[...])
    small[8:9, :] = sums
    gact[...] = dot_nt(branch[...], w2[...])
    parts = [jnp.zeros((1, D), F32) for _ in range(4)]
    for start, size in ROWS:
        rows = pl.ds(start, size)
        for part in range(4):
            cols = slice(part * D, (part + 1) * D)
            low = (gact[rows, cols] * slope[rows, cols]).astype(BF16)
            ghid[rows, cols] = low
            parts[part] = parts[part] + column_sum(low)
    for part in range(4):
        small[9 + part : 10 + part, :] = parts[part]
    for part in range(4):
        gbuf[1024 + part * D : 1024 + (part + 1) * D, :] = dot_tn(
            normed2[...], ghid[:, part * D : (part + 1) * D]
        ).astype(BF16)
    gnorm[...] = dot_nt(ghid[...], w1[...])
    gains, offsets, outs = (jnp.zeros((1, D), F32) for _ in range(3))
    for start, size in ROWS:
        rows = pl.ds(start, size)
        g = gnorm[rows, :]
        hat = hat2[rows, :]
        scale = scale2[rows, :]
        gains = gains + column_sum(g * hat)
        offsets = offsets + column_sum(g)
        full = jnp.concatenate([scale, scale], axis=1)
        total = up_ref[rows, :].astype(F32) + norm_backward(g, hat, full, vec_at(vec, 1))
        gmid[rows, :] = total
        low = total.astype(BF16)
        branch[rows, :] = low
        outs = outs + column_sum(low)
    small[1:2, :] = gains
    small[3:4, :] = offsets
    small[6:7, :] = outs
    gbuf[768:1024, :] = dot_tn(mixed[...], branch[...]).astype(BF16)
    low = dot_nt(branch[...], wp[...]).astype(BF16)
    gmix[0:MB_TOK, :] = low
    small[7:8, :] = column_sum(low)
    place_h = dot(plain[...], low[:, :HALF]).astype(BF16)
    place_v = dot(turned[...], low[:, HALF:]).astype(BF16)
    gmix[:, :HALF] = place_h
    gmix[:, HALF:] = place_v
    masks = head_masks()
    taps9 = turned_taps(taps)
    tap_sums = [jnp.zeros((1, D), F32) for _ in range(9)]
    for group in range(NGROUP):
        kind = KINDS[group]
        rows = pl.ds(group * GROUP, GROUP)
        g_low = gmix[rows, :]
        moved = dot(shifts[kind], g_low)
        low_row = lower[kind] > 0.5
        low_row = jnp.concatenate([low_row, low_row], axis=1)
        v32 = qkv[2, rows, :].astype(F32)
        g32 = g_low.astype(F32)
        tap_sums[4] = tap_sums[4] + column_sum(v32 * g32)
        left, right = moved[0:GROUP], moved[GROUP : 2 * GROUP]
        lepe = taps9[4] * g32 + taps9[3] * right + taps9[5] * left
        tap_sums[3] = tap_sums[3] + column_sum(v32 * right)
        tap_sums[5] = tap_sums[5] + column_sum(v32 * left)
        for step in range(3):
            at = moved[(4 - step) * GROUP : (5 - step) * GROUP]
            lepe = lepe + jnp.where(low_row, taps9[6 + step], taps9[step]) * at
            product = v32 * at
            tap_sums[6 + step] = tap_sums[6 + step] + column_sum(jnp.where(low_row, product, 0.0))
            tap_sums[step] = tap_sums[step] + column_sum(jnp.where(low_row, 0.0, product))
        for half in range(2):
            lanes = slice(half * HALF, (half + 1) * HALF)
            unit = group * 2 + half
            g_stack = stacked_heads(gmix[rows, lanes], masks)
            q_stack = stacked_heads(qkv[0, rows, lanes], masks)
            k = qkv[1, rows, lanes]
            gprobs = dot_nt(qkv[2, rows, lanes], g_stack)
            low_p, low_s = [], []
            for head in range(HEADS // 2):
                cols = slice(head * GROUP, (head + 1) * GROUP)
                p = probs[unit, :, cols]
                gp = gprobs[:, cols]
                down = jnp.sum(gp * p, axis=0, keepdims=True)
                low_s.append((p * (gp - down)).astype(BF16))
                low_p.append(p.astype(BF16))
            low_p = jnp.concatenate(low_p, axis=1)
            low_s = jnp.concatenate(low_s, axis=1)
            grad_v = dot(low_p, g_stack) + lepe[:, lanes]
            grad_k = dot(low_s, q_stack) * SCALE
            grad_q = picked_heads(dot(k.T, low_s)).T * SCALE
            dqkv[half, rows, 0:HALF] = grad_q.astype(BF16)
            dqkv[half, rows, HALF:D] = grad_k.astype(BF16)
            dqkv[half, rows, D : 3 * HALF] = grad_v.astype(BF16)
    for index in range(9):
        tap = index
        turned_index = 3 * (index % 3) + index // 3
        small[13 + index : 14 + index, :] = jnp.concatenate(
            [tap_sums[tap][:, :HALF], tap_sums[turned_index][:, HALF:]], axis=1
        )
    for half, table_t in enumerate((plain_t, turned_t)):
        lanes = slice(half * HALF, (half + 1) * HALF)
        both = dqkv[half]
        small[4:5, lanes] = column_sum(both[:, 0:HALF])
        small[5:6, lanes] = column_sum(both[:, D : 3 * HALF])
        grads = dot_tn(normed[half], both)
        for part in range(3):
            gbuf[part * D : (part + 1) * D, lanes] = grads[:, part * HALF : (part + 1) * HALF].astype(BF16)
        natural = dot(table_t[...], both).astype(BF16)
        for part in range(3):
            dnat[:, part * D + half * HALF : part * D + (half + 1) * HALF] = natural[
                :, part * HALF : (part + 1) * HALF
            ]
    gnorm[...] = dot_nt(dnat[...], wq[...])
    gains, offsets = (jnp.zeros((1, D), F32) for _ in range(2))
    for start, size in ROWS:
        rows = pl.ds(start, size)
        g = gnorm[rows, :]
        hat = hat1[rows, :]
        scale = scale1[rows, :]
        gains = gains + column_sum(g * hat)
        offsets = offsets + column_sum(g)
        full = jnp.concatenate([scale, scale], axis=1)
        grad_ref[rows, :] = gmid[rows, :] + norm_backward(g, hat, full, vec_at(vec, 0))
    small[0:1, :] = gains
    small[2:3, :] = offsets
    gbuf[SMALL_ROW : SMALL_ROW + 32, :] = small[...].astype(BF16)


SAVED = [
    ((MB_TOK, D), F32),
    ((MB_TOK, HALF), F32),
    ((2, ATT, D), BF16),
    ((3, ATT, D), BF16),
    ((2 * NGROUP, GROUP, 4 * GROUP), F32),
    ((MB_TOK, D), BF16),
    ((MB_TOK, D), F32),
    ((MB_TOK, HALF), F32),
    ((MB_TOK, D), BF16),
    ((MB_TOK, FF), F32),
    ((MB_TOK, FF), BF16),
]
FORWARD_WORK = [((MB_TOK, D), BF16), ((ATT, D), BF16), ((MB_TOK, D), F32), ((MB_TOK, FF), F32)]
BACKWARD_WORK = [
    ((MB_TOK, D), BF16),
    ((MB_TOK, FF), F32),
    ((MB_TOK, FF), BF16),
    ((MB_TOK, D), F32),
    ((ATT, D), BF16),
    ((2, ATT, 3 * HALF), BF16),
    ((MB_TOK, 3 * D), BF16),
    ((MB_TOK, D), F32),
]


def section_step(
    sec_ref, x_ref, c_ref, vec_own, vec_other, ker_own, ker_other, wide_own, wide_other, deep_own, deep_other, *refs
):
    tables, refs = refs[:7], refs[7:]
    (outs, grads, gsum), refs = refs[:3], refs[3:]
    count = len(SAVED)
    kept, refs = (refs[:count], refs[count : 2 * count]), refs[2 * count :]
    forward_work, refs = refs[: len(FORWARD_WORK)], refs[len(FORWARD_WORK) :]
    backward_work, refs = refs[: len(BACKWARD_WORK)], refs[len(BACKWARD_WORK) :]
    feed, small, wide, deep, sems = refs
    sec = sec_ref[0]
    copies = [
        pltpu.make_async_copy(wide_own, wide.at[sec], sems.at[0]),
        pltpu.make_async_copy(wide_other, wide.at[1 - sec], sems.at[1]),
        pltpu.make_async_copy(deep_own, deep.at[sec], sems.at[2]),
        pltpu.make_async_copy(deep_other, deep.at[1 - sec], sems.at[3]),
    ]
    for copy in copies:
        copy.start()
    small[...] = jnp.zeros_like(small)
    gsum[:, SMALL_ROW:, :] = jnp.zeros((2, GRAD_ROWS - SMALL_ROW, D), BF16)
    first = sec == 0
    vecs = (
        jnp.where(first, vec_own[...], vec_other[...]),
        jnp.where(first, vec_other[...], vec_own[...]),
    )
    taps = (
        jnp.where(first, ker_own[...], ker_other[...]),
        jnp.where(first, ker_other[...], ker_own[...]),
    )
    weights = [
        (wide.at[b, :, 0:768], wide.at[b, :, 768:1024], wide.at[b, :, 1024:2048], deep.at[b])
        for b in range(2)
    ]
    at = pl.multiple_of(sec * MB_TOK, 16)
    for copy in copies:
        copy.wait()
    slot = (sec, 1 - sec)
    x_own, c_own = x_ref.at[pl.ds(at, MB_TOK)], c_ref.at[pl.ds(at, MB_TOK)]
    out_refs = [outs.at[slot[b]] for b in range(2)]
    grad_refs = [grads.at[slot[b]] for b in range(2)]
    sum_refs = [gsum.at[slot[b]] for b in range(2)]
    forward_block(x_own, out_refs[0], vecs[0], taps[0], weights[0], kept[0], tables, forward_work)
    feed[...] = out_refs[0][...].astype(BF16)
    forward_block(feed, out_refs[1], vecs[1], taps[1], weights[1], kept[1], tables, forward_work)
    backward_block(
        c_own, grad_refs[1], vecs[1], taps[1], weights[1], kept[1], tables, backward_work, sum_refs[1], small
    )
    feed[...] = grad_refs[1][...].astype(BF16)
    backward_block(
        feed, grad_refs[0], vecs[0], taps[0], weights[0], kept[0], tables, backward_work, sum_refs[0], small
    )


def run_blocks(sec, x, c, vec_own, vec_other, ker_own, ker_other, wide_own, wide_other, deep_own, deep_other):
    plain, turned = placement_tables()
    shifts, fence, lower = stripe_tables()
    tables = (
        jnp.asarray(plain, BF16),
        jnp.asarray(turned, BF16),
        jnp.asarray(plain.T, BF16),
        jnp.asarray(turned.T, BF16),
        jnp.asarray(shifts, BF16),
        jnp.asarray(fence, F32),
        jnp.asarray(lower, F32),
    )
    vmem = pl.BlockSpec(memory_space=pltpu.VMEM)
    hbm = pl.BlockSpec(memory_space=pl.ANY)
    smem = pl.BlockSpec(memory_space=pltpu.SMEM)
    scratch = SAVED + SAVED + FORWARD_WORK + BACKWARD_WORK
    scratch = scratch + [((MB_TOK, D), BF16), ((32, D), F32), ((2, D, 2048), BF16), ((2, FF, D), BF16)]
    return pl.pallas_call(
        section_step,
        out_shape=[
            jax.ShapeDtypeStruct((2, MB_TOK, D), F32),
            jax.ShapeDtypeStruct((2, MB_TOK, D), F32),
            jax.ShapeDtypeStruct((2, GRAD_ROWS, D), BF16),
        ],
        in_specs=[smem] + [vmem] * 6 + [hbm] * 4 + [vmem] * 7,
        out_specs=[vmem] * 3,
        scratch_shapes=[pltpu.VMEM(shape, kind) for shape, kind in scratch] + [pltpu.SemaphoreType.DMA((4,))],
        compiler_params=pltpu.CompilerParams(vmem_limit_bytes=50 << 20),
        name="blocks",
    )(sec, x, c, vec_own, vec_other, ker_own, ker_other, wide_own, wide_other, deep_own, deep_other, *tables)


def square_sum(a_ref, b_ref, c_ref, out_ref):
    total = jnp.zeros((8, D), F32)
    for ref in (a_ref, b_ref, c_ref):
        step = 64
        for start in range(0, ref.shape[0], step):
            rows = ref[start : start + step, :].astype(F32)
            square = rows * rows
            for at in range(0, step, 8):
                total = total + square[at : at + 8]
    total = jnp.sum(jnp.sum(total, axis=0, keepdims=True), axis=1, keepdims=True)
    out_ref[...] = jnp.broadcast_to(total, (8, HALF))


def run_square_sum(a, b, c):
    vmem = pl.BlockSpec(memory_space=pltpu.VMEM)
    return pl.pallas_call(
        square_sum,
        out_shape=jax.ShapeDtypeStruct((8, HALF), F32),
        in_specs=[vmem] * 3,
        out_specs=vmem,
        compiler_params=pltpu.CompilerParams(vmem_limit_bytes=16 << 20),
        name="squares",
    )(a, b, c)


def updated(grad, weight, moment, average, factor):
    decay = min(0.9999, (1.0 + STEP) / (10.0 + STEP))
    clipped = grad * factor
    direction = clipped + WEIGHT_DECAY * weight
    moment_new = MOMENTUM_DECAY * moment + direction
    weight_new = weight - LEARN_RATE * (direction + MOMENTUM_DECAY * moment_new)
    average_new = decay * average + (1.0 - decay) * weight_new
    return clipped, moment_new, weight_new, average_new


def optimizer_step(*refs):
    (own, other), refs = refs[:2], refs[2:]
    grads, refs = refs[:10], refs[10:]
    states, refs = refs[:18], refs[18:]
    outs, (norm_ref,) = refs[:28], refs[28:]
    norm = jnp.sqrt(own[0:1, 0:1] + other[0:1, 0:1])
    factor = jnp.minimum(1.0, CLIP_LIMIT / (norm + 1e-06))

    def put(index, lanes, grad):
        weight, moment, average = (states[kind * 6 + index][:, lanes] for kind in range(3))
        new = updated(grad, weight, moment, average, factor)
        for kind in range(4):
            outs[kind * 6 + index][:, lanes] = new[kind]
        if index >= 2:
            outs[24 + index - 2][:, lanes] = new[2].astype(BF16)

    for part in range(3):
        put(2, slice(part * D, (part + 1) * D), grads[part][...].astype(F32))
    put(3, slice(0, D), grads[3][...].astype(F32))
    for part in range(4):
        put(4, slice(part * D, (part + 1) * D), grads[4 + part][...].astype(F32))
    put(5, slice(0, D), grads[8][...].astype(F32))

    @pl.when(pl.program_id(0) == 0)
    def _():
        rows = grads[9][...].astype(F32)
        for part in range(13):
            put(0, slice(part * D, (part + 1) * D), rows[part : part + 1, :])
        put(1, slice(0, D), rows[13:22, :])
        norm_ref[...] = jnp.broadcast_to(norm, (8, HALF))


STEPS = 8


def run_optimizer(own, other, a, b, c, states):
    rows = D // STEPS
    deep = FF // STEPS

    def fixed(shape):
        return pl.BlockSpec(shape, lambda i: (0, 0))

    def strip(first):
        return pl.BlockSpec((rows, D), lambda i: (first * STEPS + i, 0))

    grad_specs = [strip(0), strip(1), strip(2), strip(3)] + [strip(part) for part in range(4)]
    grad_specs += [pl.BlockSpec((deep, D), lambda i: (i, 0)), pl.BlockSpec((32, D), lambda i: (FF // 32, 0))]
    state_specs = [
        fixed((1, VEC)),
        fixed((9, D)),
        pl.BlockSpec((rows, 3 * D), lambda i: (i, 0)),
        pl.BlockSpec((rows, D), lambda i: (i, 0)),
        pl.BlockSpec((rows, FF), lambda i: (i, 0)),
        pl.BlockSpec((deep, D), lambda i: (i, 0)),
    ]
    shapes = [(1, VEC), (9, D), (D, 3 * D), (D, D), (D, FF), (FF, D)]
    return pl.pallas_call(
        optimizer_step,
        grid=(STEPS,),
        out_shape=[jax.ShapeDtypeStruct(shape, F32) for shape in shapes] * 4
        + [jax.ShapeDtypeStruct(shape, BF16) for shape in shapes[2:]]
        + [jax.ShapeDtypeStruct((8, HALF), F32)],
        in_specs=[fixed((8, HALF))] * 2 + grad_specs + state_specs * 3,
        out_specs=state_specs * 4 + state_specs[2:] + [fixed((8, HALF))],
        compiler_params=pltpu.CompilerParams(vmem_limit_bytes=32 << 20),
        name="optimizer",
    )(own, other, a, a, a, a, b, b, b, b, c, c, *states)


def swapped(value):
    return lax.ppermute(value, "section", [(0, 1), (1, 0)])


def exchange_orders(bits):
    if bits == 4:
        return ((0, 1, 2, 3), (1, 2, 0, 3), (2, 0, 1, 3))
    turn = max(1, bits // 3)
    every = tuple(range(bits))
    return tuple(every[turn * part :] + every[: turn * part] for part in range(3))


def exchanged(value, bit, size):
    return lax.ppermute(value, "dp", [(index, index ^ (1 << bit)) for index in range(size)])


def summed_over_dp(parts):
    size = lax.axis_size("dp")
    bits = size.bit_length() - 1
    if size != 1 << bits or any(part.shape[0] % size for part in parts):
        return [lax.psum(part.astype(F32), "dp").astype(BF16) for part in parts]
    index = lax.axis_index("dp")
    orders = exchange_orders(bits)
    shapes = [part.shape for part in parts]
    held = [part.reshape((2,) * bits + (part.shape[0] // size, D)) for part in parts]
    for step in range(bits):
        kept, came = [], []
        for value, order in zip(held, orders):
            mine = (index >> order[step]) & 1
            kept.append(lax.dynamic_index_in_dim(value, mine, 0, keepdims=False))
            came.append(exchanged(lax.dynamic_index_in_dim(value, 1 - mine, 0, keepdims=False), order[step], size))
        held = [(a.astype(F32) + b.astype(F32)).astype(BF16) for a, b in zip(kept, came)]
    for step in reversed(range(bits)):
        grown = []
        for value, order in zip(held, orders):
            low = ((index >> order[step]) & 1) == 0
            came = exchanged(value, order[step], size)
            grown.append(jnp.stack([jnp.where(low, value, came), jnp.where(low, came, value)]))
        held = grown
    return [value.reshape(shape) for value, shape in zip(held, shapes)]


def per_device(inputs, cotangent, *states):
    states = [array.reshape(array.shape[-2:]) if array.ndim == 3 else array for array in states]
    vectors, kernels, w_qkv, w_proj, w_fc1, w_fc2 = states[:6]
    section = lax.axis_index("section")
    wide = jnp.concatenate([w_qkv, w_proj, w_fc1], axis=1).astype(BF16)
    deep = w_fc2.astype(BF16)
    outs, grads, sums = run_blocks(
        section.astype(jnp.int32).reshape(1),
        inputs,
        cotangent,
        vectors,
        swapped(vectors),
        kernels,
        swapped(kernels),
        wide,
        swapped(wide),
        deep,
        swapped(deep),
    )
    came = swapped(sums[1])
    total = (sums[0].astype(F32) + came.astype(F32)).astype(BF16)
    a, b, c = summed_over_dp([total[0:1024], total[1024:2048], total[2048:]])
    squares = run_square_sum(a, b, c)
    new = run_optimizer(squares, swapped(squares), a, b, c, states)
    first = section == 0

    def both_rows(value):
        own, came = value[0], swapped(value[1])
        return jnp.stack([jnp.where(first, own, came), jnp.where(first, came, own)]).reshape(1, 2 * MB_TOK, D)

    def whole(arrays):
        return [array if array.shape == (1, VEC) else array[None] for array in arrays]

    return (
        both_rows(outs),
        both_rows(grads),
        *whole(new[0:6]),
        new[28][0, 0],
        *whole(new[6:28]),
    )


def solution(mesh):
    rows = P("dp", None)
    state = (P("section", None),) + (P("section", None, None),) * 5
    return jax.shard_map(
        per_device,
        mesh=mesh,
        in_specs=(rows, rows) + state * 3,
        out_specs=(P("section", "dp", None),) * 2 + state + (P(),) + state * 3 + state[2:],
        check_vma=False,
    )
```

profile of v0, /device:TPU:0, one launch (start us, length us, event | category | flops | bytes accessed | tf_op | source)
XLA Modules:
  0.0 130.4 jit_solution(10287973017153208335)
XLA Ops:
  0.7 1.1 bitcast_convert_fusion.2
  1.7 1.2 bitcast_convert_fusion.3
  3.1 1.1 pad_maximum_fusion.wide_own
  5.4 0.6 copy-done.21
  6.0 1.6 %collective-permute-done.1.ker_other = f32[9,256]{1,0:T(8,128)S(1)} collective-permute-done((f32[9,256]{1,0:T(8,128)S(1)}, f32[9,256]{1,0:T(8,128)S(1)}, u32[]{:S(2)}, u32[]{:S(2)}) %collective-permute-start.1) | collective-permute-done | bytes 9248 | tf_op jit(solution)/shard_map/ppermute | solution.py:569
  7.7 0.6 copy-done.29
  8.3 0.6 copy-done.33
  8.9 0.8 copy-done.10
  9.7 1.0 copy-done.11
  10.7 1.0 copy-done.12
  11.7 1.0 copy-done.14
  12.7 1.0 copy-done.15
  13.6 1.0 copy-done.16
  14.6 0.9 copy-done.19
  15.5 0.9 copy-done.20
  16.5 0.7 copy-done.22
  17.2 0.9 copy-done.24
  18.1 0.9 copy-done.25
  19.0 0.7 copy-done.27
  19.7 0.7 copy-done.30
  20.4 0.7 copy-done.34
  21.1 20.5 %blocks.1 = (f32[2,304,256]{2,1,0:T(8,128)S(1)}, f32[2,304,256]{2,1,0:T(8,128)}, bf16[2,3328,256]{2,1,0:T(8,128)(2,1)}) custom-call(s32[1]{0:T(128)} %bitcast.sec_ref, bf16[608,256]{1,0:T(8,128)(2,1)S(1)} %copy-done.13, bf16[608,256]{1,0:T(8,128)(2,1)S(1)} %copy-done.14, f32[1,3328]{1,0:T(1,128)S(1)} %copy-done.27, f32[1,3328]{1,0:T(1,128)S(1)} %copy-done.34, ...), custom_call_target="tpu_custom_call" | custom-call | tf_op jit(solution)/shard_map/blocks/pallas_call | solution.py:449
  41.7 2.8 %slice_bitcast_fusion = bf16[3328,256]{1,0:T(8,128)(2,1)} fusion(bf16[2,3328,256]{2,1,0:T(8,128)(2,1)} %get-tuple-element.65), kind=kLoop, calls=%fused_computation.2 | loop fusion | bytes 3407872 | tf_op jit(solution)/shard_map/squeeze | solution.py:629
  44.9 0.7 slice_bitcast_fusion.1
  45.8 0.7 slice_bitcast_fusion.2
  46.9 1.9 %collective-permute-done.5 = f32[304,256]{1,0:T(8,128)S(1)} collective-permute-done((f32[304,256]{1,0:T(8,128)}, f32[304,256]{1,0:T(8,128)S(1)}, u32[]{:S(2)}, u32[]{:S(2)}) %collective-permute-start.5) | collective-permute-done | bytes 311328 | tf_op jit(solution)/shard_map/ppermute | solution.py:569
  48.8 1.0 fusion.5
  49.9 2.4 %fusion = bf16[3328,256]{1,0:T(8,128)(2,1)S(1)} fusion(bf16[3328,256]{1,0:T(8,128)(2,1)} %collective-permute-done.6, bf16[2,3328,256]{2,1,0:T(8,128)(2,1)} %get-tuple-element.65), kind=kLoop, calls=%fused_computation.1 | loop fusion | flops 3407872 | bytes 5111808 | tf_op jit(solution)/shard_map/convert_element_type | solution.py:630
  52.4 3.0 %collective-permute-start.15 = (bf16[2,2,2,64,256]{4,3,2,1,0:T(8,128)(2,1)S(1)}, bf16[2,2,2,64,256]{4,3,2,1,0:T(8,128)(2,1)S(1)}, u32[]{:S(2)}, u32[]{:S(2)}) collective-permute-start(bf16[2,2,2,64,256]{4,3,2,1,0:T(8,128)(2,1)S(1)} %dynamic-slice_bitcast_fusion.1), channel_id=1, source_target_pairs={{0,2},{1,3},{2,0},{3,1},{4,6},{5,7},{6,4},{7,5},{8,10},{9,11},{10,... | collective-permute-start | bytes 786440 | tf_op jit(solution)/shard_map/ppermute | solution.py:581
  55.3 0.9 pad_maximum_fusion.3
  56.3 1.6 %collective-permute-start.7 = (bf16[2,2,2,64,256]{4,3,2,1,0:T(8,128)(2,1)S(1)}, bf16[2,2,2,64,256]{4,3,2,1,0:T(8,128)(2,1)S(1)}, u32[]{:S(2)}, u32[]{:S(2)}) collective-permute-start(bf16[2,2,2,64,256]{4,3,2,1,0:T(8,128)(2,1)S(1)} %dynamic-slice_bitcast_fusion.2), channel_id=1, source_target_pairs={{0,1},{1,0},{2,3},{3,2},{4,5},{5,4},{6,7},{7,6},{8,9},{9,8},{10,11... | collective-permute-start | bytes 786440 | tf_op jit(solution)/shard_map/ppermute | solution.py:581
  57.9 1.6 %collective-permute-start.23 = (bf16[2,2,2,80,256]{4,3,2,1,0:T(8,128)(2,1)S(1)}, bf16[2,2,2,80,256]{4,3,2,1,0:T(8,128)(2,1)S(1)}, u32[]{:S(2)}, u32[]{:S(2)}) collective-permute-start(bf16[2,2,2,80,256]{4,3,2,1,0:T(8,128)(2,1)S(1)} %dynamic-slice_bitcast_fusion), channel_id=1, source_target_pairs={{0,4},{1,5},{2,6},{3,7},{4,0},{5,1},{6,2},{7,3},{8,12},{9,13},{10,... | collective-permute-start | bytes 983048 | tf_op jit(solution)/shard_map/ppermute | solution.py:581
  59.5 2.4 %collective-permute-done.15 = bf16[2,2,2,64,256]{4,3,2,1,0:T(8,128)(2,1)S(1)} collective-permute-done((bf16[2,2,2,64,256]{4,3,2,1,0:T(8,128)(2,1)S(1)}, bf16[2,2,2,64,256]{4,3,2,1,0:T(8,128)(2,1)S(1)}, u32[]{:S(2)}, u32[]{:S(2)}) %collective-permute-start.15) | collective-permute-done | bytes 262176 | tf_op jit(solution)/shard_map/ppermute | solution.py:581
  62.0 1.9 %collective-permute-start.16 = (bf16[2,2,64,256]{3,2,1,0:T(8,128)(2,1)S(1)}, bf16[2,2,64,256]{3,2,1,0:T(8,128)(2,1)S(1)}, u32[]{:S(2)}, u32[]{:S(2)}) collective-permute-start(bf16[2,2,64,256]{3,2,1,0:T(8,128)(2,1)S(1)} %dynamic-slice_bitcast_fusion.4), channel_id=1, source_target_pairs={{0,4},{1,5},{2,6},{3,7},{4,0},{5,1},{6,2},{7,3},{8,12},{9,13},{10,... | collective-permute-start | bytes 393224 | tf_op jit(solution)/shard_map/ppermute | solution.py:581
  64.5 1.1 collective-permute-start.8
  65.6 2.9 %collective-permute-done.23 = bf16[2,2,2,80,256]{4,3,2,1,0:T(8,128)(2,1)S(1)} collective-permute-done((bf16[2,2,2,80,256]{4,3,2,1,0:T(8,128)(2,1)S(1)}, bf16[2,2,2,80,256]{4,3,2,1,0:T(8,128)(2,1)S(1)}, u32[]{:S(2)}, u32[]{:S(2)}) %collective-permute-start.23) | collective-permute-done | bytes 327712 | tf_op jit(solution)/shard_map/ppermute | solution.py:581
  69.2 0.7 collective-permute-done.16
  70.0 0.9 collective-permute-start.17
  71.0 1.6 %collective-permute-start.9 = (bf16[2,64,256]{2,1,0:T(8,128)(2,1)S(1)}, bf16[2,64,256]{2,1,0:T(8,128)(2,1)S(1)}, u32[]{:S(2)}, u32[]{:S(2)}) collective-permute-start(bf16[2,64,256]{2,1,0:T(8,128)(2,1)S(1)} %dynamic-slice_bitcast_fusion.8), channel_id=1, source_target_pairs={{0,4},{1,5},{2,6},{3,7},{4,0},{5,1},{6,2},{7,3},{8,12},{9,13},{10,... | collective-permute-start | bytes 196616 | tf_op jit(solution)/shard_map/ppermute | solution.py:581
  72.6 2.1 %collective-permute-done.17 = bf16[2,64,256]{2,1,0:T(8,128)(2,1)S(1)} collective-permute-done((bf16[2,64,256]{2,1,0:T(8,128)(2,1)S(1)}, bf16[2,64,256]{2,1,0:T(8,128)(2,1)S(1)}, u32[]{:S(2)}, u32[]{:S(2)}) %collective-permute-start.17) | collective-permute-done | bytes 65568 | tf_op jit(solution)/shard_map/ppermute | solution.py:581
  74.8 2.7 %collective-permute-start.18 = (bf16[64,256]{1,0:T(8,128)(2,1)S(1)}, bf16[64,256]{1,0:T(8,128)(2,1)S(1)}, u32[]{:S(2)}, u32[]{:S(2)}) collective-permute-start(bf16[64,256]{1,0:T(8,128)(2,1)S(1)} %dynamic-slice_bitcast_fusion.10), channel_id=1, source_target_pairs={{0,8},{1,9},{2,10},{3,11},{4,12},{5,13},{6,14},{7,15},{8,0},{9,1},... | collective-permute-start | bytes 98312 | tf_op jit(solution)/shard_map/ppermute | solution.py:581
  77.5 0.7 collective-permute-start.10
  78.2 1.8 %collective-permute-done.18 = bf16[64,256]{1,0:T(8,128)(2,1)S(1)} collective-permute-done((bf16[64,256]{1,0:T(8,128)(2,1)S(1)}, bf16[64,256]{1,0:T(8,128)(2,1)S(1)}, u32[]{:S(2)}, u32[]{:S(2)}) %collective-permute-start.18) | collective-permute-done | bytes 32800 | tf_op jit(solution)/shard_map/ppermute | solution.py:581
  79.9 2.7 %collective-permute-start.19 = (bf16[64,256]{1,0:T(8,128)(2,1)S(1)}, bf16[64,256]{1,0:T(8,128)(2,1)S(1)}, u32[]{:S(2)}, u32[]{:S(2)}) collective-permute-start(bf16[64,256]{1,0:T(8,128)(2,1)S(1)} %fusion.15), channel_id=1, source_target_pairs={{0,8},{1,9},{2,10},{3,11},{4,12},{5,13},{6,14},{7,15},{8,0},{9,1},... | collective-permute-start | bytes 98312 | tf_op jit(solution)/shard_map/ppermute | solution.py:581
  82.7 0.7 collective-permute-start.11
  83.7 1.1 collective-permute-done.19
  85.3 2.7 %collective-permute-done.11 = bf16[64,256]{1,0:T(8,128)(2,1)S(1)} collective-permute-done((bf16[64,256]{1,0:T(8,128)(2,1)S(1)}, bf16[64,256]{1,0:T(8,128)(2,1)S(1)}, u32[]{:S(2)}, u32[]{:S(2)}) %collective-permute-start.11) | collective-permute-done | bytes 32800 | tf_op jit(solution)/shard_map/ppermute | solution.py:581
  88.1 2.7 %collective-permute-start.12 = (bf16[2,64,256]{2,1,0:T(8,128)(2,1)S(1)}, bf16[2,64,256]{2,1,0:T(8,128)(2,1)S(1)}, u32[]{:S(2)}, u32[]{:S(2)}) collective-permute-start(bf16[2,64,256]{2,1,0:T(8,128)(2,1)S(1)} %pad_maximum_fusion.13), channel_id=1, source_target_pairs={{0,4},{1,5},{2,6},{3,7},{4,0},{5,1},{6,2},{7,3},{8,12},{9,13},{10,... | collective-permute-start | bytes 196616 | tf_op jit(solution)/shard_map/ppermute | solution.py:581
  90.8 0.6 collective-permute-start.26
  91.5 1.8 %collective-permute-start.21 = (bf16[2,2,64,256]{3,2,1,0:T(8,128)(2,1)S(1)}, bf16[2,2,64,256]{3,2,1,0:T(8,128)(2,1)S(1)}, u32[]{:S(2)}, u32[]{:S(2)}) collective-permute-start(bf16[2,2,64,256]{3,2,1,0:T(8,128)(2,1)S(1)} %pad_maximum_fusion.11), channel_id=1, source_target_pairs={{0,4},{1,5},{2,6},{3,7},{4,0},{5,1},{6,2},{7,3},{8,12},{9,13},{10,... | collective-permute-start | bytes 393224 | tf_op jit(solution)/shard_map/ppermute | solution.py:581
  93.3 2.6 %collective-permute-done.26 = bf16[80,256]{1,0:T(8,128)(2,1)S(1)} collective-permute-done((bf16[80,256]{1,0:T(8,128)(2,1)S(1)}, bf16[80,256]{1,0:T(8,128)(2,1)S(1)}, u32[]{:S(2)}, u32[]{:S(2)}) %collective-permute-start.26) | collective-permute-done | bytes 40992 | tf_op jit(solution)/shard_map/ppermute | solution.py:581
  97.1 3.8 %collective-permute-done.27 = bf16[80,256]{1,0:T(8,128)(2,1)S(1)} collective-permute-done((bf16[80,256]{1,0:T(8,128)(2,1)S(1)}, bf16[80,256]{1,0:T(8,128)(2,1)S(1)}, u32[]{:S(2)}, u32[]{:S(2)}) %collective-permute-start.27) | collective-permute-done | bytes 40992 | tf_op jit(solution)/shard_map/ppermute | solution.py:581
  101.6 1.6 %collective-permute-start.22 = (bf16[2,2,2,64,256]{4,3,2,1,0:T(8,128)(2,1)S(1)}, bf16[2,2,2,64,256]{4,3,2,1,0:T(8,128)(2,1)S(1)}, u32[]{:S(2)}, u32[]{:S(2)}) collective-permute-start(bf16[2,2,2,64,256]{4,3,2,1,0:T(8,128)(2,1)S(1)} %pad_maximum_fusion.8), channel_id=1, source_target_pairs={{0,2},{1,3},{2,0},{3,1},{4,6},{5,7},{6,4},{7,5},{8,10},{9,11},{10,... | collective-permute-start | bytes 786440 | tf_op jit(solution)/shard_map/ppermute | solution.py:581
  103.1 2.3 %collective-permute-done.28 = bf16[2,80,256]{2,1,0:T(8,128)(2,1)S(1)} collective-permute-done((bf16[2,80,256]{2,1,0:T(8,128)(2,1)S(1)}, bf16[2,80,256]{2,1,0:T(8,128)(2,1)S(1)}, u32[]{:S(2)}, u32[]{:S(2)}) %collective-permute-start.28) | collective-permute-done | bytes 81952 | tf_op jit(solution)/shard_map/ppermute | solution.py:581
  106.1 1.6 %collective-permute-start.14 = (bf16[2,2,2,64,256]{4,3,2,1,0:T(8,128)(2,1)S(1)}, bf16[2,2,2,64,256]{4,3,2,1,0:T(8,128)(2,1)S(1)}, u32[]{:S(2)}, u32[]{:S(2)}) collective-permute-start(bf16[2,2,2,64,256]{4,3,2,1,0:T(8,128)(2,1)S(1)} %pad_maximum_fusion.7), channel_id=1, source_target_pairs={{0,1},{1,0},{2,3},{3,2},{4,5},{5,4},{6,7},{7,6},{8,9},{9,8},{10,11... | collective-permute-start | bytes 786440 | tf_op jit(solution)/shard_map/ppermute | solution.py:581
  107.7 3.2 %collective-permute-done.29 = bf16[2,2,80,256]{3,2,1,0:T(8,128)(2,1)S(1)} collective-permute-done((bf16[2,2,80,256]{3,2,1,0:T(8,128)(2,1)S(1)}, bf16[2,2,80,256]{3,2,1,0:T(8,128)(2,1)S(1)}, u32[]{:S(2)}, u32[]{:S(2)}) %collective-permute-start.29) | collective-permute-done | bytes 163872 | tf_op jit(solution)/shard_map/ppermute | solution.py:581
  111.1 2.5 %collective-permute-done.14 = bf16[2,2,2,64,256]{4,3,2,1,0:T(8,128)(2,1)S(1)} collective-permute-done((bf16[2,2,2,64,256]{4,3,2,1,0:T(8,128)(2,1)S(1)}, bf16[2,2,2,64,256]{4,3,2,1,0:T(8,128)(2,1)S(1)}, u32[]{:S(2)}, u32[]{:S(2)}) %collective-permute-start.14) | collective-permute-done | bytes 262176 | tf_op jit(solution)/shard_map/ppermute | solution.py:581
  113.8 4.3 %collective-permute-done.30 = bf16[2,2,2,80,256]{4,3,2,1,0:T(8,128)(2,1)S(1)} collective-permute-done((bf16[2,2,2,80,256]{4,3,2,1,0:T(8,128)(2,1)S(1)}, bf16[2,2,2,80,256]{4,3,2,1,0:T(8,128)(2,1)S(1)}, u32[]{:S(2)}, u32[]{:S(2)}) %collective-permute-start.30) | collective-permute-done | bytes 327712 | tf_op jit(solution)/shard_map/ppermute | solution.py:581
  118.6 0.9 pad_maximum_fusion.2
  120.9 6.6 %optimizer.1 = (f32[1,3328]{1,0:T(1,128)}, f32[9,256]{1,0:T(8,128)S(1)}, f32[256,768]{1,0:T(8,128)}, f32[256,256]{1,0:T(8,128)}, f32[256,1024]{1,0:T(8,128)}, /*...) custom-call(f32[8,128]{1,0:T(8,128)S(1)} %squares.1.refs_0_, ...), custom_call_target="tpu_custom_call" | custom-call | tf_op jit(solution)/shard_map/optimizer/pallas_call | solution.py:555
  128.0 0.6 copy.58
  128.6 0.6 copy.59
  129.2 0.6 copy.60
  129.8 0.6 copy.61
  (151 shorter events, 10.3 us)
Async XLA Ops:
  0.7 2.2 %copy-start = (f32[1,256,1024]{2,1,0:T(8,128)S(1)}, f32[1,256,1024]{2,1,0:T(8,128)}, u32[]{:S(2)}) copy-start(f32[1,256,1024]{2,1,0:T(8,128)} %param.33) | copy-start | bytes 3145732
  2.9 1.7 %copy-start.1 = (f32[1,1024,256]{2,1,0:T(8,128)S(1)}, f32[1,1024,256]{2,1,0:T(8,128)}, u32[]{:S(2)}) copy-start(f32[1,1024,256]{2,1,0:T(8,128)} %param.34) | copy-start | bytes 3145732
  3.0 1.9 %copy-start.26 = (f32[1,3328]{1,0:T(1,128)S(1)}, f32[1,3328]{1,0:T(1,128)}, u32[]{:S(2)}) copy-start(f32[1,3328]{1,0:T(1,128)} %refs_12_.1) | copy-start | bytes 39940
  3.0 2.2 %copy-start.36 = (f32[1,9,256]{2,0,1:T(1,128)S(1)}, f32[1,9,256]{2,0,1:T(1,128)}, u32[]{:S(2)}) copy-start(f32[1,9,256]{2,0,1:T(1,128)} %param.30) | copy-start | bytes 27652
  3.0 6.6 %copy-start.13 = (bf16[608,256]{1,0:T(8,128)(2,1)S(1)}, bf16[608,256]{1,0:T(8,128)(2,1)}, u32[]{:S(2)}) copy-start(bf16[608,256]{1,0:T(8,128)(2,1)} %x_ref.1) | copy-start | bytes 933892
  4.1 5.5 %collective-permute-start.2 = (bf16[256,2048]{1,0:T(8,128)(2,1)}, bf16[256,2048]{1,0:T(8,128)(2,1)}, u32[]{:S(2)}, u32[]{:S(2)}) collective-permute-start(bf16[256,2048]{1,0:T(8,128)(2,1)} %pad_maximum_fusion.wide_own), channel_id=1, source_target_pairs={{0,16},{16,0},{1,17},{17,1},{2,18},{18,2},{3,19},{19,3},{4,20},{20... | collective-permute-start | bytes 3145736 | tf_op jit(solution)/shard_map/ppermute | solution.py:569
  4.6 4.2 %collective-permute-start.3 = (bf16[1024,256]{1,0:T(8,128)(2,1)S(1)}, bf16[1024,256]{1,0:T(8,128)(2,1)S(1)}, u32[]{:S(2)}, u32[]{:S(2)}) collective-permute-start(bf16[1024,256]{1,0:T(8,128)(2,1)S(1)} %bitcast_convert_fusion.deep_own), channel_id=1, source_target_pairs={{0,16},{16,0},{1,17},{17,1},{2,18},{18,2},{3,19},{19,3},{4,20},{20... | collective-permute-start | bytes 1572872 | tf_op jit(solution)/shard_map/ppermute | solution.py:569
  4.9 3.4 %collective-permute-start = (f32[1,3328]{1,0:T(1,128)S(1)}, f32[1,3328]{1,0:T(1,128)S(1)}, u32[]{:S(2)}, u32[]{:S(2)}) collective-permute-start(f32[1,3328]{1,0:T(1,128)S(1)} %copy-done.26), channel_id=1, source_target_pairs={{0,16},{16,0},{1,17},{17,1},{2,18},{18,2},{3,19},{19,3},{4,20},{20... | collective-permute-start | bytes 39944 | tf_op jit(solution)/shard_map/ppermute | solution.py:569
  5.2 2.4 %collective-permute-start.1 = (f32[9,256]{1,0:T(8,128)S(1)}, f32[9,256]{1,0:T(8,128)S(1)}, u32[]{:S(2)}, u32[]{:S(2)}) collective-permute-start(f32[9,256]{1,0:T(8,128)S(1)} %bitcast.221), channel_id=1, source_target_pairs={{0,16},{16,0},{1,17},{17,1},{2,18},{18,2},{3,19},{19,3},{4,20},{20... | collective-permute-start | bytes 27656 | tf_op jit(solution)/shard_map/ppermute | solution.py:569
  8.9 0.8 copy-start.10
  9.7 1.0 copy-start.11
  10.7 1.0 copy-start.12
  11.7 1.0 copy-start.14
  12.7 1.0 copy-start.15
  13.6 1.0 copy-start.16
  14.6 0.9 copy-start.19
  15.5 0.9 copy-start.20
  17.2 0.9 copy-start.24
  18.1 0.9 copy-start.25
  41.7 3.2 %copy-start.35 = (f32[2,304,256]{2,1,0:T(8,128)S(1)}, f32[2,304,256]{2,1,0:T(8,128)}, u32[]{:S(2)}) copy-start(f32[2,304,256]{2,1,0:T(8,128)} %get-tuple-element.64) | copy-start | bytes 1867780
  41.7 5.2 %copy-start.37 = (f32[1,9,256]{2,0,1:T(1,128)S(1)}, f32[1,9,256]{2,0,1:T(1,128)}, u32[]{:S(2)}) copy-start(f32[1,9,256]{2,0,1:T(1,128)} %param.42) | copy-start | bytes 27652
  41.7 5.2 %copy-start.38 = (f32[1,9,256]{2,0,1:T(1,128)S(1)}, f32[1,9,256]{2,0,1:T(1,128)}, u32[]{:S(2)}) copy-start(f32[1,9,256]{2,0,1:T(1,128)} %param.36) | copy-start | bytes 27652
  44.5 5.3 %collective-permute-start.6 = (bf16[3328,256]{1,0:T(8,128)(2,1)}, bf16[3328,256]{1,0:T(8,128)(2,1)}, u32[]{:S(2)}, u32[]{:S(2)}) collective-permute-start(bf16[3328,256]{1,0:T(8,128)(2,1)} %slice_bitcast_fusion), channel_id=1, source_target_pairs={{0,16},{16,0},{1,17},{17,1},{2,18},{18,2},{3,19},{19,3},{4,20},{20... | collective-permute-start | bytes 5111816 | tf_op jit(solution)/shard_map/ppermute | solution.py:569
  45.6 3.1 %collective-permute-start.5 = (f32[304,256]{1,0:T(8,128)}, f32[304,256]{1,0:T(8,128)S(1)}, u32[]{:S(2)}, u32[]{:S(2)}) collective-permute-start(f32[304,256]{1,0:T(8,128)} %slice_bitcast_fusion.1), channel_id=1, source_target_pairs={{0,16},{16,0},{1,17},{17,1},{2,18},{18,2},{3,19},{19,3},{4,20},{20... | collective-permute-start | bytes 933896 | tf_op jit(solution)/shard_map/ppermute | solution.py:569
  46.5 3.3 %collective-permute-start.4 = (f32[304,256]{1,0:T(8,128)}, f32[304,256]{1,0:T(8,128)S(1)}, u32[]{:S(2)}, u32[]{:S(2)}) collective-permute-start(f32[304,256]{1,0:T(8,128)} %slice_bitcast_fusion.2), channel_id=1, source_target_pairs={{0,16},{16,0},{1,17},{17,1},{2,18},{18,2},{3,19},{19,3},{4,20},{20... | collective-permute-start | bytes 933896 | tf_op jit(solution)/shard_map/ppermute | solution.py:569
  52.4 9.6 %collective-permute-start.15 = (bf16[2,2,2,64,256]{4,3,2,1,0:T(8,128)(2,1)S(1)}, bf16[2,2,2,64,256]{4,3,2,1,0:T(8,128)(2,1)S(1)}, u32[]{:S(2)}, u32[]{:S(2)}) collective-permute-start(bf16[2,2,2,64,256]{4,3,2,1,0:T(8,128)(2,1)S(1)} %dynamic-slice_bitcast_fusion.1), channel_id=1, source_target_pairs={{0,2},{1,3},{2,0},{3,1},{4,6},{5,7},{6,4},{7,5},{8,10},{9,11},{10,... | collective-permute-start | bytes 786440 | tf_op jit(solution)/shard_map/ppermute | solution.py:581
  56.3 8.1 %collective-permute-start.7 = (bf16[2,2,2,64,256]{4,3,2,1,0:T(8,128)(2,1)S(1)}, bf16[2,2,2,64,256]{4,3,2,1,0:T(8,128)(2,1)S(1)}, u32[]{:S(2)}, u32[]{:S(2)}) collective-permute-start(bf16[2,2,2,64,256]{4,3,2,1,0:T(8,128)(2,1)S(1)} %dynamic-slice_bitcast_fusion.2), channel_id=1, source_target_pairs={{0,1},{1,0},{2,3},{3,2},{4,5},{5,4},{6,7},{7,6},{8,9},{9,8},{10,11... | collective-permute-start | bytes 786440 | tf_op jit(solution)/shard_map/ppermute | solution.py:581
  57.9 10.7 %collective-permute-start.23 = (bf16[2,2,2,80,256]{4,3,2,1,0:T(8,128)(2,1)S(1)}, bf16[2,2,2,80,256]{4,3,2,1,0:T(8,128)(2,1)S(1)}, u32[]{:S(2)}, u32[]{:S(2)}) collective-permute-start(bf16[2,2,2,80,256]{4,3,2,1,0:T(8,128)(2,1)S(1)} %dynamic-slice_bitcast_fusion), channel_id=1, source_target_pairs={{0,4},{1,5},{2,6},{3,7},{4,0},{5,1},{6,2},{7,3},{8,12},{9,13},{10,... | collective-permute-start | bytes 983048 | tf_op jit(solution)/shard_map/ppermute | solution.py:581
  62.0 7.9 %collective-permute-start.16 = (bf16[2,2,64,256]{3,2,1,0:T(8,128)(2,1)S(1)}, bf16[2,2,64,256]{3,2,1,0:T(8,128)(2,1)S(1)}, u32[]{:S(2)}, u32[]{:S(2)}) collective-permute-start(bf16[2,2,64,256]{3,2,1,0:T(8,128)(2,1)S(1)} %dynamic-slice_bitcast_fusion.4), channel_id=1, source_target_pairs={{0,4},{1,5},{2,6},{3,7},{4,0},{5,1},{6,2},{7,3},{8,12},{9,13},{10,... | collective-permute-start | bytes 393224 | tf_op jit(solution)/shard_map/ppermute | solution.py:581
  64.5 6.4 %collective-permute-start.8 = (bf16[2,2,64,256]{3,2,1,0:T(8,128)(2,1)S(1)}, bf16[2,2,64,256]{3,2,1,0:T(8,128)(2,1)S(1)}, u32[]{:S(2)}, u32[]{:S(2)}) collective-permute-start(bf16[2,2,64,256]{3,2,1,0:T(8,128)(2,1)S(1)} %dynamic-slice_bitcast_fusion.5), channel_id=1, source_target_pairs={{0,2},{1,3},{2,0},{3,1},{4,6},{5,7},{6,4},{7,5},{8,10},{9,11},{10,... | collective-permute-start | bytes 393224 | tf_op jit(solution)/shard_map/ppermute | solution.py:581
  68.7 14.7 %collective-permute-start.24 = (bf16[2,2,80,256]{3,2,1,0:T(8,128)(2,1)S(1)}, bf16[2,2,80,256]{3,2,1,0:T(8,128)(2,1)S(1)}, u32[]{:S(2)}, u32[]{:S(2)}) collective-permute-start(bf16[2,2,80,256]{3,2,1,0:T(8,128)(2,1)S(1)} %dynamic-slice_bitcast_fusion.3), channel_id=1, source_target_pairs={{0,1},{1,0},{2,3},{3,2},{4,5},{5,4},{6,7},{7,6},{8,9},{9,8},{10,11... | collective-permute-start | bytes 491528 | tf_op jit(solution)/shard_map/ppermute | solution.py:581
  70.0 4.7 %collective-permute-start.17 = (bf16[2,64,256]{2,1,0:T(8,128)(2,1)S(1)}, bf16[2,64,256]{2,1,0:T(8,128)(2,1)S(1)}, u32[]{:S(2)}, u32[]{:S(2)}) collective-permute-start(bf16[2,64,256]{2,1,0:T(8,128)(2,1)S(1)} %dynamic-slice_bitcast_fusion.7), channel_id=1, source_target_pairs={{0,1},{1,0},{2,3},{3,2},{4,5},{5,4},{6,7},{7,6},{8,9},{9,8},{10,11... | collective-permute-start | bytes 196616 | tf_op jit(solution)/shard_map/ppermute | solution.py:581
  71.0 6.5 %collective-permute-start.9 = (bf16[2,64,256]{2,1,0:T(8,128)(2,1)S(1)}, bf16[2,64,256]{2,1,0:T(8,128)(2,1)S(1)}, u32[]{:S(2)}, u32[]{:S(2)}) collective-permute-start(bf16[2,64,256]{2,1,0:T(8,128)(2,1)S(1)} %dynamic-slice_bitcast_fusion.8), channel_id=1, source_target_pairs={{0,4},{1,5},{2,6},{3,7},{4,0},{5,1},{6,2},{7,3},{8,12},{9,13},{10,... | collective-permute-start | bytes 196616 | tf_op jit(solution)/shard_map/ppermute | solution.py:581
  74.8 5.2 %collective-permute-start.18 = (bf16[64,256]{1,0:T(8,128)(2,1)S(1)}, bf16[64,256]{1,0:T(8,128)(2,1)S(1)}, u32[]{:S(2)}, u32[]{:S(2)}) collective-permute-start(bf16[64,256]{1,0:T(8,128)(2,1)S(1)} %dynamic-slice_bitcast_fusion.10), channel_id=1, source_target_pairs={{0,8},{1,9},{2,10},{3,11},{4,12},{5,13},{6,14},{7,15},{8,0},{9,1},... | collective-permute-start | bytes 98312 | tf_op jit(solution)/shard_map/ppermute | solution.py:581
  77.5 5.2 %collective-permute-start.10 = (bf16[64,256]{1,0:T(8,128)(2,1)S(1)}, bf16[64,256]{1,0:T(8,128)(2,1)S(1)}, u32[]{:S(2)}, u32[]{:S(2)}) collective-permute-start(bf16[64,256]{1,0:T(8,128)(2,1)S(1)} %dynamic-slice_bitcast_fusion.11), channel_id=1, source_target_pairs={{0,8},{1,9},{2,10},{3,11},{4,12},{5,13},{6,14},{7,15},{8,0},{9,1},... | collective-permute-start | bytes 98312 | tf_op jit(solution)/shard_map/ppermute | solution.py:581
  79.9 4.9 %collective-permute-start.19 = (bf16[64,256]{1,0:T(8,128)(2,1)S(1)}, bf16[64,256]{1,0:T(8,128)(2,1)S(1)}, u32[]{:S(2)}, u32[]{:S(2)}) collective-permute-start(bf16[64,256]{1,0:T(8,128)(2,1)S(1)} %fusion.15), channel_id=1, source_target_pairs={{0,8},{1,9},{2,10},{3,11},{4,12},{5,13},{6,14},{7,15},{8,0},{9,1},... | collective-permute-start | bytes 98312 | tf_op jit(solution)/shard_map/ppermute | solution.py:581
  82.7 5.4 %collective-permute-start.11 = (bf16[64,256]{1,0:T(8,128)(2,1)S(1)}, bf16[64,256]{1,0:T(8,128)(2,1)S(1)}, u32[]{:S(2)}, u32[]{:S(2)}) collective-permute-start(bf16[64,256]{1,0:T(8,128)(2,1)S(1)} %fusion.16), channel_id=1, source_target_pairs={{0,8},{1,9},{2,10},{3,11},{4,12},{5,13},{6,14},{7,15},{8,0},{9,1},... | collective-permute-start | bytes 98312 | tf_op jit(solution)/shard_map/ppermute | solution.py:581
  83.5 7.3 %collective-permute-start.25 = (bf16[2,80,256]{2,1,0:T(8,128)(2,1)S(1)}, bf16[2,80,256]{2,1,0:T(8,128)(2,1)S(1)}, u32[]{:S(2)}, u32[]{:S(2)}) collective-permute-start(bf16[2,80,256]{2,1,0:T(8,128)(2,1)S(1)} %dynamic-slice_bitcast_fusion.6), channel_id=1, source_target_pairs={{0,2},{1,3},{2,0},{3,1},{4,6},{5,7},{6,4},{7,5},{8,10},{9,11},{10,... | collective-permute-start | bytes 245768 | tf_op jit(solution)/shard_map/ppermute | solution.py:581
  84.9 6.6 %collective-permute-start.20 = (bf16[2,64,256]{2,1,0:T(8,128)(2,1)S(1)}, bf16[2,64,256]{2,1,0:T(8,128)(2,1)S(1)}, u32[]{:S(2)}, u32[]{:S(2)}) collective-permute-start(bf16[2,64,256]{2,1,0:T(8,128)(2,1)S(1)} %pad_maximum_fusion.14), channel_id=1, source_target_pairs={{0,1},{1,0},{2,3},{3,2},{4,5},{5,4},{6,7},{7,6},{8,9},{9,8},{10,11... | collective-permute-start | bytes 196616 | tf_op jit(solution)/shard_map/ppermute | solution.py:581
  88.1 5.1 %collective-permute-start.12 = (bf16[2,64,256]{2,1,0:T(8,128)(2,1)S(1)}, bf16[2,64,256]{2,1,0:T(8,128)(2,1)S(1)}, u32[]{:S(2)}, u32[]{:S(2)}) collective-permute-start(bf16[2,64,256]{2,1,0:T(8,128)(2,1)S(1)} %pad_maximum_fusion.13), channel_id=1, source_target_pairs={{0,4},{1,5},{2,6},{3,7},{4,0},{5,1},{6,2},{7,3},{8,12},{9,13},{10,... | collective-permute-start | bytes 196616 | tf_op jit(solution)/shard_map/ppermute | solution.py:581
  90.8 5.1 %collective-permute-start.26 = (bf16[80,256]{1,0:T(8,128)(2,1)S(1)}, bf16[80,256]{1,0:T(8,128)(2,1)S(1)}, u32[]{:S(2)}, u32[]{:S(2)}) collective-permute-start(bf16[80,256]{1,0:T(8,128)(2,1)S(1)} %dynamic-slice_bitcast_fusion.9), channel_id=1, source_target_pairs={{0,8},{1,9},{2,10},{3,11},{4,12},{5,13},{6,14},{7,15},{8,0},{9,1},... | collective-permute-start | bytes 122888 | tf_op jit(solution)/shard_map/ppermute | solution.py:581
  91.5 10.0 %collective-permute-start.21 = (bf16[2,2,64,256]{3,2,1,0:T(8,128)(2,1)S(1)}, bf16[2,2,64,256]{3,2,1,0:T(8,128)(2,1)S(1)}, u32[]{:S(2)}, u32[]{:S(2)}) collective-permute-start(bf16[2,2,64,256]{3,2,1,0:T(8,128)(2,1)S(1)} %pad_maximum_fusion.11), channel_id=1, source_target_pairs={{0,4},{1,5},{2,6},{3,7},{4,0},{5,1},{6,2},{7,3},{8,12},{9,13},{10,... | collective-permute-start | bytes 393224 | tf_op jit(solution)/shard_map/ppermute | solution.py:581
  95.9 5.0 %collective-permute-start.27 = (bf16[80,256]{1,0:T(8,128)(2,1)S(1)}, bf16[80,256]{1,0:T(8,128)(2,1)S(1)}, u32[]{:S(2)}, u32[]{:S(2)}) collective-permute-start(bf16[80,256]{1,0:T(8,128)(2,1)S(1)} %fusion.14), channel_id=1, source_target_pairs={{0,8},{1,9},{2,10},{3,11},{4,12},{5,13},{6,14},{7,15},{8,0},{9,1},... | collective-permute-start | bytes 122888 | tf_op jit(solution)/shard_map/ppermute | solution.py:581
  96.5 9.6 %collective-permute-start.13 = (bf16[2,2,64,256]{3,2,1,0:T(8,128)(2,1)S(1)}, bf16[2,2,64,256]{3,2,1,0:T(8,128)(2,1)S(1)}, u32[]{:S(2)}, u32[]{:S(2)}) collective-permute-start(bf16[2,2,64,256]{3,2,1,0:T(8,128)(2,1)S(1)} %pad_maximum_fusion.10), channel_id=1, source_target_pairs={{0,2},{1,3},{2,0},{3,1},{4,6},{5,7},{6,4},{7,5},{8,10},{9,11},{10,... | collective-permute-start | bytes 393224 | tf_op jit(solution)/shard_map/ppermute | solution.py:581
  100.9 4.5 %collective-permute-start.28 = (bf16[2,80,256]{2,1,0:T(8,128)(2,1)S(1)}, bf16[2,80,256]{2,1,0:T(8,128)(2,1)S(1)}, u32[]{:S(2)}, u32[]{:S(2)}) collective-permute-start(bf16[2,80,256]{2,1,0:T(8,128)(2,1)S(1)} %pad_maximum_fusion.12), channel_id=1, source_target_pairs={{0,2},{1,3},{2,0},{3,1},{4,6},{5,7},{6,4},{7,5},{8,10},{9,11},{10,... | collective-permute-start | bytes 245768 | tf_op jit(solution)/shard_map/ppermute | solution.py:581
  101.6 9.4 %collective-permute-start.22 = (bf16[2,2,2,64,256]{4,3,2,1,0:T(8,128)(2,1)S(1)}, bf16[2,2,2,64,256]{4,3,2,1,0:T(8,128)(2,1)S(1)}, u32[]{:S(2)}, u32[]{:S(2)}) collective-permute-start(bf16[2,2,2,64,256]{4,3,2,1,0:T(8,128)(2,1)S(1)} %pad_maximum_fusion.8), channel_id=1, source_target_pairs={{0,2},{1,3},{2,0},{3,1},{4,6},{5,7},{6,4},{7,5},{8,10},{9,11},{10,... | collective-permute-start | bytes 786440 | tf_op jit(solution)/shard_map/ppermute | solution.py:581
  105.5 5.4 %collective-permute-start.29 = (bf16[2,2,80,256]{3,2,1,0:T(8,128)(2,1)S(1)}, bf16[2,2,80,256]{3,2,1,0:T(8,128)(2,1)S(1)}, u32[]{:S(2)}, u32[]{:S(2)}) collective-permute-start(bf16[2,2,80,256]{3,2,1,0:T(8,128)(2,1)S(1)} %pad_maximum_fusion.9), channel_id=1, source_target_pairs={{0,1},{1,0},{2,3},{3,2},{4,5},{5,4},{6,7},{7,6},{8,9},{9,8},{10,11... | collective-permute-start | bytes 491528 | tf_op jit(solution)/shard_map/ppermute | solution.py:581
  106.1 7.5 %collective-permute-start.14 = (bf16[2,2,2,64,256]{4,3,2,1,0:T(8,128)(2,1)S(1)}, bf16[2,2,2,64,256]{4,3,2,1,0:T(8,128)(2,1)S(1)}, u32[]{:S(2)}, u32[]{:S(2)}) collective-permute-start(bf16[2,2,2,64,256]{4,3,2,1,0:T(8,128)(2,1)S(1)} %pad_maximum_fusion.7), channel_id=1, source_target_pairs={{0,1},{1,0},{2,3},{3,2},{4,5},{5,4},{6,7},{7,6},{8,9},{9,8},{10,11... | collective-permute-start | bytes 786440 | tf_op jit(solution)/shard_map/ppermute | solution.py:581
  110.9 7.1 %collective-permute-start.30 = (bf16[2,2,2,80,256]{4,3,2,1,0:T(8,128)(2,1)S(1)}, bf16[2,2,2,80,256]{4,3,2,1,0:T(8,128)(2,1)S(1)}, u32[]{:S(2)}, u32[]{:S(2)}) collective-permute-start(bf16[2,2,2,80,256]{4,3,2,1,0:T(8,128)(2,1)S(1)} %pad_maximum_fusion.6), channel_id=1, source_target_pairs={{0,4},{1,5},{2,6},{3,7},{4,0},{5,1},{6,2},{7,3},{8,12},{9,13},{10,... | collective-permute-start | bytes 983048 | tf_op jit(solution)/shard_map/ppermute | solution.py:581
  113.6 6.1 %copy-start.9 = (f32[1,256,768]{2,1,0:T(8,128)S(1)}, f32[1,256,768]{2,1,0:T(8,128)}, u32[]{:S(2)}) copy-start(f32[1,256,768]{2,1,0:T(8,128)} %param.43) | copy-start | bytes 2359300
  113.7 6.1 %copy-start.8 = (f32[1,256,768]{2,1,0:T(8,128)S(1)}, f32[1,256,768]{2,1,0:T(8,128)}, u32[]{:S(2)}) copy-start(f32[1,256,768]{2,1,0:T(8,128)} %param.37) | copy-start | bytes 2359300
  113.7 6.1 %copy-start.18 = (f32[1,256,256]{2,1,0:T(8,128)S(1)}, f32[1,256,256]{2,1,0:T(8,128)}, u32[]{:S(2)}) copy-start(f32[1,256,256]{2,1,0:T(8,128)} %param.44) | copy-start | bytes 786436
  118.0 1.7 %copy-start.7 = (f32[1,1024,256]{2,1,0:T(8,128)S(1)}, f32[1,1024,256]{2,1,0:T(8,128)}, u32[]{:S(2)}) copy-start(f32[1,1024,256]{2,1,0:T(8,128)} %param.46) | copy-start | bytes 3145732
  118.1 1.7 %copy-start.17 = (f32[1,256,256]{2,1,0:T(8,128)S(1)}, f32[1,256,256]{2,1,0:T(8,128)}, u32[]{:S(2)}) copy-start(f32[1,256,256]{2,1,0:T(8,128)} %param.38) | copy-start | bytes 786436
  118.1 1.7 %copy-start.2 = (f32[1,256,768]{2,1,0:T(8,128)S(1)}, f32[1,256,768]{2,1,0:T(8,128)}, u32[]{:S(2)}) copy-start(f32[1,256,768]{2,1,0:T(8,128)} %param.31) | copy-start | bytes 2359300
  118.1 1.7 %copy-start.3 = (f32[1,256,256]{2,1,0:T(8,128)S(1)}, f32[1,256,256]{2,1,0:T(8,128)}, u32[]{:S(2)}) copy-start(f32[1,256,256]{2,1,0:T(8,128)} %param.32) | copy-start | bytes 786436
  118.1 2.1 %copy-start.4 = (f32[1,256,1024]{2,1,0:T(8,128)S(1)}, f32[1,256,1024]{2,1,0:T(8,128)}, u32[]{:S(2)}) copy-start(f32[1,256,1024]{2,1,0:T(8,128)} %param.39) | copy-start | bytes 3145732
  118.1 2.4 %copy-start.5 = (f32[1,1024,256]{2,1,0:T(8,128)S(1)}, f32[1,1024,256]{2,1,0:T(8,128)}, u32[]{:S(2)}) copy-start(f32[1,1024,256]{2,1,0:T(8,128)} %param.40) | copy-start | bytes 3145732
  118.2 2.7 %copy-start.6 = (f32[1,256,1024]{2,1,0:T(8,128)S(1)}, f32[1,256,1024]{2,1,0:T(8,128)}, u32[]{:S(2)}) copy-start(f32[1,256,1024]{2,1,0:T(8,128)} %param.45) | copy-start | bytes 3145732
  118.2 2.7 %copy-start.23 = (f32[1,9,256]{2,1,0:T(8,128)S(1)}, f32[1,9,256]{2,1,0:T(8,128)}, u32[]{:S(2)}) copy-start(f32[1,9,256]{2,1,0:T(8,128)} %copy-done.21) | copy-start | bytes 27652
  118.2 2.7 %copy-start.28 = (f32[1,3328]{1,0:T(1,128)S(1)}, f32[1,3328]{1,0:T(1,128)}, u32[]{:S(2)}) copy-start(f32[1,3328]{1,0:T(1,128)} %refs_12_.1) | copy-start | bytes 39940
  118.2 2.7 %copy-start.31 = (f32[1,3328]{1,0:T(1,128)S(1)}, f32[1,3328]{1,0:T(1,128)}, u32[]{:S(2)}) copy-start(f32[1,3328]{1,0:T(1,128)} %refs_18_.1) | copy-start | bytes 39940
  118.2 2.7 %copy-start.32 = (f32[1,3328]{1,0:T(1,128)S(1)}, f32[1,3328]{1,0:T(1,128)}, u32[]{:S(2)}) copy-start(f32[1,3328]{1,0:T(1,128)} %refs_24_.1) | copy-start | bytes 39940
  118.6 1.2 collective-permute-start.31
  (7 other events, 4.7 us)
where the time goes:
time: 131 us; the launch traced here: 130 us
  waiting for transfers between devices  36.8 us (28%)
  starting transfers between devices  32.4 us (25%)
  Pallas kernels  27.4 us (21%)
  local copies, waits for them, and re-layouts  22.8 us (17%)
  other arithmetic  9.72 us (7%)
  between operations  1.32 us (1%)
    ppermute x24, waiting for transfers between devices, exchanged(): lax.ppermute(value, 'dp', [(index, index ^ 1 << bit) for index in range(s...  33 us
    ppermute x24, starting transfers between devices, exchanged(): lax.ppermute(value, 'dp', [(index, index ^ 1 << bit) for index in range(s...  30.3 us
    pallas_call x1, Pallas kernels, run_blocks(): pl.pallas_call(section_step, out_shape=[jax.ShapeDtypeStruct((2, MB_TOK,...  20.5 us
    unnamed x84, local copies, waits for them, and re-layouts  17.7 us
    pallas_call x1, Pallas kernels, run_optimizer(): pl.pallas_call(optimizer_step, grid=(STEPS,), out_shape=[jax.ShapeDtypeSt...  6.55 us
    ppermute x8, waiting for transfers between devices, swapped(): return lax.ppermute(value, 'section', [(0, 1), (1, 0)])  3.78 us
    squeeze x1, local copies, waits for them, and re-layouts, per_device(): came = swapped(sums[1])  2.82 us
    another operation x4, other arithmetic, both_rows(): jnp.stack([jnp.where(first, own, came), jnp.where(first, came, own)])  2.81 us
  transfers between devices with their start and end apart: 32, of which 17 were waited for; matrix products, arithmetic and copies ran while one was open for 4% of the time, Pallas kernels for 0%

commit v1 on v0

--- a/solution.py
+++ b/solution.py
@@ -38,8 +38,7 @@
 EXP_SCALE = SCALE * LOG2E
 OFF = -1e30
 ROWS = ((0, 80), (80, 80), (160, 80), (240, 64))
-GRAD_ROWS = 3328
-SMALL_ROW = 3072
+PARTS = (1152, 1152, 1152)
 
 
 def placement_tables():
@@ -80,6 +79,10 @@
     return shifts, fence, lower
 
 
+def kept_in(arrays, spaces):
+    return [pltpu.with_memory_space_constraint(array, space) for array, space in zip(arrays, spaces)]
+
+
 def dot(a, b):
     return jnp.dot(a, b, preferred_element_type=F32)
 
@@ -112,9 +115,14 @@
 
 
 def turned_taps(taps):
-    first = [taps[index : index + 1, :HALF] for index in range(9)]
-    second = [taps[3 * (index % 3) + index // 3 :, HALF:][:1] for index in range(9)]
-    return [jnp.concatenate([a, b], axis=1) for a, b in zip(first, second)]
+    turned = [3 * (index % 3) + index // 3 for index in range(9)]
+    return [
+        jnp.concatenate(
+            [taps[:, index * D : index * D + HALF], taps[:, turned[index] * D + HALF : (turned[index] + 1) * D]],
+            axis=1,
+        )
+        for index in range(9)
+    ]
 
 
 def norm_forward(x, gain, offset):
@@ -140,17 +148,20 @@
     return vec[:, index * D : (index + width) * D]
 
 
-def forward_block(x_ref, out_ref, vec, taps, w, saved, tables, work):
+def forward_block(x_ref, out_ref, vec_ref, taps_ref, w, saved, tables, work, need):
     wq, wp, w1, w2 = w
     (hat1, scale1, normed, qkv, probs, mixed, hat2, scale2, normed2, slope, activ) = saved
     plain, turned, plain_t, turned_t, shifts, fence, lower = tables
     normed_nat, mixed_att, middle, hidden = work
+    need("x", "vec")
+    vec = vec_ref[...]
     for start, size in ROWS:
         rows = pl.ds(start, size)
         hat, scale, y = norm_forward(x_ref[rows, :].astype(F32), vec_at(vec, 0), vec_at(vec, 2))
         hat1[rows, :] = hat
         scale1[rows, :] = jnp.broadcast_to(scale, (size, HALF))
         normed_nat[rows, :] = y.astype(BF16)
+    need("place", "wide")
     base = normed_nat[...]
     biases = (vec_at(vec, 4), None, vec_at(vec, 5))
     for half, table in enumerate((plain, turned)):
@@ -163,7 +174,8 @@
                 got = got + biases[part][:, lanes]
             qkv[part, :, lanes] = got.astype(BF16)
     masks = head_masks()
-    taps9 = turned_taps(taps)
+    need("stripe")
+    taps9 = turned_taps(taps_ref[...])
     bias = vec_at(vec, 7)
     for group in range(NGROUP):
         kind = KINDS[group]
@@ -191,6 +203,7 @@
                 low.append(p.astype(BF16))
             attended = picked_heads(dot(v[:, lanes].T, jnp.concatenate(low, axis=1))).T
             mixed_att[rows, lanes] = (attended + lepe[:, lanes]).astype(BF16)
+    need("place_t")
     mixed[:, :HALF] = dot(plain_t[...], mixed_att[:, :HALF]).astype(BF16)
     mixed[:, HALF:] = dot(turned_t[...], mixed_att[:, HALF:]).astype(BF16)
     middle[...] = dot(mixed[...], wp[...])
@@ -212,19 +225,22 @@
             pdf = 0.3989422804014327 * jnp.exp(-0.5 * h * h)
             activ[rows, cols] = (h * cdf).astype(BF16)
             slope[rows, cols] = cdf + h * pdf
+    need("deep")
     out_ref[...] = dot(activ[...], w2[...])
     for start, size in ROWS:
         rows = pl.ds(start, size)
         out_ref[rows, :] = out_ref[rows, :] + middle[rows, :] + vec_at(vec, 8)
 
 
-def backward_block(up_ref, grad_ref, vec, taps, w, saved, tables, work, gbuf, small):
+def backward_block(up_ref, grad_ref, vec_ref, taps_ref, w, saved, tables, work, sums, small):
     wq, wp, w1, w2 = w
     (hat1, scale1, normed, qkv, probs, mixed, hat2, scale2, normed2, slope, activ) = saved
     plain, turned, plain_t, turned_t, shifts, fence, lower = tables
     branch, gact, ghid, gmid, gmix, dqkv, dnat, gnorm = work
+    early, inner, outer = sums
+    vec = vec_ref[...]
     branch[...] = up_ref[...].astype(BF16)
-    gbuf[2048:3072, :] = dot_tn(activ[...], branch[...]).astype(BF16)
+    outer[0:FF, :] = dot_tn(activ[...], branch[...]).astype(BF16)
     sums = column_sum(branch[...])
     small[8:9, :] = sums
     gact[...] = dot_nt(branch[...], w2[...])
@@ -239,7 +255,7 @@
     for part in range(4):
         small[9 + part : 10 + part, :] = parts[part]
     for part in range(4):
-        gbuf[1024 + part * D : 1024 + (part + 1) * D, :] = dot_tn(
+        inner[part * D : (part + 1) * D, :] = dot_tn(
             normed2[...], ghid[:, part * D : (part + 1) * D]
         ).astype(BF16)
     gnorm[...] = dot_nt(ghid[...], w1[...])
@@ -260,7 +276,7 @@
     small[1:2, :] = gains
     small[3:4, :] = offsets
     small[6:7, :] = outs
-    gbuf[768:1024, :] = dot_tn(mixed[...], branch[...]).astype(BF16)
+    early[3 * D : 4 * D, :] = dot_tn(mixed[...], branch[...]).astype(BF16)
     low = dot_nt(branch[...], wp[...]).astype(BF16)
     gmix[0:MB_TOK, :] = low
     small[7:8, :] = column_sum(low)
@@ -269,7 +285,7 @@
     gmix[:, :HALF] = place_h
     gmix[:, HALF:] = place_v
     masks = head_masks()
-    taps9 = turned_taps(taps)
+    taps9 = turned_taps(taps_ref[...])
     tap_sums = [jnp.zeros((1, D), F32) for _ in range(9)]
     for group in range(NGROUP):
         kind = KINDS[group]
@@ -327,7 +343,7 @@
         small[5:6, lanes] = column_sum(both[:, D : 3 * HALF])
         grads = dot_tn(normed[half], both)
         for part in range(3):
-            gbuf[part * D : (part + 1) * D, lanes] = grads[:, part * HALF : (part + 1) * HALF].astype(BF16)
+            early[part * D : (part + 1) * D, lanes] = grads[:, part * HALF : (part + 1) * HALF].astype(BF16)
         natural = dot(table_t[...], both).astype(BF16)
         for part in range(3):
             dnat[:, part * D + half * HALF : part * D + (half + 1) * HALF] = natural[
@@ -346,7 +362,7 @@
         grad_ref[rows, :] = gmid[rows, :] + norm_backward(g, hat, full, vec_at(vec, 0))
     small[0:1, :] = gains
     small[2:3, :] = offsets
-    gbuf[SMALL_ROW : SMALL_ROW + 32, :] = small[...].astype(BF16)
+    outer[FF : FF + 32, :] = small[...].astype(BF16)
 
 
 SAVED = [
@@ -375,61 +391,117 @@
 ]
 
 
-def section_step(
-    sec_ref, x_ref, c_ref, vec_own, vec_other, ker_own, ker_other, wide_own, wide_other, deep_own, deep_other, *refs
-):
-    tables, refs = refs[:7], refs[7:]
-    (outs, grads, gsum), refs = refs[:3], refs[3:]
-    count = len(SAVED)
-    kept, refs = (refs[:count], refs[count : 2 * count]), refs[2 * count :]
-    forward_work, refs = refs[: len(FORWARD_WORK)], refs[len(FORWARD_WORK) :]
-    backward_work, refs = refs[: len(BACKWARD_WORK)], refs[len(BACKWARD_WORK) :]
-    feed, small, wide, deep, sems = refs
+INPUTS = [
+    ((MB_TOK, D), BF16),
+    ((MB_TOK, D), BF16),
+    ((2, 1, VEC), F32),
+    ((2, 1, 9 * D), F32),
+    ((2, D, 8 * D), BF16),
+    ((2, FF, D), BF16),
+    ((ATT, MB_TOK), BF16),
+    ((ATT, MB_TOK), BF16),
+    ((MB_TOK, ATT), BF16),
+    ((MB_TOK, ATT), BF16),
+    ((2, 5 * GROUP, GROUP), BF16),
+    ((2, GROUP, GROUP), F32),
+    ((2, GROUP, HALF), F32),
+]
+RESULTS = [((2, MB_TOK, D), F32), ((2, MB_TOK, D), F32)] + [((2, rows, D), BF16) for rows in PARTS]
+OTHER_WORK = [((MB_TOK, D), BF16), ((32, D), F32)]
+
+
+def section_step(sec_ref, *refs):
+    def take(count):
+        nonlocal refs
+        taken, refs = refs[:count], refs[count:]
+        return taken
+
+    x_in, c_in, vec_own, vec_other, ker_own, ker_other, wide_own, wide_other, deep_own, deep_other = take(10)
+    table_in = take(7)
+    sent = [take(2) for _ in RESULTS]
+    held = take(len(INPUTS))
+    results = take(len(RESULTS))
+    kept = (take(len(SAVED)), take(len(SAVED)))
+    forward_work = take(len(FORWARD_WORK))
+    backward_work = take(len(BACKWARD_WORK))
+    feed, small, in_sems, out_sems = refs
+    x, c, vecs, taps, wide, deep = held[:6]
+    tables = held[6:]
     sec = sec_ref[0]
-    copies = [
-        pltpu.make_async_copy(wide_own, wide.at[sec], sems.at[0]),
-        pltpu.make_async_copy(wide_other, wide.at[1 - sec], sems.at[1]),
-        pltpu.make_async_copy(deep_own, deep.at[sec], sems.at[2]),
-        pltpu.make_async_copy(deep_other, deep.at[1 - sec], sems.at[3]),
+    at = pl.multiple_of(sec * MB_TOK, 16)
+    moves = [
+        ("x", x_in.at[pl.ds(at, MB_TOK)], x),
+        ("vec", vec_own, vecs.at[sec]),
+        ("vec", vec_other, vecs.at[1 - sec]),
+        ("place", table_in[0], tables[0]),
+        ("place", table_in[1], tables[1]),
+        ("wide", wide_own, wide.at[sec]),
+        ("wide", wide_other, wide.at[1 - sec]),
+        ("stripe", table_in[4], tables[4]),
+        ("stripe", table_in[5], tables[5]),
+        ("stripe", table_in[6], tables[6]),
+        ("stripe", ker_own, taps.at[sec]),
+        ("stripe", ker_other, taps.at[1 - sec]),
+        ("place_t", table_in[2], tables[2]),
+        ("place_t", table_in[3], tables[3]),
+        ("deep", deep_own, deep.at[sec]),
+        ("deep", deep_other, deep.at[1 - sec]),
+        ("c", c_in.at[pl.ds(at, MB_TOK)], c),
     ]
-    for copy in copies:
+    pending = {}
+    for index, (name, source, target) in enumerate(moves):
+        copy = pltpu.make_async_copy(source, target, in_sems.at[index])
         copy.start()
+        pending.setdefault(name, []).append(copy)
+
+    def need(*names):
+        for name in names:
+            for copy in pending.pop(name, []):
+                copy.wait()
+
+    leaving = []
+
+    def leave(index):
+        for which, slot in enumerate((sec, 1 - sec)):
+            copy = pltpu.make_async_copy(results[index].at[slot], sent[index][which], out_sems.at[2 * index + which])
+            copy.start()
+            leaving.append(copy)
+
+    outs, grads, early, inner, outer = results
     small[...] = jnp.zeros_like(small)
-    gsum[:, SMALL_ROW:, :] = jnp.zeros((2, GRAD_ROWS - SMALL_ROW, D), BF16)
-    first = sec == 0
-    vecs = (
-        jnp.where(first, vec_own[...], vec_other[...]),
-        jnp.where(first, vec_other[...], vec_own[...]),
-    )
-    taps = (
-        jnp.where(first, ker_own[...], ker_other[...]),
-        jnp.where(first, ker_other[...], ker_own[...]),
-    )
+    for part, rows in zip((early, inner, outer), PARTS):
+        part[:, FF:, :] = jnp.zeros((2, rows - FF, D), BF16)
     weights = [
-        (wide.at[b, :, 0:768], wide.at[b, :, 768:1024], wide.at[b, :, 1024:2048], deep.at[b])
+        (wide.at[b, :, 0 : 3 * D], wide.at[b, :, 3 * D : 4 * D], wide.at[b, :, 4 * D : 8 * D], deep.at[b])
         for b in range(2)
     ]
-    at = pl.multiple_of(sec * MB_TOK, 16)
-    for copy in copies:
+    sums = [(early.at[b], inner.at[b], outer.at[b]) for b in range(2)]
+
+    def forward(b, source):
+        forward_block(
+            source, outs.at[b], vecs.at[b], taps.at[b], weights[b], kept[b], tables, forward_work, need
+        )
+
+    def backward(b, source):
+        backward_block(
+            source, grads.at[b], vecs.at[b], taps.at[b], weights[b], kept[b], tables, backward_work, sums[b], small
+        )
+
+    forward(0, x)
+    feed[...] = outs[0].astype(BF16)
+    forward(1, feed)
+    leave(0)
+    need("c")
+    backward(1, c)
+    feed[...] = grads[1].astype(BF16)
+    backward(0, feed)
+    for index in range(1, len(RESULTS)):
+        leave(index)
+    for copy in leaving:
         copy.wait()
-    slot = (sec, 1 - sec)
-    x_own, c_own = x_ref.at[pl.ds(at, MB_TOK)], c_ref.at[pl.ds(at, MB_TOK)]
-    out_refs = [outs.at[slot[b]] for b in range(2)]
-    grad_refs = [grads.at[slot[b]] for b in range(2)]
-    sum_refs = [gsum.at[slot[b]] for b in range(2)]
-    forward_block(x_own, out_refs[0], vecs[0], taps[0], weights[0], kept[0], tables, forward_work)
-    feed[...] = out_refs[0][...].astype(BF16)
-    forward_block(feed, out_refs[1], vecs[1], taps[1], weights[1], kept[1], tables, forward_work)
-    backward_block(
-        c_own, grad_refs[1], vecs[1], taps[1], weights[1], kept[1], tables, backward_work, sum_refs[1], small
-    )
-    feed[...] = grad_refs[1][...].astype(BF16)
-    backward_block(
-        feed, grad_refs[0], vecs[0], taps[0], weights[0], kept[0], tables, backward_work, sum_refs[0], small
-    )
-
-
-def run_blocks(sec, x, c, vec_own, vec_other, ker_own, ker_other, wide_own, wide_other, deep_own, deep_other):
+
+
+def run_blocks(sec, *arrays):
     plain, turned = placement_tables()
     shifts, fence, lower = stripe_tables()
     tables = (
@@ -441,24 +513,61 @@
         jnp.asarray(fence, F32),
         jnp.asarray(lower, F32),
     )
-    vmem = pl.BlockSpec(memory_space=pltpu.VMEM)
-    hbm = pl.BlockSpec(memory_space=pl.ANY)
+    spaces = [pltpu.HBM] * 3 + [pltpu.VMEM, pltpu.HBM] * 3 + [pltpu.VMEM] + [pltpu.HBM] * 7
     smem = pl.BlockSpec(memory_space=pltpu.SMEM)
-    scratch = SAVED + SAVED + FORWARD_WORK + BACKWARD_WORK
-    scratch = scratch + [((MB_TOK, D), BF16), ((32, D), F32), ((2, D, 2048), BF16), ((2, FF, D), BF16)]
+    scratch = INPUTS + RESULTS + SAVED + SAVED + FORWARD_WORK + BACKWARD_WORK + OTHER_WORK
+    out_shape = [pltpu.VMEM(shape[1:], kind) for shape, kind in RESULTS for _ in range(2)]
     return pl.pallas_call(
         section_step,
-        out_shape=[
-            jax.ShapeDtypeStruct((2, MB_TOK, D), F32),
-            jax.ShapeDtypeStruct((2, MB_TOK, D), F32),
-            jax.ShapeDtypeStruct((2, GRAD_ROWS, D), BF16),
-        ],
-        in_specs=[smem] + [vmem] * 6 + [hbm] * 4 + [vmem] * 7,
-        out_specs=[vmem] * 3,
-        scratch_shapes=[pltpu.VMEM(shape, kind) for shape, kind in scratch] + [pltpu.SemaphoreType.DMA((4,))],
-        compiler_params=pltpu.CompilerParams(vmem_limit_bytes=50 << 20),
+        out_shape=out_shape,
+        in_specs=[smem] + [pl.BlockSpec(memory_space=space) for space in spaces],
+        out_specs=[pl.BlockSpec(memory_space=pl.ANY)] * len(out_shape),
+        scratch_shapes=[pltpu.VMEM(shape, kind) for shape, kind in scratch]
+        + [pltpu.SemaphoreType.DMA((17,)), pltpu.SemaphoreType.DMA((2 * len(RESULTS),))],
+        compiler_params=pltpu.CompilerParams(vmem_limit_bytes=34 << 20),
         name="blocks",
-    )(sec, x, c, vec_own, vec_other, ker_own, ker_other, wide_own, wide_other, deep_own, deep_other, *tables)
+    )(sec, *kept_in(arrays + tables, spaces))
+
+
+NARROW = (((D, 3 * D), 0), ((D, D), 3 * D), ((D, FF), 4 * D), ((FF, D), None))
+
+
+def narrowed(*refs):
+    sources, (wide_out, deep_out), held, made, (in_sems, out_sems) = (
+        refs[:4],
+        refs[4:6],
+        refs[6:10],
+        refs[10:14],
+        refs[14:],
+    )
+    coming = [pltpu.make_async_copy(sources[k], held[k], in_sems.at[k]) for k in range(4)]
+    for copy in coming:
+        copy.start()
+    going = []
+    for k, (shape, first) in enumerate(NARROW):
+        coming[k].wait()
+        made[k][...] = held[k][...].astype(BF16)
+        target = deep_out if first is None else wide_out.at[:, pl.ds(first, shape[1])]
+        copy = pltpu.make_async_copy(made[k], target, out_sems.at[k])
+        copy.start()
+        going.append(copy)
+    for copy in going:
+        copy.wait()
+
+
+def run_narrowed(*weights):
+    hbm = pl.BlockSpec(memory_space=pltpu.HBM)
+    return pl.pallas_call(
+        narrowed,
+        out_shape=[pltpu.HBM((D, 8 * D), BF16), pltpu.HBM((FF, D), BF16)],
+        in_specs=[hbm] * 4,
+        out_specs=[hbm] * 2,
+        scratch_shapes=[pltpu.VMEM(shape, F32) for shape, _ in NARROW]
+        + [pltpu.VMEM(shape, BF16) for shape, _ in NARROW]
+        + [pltpu.SemaphoreType.DMA((4,)), pltpu.SemaphoreType.DMA((4,))],
+        compiler_params=pltpu.CompilerParams(vmem_limit_bytes=8 << 20),
+        name="narrowed",
+    )(*kept_in(weights, [pltpu.HBM] * 4))
 
 
 def square_sum(a_ref, b_ref, c_ref, out_ref):
@@ -496,11 +605,27 @@
     return clipped, moment_new, weight_new, average_new
 
 
-def optimizer_step(*refs):
+STEPS = 8
+
+
+def optimizer_step(sec_ref, *refs):
+    rows_in, refs = refs[:4], refs[4:]
     (own, other), refs = refs[:2], refs[2:]
     grads, refs = refs[:10], refs[10:]
     states, refs = refs[:18], refs[18:]
-    outs, (norm_ref,) = refs[:28], refs[28:]
+    outs, (norm_ref, *rows_out, sems) = refs[:28], refs[28:]
+    sec = sec_ref[0]
+    moves = []
+    for index in range(4):
+        first = pl.multiple_of((sec if index % 2 == 0 else 1 - sec) * MB_TOK, 8)
+        target = rows_out[index // 2].at[pl.ds(first, MB_TOK)]
+        moves.append(pltpu.make_async_copy(rows_in[index], target, sems.at[index]))
+
+    @pl.when(pl.program_id(0) == 0)
+    def _():
+        for move in moves:
+            move.start()
+
     norm = jnp.sqrt(own[0:1, 0:1] + other[0:1, 0:1])
     factor = jnp.minimum(1.0, CLIP_LIMIT / (norm + 1e-06))
 
@@ -524,14 +649,17 @@
         rows = grads[9][...].astype(F32)
         for part in range(13):
             put(0, slice(part * D, (part + 1) * D), rows[part : part + 1, :])
-        put(1, slice(0, D), rows[13:22, :])
-        norm_ref[...] = jnp.broadcast_to(norm, (8, HALF))
-
-
-STEPS = 8
-
-
-def run_optimizer(own, other, a, b, c, states):
+        for part in range(9):
+            put(1, slice(part * D, (part + 1) * D), rows[13 + part : 14 + part, :])
+        norm_ref[...] = norm
+
+    @pl.when(pl.program_id(0) == STEPS - 1)
+    def _():
+        for move in moves:
+            move.wait()
+
+
+def run_optimizer(sec, rows_in, own, other, a, b, c, states):
     rows = D // STEPS
     deep = FF // STEPS
 
@@ -545,24 +673,32 @@
     grad_specs += [pl.BlockSpec((deep, D), lambda i: (i, 0)), pl.BlockSpec((32, D), lambda i: (FF // 32, 0))]
     state_specs = [
         fixed((1, VEC)),
-        fixed((9, D)),
+        fixed((1, 9 * D)),
         pl.BlockSpec((rows, 3 * D), lambda i: (i, 0)),
         pl.BlockSpec((rows, D), lambda i: (i, 0)),
         pl.BlockSpec((rows, FF), lambda i: (i, 0)),
         pl.BlockSpec((deep, D), lambda i: (i, 0)),
     ]
-    shapes = [(1, VEC), (9, D), (D, 3 * D), (D, D), (D, FF), (FF, D)]
+    shapes = [(1, VEC), (1, 9 * D), (D, 3 * D), (D, D), (D, FF), (FF, D)]
+    anywhere = pl.BlockSpec(memory_space=pltpu.HBM)
+    spaces = [pltpu.VMEM] * 4
     return pl.pallas_call(
         optimizer_step,
         grid=(STEPS,),
         out_shape=[jax.ShapeDtypeStruct(shape, F32) for shape in shapes] * 4
         + [jax.ShapeDtypeStruct(shape, BF16) for shape in shapes[2:]]
-        + [jax.ShapeDtypeStruct((8, HALF), F32)],
-        in_specs=[fixed((8, HALF))] * 2 + grad_specs + state_specs * 3,
-        out_specs=state_specs * 4 + state_specs[2:] + [fixed((8, HALF))],
-        compiler_params=pltpu.CompilerParams(vmem_limit_bytes=32 << 20),
+        + [jax.ShapeDtypeStruct((1, 1), F32)]
+        + [jax.ShapeDtypeStruct((2 * MB_TOK, D), F32)] * 2,
+        in_specs=[pl.BlockSpec(memory_space=pltpu.SMEM)]
+        + [pl.BlockSpec(memory_space=space) for space in spaces]
+        + [fixed((8, HALF))] * 2
+        + grad_specs
+        + state_specs * 3,
+        out_specs=state_specs * 4 + state_specs[2:] + [fixed((1, 1))] + [anywhere] * 2,
+        scratch_shapes=[pltpu.SemaphoreType.DMA((4,))],
+        compiler_params=pltpu.CompilerParams(vmem_limit_bytes=24 << 20),
         name="optimizer",
-    )(own, other, a, a, a, a, b, b, b, b, c, c, *states)
+    )(sec, *kept_in(rows_in, spaces), own, other, a, a, a, a, b, b, b, b, c, c, *states)
 
 
 def swapped(value):
@@ -581,26 +717,34 @@
     return lax.ppermute(value, "dp", [(index, index ^ (1 << bit)) for index in range(size)])
 
 
-def summed_over_dp(parts):
+def exchange_bits():
     size = lax.axis_size("dp")
     bits = size.bit_length() - 1
-    if size != 1 << bits or any(part.shape[0] % size for part in parts):
+    if size != 1 << bits or any(rows % size for rows in PARTS):
+        return []
+    index = lax.axis_index("dp")
+    return [((index >> bit) & 1) == 0 for bit in range(bits)]
+
+
+def summed_over_dp(parts, clear):
+    size = lax.axis_size("dp")
+    bits = len(clear)
+    if not bits:
         return [lax.psum(part.astype(F32), "dp").astype(BF16) for part in parts]
-    index = lax.axis_index("dp")
     orders = exchange_orders(bits)
     shapes = [part.shape for part in parts]
     held = [part.reshape((2,) * bits + (part.shape[0] // size, D)) for part in parts]
     for step in range(bits):
         kept, came = [], []
         for value, order in zip(held, orders):
-            mine = (index >> order[step]) & 1
-            kept.append(lax.dynamic_index_in_dim(value, mine, 0, keepdims=False))
-            came.append(exchanged(lax.dynamic_index_in_dim(value, 1 - mine, 0, keepdims=False), order[step], size))
+            low = clear[order[step]]
+            kept.append(jnp.where(low, value[0], value[1]))
+            came.append(exchanged(jnp.where(low, value[1], value[0]), order[step], size))
         held = [(a.astype(F32) + b.astype(F32)).astype(BF16) for a, b in zip(kept, came)]
     for step in reversed(range(bits)):
         grown = []
         for value, order in zip(held, orders):
-            low = ((index >> order[step]) & 1) == 0
+            low = clear[order[step]]
             came = exchanged(value, order[step], size)
             grown.append(jnp.stack([jnp.where(low, value, came), jnp.where(low, came, value)]))
         held = grown
@@ -608,13 +752,14 @@
 
 
 def per_device(inputs, cotangent, *states):
-    states = [array.reshape(array.shape[-2:]) if array.ndim == 3 else array for array in states]
-    vectors, kernels, w_qkv, w_proj, w_fc1, w_fc2 = states[:6]
-    section = lax.axis_index("section")
-    wide = jnp.concatenate([w_qkv, w_proj, w_fc1], axis=1).astype(BF16)
-    deep = w_fc2.astype(BF16)
-    outs, grads, sums = run_blocks(
-        section.astype(jnp.int32).reshape(1),
+    states = [array.reshape(1, 9 * D) if array.shape == (1, 9, D) else array for array in states]
+    states = [array.reshape(array.shape[1:]) if array.ndim == 3 else array for array in states]
+    vectors, kernels = states[:2]
+    section = lax.axis_index("section").astype(jnp.int32).reshape(1)
+    section, *clear = lax.optimization_barrier((section, *exchange_bits()))
+    wide, deep = run_narrowed(*states[2:6])
+    results = run_blocks(
+        section,
         inputs,
         cotangent,
         vectors,
@@ -626,27 +771,22 @@
         deep,
         swapped(deep),
     )
-    came = swapped(sums[1])
-    total = (sums[0].astype(F32) + came.astype(F32)).astype(BF16)
-    a, b, c = summed_over_dp([total[0:1024], total[1024:2048], total[2048:]])
+    totals = [
+        (own.astype(F32) + swapped(other).astype(F32)).astype(BF16)
+        for own, other in zip(results[4::2], results[5::2])
+    ]
+    a, b, c = summed_over_dp(lax.optimization_barrier(totals), clear)
     squares = run_square_sum(a, b, c)
-    new = run_optimizer(squares, swapped(squares), a, b, c, states)
-    first = section == 0
-
-    def both_rows(value):
-        own, came = value[0], swapped(value[1])
-        return jnp.stack([jnp.where(first, own, came), jnp.where(first, came, own)]).reshape(1, 2 * MB_TOK, D)
+    rows_in = (results[0], swapped(results[1]), results[2], swapped(results[3]))
+    new = run_optimizer(section, rows_in, squares, swapped(squares), a, b, c, states)
 
     def whole(arrays):
-        return [array if array.shape == (1, VEC) else array[None] for array in arrays]
-
-    return (
-        both_rows(outs),
-        both_rows(grads),
-        *whole(new[0:6]),
-        new[28][0, 0],
-        *whole(new[6:28]),
-    )
+        return [
+            array if array.shape == (1, VEC) else array.reshape(1, 9, D) if array.shape == (1, 9 * D) else array[None]
+            for array in arrays
+        ]
+
+    return (new[29][None], new[30][None], *whole(new[0:6]), new[28].reshape(()), *whole(new[6:28]))
 
 
 def solution(mesh):

time: 131 us -> 97.5 us (0.74)
  local copies, waits for them, and re-layouts: 22.8 us -> 1.04 us
  waiting for transfers between devices: 36.8 us -> 19.5 us
  starting transfers between devices: 32.4 us -> 42 us
  other arithmetic: 9.72 us -> 1.96 us
  Pallas kernels: 27.4 us -> 31.5 us
    ppermute x24, waiting for transfers between devices: 33 us -> 12.9 us  [exchanged(): lax.ppermute(value, 'dp', [(index, index ^ 1 << bit) for index in range(s...]
    unnamed x84 -> x40, local copies, waits for them, and re-layouts: 17.7 us -> 1.04 us
    ppermute x24, starting transfers between devices: 30.3 us -> 39.4 us  [exchanged(): lax.ppermute(value, 'dp', [(index, index ^ 1 << bit) for index in range(s...]
    another operation x7 -> x0, other arithmetic: 5.11 us -> none  [the longest x4 2.81 us: both_rows(): jnp.stack([jnp.where(first, own, came), jnp.where(first, came, own)])]
    squeeze x15 -> x0, local copies, waits for them, and re-layouts: 4.51 us -> none  [the longest x1 2.82 us: per_device(): came = swapped(sums[1])]
    pallas_call x1 -> x2, Pallas kernels: 20.5 us -> 24.5 us  [the longest x1 21.7 us: run_blocks(): pl.pallas_call(section_step, out_shape=out_shape, in_specs=[smem] + [pl.B...]
    ppermute x8 -> x10, waiting for transfers between devices: 3.78 us -> 6.67 us  [swapped(): return lax.ppermute(value, 'section', [(0, 1), (1, 0)])]
    convert_element_type x2 -> x3, other arithmetic: 2.45 us -> 0.51 us  [per_device(): (own.astype(F32) + swapped(other).astype(F32)).astype(BF16)]
  transfers between devices with their start and end apart: 32 -> 34, of which waited for: 17 -> 18; matrix products, arithmetic and copies ran while one was open for 4% -> 2% of each run, Pallas kernels for 0% -> 0%
where the time goes in v1:
time: 97.5 us; the launch traced here: 97.4 us
  starting transfers between devices  42 us (43%)
  Pallas kernels  31.5 us (32%)
  waiting for transfers between devices  19.5 us (20%)
  other arithmetic  1.96 us (2%)
  between operations  1.37 us (1%)
  local copies, waits for them, and re-layouts  1.04 us (1%)
    ppermute x24, starting transfers between devices, exchanged(): lax.ppermute(value, 'dp', [(index, index ^ 1 << bit) for index in range(s...  39.4 us
    pallas_call x1, Pallas kernels, run_blocks(): pl.pallas_call(section_step, out_shape=out_shape, in_specs=[smem] + [pl.B...  21.7 us
    ppermute x24, waiting for transfers between devices, exchanged(): lax.ppermute(value, 'dp', [(index, index ^ 1 << bit) for index in range(s...  12.9 us
    ppermute x10, waiting for transfers between devices, swapped(): return lax.ppermute(value, 'section', [(0, 1), (1, 0)])  6.67 us
    pallas_call x1, Pallas kernels, run_optimizer(): pl.pallas_call(optimizer_step, grid=(STEPS,), out_shape=[jax.ShapeDtypeSt...  6.63 us
    pallas_call x1, Pallas kernels, run_narrowed(): pl.pallas_call(narrowed, out_shape=[pltpu.HBM((D, 8 * D), BF16), pltpu.HB...  2.78 us
    ppermute x10, starting transfers between devices, swapped(): return lax.ppermute(value, 'section', [(0, 1), (1, 0)])  2.58 us
  transfers between devices with their start and end apart: 34, of which 18 were waited for; matrix products, arithmetic and copies ran while one was open for 2% of the time, Pallas kernels for 0%

profile of v1, /device:TPU:0, one launch (start us, length us, event | category | flops | bytes accessed | tf_op | source)
XLA Modules:
  0.0 97.4 jit_solution(6338588363864607792)
XLA Ops:
  0.7 2.8 %narrowed.1 = (bf16[256,2048]{1,0:T(8,128)(2,1)}, bf16[1024,256]{1,0:T(8,128)(2,1)}) custom-call(f32[256,768]{1,0:T(8,128)} %bitcast.165, f32[256,256]{1,0:T(8,128)} %bitcast.167, f32[256,1024]{1,0:T(8,128)} %bitcast.161, f32[1024,256]{1,0:T(8,128)} %bitcast.163), custom_call_target="tpu_custom_call" | custom-call | tf_op jit(solution)/shard_map/narrowed/pallas_call | solution.py:560
  3.5 0.5 collective-permute-start.2
  4.0 0.1 collective-permute-start.3
  4.1 0.4 collective-permute-start
  4.5 0.1 collective-permute-start.1
  4.6 1.8 %collective-permute-done.1.refs_5_ = f32[1,2304]{1,0:T(1,128)S(1)} collective-permute-done((f32[1,2304]{1,0:T(1,128)S(1)}, f32[1,2304]{1,0:T(1,128)S(1)}, u32[]{:S(2)}, u32[]{:S(2)}) %collective-permute-start.1) | collective-permute-done | bytes 9248 | tf_op jit(solution)/shard_map/ppermute | solution.py:705
  6.4 0.9 collective-permute-done.3.refs_9_
  7.3 21.7 %blocks.1 = (f32[304,256]{1,0:T(8,128)S(1)}, f32[304,256]{1,0:T(8,128)S(1)}, f32[304,256]{1,0:T(8,128)S(1)}, f32[304,256]{1,0:T(8,128)S(1)}, bf16[1152,256]{1,0:...) custom-call(s32[1]{0:T(128)} %bitcast.sec_ref, ...), custom_call_target="tpu_custom_call" | custom-call | tf_op jit(solution)/shard_map/blocks/pallas_call | solution.py:520
  29.0 0.4 collective-permute-start.6
  29.5 0.1 collective-permute-start.7
  29.6 0.4 collective-permute-start.4
  30.0 0.1 collective-permute-start.5
  30.1 0.4 collective-permute-start.8
  30.5 0.6 collective-permute-done.6
  31.1 0.2 add_convert_fusion.2
  31.3 0.7 collective-permute-done.7
  31.9 0.2 add_convert_fusion.1
  32.1 1.6 %collective-permute-done.8 = bf16[1152,256]{1,0:T(8,128)(2,1)S(1)} collective-permute-done((bf16[1152,256]{1,0:T(8,128)(2,1)S(1)}, bf16[1152,256]{1,0:T(8,128)(2,1)S(1)}, u32[]{:S(2)}, u32[]{:S(2)}) %collective-permute-start.8) | collective-permute-done | bytes 589856 | tf_op jit(solution)/shard_map/ppermute | solution.py:705
  33.7 0.2 add_convert_fusion
  33.9 2.9 %collective-permute-start.9 = (bf16[2,2,2,72,256]{4,3,2,1,0:T(8,128)(2,1)S(1)}, bf16[2,2,2,72,256]{4,3,2,1,0:T(8,128)(2,1)S(1)}, u32[]{:S(2)}, u32[]{:S(2)}) collective-permute-start(bf16[2,2,2,72,256]{4,3,2,1,0:T(8,128)(2,1)S(1)} %bitcast.187), channel_id=1, source_target_pairs={{0,1},{1,0},{2,3},{3,2},{4,5},{5,4},{6,7},{7,6},{8,9},{9,8},{10,11... | collective-permute-start | bytes 884744 | tf_op jit(solution)/shard_map/ppermute | solution.py:717
  36.9 1.7 %collective-permute-start.25 = (bf16[2,2,2,72,256]{4,3,2,1,0:T(8,128)(2,1)S(1)}, bf16[2,2,2,72,256]{4,3,2,1,0:T(8,128)(2,1)S(1)}, u32[]{:S(2)}, u32[]{:S(2)}) collective-permute-start(bf16[2,2,2,72,256]{4,3,2,1,0:T(8,128)(2,1)S(1)} %bitcast.186), channel_id=1, source_target_pairs={{0,4},{1,5},{2,6},{3,7},{4,0},{5,1},{6,2},{7,3},{8,12},{9,13},{10,... | collective-permute-start | bytes 884744 | tf_op jit(solution)/shard_map/ppermute | solution.py:717
  38.6 1.6 %collective-permute-start.17 = (bf16[2,2,2,72,256]{4,3,2,1,0:T(8,128)(2,1)S(1)}, bf16[2,2,2,72,256]{4,3,2,1,0:T(8,128)(2,1)S(1)}, u32[]{:S(2)}, u32[]{:S(2)}) collective-permute-start(bf16[2,2,2,72,256]{4,3,2,1,0:T(8,128)(2,1)S(1)} %bitcast.185), channel_id=1, source_target_pairs={{0,2},{1,3},{2,0},{3,1},{4,6},{5,7},{6,4},{7,5},{8,10},{9,11},{10,... | collective-permute-start | bytes 884744 | tf_op jit(solution)/shard_map/ppermute | solution.py:717
  40.1 4.0 %collective-permute-done.9 = bf16[2,2,2,72,256]{4,3,2,1,0:T(8,128)(2,1)S(1)} collective-permute-done((bf16[2,2,2,72,256]{4,3,2,1,0:T(8,128)(2,1)S(1)}, bf16[2,2,2,72,256]{4,3,2,1,0:T(8,128)(2,1)S(1)}, u32[]{:S(2)}, u32[]{:S(2)}) %collective-permute-start.9) | collective-permute-done | bytes 294944 | tf_op jit(solution)/shard_map/ppermute | solution.py:717
  44.1 0.1 fusion.2
  44.2 1.8 %collective-permute-start.10 = (bf16[2,2,72,256]{3,2,1,0:T(8,128)(2,1)S(1)}, bf16[2,2,72,256]{3,2,1,0:T(8,128)(2,1)S(1)}, u32[]{:S(2)}, u32[]{:S(2)}) collective-permute-start(bf16[2,2,72,256]{3,2,1,0:T(8,128)(2,1)S(1)} %select_bitcast_fusion.14), channel_id=1, source_target_pairs={{0,2},{1,3},{2,0},{3,1},{4,6},{5,7},{6,4},{7,5},{8,10},{9,11},{10,... | collective-permute-start | bytes 442376 | tf_op jit(solution)/shard_map/ppermute | solution.py:717
  46.1 0.1 fusion
  46.2 1.6 %collective-permute-start.26 = (bf16[2,2,72,256]{3,2,1,0:T(8,128)(2,1)S(1)}, bf16[2,2,72,256]{3,2,1,0:T(8,128)(2,1)S(1)}, u32[]{:S(2)}, u32[]{:S(2)}) collective-permute-start(bf16[2,2,72,256]{3,2,1,0:T(8,128)(2,1)S(1)} %select_bitcast_fusion.8), channel_id=1, source_target_pairs={{0,1},{1,0},{2,3},{3,2},{4,5},{5,4},{6,7},{7,6},{8,9},{9,8},{10,11... | collective-permute-start | bytes 442376 | tf_op jit(solution)/shard_map/ppermute | solution.py:717
  47.8 0.1 fusion.1
  47.9 1.6 %collective-permute-start.18 = (bf16[2,2,72,256]{3,2,1,0:T(8,128)(2,1)S(1)}, bf16[2,2,72,256]{3,2,1,0:T(8,128)(2,1)S(1)}, u32[]{:S(2)}, u32[]{:S(2)}) collective-permute-start(bf16[2,2,72,256]{3,2,1,0:T(8,128)(2,1)S(1)} %select_bitcast_fusion.11), channel_id=1, source_target_pairs={{0,4},{1,5},{2,6},{3,7},{4,0},{5,1},{6,2},{7,3},{8,12},{9,13},{10,... | collective-permute-start | bytes 442376 | tf_op jit(solution)/shard_map/ppermute | solution.py:717
  49.5 0.8 collective-permute-done.10
  50.4 1.1 %collective-permute-start.11 = (bf16[2,72,256]{2,1,0:T(8,128)(2,1)S(1)}, bf16[2,72,256]{2,1,0:T(8,128)(2,1)S(1)}, u32[]{:S(2)}, u32[]{:S(2)}) collective-permute-start(bf16[2,72,256]{2,1,0:T(8,128)(2,1)S(1)} %select_bitcast_fusion.23), channel_id=1, source_target_pairs={{0,4},{1,5},{2,6},{3,7},{4,0},{5,1},{6,2},{7,3},{8,12},{9,13},{10,... | collective-permute-start | bytes 221192 | tf_op jit(solution)/shard_map/ppermute | solution.py:717
  51.5 1.6 %collective-permute-start.27 = (bf16[2,72,256]{2,1,0:T(8,128)(2,1)S(1)}, bf16[2,72,256]{2,1,0:T(8,128)(2,1)S(1)}, u32[]{:S(2)}, u32[]{:S(2)}) collective-permute-start(bf16[2,72,256]{2,1,0:T(8,128)(2,1)S(1)} %select_bitcast_fusion.17), channel_id=1, source_target_pairs={{0,2},{1,3},{2,0},{3,1},{4,6},{5,7},{6,4},{7,5},{8,10},{9,11},{10,... | collective-permute-start | bytes 221192 | tf_op jit(solution)/shard_map/ppermute | solution.py:717
  53.1 0.7 collective-permute-done.18
  53.9 0.9 collective-permute-start.19
  54.8 2.6 %collective-permute-start.12 = (bf16[72,256]{1,0:T(8,128)(2,1)S(1)}, bf16[72,256]{1,0:T(8,128)(2,1)S(1)}, u32[]{:S(2)}, u32[]{:S(2)}) collective-permute-start(bf16[72,256]{1,0:T(8,128)(2,1)S(1)} %select_bitcast_fusion.32), channel_id=1, source_target_pairs={{0,8},{1,9},{2,10},{3,11},{4,12},{5,13},{6,14},{7,15},{8,0},{9,1},... | collective-permute-start | bytes 110600 | tf_op jit(solution)/shard_map/ppermute | solution.py:717
  57.5 1.1 %collective-permute-start.28 = (bf16[72,256]{1,0:T(8,128)(2,1)S(1)}, bf16[72,256]{1,0:T(8,128)(2,1)S(1)}, u32[]{:S(2)}, u32[]{:S(2)}) collective-permute-start(bf16[72,256]{1,0:T(8,128)(2,1)S(1)} %select_bitcast_fusion.26), channel_id=1, source_target_pairs={{0,8},{1,9},{2,10},{3,11},{4,12},{5,13},{6,14},{7,15},{8,0},{9,1},... | collective-permute-start | bytes 110600 | tf_op jit(solution)/shard_map/ppermute | solution.py:717
  58.7 2.4 %collective-permute-start.20 = (bf16[72,256]{1,0:T(8,128)(2,1)S(1)}, bf16[72,256]{1,0:T(8,128)(2,1)S(1)}, u32[]{:S(2)}, u32[]{:S(2)}) collective-permute-start(bf16[72,256]{1,0:T(8,128)(2,1)S(1)} %select_bitcast_fusion.29), channel_id=1, source_target_pairs={{0,8},{1,9},{2,10},{3,11},{4,12},{5,13},{6,14},{7,15},{8,0},{9,1},... | collective-permute-start | bytes 110600 | tf_op jit(solution)/shard_map/ppermute | solution.py:717
  61.1 1.4 %collective-permute-start.13 = (bf16[72,256]{1,0:T(8,128)(2,1)S(1)}, bf16[72,256]{1,0:T(8,128)(2,1)S(1)}, u32[]{:S(2)}, u32[]{:S(2)}) collective-permute-start(bf16[72,256]{1,0:T(8,128)(2,1)S(1)} %fusion.11), channel_id=1, source_target_pairs={{0,8},{1,9},{2,10},{3,11},{4,12},{5,13},{6,14},{7,15},{8,0},{9,1},... | collective-permute-start | bytes 110600 | tf_op jit(solution)/shard_map/ppermute | solution.py:717
  62.5 0.1 collective-permute-done.28
  62.6 1.5 %collective-permute-start.29 = (bf16[72,256]{1,0:T(8,128)(2,1)S(1)}, bf16[72,256]{1,0:T(8,128)(2,1)S(1)}, u32[]{:S(2)}, u32[]{:S(2)}) collective-permute-start(bf16[72,256]{1,0:T(8,128)(2,1)S(1)} %fusion.9), channel_id=1, source_target_pairs={{0,8},{1,9},{2,10},{3,11},{4,12},{5,13},{6,14},{7,15},{8,0},{9,1},... | collective-permute-start | bytes 110600 | tf_op jit(solution)/shard_map/ppermute | solution.py:717
  64.2 0.6 collective-permute-done.20
  64.8 1.2 %collective-permute-start.21 = (bf16[72,256]{1,0:T(8,128)(2,1)S(1)}, bf16[72,256]{1,0:T(8,128)(2,1)S(1)}, u32[]{:S(2)}, u32[]{:S(2)}) collective-permute-start(bf16[72,256]{1,0:T(8,128)(2,1)S(1)} %fusion.10), channel_id=1, source_target_pairs={{0,8},{1,9},{2,10},{3,11},{4,12},{5,13},{6,14},{7,15},{8,0},{9,1},... | collective-permute-start | bytes 110600 | tf_op jit(solution)/shard_map/ppermute | solution.py:717
  66.0 0.1 collective-permute-done.13
  66.1 2.5 %collective-permute-start.14 = (bf16[2,72,256]{2,1,0:T(8,128)(2,1)S(1)}, bf16[2,72,256]{2,1,0:T(8,128)(2,1)S(1)}, u32[]{:S(2)}, u32[]{:S(2)}) collective-permute-start(bf16[2,72,256]{2,1,0:T(8,128)(2,1)S(1)} %pad_maximum_fusion.9), channel_id=1, source_target_pairs={{0,4},{1,5},{2,6},{3,7},{4,0},{5,1},{6,2},{7,3},{8,12},{9,13},{10,... | collective-permute-start | bytes 221192 | tf_op jit(solution)/shard_map/ppermute | solution.py:717
  68.7 1.4 %collective-permute-start.30 = (bf16[2,72,256]{2,1,0:T(8,128)(2,1)S(1)}, bf16[2,72,256]{2,1,0:T(8,128)(2,1)S(1)}, u32[]{:S(2)}, u32[]{:S(2)}) collective-permute-start(bf16[2,72,256]{2,1,0:T(8,128)(2,1)S(1)} %pad_maximum_fusion.11), channel_id=1, source_target_pairs={{0,2},{1,3},{2,0},{3,1},{4,6},{5,7},{6,4},{7,5},{8,10},{9,11},{10,... | collective-permute-start | bytes 221192 | tf_op jit(solution)/shard_map/ppermute | solution.py:717
  70.1 1.2 %collective-permute-start.22 = (bf16[2,72,256]{2,1,0:T(8,128)(2,1)S(1)}, bf16[2,72,256]{2,1,0:T(8,128)(2,1)S(1)}, u32[]{:S(2)}, u32[]{:S(2)}) collective-permute-start(bf16[2,72,256]{2,1,0:T(8,128)(2,1)S(1)} %pad_maximum_fusion.10), channel_id=1, source_target_pairs={{0,1},{1,0},{2,3},{3,2},{4,5},{5,4},{6,7},{7,6},{8,9},{9,8},{10,11... | collective-permute-start | bytes 221192 | tf_op jit(solution)/shard_map/ppermute | solution.py:717
  71.4 1.6 %collective-permute-start.15 = (bf16[2,2,72,256]{3,2,1,0:T(8,128)(2,1)S(1)}, bf16[2,2,72,256]{3,2,1,0:T(8,128)(2,1)S(1)}, u32[]{:S(2)}, u32[]{:S(2)}) collective-permute-start(bf16[2,2,72,256]{3,2,1,0:T(8,128)(2,1)S(1)} %pad_maximum_fusion.6), channel_id=1, source_target_pairs={{0,2},{1,3},{2,0},{3,1},{4,6},{5,7},{6,4},{7,5},{8,10},{9,11},{10,... | collective-permute-start | bytes 442376 | tf_op jit(solution)/shard_map/ppermute | solution.py:717
  72.9 0.1 collective-permute-done.30
  73.1 1.5 %collective-permute-start.31 = (bf16[2,2,72,256]{3,2,1,0:T(8,128)(2,1)S(1)}, bf16[2,2,72,256]{3,2,1,0:T(8,128)(2,1)S(1)}, u32[]{:S(2)}, u32[]{:S(2)}) collective-permute-start(bf16[2,2,72,256]{3,2,1,0:T(8,128)(2,1)S(1)} %pad_maximum_fusion.8), channel_id=1, source_target_pairs={{0,1},{1,0},{2,3},{3,2},{4,5},{5,4},{6,7},{7,6},{8,9},{9,8},{10,11... | collective-permute-start | bytes 442376 | tf_op jit(solution)/shard_map/ppermute | solution.py:717
  74.7 0.4 collective-permute-done.22
  75.1 1.5 %collective-permute-start.23 = (bf16[2,2,72,256]{3,2,1,0:T(8,128)(2,1)S(1)}, bf16[2,2,72,256]{3,2,1,0:T(8,128)(2,1)S(1)}, u32[]{:S(2)}, u32[]{:S(2)}) collective-permute-start(bf16[2,2,72,256]{3,2,1,0:T(8,128)(2,1)S(1)} %pad_maximum_fusion.7), channel_id=1, source_target_pairs={{0,4},{1,5},{2,6},{3,7},{4,0},{5,1},{6,2},{7,3},{8,12},{9,13},{10,... | collective-permute-start | bytes 442376 | tf_op jit(solution)/shard_map/ppermute | solution.py:717
  76.7 1.2 %collective-permute-start.16 = (bf16[2,2,2,72,256]{4,3,2,1,0:T(8,128)(2,1)S(1)}, bf16[2,2,2,72,256]{4,3,2,1,0:T(8,128)(2,1)S(1)}, u32[]{:S(2)}, u32[]{:S(2)}) collective-permute-start(bf16[2,2,2,72,256]{4,3,2,1,0:T(8,128)(2,1)S(1)} %pad_maximum_fusion.3), channel_id=1, source_target_pairs={{0,1},{1,0},{2,3},{3,2},{4,5},{5,4},{6,7},{7,6},{8,9},{9,8},{10,11... | collective-permute-start | bytes 884744 | tf_op jit(solution)/shard_map/ppermute | solution.py:717
  77.9 1.4 %collective-permute-done.31 = bf16[2,2,72,256]{3,2,1,0:T(8,128)(2,1)S(1)} collective-permute-done((bf16[2,2,72,256]{3,2,1,0:T(8,128)(2,1)S(1)}, bf16[2,2,72,256]{3,2,1,0:T(8,128)(2,1)S(1)}, u32[]{:S(2)}, u32[]{:S(2)}) %collective-permute-start.31) | collective-permute-done | bytes 147488 | tf_op jit(solution)/shard_map/ppermute | solution.py:717
  79.3 1.3 %collective-permute-start.32 = (bf16[2,2,2,72,256]{4,3,2,1,0:T(8,128)(2,1)S(1)}, bf16[2,2,2,72,256]{4,3,2,1,0:T(8,128)(2,1)S(1)}, u32[]{:S(2)}, u32[]{:S(2)}) collective-permute-start(bf16[2,2,2,72,256]{4,3,2,1,0:T(8,128)(2,1)S(1)} %pad_maximum_fusion.5), channel_id=1, source_target_pairs={{0,4},{1,5},{2,6},{3,7},{4,0},{5,1},{6,2},{7,3},{8,12},{9,13},{10,... | collective-permute-start | bytes 884744 | tf_op jit(solution)/shard_map/ppermute | solution.py:717
  80.7 2.2 %collective-permute-start.24 = (bf16[2,2,2,72,256]{4,3,2,1,0:T(8,128)(2,1)S(1)}, bf16[2,2,2,72,256]{4,3,2,1,0:T(8,128)(2,1)S(1)}, u32[]{:S(2)}, u32[]{:S(2)}) collective-permute-start(bf16[2,2,2,72,256]{4,3,2,1,0:T(8,128)(2,1)S(1)} %pad_maximum_fusion.4), channel_id=1, source_target_pairs={{0,2},{1,3},{2,0},{3,1},{4,6},{5,7},{6,4},{7,5},{8,10},{9,11},{10,... | collective-permute-start | bytes 884744 | tf_op jit(solution)/shard_map/ppermute | solution.py:717
  83.0 0.5 collective-permute-done.16
  83.5 2.6 %collective-permute-done.32 = bf16[2,2,2,72,256]{4,3,2,1,0:T(8,128)(2,1)S(1)} collective-permute-done((bf16[2,2,2,72,256]{4,3,2,1,0:T(8,128)(2,1)S(1)}, bf16[2,2,2,72,256]{4,3,2,1,0:T(8,128)(2,1)S(1)}, u32[]{:S(2)}, u32[]{:S(2)}) %collective-permute-start.32) | collective-permute-done | bytes 294944 | tf_op jit(solution)/shard_map/ppermute | solution.py:717
  86.2 1.5 %collective-permute-done.24 = bf16[2,2,2,72,256]{4,3,2,1,0:T(8,128)(2,1)S(1)} collective-permute-done((bf16[2,2,2,72,256]{4,3,2,1,0:T(8,128)(2,1)S(1)}, bf16[2,2,2,72,256]{4,3,2,1,0:T(8,128)(2,1)S(1)}, u32[]{:S(2)}, u32[]{:S(2)}) %collective-permute-start.24) | collective-permute-done | bytes 294944 | tf_op jit(solution)/shard_map/ppermute | solution.py:717
  88.0 0.3 squares.1.refs_4_
  88.4 1.1 %collective-permute-done.33.refs_5_ = f32[8,128]{1,0:T(8,128)S(1)} collective-permute-done((f32[8,128]{1,0:T(8,128)S(1)}, f32[8,128]{1,0:T(8,128)S(1)}, u32[]{:S(2)}, u32[]{:S(2)}) %collective-permute-start.33) | collective-permute-done | bytes 4128 | tf_op jit(solution)/shard_map/ppermute | solution.py:705
  89.6 0.4 copy-done.1
  90.0 0.2 copy-done.2
  90.2 0.3 copy-done
  90.5 6.6 %optimizer.1 = (f32[1,3328]{1,0:T(1,128)}, f32[1,2304]{1,0:T(1,128)}, f32[256,768]{1,0:T(8,128)}, f32[256,256]{1,0:T(8,128)}, f32[256,1024]{1,0:T(8,128)}, /*ind...) custom-call(s32[1]{0:T(128)} %bitcast.sec_ref, ...), custom_call_target="tpu_custom_call" | custom-call | tf_op jit(solution)/shard_map/optimizer/pallas_call | solution.py:685
  (99 shorter events, 1.5 us)
Async XLA Ops:
  0.7 3.4 %copy-start.12 = (f32[1,3328]{1,0:T(1,128)S(1)}, f32[1,3328]{1,0:T(1,128)}, u32[]{:S(2)}) copy-start(f32[1,3328]{1,0:T(1,128)} %refs_16_.2) | copy-start | bytes 39940
  0.7 3.8 %copy-start.14 = (f32[1,9,256]{2,0,1:T(1,128)S(1)}, f32[1,9,256]{2,0,1:T(1,128)}, u32[]{:S(2)}) copy-start(f32[1,9,256]{2,0,1:T(1,128)} %param.30) | copy-start | bytes 27652
  3.5 3.8 %collective-permute-start.2 = (bf16[256,2048]{1,0:T(8,128)(2,1)}, bf16[256,2048]{1,0:T(8,128)(2,1)S(1)}, u32[]{:S(2)}, u32[]{:S(2)}) collective-permute-start(bf16[256,2048]{1,0:T(8,128)(2,1)} %get-tuple-element.83.refs_6_), channel_id=1, source_target_pairs={{0,16},{16,0},{1,17},{17,1},{2,18},{18,2},{3,19},{19,3},{4,20},{20... | collective-permute-start | bytes 3145736 | tf_op jit(solution)/shard_map/ppermute | solution.py:705
  4.0 3.3 %collective-permute-start.3 = (bf16[1024,256]{1,0:T(8,128)(2,1)}, bf16[1024,256]{1,0:T(8,128)(2,1)S(1)}, u32[]{:S(2)}, u32[]{:S(2)}) collective-permute-start(bf16[1024,256]{1,0:T(8,128)(2,1)} %get-tuple-element.84.refs_8_), channel_id=1, source_target_pairs={{0,16},{16,0},{1,17},{17,1},{2,18},{18,2},{3,19},{19,3},{4,20},{20... | collective-permute-start | bytes 1572872 | tf_op jit(solution)/shard_map/ppermute | solution.py:705
  4.1 2.3 %collective-permute-start = (f32[1,3328]{1,0:T(1,128)S(1)}, f32[1,3328]{1,0:T(1,128)S(1)}, u32[]{:S(2)}, u32[]{:S(2)}) collective-permute-start(f32[1,3328]{1,0:T(1,128)S(1)} %copy-done.12), channel_id=1, source_target_pairs={{0,16},{16,0},{1,17},{17,1},{2,18},{18,2},{3,19},{19,3},{4,20},{20... | collective-permute-start | bytes 39944 | tf_op jit(solution)/shard_map/ppermute | solution.py:705
  4.5 1.8 %collective-permute-start.1 = (f32[1,2304]{1,0:T(1,128)S(1)}, f32[1,2304]{1,0:T(1,128)S(1)}, u32[]{:S(2)}, u32[]{:S(2)}) collective-permute-start(f32[1,2304]{1,0:T(1,128)S(1)} %bitcast.178), channel_id=1, source_target_pairs={{0,16},{16,0},{1,17},{17,1},{2,18},{18,2},{3,19},{19,3},{4,20},{20... | collective-permute-start | bytes 27656 | tf_op jit(solution)/shard_map/ppermute | solution.py:705
  29.0 2.1 %collective-permute-start.6 = (bf16[1152,256]{1,0:T(8,128)(2,1)S(1)}, bf16[1152,256]{1,0:T(8,128)(2,1)S(1)}, u32[]{:S(2)}, u32[]{:S(2)}) collective-permute-start(bf16[1152,256]{1,0:T(8,128)(2,1)S(1)} %get-tuple-element.94), channel_id=1, source_target_pairs={{0,16},{16,0},{1,17},{17,1},{2,18},{18,2},{3,19},{19,3},{4,20},{20... | collective-permute-start | bytes 1769480 | tf_op jit(solution)/shard_map/ppermute | solution.py:705
  29.5 2.5 %collective-permute-start.7 = (bf16[1152,256]{1,0:T(8,128)(2,1)S(1)}, bf16[1152,256]{1,0:T(8,128)(2,1)S(1)}, u32[]{:S(2)}, u32[]{:S(2)}) collective-permute-start(bf16[1152,256]{1,0:T(8,128)(2,1)S(1)} %get-tuple-element.96), channel_id=1, source_target_pairs={{0,16},{16,0},{1,17},{17,1},{2,18},{18,2},{3,19},{19,3},{4,20},{20... | collective-permute-start | bytes 1769480 | tf_op jit(solution)/shard_map/ppermute | solution.py:705
  29.6 58.8 %collective-permute-start.4 = (f32[304,256]{1,0:T(8,128)S(1)}, f32[304,256]{1,0:T(8,128)S(1)}, u32[]{:S(2)}, u32[]{:S(2)}) collective-permute-start(f32[304,256]{1,0:T(8,128)S(1)} %get-tuple-element.86), channel_id=1, source_target_pairs={{0,16},{16,0},{1,17},{17,1},{2,18},{18,2},{3,19},{19,3},{4,20},{20... | collective-permute-start | bytes 933896 | tf_op jit(solution)/shard_map/ppermute | solution.py:705
  30.0 58.4 %collective-permute-start.5 = (f32[304,256]{1,0:T(8,128)S(1)}, f32[304,256]{1,0:T(8,128)S(1)}, u32[]{:S(2)}, u32[]{:S(2)}) collective-permute-start(f32[304,256]{1,0:T(8,128)S(1)} %get-tuple-element.88), channel_id=1, source_target_pairs={{0,16},{16,0},{1,17},{17,1},{2,18},{18,2},{3,19},{19,3},{4,20},{20... | collective-permute-start | bytes 933896 | tf_op jit(solution)/shard_map/ppermute | solution.py:705
  30.1 3.6 %collective-permute-start.8 = (bf16[1152,256]{1,0:T(8,128)(2,1)S(1)}, bf16[1152,256]{1,0:T(8,128)(2,1)S(1)}, u32[]{:S(2)}, u32[]{:S(2)}) collective-permute-start(bf16[1152,256]{1,0:T(8,128)(2,1)S(1)} %get-tuple-element.98), channel_id=1, source_target_pairs={{0,16},{16,0},{1,17},{17,1},{2,18},{18,2},{3,19},{19,3},{4,20},{20... | collective-permute-start | bytes 1769480 | tf_op jit(solution)/shard_map/ppermute | solution.py:705
  33.9 10.2 %collective-permute-start.9 = (bf16[2,2,2,72,256]{4,3,2,1,0:T(8,128)(2,1)S(1)}, bf16[2,2,2,72,256]{4,3,2,1,0:T(8,128)(2,1)S(1)}, u32[]{:S(2)}, u32[]{:S(2)}) collective-permute-start(bf16[2,2,2,72,256]{4,3,2,1,0:T(8,128)(2,1)S(1)} %bitcast.187), channel_id=1, source_target_pairs={{0,1},{1,0},{2,3},{3,2},{4,5},{5,4},{6,7},{7,6},{8,9},{9,8},{10,11... | collective-permute-start | bytes 884744 | tf_op jit(solution)/shard_map/ppermute | solution.py:717
  36.9 9.2 %collective-permute-start.25 = (bf16[2,2,2,72,256]{4,3,2,1,0:T(8,128)(2,1)S(1)}, bf16[2,2,2,72,256]{4,3,2,1,0:T(8,128)(2,1)S(1)}, u32[]{:S(2)}, u32[]{:S(2)}) collective-permute-start(bf16[2,2,2,72,256]{4,3,2,1,0:T(8,128)(2,1)S(1)} %bitcast.186), channel_id=1, source_target_pairs={{0,4},{1,5},{2,6},{3,7},{4,0},{5,1},{6,2},{7,3},{8,12},{9,13},{10,... | collective-permute-start | bytes 884744 | tf_op jit(solution)/shard_map/ppermute | solution.py:717
  38.6 9.2 %collective-permute-start.17 = (bf16[2,2,2,72,256]{4,3,2,1,0:T(8,128)(2,1)S(1)}, bf16[2,2,2,72,256]{4,3,2,1,0:T(8,128)(2,1)S(1)}, u32[]{:S(2)}, u32[]{:S(2)}) collective-permute-start(bf16[2,2,2,72,256]{4,3,2,1,0:T(8,128)(2,1)S(1)} %bitcast.185), channel_id=1, source_target_pairs={{0,2},{1,3},{2,0},{3,1},{4,6},{5,7},{6,4},{7,5},{8,10},{9,11},{10,... | collective-permute-start | bytes 884744 | tf_op jit(solution)/shard_map/ppermute | solution.py:717
  44.2 6.0 %collective-permute-start.10 = (bf16[2,2,72,256]{3,2,1,0:T(8,128)(2,1)S(1)}, bf16[2,2,72,256]{3,2,1,0:T(8,128)(2,1)S(1)}, u32[]{:S(2)}, u32[]{:S(2)}) collective-permute-start(bf16[2,2,72,256]{3,2,1,0:T(8,128)(2,1)S(1)} %select_bitcast_fusion.14), channel_id=1, source_target_pairs={{0,2},{1,3},{2,0},{3,1},{4,6},{5,7},{6,4},{7,5},{8,10},{9,11},{10,... | collective-permute-start | bytes 442376 | tf_op jit(solution)/shard_map/ppermute | solution.py:717
  46.2 5.2 %collective-permute-start.26 = (bf16[2,2,72,256]{3,2,1,0:T(8,128)(2,1)S(1)}, bf16[2,2,72,256]{3,2,1,0:T(8,128)(2,1)S(1)}, u32[]{:S(2)}, u32[]{:S(2)}) collective-permute-start(bf16[2,2,72,256]{3,2,1,0:T(8,128)(2,1)S(1)} %select_bitcast_fusion.8), channel_id=1, source_target_pairs={{0,1},{1,0},{2,3},{3,2},{4,5},{5,4},{6,7},{7,6},{8,9},{9,8},{10,11... | collective-permute-start | bytes 442376 | tf_op jit(solution)/shard_map/ppermute | solution.py:717
  47.9 5.9 %collective-permute-start.18 = (bf16[2,2,72,256]{3,2,1,0:T(8,128)(2,1)S(1)}, bf16[2,2,72,256]{3,2,1,0:T(8,128)(2,1)S(1)}, u32[]{:S(2)}, u32[]{:S(2)}) collective-permute-start(bf16[2,2,72,256]{3,2,1,0:T(8,128)(2,1)S(1)} %select_bitcast_fusion.11), channel_id=1, source_target_pairs={{0,4},{1,5},{2,6},{3,7},{4,0},{5,1},{6,2},{7,3},{8,12},{9,13},{10,... | collective-permute-start | bytes 442376 | tf_op jit(solution)/shard_map/ppermute | solution.py:717
  50.4 4.4 %collective-permute-start.11 = (bf16[2,72,256]{2,1,0:T(8,128)(2,1)S(1)}, bf16[2,72,256]{2,1,0:T(8,128)(2,1)S(1)}, u32[]{:S(2)}, u32[]{:S(2)}) collective-permute-start(bf16[2,72,256]{2,1,0:T(8,128)(2,1)S(1)} %select_bitcast_fusion.23), channel_id=1, source_target_pairs={{0,4},{1,5},{2,6},{3,7},{4,0},{5,1},{6,2},{7,3},{8,12},{9,13},{10,... | collective-permute-start | bytes 221192 | tf_op jit(solution)/shard_map/ppermute | solution.py:717
  51.5 6.0 %collective-permute-start.27 = (bf16[2,72,256]{2,1,0:T(8,128)(2,1)S(1)}, bf16[2,72,256]{2,1,0:T(8,128)(2,1)S(1)}, u32[]{:S(2)}, u32[]{:S(2)}) collective-permute-start(bf16[2,72,256]{2,1,0:T(8,128)(2,1)S(1)} %select_bitcast_fusion.17), channel_id=1, source_target_pairs={{0,2},{1,3},{2,0},{3,1},{4,6},{5,7},{6,4},{7,5},{8,10},{9,11},{10,... | collective-permute-start | bytes 221192 | tf_op jit(solution)/shard_map/ppermute | solution.py:717
  53.9 4.8 %collective-permute-start.19 = (bf16[2,72,256]{2,1,0:T(8,128)(2,1)S(1)}, bf16[2,72,256]{2,1,0:T(8,128)(2,1)S(1)}, u32[]{:S(2)}, u32[]{:S(2)}) collective-permute-start(bf16[2,72,256]{2,1,0:T(8,128)(2,1)S(1)} %select_bitcast_fusion.20), channel_id=1, source_target_pairs={{0,1},{1,0},{2,3},{3,2},{4,5},{5,4},{6,7},{7,6},{8,9},{9,8},{10,11... | collective-permute-start | bytes 221192 | tf_op jit(solution)/shard_map/ppermute | solution.py:717
  54.8 6.2 %collective-permute-start.12 = (bf16[72,256]{1,0:T(8,128)(2,1)S(1)}, bf16[72,256]{1,0:T(8,128)(2,1)S(1)}, u32[]{:S(2)}, u32[]{:S(2)}) collective-permute-start(bf16[72,256]{1,0:T(8,128)(2,1)S(1)} %select_bitcast_fusion.32), channel_id=1, source_target_pairs={{0,8},{1,9},{2,10},{3,11},{4,12},{5,13},{6,14},{7,15},{8,0},{9,1},... | collective-permute-start | bytes 110600 | tf_op jit(solution)/shard_map/ppermute | solution.py:717
  57.5 5.1 %collective-permute-start.28 = (bf16[72,256]{1,0:T(8,128)(2,1)S(1)}, bf16[72,256]{1,0:T(8,128)(2,1)S(1)}, u32[]{:S(2)}, u32[]{:S(2)}) collective-permute-start(bf16[72,256]{1,0:T(8,128)(2,1)S(1)} %select_bitcast_fusion.26), channel_id=1, source_target_pairs={{0,8},{1,9},{2,10},{3,11},{4,12},{5,13},{6,14},{7,15},{8,0},{9,1},... | collective-permute-start | bytes 110600 | tf_op jit(solution)/shard_map/ppermute | solution.py:717
  58.7 6.1 %collective-permute-start.20 = (bf16[72,256]{1,0:T(8,128)(2,1)S(1)}, bf16[72,256]{1,0:T(8,128)(2,1)S(1)}, u32[]{:S(2)}, u32[]{:S(2)}) collective-permute-start(bf16[72,256]{1,0:T(8,128)(2,1)S(1)} %select_bitcast_fusion.29), channel_id=1, source_target_pairs={{0,8},{1,9},{2,10},{3,11},{4,12},{5,13},{6,14},{7,15},{8,0},{9,1},... | collective-permute-start | bytes 110600 | tf_op jit(solution)/shard_map/ppermute | solution.py:717
  61.1 5.0 %collective-permute-start.13 = (bf16[72,256]{1,0:T(8,128)(2,1)S(1)}, bf16[72,256]{1,0:T(8,128)(2,1)S(1)}, u32[]{:S(2)}, u32[]{:S(2)}) collective-permute-start(bf16[72,256]{1,0:T(8,128)(2,1)S(1)} %fusion.11), channel_id=1, source_target_pairs={{0,8},{1,9},{2,10},{3,11},{4,12},{5,13},{6,14},{7,15},{8,0},{9,1},... | collective-permute-start | bytes 110600 | tf_op jit(solution)/shard_map/ppermute | solution.py:717
  62.6 6.0 %collective-permute-start.29 = (bf16[72,256]{1,0:T(8,128)(2,1)S(1)}, bf16[72,256]{1,0:T(8,128)(2,1)S(1)}, u32[]{:S(2)}, u32[]{:S(2)}) collective-permute-start(bf16[72,256]{1,0:T(8,128)(2,1)S(1)} %fusion.9), channel_id=1, source_target_pairs={{0,8},{1,9},{2,10},{3,11},{4,12},{5,13},{6,14},{7,15},{8,0},{9,1},... | collective-permute-start | bytes 110600 | tf_op jit(solution)/shard_map/ppermute | solution.py:717
  64.8 5.3 %collective-permute-start.21 = (bf16[72,256]{1,0:T(8,128)(2,1)S(1)}, bf16[72,256]{1,0:T(8,128)(2,1)S(1)}, u32[]{:S(2)}, u32[]{:S(2)}) collective-permute-start(bf16[72,256]{1,0:T(8,128)(2,1)S(1)} %fusion.10), channel_id=1, source_target_pairs={{0,8},{1,9},{2,10},{3,11},{4,12},{5,13},{6,14},{7,15},{8,0},{9,1},... | collective-permute-start | bytes 110600 | tf_op jit(solution)/shard_map/ppermute | solution.py:717
  66.1 5.2 %collective-permute-start.14 = (bf16[2,72,256]{2,1,0:T(8,128)(2,1)S(1)}, bf16[2,72,256]{2,1,0:T(8,128)(2,1)S(1)}, u32[]{:S(2)}, u32[]{:S(2)}) collective-permute-start(bf16[2,72,256]{2,1,0:T(8,128)(2,1)S(1)} %pad_maximum_fusion.9), channel_id=1, source_target_pairs={{0,4},{1,5},{2,6},{3,7},{4,0},{5,1},{6,2},{7,3},{8,12},{9,13},{10,... | collective-permute-start | bytes 221192 | tf_op jit(solution)/shard_map/ppermute | solution.py:717
  68.7 4.4 %collective-permute-start.30 = (bf16[2,72,256]{2,1,0:T(8,128)(2,1)S(1)}, bf16[2,72,256]{2,1,0:T(8,128)(2,1)S(1)}, u32[]{:S(2)}, u32[]{:S(2)}) collective-permute-start(bf16[2,72,256]{2,1,0:T(8,128)(2,1)S(1)} %pad_maximum_fusion.11), channel_id=1, source_target_pairs={{0,2},{1,3},{2,0},{3,1},{4,6},{5,7},{6,4},{7,5},{8,10},{9,11},{10,... | collective-permute-start | bytes 221192 | tf_op jit(solution)/shard_map/ppermute | solution.py:717
  70.1 4.9 %collective-permute-start.22 = (bf16[2,72,256]{2,1,0:T(8,128)(2,1)S(1)}, bf16[2,72,256]{2,1,0:T(8,128)(2,1)S(1)}, u32[]{:S(2)}, u32[]{:S(2)}) collective-permute-start(bf16[2,72,256]{2,1,0:T(8,128)(2,1)S(1)} %pad_maximum_fusion.10), channel_id=1, source_target_pairs={{0,1},{1,0},{2,3},{3,2},{4,5},{5,4},{6,7},{7,6},{8,9},{9,8},{10,11... | collective-permute-start | bytes 221192 | tf_op jit(solution)/shard_map/ppermute | solution.py:717
  71.4 5.2 %collective-permute-start.15 = (bf16[2,2,72,256]{3,2,1,0:T(8,128)(2,1)S(1)}, bf16[2,2,72,256]{3,2,1,0:T(8,128)(2,1)S(1)}, u32[]{:S(2)}, u32[]{:S(2)}) collective-permute-start(bf16[2,2,72,256]{3,2,1,0:T(8,128)(2,1)S(1)} %pad_maximum_fusion.6), channel_id=1, source_target_pairs={{0,2},{1,3},{2,0},{3,1},{4,6},{5,7},{6,4},{7,5},{8,10},{9,11},{10,... | collective-permute-start | bytes 442376 | tf_op jit(solution)/shard_map/ppermute | solution.py:717
  73.1 6.2 %collective-permute-start.31 = (bf16[2,2,72,256]{3,2,1,0:T(8,128)(2,1)S(1)}, bf16[2,2,72,256]{3,2,1,0:T(8,128)(2,1)S(1)}, u32[]{:S(2)}, u32[]{:S(2)}) collective-permute-start(bf16[2,2,72,256]{3,2,1,0:T(8,128)(2,1)S(1)} %pad_maximum_fusion.8), channel_id=1, source_target_pairs={{0,1},{1,0},{2,3},{3,2},{4,5},{5,4},{6,7},{7,6},{8,9},{9,8},{10,11... | collective-permute-start | bytes 442376 | tf_op jit(solution)/shard_map/ppermute | solution.py:717
  75.1 5.6 %collective-permute-start.23 = (bf16[2,2,72,256]{3,2,1,0:T(8,128)(2,1)S(1)}, bf16[2,2,72,256]{3,2,1,0:T(8,128)(2,1)S(1)}, u32[]{:S(2)}, u32[]{:S(2)}) collective-permute-start(bf16[2,2,72,256]{3,2,1,0:T(8,128)(2,1)S(1)} %pad_maximum_fusion.7), channel_id=1, source_target_pairs={{0,4},{1,5},{2,6},{3,7},{4,0},{5,1},{6,2},{7,3},{8,12},{9,13},{10,... | collective-permute-start | bytes 442376 | tf_op jit(solution)/shard_map/ppermute | solution.py:717
  76.7 6.8 %collective-permute-start.16 = (bf16[2,2,2,72,256]{4,3,2,1,0:T(8,128)(2,1)S(1)}, bf16[2,2,2,72,256]{4,3,2,1,0:T(8,128)(2,1)S(1)}, u32[]{:S(2)}, u32[]{:S(2)}) collective-permute-start(bf16[2,2,2,72,256]{4,3,2,1,0:T(8,128)(2,1)S(1)} %pad_maximum_fusion.3), channel_id=1, source_target_pairs={{0,1},{1,0},{2,3},{3,2},{4,5},{5,4},{6,7},{7,6},{8,9},{9,8},{10,11... | collective-permute-start | bytes 884744 | tf_op jit(solution)/shard_map/ppermute | solution.py:717
  79.3 6.8 %collective-permute-start.32 = (bf16[2,2,2,72,256]{4,3,2,1,0:T(8,128)(2,1)S(1)}, bf16[2,2,2,72,256]{4,3,2,1,0:T(8,128)(2,1)S(1)}, u32[]{:S(2)}, u32[]{:S(2)}) collective-permute-start(bf16[2,2,2,72,256]{4,3,2,1,0:T(8,128)(2,1)S(1)} %pad_maximum_fusion.5), channel_id=1, source_target_pairs={{0,4},{1,5},{2,6},{3,7},{4,0},{5,1},{6,2},{7,3},{8,12},{9,13},{10,... | collective-permute-start | bytes 884744 | tf_op jit(solution)/shard_map/ppermute | solution.py:717
  80.6 8.9 %copy-start.17 = (f32[1,3328]{1,0:T(1,128)S(1)}, f32[1,3328]{1,0:T(1,128)}, u32[]{:S(2)}) copy-start(f32[1,3328]{1,0:T(1,128)} %refs_28_.1) | copy-start | bytes 39940
  80.6 8.9 %copy-start.19 = (f32[1,9,256]{2,0,1:T(1,128)S(1)}, f32[1,9,256]{2,0,1:T(1,128)}, u32[]{:S(2)}) copy-start(f32[1,9,256]{2,0,1:T(1,128)} %param.42) | copy-start | bytes 27652
  80.7 8.8 %copy-start.9 = (f32[1,256,768]{2,1,0:T(8,128)S(1)}, f32[1,256,768]{2,1,0:T(8,128)}, u32[]{:S(2)}) copy-start(f32[1,256,768]{2,1,0:T(8,128)} %param.43) | copy-start | bytes 2359300
  80.7 6.9 %collective-permute-start.24 = (bf16[2,2,2,72,256]{4,3,2,1,0:T(8,128)(2,1)S(1)}, bf16[2,2,2,72,256]{4,3,2,1,0:T(8,128)(2,1)S(1)}, u32[]{:S(2)}, u32[]{:S(2)}) collective-permute-start(bf16[2,2,2,72,256]{4,3,2,1,0:T(8,128)(2,1)S(1)} %pad_maximum_fusion.4), channel_id=1, source_target_pairs={{0,2},{1,3},{2,0},{3,1},{4,6},{5,7},{6,4},{7,5},{8,10},{9,11},{10,... | collective-permute-start | bytes 884744 | tf_op jit(solution)/shard_map/ppermute | solution.py:717
  83.5 6.1 %copy-start.8 = (f32[1,256,768]{2,1,0:T(8,128)S(1)}, f32[1,256,768]{2,1,0:T(8,128)}, u32[]{:S(2)}) copy-start(f32[1,256,768]{2,1,0:T(8,128)} %param.37) | copy-start | bytes 2359300
  83.5 6.1 %copy-start.11 = (f32[1,256,256]{2,1,0:T(8,128)S(1)}, f32[1,256,256]{2,1,0:T(8,128)}, u32[]{:S(2)}) copy-start(f32[1,256,256]{2,1,0:T(8,128)} %param.44) | copy-start | bytes 786436
  86.1 3.4 %copy-start.7 = (f32[1,1024,256]{2,1,0:T(8,128)S(1)}, f32[1,1024,256]{2,1,0:T(8,128)}, u32[]{:S(2)}) copy-start(f32[1,1024,256]{2,1,0:T(8,128)} %param.46) | copy-start | bytes 3145732
  86.1 3.4 %copy-start.10 = (f32[1,256,256]{2,1,0:T(8,128)S(1)}, f32[1,256,256]{2,1,0:T(8,128)}, u32[]{:S(2)}) copy-start(f32[1,256,256]{2,1,0:T(8,128)} %param.38) | copy-start | bytes 786436
  87.7 1.9 %copy-start.6 = (f32[1,256,1024]{2,1,0:T(8,128)S(1)}, f32[1,256,1024]{2,1,0:T(8,128)}, u32[]{:S(2)}) copy-start(f32[1,256,1024]{2,1,0:T(8,128)} %param.45) | copy-start | bytes 3145732
  87.7 1.9 %copy-start.4 = (f32[1,256,1024]{2,1,0:T(8,128)S(1)}, f32[1,256,1024]{2,1,0:T(8,128)}, u32[]{:S(2)}) copy-start(f32[1,256,1024]{2,1,0:T(8,128)} %param.39) | copy-start | bytes 3145732
  87.7 1.9 %copy-start.5 = (f32[1,1024,256]{2,1,0:T(8,128)S(1)}, f32[1,1024,256]{2,1,0:T(8,128)}, u32[]{:S(2)}) copy-start(f32[1,1024,256]{2,1,0:T(8,128)} %param.40) | copy-start | bytes 3145732
  87.8 1.8 %copy-start.3 = (f32[1,256,256]{2,1,0:T(8,128)S(1)}, f32[1,256,256]{2,1,0:T(8,128)}, u32[]{:S(2)}) copy-start(f32[1,256,256]{2,1,0:T(8,128)} %param.32) | copy-start | bytes 786436
  87.9 2.1 %copy-start.1 = (f32[1,1024,256]{2,1,0:T(8,128)S(1)}, f32[1,1024,256]{2,1,0:T(8,128)}, u32[]{:S(2)}) copy-start(f32[1,1024,256]{2,1,0:T(8,128)} %param.34) | copy-start | bytes 3145732
  87.9 2.3 %copy-start.2 = (f32[1,256,768]{2,1,0:T(8,128)S(1)}, f32[1,256,768]{2,1,0:T(8,128)}, u32[]{:S(2)}) copy-start(f32[1,256,768]{2,1,0:T(8,128)} %param.31) | copy-start | bytes 2359300
  88.0 2.6 %copy-start = (f32[1,256,1024]{2,1,0:T(8,128)S(1)}, f32[1,256,1024]{2,1,0:T(8,128)}, u32[]{:S(2)}) copy-start(f32[1,256,1024]{2,1,0:T(8,128)} %param.33) | copy-start | bytes 3145732
  88.0 2.6 %copy-start.13 = (f32[1,3328]{1,0:T(1,128)S(1)}, f32[1,3328]{1,0:T(1,128)}, u32[]{:S(2)}) copy-start(f32[1,3328]{1,0:T(1,128)} %refs_16_.2) | copy-start | bytes 39940
  88.0 2.6 %copy-start.15 = (f32[1,9,256]{2,0,1:T(1,128)S(1)}, f32[1,9,256]{2,0,1:T(1,128)}, u32[]{:S(2)}) copy-start(f32[1,9,256]{2,0,1:T(1,128)} %param.30) | copy-start | bytes 27652
  88.0 2.5 %copy-start.16 = (f32[1,3328]{1,0:T(1,128)S(1)}, f32[1,3328]{1,0:T(1,128)}, u32[]{:S(2)}) copy-start(f32[1,3328]{1,0:T(1,128)} %refs_22_.1) | copy-start | bytes 39940
  88.0 2.5 %copy-start.18 = (f32[1,9,256]{2,0,1:T(1,128)S(1)}, f32[1,9,256]{2,0,1:T(1,128)}, u32[]{:S(2)}) copy-start(f32[1,9,256]{2,0,1:T(1,128)} %param.36) | copy-start | bytes 27652
  88.3 1.2 %collective-permute-start.33 = (f32[8,128]{1,0:T(8,128)S(1)}, f32[8,128]{1,0:T(8,128)S(1)}, u32[]{:S(2)}, u32[]{:S(2)}) collective-permute-start(f32[8,128]{1,0:T(8,128)S(1)} %squares.1.refs_4_), channel_id=1, source_target_pairs={{0,16},{16,0},{1,17},{17,1},{2,18},{18,2},{3,19},{19,3},{4,20},{20... | collective-permute-start | bytes 12296 | tf_op jit(solution)/shard_map/ppermute | solution.py:705

commit v2 on v1

--- a/solution.py
+++ b/solution.py
@@ -38,7 +38,7 @@
 EXP_SCALE = SCALE * LOG2E
 OFF = -1e30
 ROWS = ((0, 80), (80, 80), (160, 80), (240, 64))
-PARTS = (1152, 1152, 1152)
+PARTS = (1024, 1024, 1088)
 
 
 def placement_tables():
@@ -470,7 +470,8 @@
     outs, grads, early, inner, outer = results
     small[...] = jnp.zeros_like(small)
     for part, rows in zip((early, inner, outer), PARTS):
-        part[:, FF:, :] = jnp.zeros((2, rows - FF, D), BF16)
+        if rows > FF:
+            part[:, FF:, :] = jnp.zeros((2, rows - FF, D), BF16)
     weights = [
         (wide.at[b, :, 0 : 3 * D], wide.at[b, :, 3 * D : 4 * D], wide.at[b, :, 4 * D : 8 * D], deep.at[b])
         for b in range(2)
@@ -605,100 +606,92 @@
     return clipped, moment_new, weight_new, average_new
 
 
-STEPS = 8
+SHAPES = ((1, VEC), (1, 9 * D), (D, 3 * D), (D, D), (D, FF), (FF, D))
+PIECES = (
+    (3, 0, 128),
+    (3, 128, 128),
+    (2, 0, 128),
+    (2, 128, 128),
+    (4, 0, 128),
+    (4, 128, 128),
+    (5, 0, 256),
+    (5, 256, 256),
+    (5, 512, 256),
+    (5, 768, 256),
+)
+OUT_SHAPES = [(shape, F32) for shape in SHAPES] * 4 + [(shape, BF16) for shape in SHAPES[2:]]
+MOVES = 4 + 4 * 2 + 5 * len(PIECES)
 
 
 def optimizer_step(sec_ref, *refs):
-    rows_in, refs = refs[:4], refs[4:]
-    (own, other), refs = refs[:2], refs[2:]
-    grads, refs = refs[:10], refs[10:]
-    states, refs = refs[:18], refs[18:]
-    outs, (norm_ref, *rows_out, sems) = refs[:28], refs[28:]
+    def take(count):
+        nonlocal refs
+        taken, refs = refs[:count], refs[count:]
+        return taken
+
+    rows_in, (own, other), (a, b, c), states = take(4), take(2), take(3), take(18)
+    outs, (norm_ref,), rows_out, made, (sems,) = take(28), take(1), take(2), take(28), take(1)
     sec = sec_ref[0]
     moves = []
+
+    def leave(source, target):
+        move = pltpu.make_async_copy(source, target, sems.at[len(moves)])
+        move.start()
+        moves.append(move)
+
     for index in range(4):
         first = pl.multiple_of((sec if index % 2 == 0 else 1 - sec) * MB_TOK, 8)
-        target = rows_out[index // 2].at[pl.ds(first, MB_TOK)]
-        moves.append(pltpu.make_async_copy(rows_in[index], target, sems.at[index]))
-
-    @pl.when(pl.program_id(0) == 0)
-    def _():
-        for move in moves:
-            move.start()
-
+        leave(rows_in[index], rows_out[index // 2].at[pl.ds(first, MB_TOK)])
     norm = jnp.sqrt(own[0:1, 0:1] + other[0:1, 0:1])
     factor = jnp.minimum(1.0, CLIP_LIMIT / (norm + 1e-06))
-
-    def put(index, lanes, grad):
-        weight, moment, average = (states[kind * 6 + index][:, lanes] for kind in range(3))
+    norm_ref[...] = norm
+
+    def put(index, rows, lanes, grad):
+        weight, moment, average = (states[kind * 6 + index][rows, lanes] for kind in range(3))
         new = updated(grad, weight, moment, average, factor)
         for kind in range(4):
-            outs[kind * 6 + index][:, lanes] = new[kind]
+            made[kind * 6 + index][rows, lanes] = new[kind]
         if index >= 2:
-            outs[24 + index - 2][:, lanes] = new[2].astype(BF16)
-
-    for part in range(3):
-        put(2, slice(part * D, (part + 1) * D), grads[part][...].astype(F32))
-    put(3, slice(0, D), grads[3][...].astype(F32))
-    for part in range(4):
-        put(4, slice(part * D, (part + 1) * D), grads[4 + part][...].astype(F32))
-    put(5, slice(0, D), grads[8][...].astype(F32))
-
-    @pl.when(pl.program_id(0) == 0)
-    def _():
-        rows = grads[9][...].astype(F32)
-        for part in range(13):
-            put(0, slice(part * D, (part + 1) * D), rows[part : part + 1, :])
-        for part in range(9):
-            put(1, slice(part * D, (part + 1) * D), rows[13 + part : 14 + part, :])
-        norm_ref[...] = norm
-
-    @pl.when(pl.program_id(0) == STEPS - 1)
-    def _():
-        for move in moves:
-            move.wait()
+            made[24 + index - 2][rows, lanes] = new[2].astype(BF16)
+
+    places = {2: [(a, 0), (a, D), (a, 2 * D)], 3: [(a, 3 * D)], 4: [(b, part * D) for part in range(4)], 5: [(c, 0)]}
+    step = 32
+    for index, first, count in PIECES:
+        for row in range(first, first + count, step):
+            for part, (ref, base) in enumerate(places[index]):
+                grad = ref[base + row : base + row + step, :].astype(F32)
+                put(index, slice(row, row + step), slice(part * D, (part + 1) * D), grad)
+        rows = pl.ds(first, count)
+        for kind in range(5):
+            at = kind * 6 + index if kind < 4 else 24 + index - 2
+            leave(made[at].at[rows], outs[at].at[rows])
+    rows = c[FF : FF + 32, :].astype(F32)
+    whole = slice(0, 1)
+    for part in range(13):
+        put(0, whole, slice(part * D, (part + 1) * D), rows[part : part + 1, :])
+    for part in range(9):
+        put(1, whole, slice(part * D, (part + 1) * D), rows[13 + part : 14 + part, :])
+    for index in range(2):
+        for kind in range(4):
+            leave(made[kind * 6 + index], outs[kind * 6 + index])
+    for move in moves:
+        move.wait()
 
 
 def run_optimizer(sec, rows_in, own, other, a, b, c, states):
-    rows = D // STEPS
-    deep = FF // STEPS
-
-    def fixed(shape):
-        return pl.BlockSpec(shape, lambda i: (0, 0))
-
-    def strip(first):
-        return pl.BlockSpec((rows, D), lambda i: (first * STEPS + i, 0))
-
-    grad_specs = [strip(0), strip(1), strip(2), strip(3)] + [strip(part) for part in range(4)]
-    grad_specs += [pl.BlockSpec((deep, D), lambda i: (i, 0)), pl.BlockSpec((32, D), lambda i: (FF // 32, 0))]
-    state_specs = [
-        fixed((1, VEC)),
-        fixed((1, 9 * D)),
-        pl.BlockSpec((rows, 3 * D), lambda i: (i, 0)),
-        pl.BlockSpec((rows, D), lambda i: (i, 0)),
-        pl.BlockSpec((rows, FF), lambda i: (i, 0)),
-        pl.BlockSpec((deep, D), lambda i: (i, 0)),
-    ]
-    shapes = [(1, VEC), (1, 9 * D), (D, 3 * D), (D, D), (D, FF), (FF, D)]
-    anywhere = pl.BlockSpec(memory_space=pltpu.HBM)
-    spaces = [pltpu.VMEM] * 4
+    vmem = pl.BlockSpec(memory_space=pltpu.VMEM)
+    hbm = pl.BlockSpec(memory_space=pltpu.HBM)
     return pl.pallas_call(
         optimizer_step,
-        grid=(STEPS,),
-        out_shape=[jax.ShapeDtypeStruct(shape, F32) for shape in shapes] * 4
-        + [jax.ShapeDtypeStruct(shape, BF16) for shape in shapes[2:]]
+        out_shape=[pltpu.HBM(shape, kind) for shape, kind in OUT_SHAPES]
         + [jax.ShapeDtypeStruct((1, 1), F32)]
-        + [jax.ShapeDtypeStruct((2 * MB_TOK, D), F32)] * 2,
-        in_specs=[pl.BlockSpec(memory_space=pltpu.SMEM)]
-        + [pl.BlockSpec(memory_space=space) for space in spaces]
-        + [fixed((8, HALF))] * 2
-        + grad_specs
-        + state_specs * 3,
-        out_specs=state_specs * 4 + state_specs[2:] + [fixed((1, 1))] + [anywhere] * 2,
-        scratch_shapes=[pltpu.SemaphoreType.DMA((4,))],
-        compiler_params=pltpu.CompilerParams(vmem_limit_bytes=24 << 20),
+        + [pltpu.HBM((2 * MB_TOK, D), F32)] * 2,
+        in_specs=[pl.BlockSpec(memory_space=pltpu.SMEM)] + [vmem] * (4 + 2 + 3 + 18),
+        out_specs=[hbm] * 28 + [vmem] + [hbm] * 2,
+        scratch_shapes=[pltpu.VMEM(shape, kind) for shape, kind in OUT_SHAPES] + [pltpu.SemaphoreType.DMA((MOVES,))],
+        compiler_params=pltpu.CompilerParams(vmem_limit_bytes=20 << 20),
         name="optimizer",
-    )(sec, *kept_in(rows_in, spaces), own, other, a, a, a, a, b, b, b, b, c, c, *states)
+    )(sec, *kept_in((*rows_in, own, other, a, b, c, *states), [pltpu.VMEM] * 27))
 
 
 def swapped(value):
@@ -720,7 +713,7 @@
 def exchange_bits():
     size = lax.axis_size("dp")
     bits = size.bit_length() - 1
-    if size != 1 << bits or any(rows % size for rows in PARTS):
+    if size < 2 or size != 1 << bits or any(2 * rows % size for rows in PARTS):
         return []
     index = lax.axis_index("dp")
     return [((index >> bit) & 1) == 0 for bit in range(bits)]
@@ -733,15 +726,15 @@
         return [lax.psum(part.astype(F32), "dp").astype(BF16) for part in parts]
     orders = exchange_orders(bits)
     shapes = [part.shape for part in parts]
-    held = [part.reshape((2,) * bits + (part.shape[0] // size, D)) for part in parts]
+    held = [part.reshape((2,) * (bits - 1) + (2 * part.shape[0] // size, D)) for part in parts]
     for step in range(bits):
-        kept, came = [], []
-        for value, order in zip(held, orders):
-            low = clear[order[step]]
-            kept.append(jnp.where(low, value[0], value[1]))
-            came.append(exchanged(jnp.where(low, value[1], value[0]), order[step], size))
+        kept, came = held, []
+        if step < bits - 1:
+            kept = [jnp.where(clear[order[step]], value[0], value[1]) for value, order in zip(held, orders)]
+            held = [jnp.where(clear[order[step]], value[1], value[0]) for value, order in zip(held, orders)]
+        came = [exchanged(value, order[step], size) for value, order in zip(held, orders)]
         held = [(a.astype(F32) + b.astype(F32)).astype(BF16) for a, b in zip(kept, came)]
-    for step in reversed(range(bits)):
+    for step in reversed(range(bits - 1)):
         grown = []
         for value, order in zip(held, orders):
             low = clear[order[step]]
@@ -775,7 +768,7 @@
         (own.astype(F32) + swapped(other).astype(F32)).astype(BF16)
         for own, other in zip(results[4::2], results[5::2])
     ]
-    a, b, c = summed_over_dp(lax.optimization_barrier(totals), clear)
+    a, b, c = summed_over_dp(totals, clear)
     squares = run_square_sum(a, b, c)
     rows_in = (results[0], swapped(results[1]), results[2], swapped(results[3]))
     new = run_optimizer(section, rows_in, squares, swapped(squares), a, b, c, states)

time: 97.5 us -> 86.8 us (0.89)
  starting transfers between devices: 42 us -> 33 us
    ppermute x24 -> x21, starting transfers between devices: 39.4 us -> 30.5 us  [exchanged(): lax.ppermute(value, 'dp', [(index, index ^ 1 << bit) for index in range(s...]
    ppermute x10, waiting for transfers between devices: 6.67 us -> 4.35 us  [swapped(): return lax.ppermute(value, 'section', [(0, 1), (1, 0)])]
    ppermute x24 -> x21, waiting for transfers between devices: 12.9 us -> 15.1 us  [exchanged(): lax.ppermute(value, 'dp', [(index, index ^ 1 << bit) for index in range(s...]
  transfers between devices with their start and end apart: 34 -> 31, of which waited for: 18 -> 18; matrix products, arithmetic and copies ran while one was open for 2% -> 2% of each run, Pallas kernels for 0% -> 0%
where the time goes in v2:
time: 86.8 us; the launch traced here: 86.7 us
  starting transfers between devices  33 us (38%)
  Pallas kernels  30.7 us (35%)
  waiting for transfers between devices  19.5 us (22%)
  other arithmetic  1.67 us (2%)
  between operations  1.37 us (2%)
    ppermute x21, starting transfers between devices, exchanged(): lax.ppermute(value, 'dp', [(index, index ^ 1 << bit) for index in range(s...  30.5 us
    pallas_call x1, Pallas kernels, run_blocks(): pl.pallas_call(section_step, out_shape=out_shape, in_specs=[smem] + [pl.B...  21.2 us
    ppermute x21, waiting for transfers between devices, exchanged(): lax.ppermute(value, 'dp', [(index, index ^ 1 << bit) for index in range(s...  15.1 us
    pallas_call x1, Pallas kernels, run_optimizer(): pl.pallas_call(optimizer_step, out_shape=[pltpu.HBM(shape, kind) for shap...  6.42 us
    ppermute x10, waiting for transfers between devices, swapped(): return lax.ppermute(value, 'section', [(0, 1), (1, 0)])  4.35 us
    pallas_call x1, Pallas kernels, run_narrowed(): pl.pallas_call(narrowed, out_shape=[pltpu.HBM((D, 8 * D), BF16), pltpu.HB...  2.78 us
    ppermute x10, starting transfers between devices, swapped(): return lax.ppermute(value, 'section', [(0, 1), (1, 0)])  2.58 us
  transfers between devices with their start and end apart: 31, of which 18 were waited for; matrix products, arithmetic and copies ran while one was open for 2% of the time, Pallas kernels for 0%

profile of v2, /device:TPU:0, one launch (start us, length us, event | category | flops | bytes accessed | tf_op | source)
XLA Modules:
  0.0 86.7 jit_solution(10397376718243119137)
XLA Ops:
  0.7 2.8 %narrowed.1 = (bf16[256,2048]{1,0:T(8,128)(2,1)}, bf16[1024,256]{1,0:T(8,128)(2,1)}) custom-call(f32[256,768]{1,0:T(8,128)} %bitcast.131, f32[256,256]{1,0:T(8,128)} %bitcast.137, f32[256,1024]{1,0:T(8,128)} %bitcast.127, f32[1024,256]{1,0:T(8,128)} %bitcast.129), custom_call_target="tpu_custom_call" | custom-call | tf_op jit(solution)/shard_map/narrowed/pallas_call | solution.py:561
  3.5 0.5 collective-permute-start.2
  4.0 0.1 collective-permute-start.3
  4.1 0.4 collective-permute-start
  4.5 0.1 collective-permute-start.1
  4.6 1.8 %collective-permute-done.1.refs_5_ = f32[1,2304]{1,0:T(1,128)S(1)} collective-permute-done((f32[1,2304]{1,0:T(1,128)S(1)}, f32[1,2304]{1,0:T(1,128)S(1)}, u32[]{:S(2)}, u32[]{:S(2)}) %collective-permute-start.1) | collective-permute-done | bytes 9248 | tf_op jit(solution)/shard_map/ppermute | solution.py:698
  6.4 0.9 %collective-permute-done.3.refs_9_ = bf16[1024,256]{1,0:T(8,128)(2,1)S(1)} collective-permute-done((bf16[1024,256]{1,0:T(8,128)(2,1)}, bf16[1024,256]{1,0:T(8,128)(2,1)S(1)}, u32[]{:S(2)}, u32[]{:S(2)}) %collective-permute-start.3) | collective-permute-done | bytes 524320 | tf_op jit(solution)/shard_map/ppermute | solution.py:698
  7.3 21.2 %blocks.1 = (f32[304,256]{1,0:T(8,128)S(1)}, f32[304,256]{1,0:T(8,128)S(1)}, f32[304,256]{1,0:T(8,128)S(1)}, f32[304,256]{1,0:T(8,128)S(1)}, bf16[1024,256]{1,0:...) custom-call(s32[1]{0:T(128)} %bitcast.sec_ref, ...), custom_call_target="tpu_custom_call" | custom-call | tf_op jit(solution)/shard_map/blocks/pallas_call | solution.py:521
  28.5 0.4 collective-permute-start.6
  29.0 0.1 collective-permute-start.14
  29.1 0.4 collective-permute-start.4
  29.5 0.1 collective-permute-start.5
  29.6 0.4 collective-permute-start.22
  30.0 0.5 collective-permute-done.6
  30.5 0.1 add_convert_fusion.2
  30.7 2.9 %collective-permute-start.7 = (bf16[2,2,128,256]{3,2,1,0:T(8,128)(2,1)S(1)}, bf16[2,2,128,256]{3,2,1,0:T(8,128)(2,1)S(1)}, u32[]{:S(2)}, u32[]{:S(2)}) collective-permute-start(bf16[2,2,128,256]{3,2,1,0:T(8,128)(2,1)S(1)} %bitcast.152), channel_id=1, source_target_pairs={{0,1},{1,0},{2,3},{3,2},{4,5},{5,4},{6,7},{7,6},{8,9},{9,8},{10,11... | collective-permute-start | bytes 786440 | tf_op jit(solution)/shard_map/ppermute | solution.py:710
  33.6 0.2 add_convert_fusion.1
  33.8 1.6 %collective-permute-start.15 = (bf16[2,2,128,256]{3,2,1,0:T(8,128)(2,1)S(1)}, bf16[2,2,128,256]{3,2,1,0:T(8,128)(2,1)S(1)}, u32[]{:S(2)}, u32[]{:S(2)}) collective-permute-start(bf16[2,2,128,256]{3,2,1,0:T(8,128)(2,1)S(1)} %bitcast.153), channel_id=1, source_target_pairs={{0,2},{1,3},{2,0},{3,1},{4,6},{5,7},{6,4},{7,5},{8,10},{9,11},{10,... | collective-permute-start | bytes 786440 | tf_op jit(solution)/shard_map/ppermute | solution.py:710
  35.4 0.2 add_convert_fusion
  35.6 1.6 %collective-permute-start.23 = (bf16[2,2,136,256]{3,2,1,0:T(8,128)(2,1)S(1)}, bf16[2,2,136,256]{3,2,1,0:T(8,128)(2,1)S(1)}, u32[]{:S(2)}, u32[]{:S(2)}) collective-permute-start(bf16[2,2,136,256]{3,2,1,0:T(8,128)(2,1)S(1)} %bitcast.151), channel_id=1, source_target_pairs={{0,4},{1,5},{2,6},{3,7},{4,0},{5,1},{6,2},{7,3},{8,12},{9,13},{10,... | collective-permute-start | bytes 835592 | tf_op jit(solution)/shard_map/ppermute | solution.py:710
  37.3 3.0 %collective-permute-done.7 = bf16[2,2,128,256]{3,2,1,0:T(8,128)(2,1)S(1)} collective-permute-done((bf16[2,2,128,256]{3,2,1,0:T(8,128)(2,1)S(1)}, bf16[2,2,128,256]{3,2,1,0:T(8,128)(2,1)S(1)}, u32[]{:S(2)}, u32[]{:S(2)}) %collective-permute-start.7) | collective-permute-done | bytes 262176 | tf_op jit(solution)/shard_map/ppermute | solution.py:710
  40.2 0.1 fusion.2
  40.3 1.8 %collective-permute-start.8 = (bf16[2,128,256]{2,1,0:T(8,128)(2,1)S(1)}, bf16[2,128,256]{2,1,0:T(8,128)(2,1)S(1)}, u32[]{:S(2)}, u32[]{:S(2)}) collective-permute-start(bf16[2,128,256]{2,1,0:T(8,128)(2,1)S(1)} %select_bitcast_fusion.14), channel_id=1, source_target_pairs={{0,2},{1,3},{2,0},{3,1},{4,6},{5,7},{6,4},{7,5},{8,10},{9,11},{10,... | collective-permute-start | bytes 393224 | tf_op jit(solution)/shard_map/ppermute | solution.py:710
  42.2 0.1 fusion.1
  42.2 1.6 %collective-permute-start.16 = (bf16[2,128,256]{2,1,0:T(8,128)(2,1)S(1)}, bf16[2,128,256]{2,1,0:T(8,128)(2,1)S(1)}, u32[]{:S(2)}, u32[]{:S(2)}) collective-permute-start(bf16[2,128,256]{2,1,0:T(8,128)(2,1)S(1)} %select_bitcast_fusion.11), channel_id=1, source_target_pairs={{0,4},{1,5},{2,6},{3,7},{4,0},{5,1},{6,2},{7,3},{8,12},{9,13},{10,... | collective-permute-start | bytes 393224 | tf_op jit(solution)/shard_map/ppermute | solution.py:710
  43.9 0.1 fusion
  44.0 1.6 %collective-permute-start.24 = (bf16[2,136,256]{2,1,0:T(8,128)(2,1)S(1)}, bf16[2,136,256]{2,1,0:T(8,128)(2,1)S(1)}, u32[]{:S(2)}, u32[]{:S(2)}) collective-permute-start(bf16[2,136,256]{2,1,0:T(8,128)(2,1)S(1)} %select_bitcast_fusion.8), channel_id=1, source_target_pairs={{0,1},{1,0},{2,3},{3,2},{4,5},{5,4},{6,7},{7,6},{8,9},{9,8},{10,11... | collective-permute-start | bytes 417800 | tf_op jit(solution)/shard_map/ppermute | solution.py:710
  45.6 1.7 %collective-permute-start.9 = (bf16[128,256]{1,0:T(8,128)(2,1)S(1)}, bf16[128,256]{1,0:T(8,128)(2,1)S(1)}, u32[]{:S(2)}, u32[]{:S(2)}) collective-permute-start(bf16[128,256]{1,0:T(8,128)(2,1)S(1)} %select_bitcast_fusion.23), channel_id=1, source_target_pairs={{0,4},{1,5},{2,6},{3,7},{4,0},{5,1},{6,2},{7,3},{8,12},{9,13},{10,... | collective-permute-start | bytes 196616 | tf_op jit(solution)/shard_map/ppermute | solution.py:710
  47.3 0.4 collective-permute-done.16
  47.8 1.8 %collective-permute-start.17 = (bf16[128,256]{1,0:T(8,128)(2,1)S(1)}, bf16[128,256]{1,0:T(8,128)(2,1)S(1)}, u32[]{:S(2)}, u32[]{:S(2)}) collective-permute-start(bf16[128,256]{1,0:T(8,128)(2,1)S(1)} %select_bitcast_fusion.20), channel_id=1, source_target_pairs={{0,1},{1,0},{2,3},{3,2},{4,5},{5,4},{6,7},{7,6},{8,9},{9,8},{10,11... | collective-permute-start | bytes 196616 | tf_op jit(solution)/shard_map/ppermute | solution.py:710
  49.6 0.2 collective-permute-done.24
  49.8 0.1 fusion.3
  49.9 1.4 %collective-permute-start.25 = (bf16[136,256]{1,0:T(8,128)(2,1)S(1)}, bf16[136,256]{1,0:T(8,128)(2,1)S(1)}, u32[]{:S(2)}, u32[]{:S(2)}) collective-permute-start(bf16[136,256]{1,0:T(8,128)(2,1)S(1)} %select_bitcast_fusion.17), channel_id=1, source_target_pairs={{0,2},{1,3},{2,0},{3,1},{4,6},{5,7},{6,4},{7,5},{8,10},{9,11},{10,... | collective-permute-start | bytes 208904 | tf_op jit(solution)/shard_map/ppermute | solution.py:710
  51.3 2.7 %collective-permute-start.10 = (bf16[128,256]{1,0:T(8,128)(2,1)S(1)}, bf16[128,256]{1,0:T(8,128)(2,1)S(1)}, u32[]{:S(2)}, u32[]{:S(2)}) collective-permute-start(bf16[128,256]{1,0:T(8,128)(2,1)S(1)} %fusion.8), channel_id=1, source_target_pairs={{0,8},{1,9},{2,10},{3,11},{4,12},{5,13},{6,14},{7,15},{8,0},{9,1},... | collective-permute-start | bytes 196616 | tf_op jit(solution)/shard_map/ppermute | solution.py:710
  54.0 0.9 %collective-permute-start.18 = (bf16[128,256]{1,0:T(8,128)(2,1)S(1)}, bf16[128,256]{1,0:T(8,128)(2,1)S(1)}, u32[]{:S(2)}, u32[]{:S(2)}) collective-permute-start(bf16[128,256]{1,0:T(8,128)(2,1)S(1)} %fusion.7), channel_id=1, source_target_pairs={{0,8},{1,9},{2,10},{3,11},{4,12},{5,13},{6,14},{7,15},{8,0},{9,1},... | collective-permute-start | bytes 196616 | tf_op jit(solution)/shard_map/ppermute | solution.py:710
  54.9 2.2 %collective-permute-start.26 = (bf16[136,256]{1,0:T(8,128)(2,1)S(1)}, bf16[136,256]{1,0:T(8,128)(2,1)S(1)}, u32[]{:S(2)}, u32[]{:S(2)}) collective-permute-start(bf16[136,256]{1,0:T(8,128)(2,1)S(1)} %fusion.6), channel_id=1, source_target_pairs={{0,8},{1,9},{2,10},{3,11},{4,12},{5,13},{6,14},{7,15},{8,0},{9,1},... | collective-permute-start | bytes 208904 | tf_op jit(solution)/shard_map/ppermute | solution.py:710
  57.1 1.7 %collective-permute-done.10 = bf16[128,256]{1,0:T(8,128)(2,1)S(1)} collective-permute-done((bf16[128,256]{1,0:T(8,128)(2,1)S(1)}, bf16[128,256]{1,0:T(8,128)(2,1)S(1)}, u32[]{:S(2)}, u32[]{:S(2)}) %collective-permute-start.10) | collective-permute-done | bytes 65568 | tf_op jit(solution)/shard_map/ppermute | solution.py:710
  58.9 0.2 collective-permute-start.11
  59.0 1.2 %collective-permute-done.18 = bf16[128,256]{1,0:T(8,128)(2,1)S(1)} collective-permute-done((bf16[128,256]{1,0:T(8,128)(2,1)S(1)}, bf16[128,256]{1,0:T(8,128)(2,1)S(1)}, u32[]{:S(2)}, u32[]{:S(2)}) %collective-permute-start.18) | collective-permute-done | bytes 65568 | tf_op jit(solution)/shard_map/ppermute | solution.py:710
  60.3 1.3 %collective-permute-start.19 = (bf16[128,256]{1,0:T(8,128)(2,1)S(1)}, bf16[128,256]{1,0:T(8,128)(2,1)S(1)}, u32[]{:S(2)}, u32[]{:S(2)}) collective-permute-start(bf16[128,256]{1,0:T(8,128)(2,1)S(1)} %add_convert_fusion.4), channel_id=1, source_target_pairs={{0,1},{1,0},{2,3},{3,2},{4,5},{5,4},{6,7},{7,6},{8,9},{9,8},{10,11... | collective-permute-start | bytes 196616 | tf_op jit(solution)/shard_map/ppermute | solution.py:710
  61.7 0.1 collective-permute-done.26
  61.8 1.5 %collective-permute-start.27 = (bf16[136,256]{1,0:T(8,128)(2,1)S(1)}, bf16[136,256]{1,0:T(8,128)(2,1)S(1)}, u32[]{:S(2)}, u32[]{:S(2)}) collective-permute-start(bf16[136,256]{1,0:T(8,128)(2,1)S(1)} %add_convert_fusion.3), channel_id=1, source_target_pairs={{0,2},{1,3},{2,0},{3,1},{4,6},{5,7},{6,4},{7,5},{8,10},{9,11},{10,... | collective-permute-start | bytes 208904 | tf_op jit(solution)/shard_map/ppermute | solution.py:710
  63.3 1.1 %collective-permute-start.12 = (bf16[2,128,256]{2,1,0:T(8,128)(2,1)S(1)}, bf16[2,128,256]{2,1,0:T(8,128)(2,1)S(1)}, u32[]{:S(2)}, u32[]{:S(2)}) collective-permute-start(bf16[2,128,256]{2,1,0:T(8,128)(2,1)S(1)} %pad_maximum_fusion.7), channel_id=1, source_target_pairs={{0,2},{1,3},{2,0},{3,1},{4,6},{5,7},{6,4},{7,5},{8,10},{9,11},{10,... | collective-permute-start | bytes 393224 | tf_op jit(solution)/shard_map/ppermute | solution.py:710
  64.4 0.2 collective-permute-done.19
  64.7 0.9 collective-permute-start.20
  65.5 0.6 collective-permute-done.27
  66.2 1.3 %collective-permute-start.28 = (bf16[2,136,256]{2,1,0:T(8,128)(2,1)S(1)}, bf16[2,136,256]{2,1,0:T(8,128)(2,1)S(1)}, u32[]{:S(2)}, u32[]{:S(2)}) collective-permute-start(bf16[2,136,256]{2,1,0:T(8,128)(2,1)S(1)} %pad_maximum_fusion.6), channel_id=1, source_target_pairs={{0,1},{1,0},{2,3},{3,2},{4,5},{5,4},{6,7},{7,6},{8,9},{9,8},{10,11... | collective-permute-start | bytes 417800 | tf_op jit(solution)/shard_map/ppermute | solution.py:710
  67.6 1.5 %collective-permute-done.12 = bf16[2,128,256]{2,1,0:T(8,128)(2,1)S(1)} collective-permute-done((bf16[2,128,256]{2,1,0:T(8,128)(2,1)S(1)}, bf16[2,128,256]{2,1,0:T(8,128)(2,1)S(1)}, u32[]{:S(2)}, u32[]{:S(2)}) %collective-permute-start.12) | collective-permute-done | bytes 131104 | tf_op jit(solution)/shard_map/ppermute | solution.py:710
  69.1 1.1 %collective-permute-start.13 = (bf16[2,2,128,256]{3,2,1,0:T(8,128)(2,1)S(1)}, bf16[2,2,128,256]{3,2,1,0:T(8,128)(2,1)S(1)}, u32[]{:S(2)}, u32[]{:S(2)}) collective-permute-start(bf16[2,2,128,256]{3,2,1,0:T(8,128)(2,1)S(1)} %pad_maximum_fusion.4), channel_id=1, source_target_pairs={{0,1},{1,0},{2,3},{3,2},{4,5},{5,4},{6,7},{7,6},{8,9},{9,8},{10,11... | collective-permute-start | bytes 786440 | tf_op jit(solution)/shard_map/ppermute | solution.py:710
  70.3 0.2 collective-permute-done.20
  70.6 0.5 collective-permute-start.21
  71.1 0.3 collective-permute-done.28
  71.4 0.8 collective-permute-start.29
  72.2 3.4 %collective-permute-done.13 = bf16[2,2,128,256]{3,2,1,0:T(8,128)(2,1)S(1)} collective-permute-done((bf16[2,2,128,256]{3,2,1,0:T(8,128)(2,1)S(1)}, bf16[2,2,128,256]{3,2,1,0:T(8,128)(2,1)S(1)}, u32[]{:S(2)}, u32[]{:S(2)}) %collective-permute-start.13) | collective-permute-done | bytes 262176 | tf_op jit(solution)/shard_map/ppermute | solution.py:710
  75.6 1.4 %collective-permute-done.21 = bf16[2,2,128,256]{3,2,1,0:T(8,128)(2,1)S(1)} collective-permute-done((bf16[2,2,128,256]{3,2,1,0:T(8,128)(2,1)S(1)}, bf16[2,2,128,256]{3,2,1,0:T(8,128)(2,1)S(1)}, u32[]{:S(2)}, u32[]{:S(2)}) %collective-permute-start.21) | collective-permute-done | bytes 262176 | tf_op jit(solution)/shard_map/ppermute | solution.py:710
  77.0 0.1 pad_maximum_fusion.1
  77.1 0.1 pad_maximum_fusion.2
  77.2 0.8 collective-permute-done.29
  78.1 0.1 pad_maximum_fusion
  78.2 0.3 squares.1.refs_4_
  78.5 1.1 %collective-permute-done.30.refs_5_ = f32[8,128]{1,0:T(8,128)S(1)} collective-permute-done((f32[8,128]{1,0:T(8,128)S(1)}, f32[8,128]{1,0:T(8,128)S(1)}, u32[]{:S(2)}, u32[]{:S(2)}) %collective-permute-start.30) | collective-permute-done | bytes 4128 | tf_op jit(solution)/shard_map/ppermute | solution.py:698
  79.8 0.2 copy-done
  80.0 0.1 copy-done.10
  80.1 6.4 %optimizer.1 = (f32[1,3328]{1,0:T(1,128)}, f32[1,2304]{1,0:T(1,128)}, f32[256,768]{1,0:T(8,128)}, f32[256,256]{1,0:T(8,128)}, f32[256,1024]{1,0:T(8,128)}, /*ind...) custom-call(s32[1]{0:T(128)} %bitcast.sec_ref, ...), custom_call_target="tpu_custom_call" | custom-call | tf_op jit(solution)/shard_map/optimizer/pallas_call | solution.py:684
  (84 shorter events, 1.0 us)
Async XLA Ops:
  0.7 3.4 %copy-start.12 = (f32[1,3328]{1,0:T(1,128)S(1)}, f32[1,3328]{1,0:T(1,128)}, u32[]{:S(2)}) copy-start(f32[1,3328]{1,0:T(1,128)} %refs_9_.1) | copy-start | bytes 39940
  0.7 3.8 %copy-start.14 = (f32[1,9,256]{2,0,1:T(1,128)S(1)}, f32[1,9,256]{2,0,1:T(1,128)}, u32[]{:S(2)}) copy-start(f32[1,9,256]{2,0,1:T(1,128)} %param.30) | copy-start | bytes 27652
  3.5 3.8 %collective-permute-start.2 = (bf16[256,2048]{1,0:T(8,128)(2,1)}, bf16[256,2048]{1,0:T(8,128)(2,1)S(1)}, u32[]{:S(2)}, u32[]{:S(2)}) collective-permute-start(bf16[256,2048]{1,0:T(8,128)(2,1)} %get-tuple-element.79.refs_6_), channel_id=1, source_target_pairs={{0,16},{16,0},{1,17},{17,1},{2,18},{18,2},{3,19},{19,3},{4,20},{20... | collective-permute-start | bytes 3145736 | tf_op jit(solution)/shard_map/ppermute | solution.py:698
  4.0 3.3 %collective-permute-start.3 = (bf16[1024,256]{1,0:T(8,128)(2,1)}, bf16[1024,256]{1,0:T(8,128)(2,1)S(1)}, u32[]{:S(2)}, u32[]{:S(2)}) collective-permute-start(bf16[1024,256]{1,0:T(8,128)(2,1)} %get-tuple-element.80.refs_8_), channel_id=1, source_target_pairs={{0,16},{16,0},{1,17},{17,1},{2,18},{18,2},{3,19},{19,3},{4,20},{20... | collective-permute-start | bytes 1572872 | tf_op jit(solution)/shard_map/ppermute | solution.py:698
  4.1 2.3 %collective-permute-start = (f32[1,3328]{1,0:T(1,128)S(1)}, f32[1,3328]{1,0:T(1,128)S(1)}, u32[]{:S(2)}, u32[]{:S(2)}) collective-permute-start(f32[1,3328]{1,0:T(1,128)S(1)} %copy-done.12), channel_id=1, source_target_pairs={{0,16},{16,0},{1,17},{17,1},{2,18},{18,2},{3,19},{19,3},{4,20},{20... | collective-permute-start | bytes 39944 | tf_op jit(solution)/shard_map/ppermute | solution.py:698
  4.5 1.8 %collective-permute-start.1 = (f32[1,2304]{1,0:T(1,128)S(1)}, f32[1,2304]{1,0:T(1,128)S(1)}, u32[]{:S(2)}, u32[]{:S(2)}) collective-permute-start(f32[1,2304]{1,0:T(1,128)S(1)} %bitcast.144), channel_id=1, source_target_pairs={{0,16},{16,0},{1,17},{17,1},{2,18},{18,2},{3,19},{19,3},{4,20},{20... | collective-permute-start | bytes 27656 | tf_op jit(solution)/shard_map/ppermute | solution.py:698
  28.5 2.0 %collective-permute-start.6 = (bf16[1024,256]{1,0:T(8,128)(2,1)S(1)}, bf16[1024,256]{1,0:T(8,128)(2,1)S(1)}, u32[]{:S(2)}, u32[]{:S(2)}) collective-permute-start(bf16[1024,256]{1,0:T(8,128)(2,1)S(1)} %get-tuple-element.89), channel_id=1, source_target_pairs={{0,16},{16,0},{1,17},{17,1},{2,18},{18,2},{3,19},{19,3},{4,20},{20... | collective-permute-start | bytes 1572872 | tf_op jit(solution)/shard_map/ppermute | solution.py:698
  29.0 4.6 %collective-permute-start.14 = (bf16[1024,256]{1,0:T(8,128)(2,1)S(1)}, bf16[1024,256]{1,0:T(8,128)(2,1)S(1)}, u32[]{:S(2)}, u32[]{:S(2)}) collective-permute-start(bf16[1024,256]{1,0:T(8,128)(2,1)S(1)} %get-tuple-element.91), channel_id=1, source_target_pairs={{0,16},{16,0},{1,17},{17,1},{2,18},{18,2},{3,19},{19,3},{4,20},{20... | collective-permute-start | bytes 1572872 | tf_op jit(solution)/shard_map/ppermute | solution.py:698
  29.1 49.4 %collective-permute-start.4 = (f32[304,256]{1,0:T(8,128)S(1)}, f32[304,256]{1,0:T(8,128)S(1)}, u32[]{:S(2)}, u32[]{:S(2)}) collective-permute-start(f32[304,256]{1,0:T(8,128)S(1)} %get-tuple-element.82), channel_id=1, source_target_pairs={{0,16},{16,0},{1,17},{17,1},{2,18},{18,2},{3,19},{19,3},{4,20},{20... | collective-permute-start | bytes 933896 | tf_op jit(solution)/shard_map/ppermute | solution.py:698
  29.5 49.0 %collective-permute-start.5 = (f32[304,256]{1,0:T(8,128)S(1)}, f32[304,256]{1,0:T(8,128)S(1)}, u32[]{:S(2)}, u32[]{:S(2)}) collective-permute-start(f32[304,256]{1,0:T(8,128)S(1)} %get-tuple-element.84), channel_id=1, source_target_pairs={{0,16},{16,0},{1,17},{17,1},{2,18},{18,2},{3,19},{19,3},{4,20},{20... | collective-permute-start | bytes 933896 | tf_op jit(solution)/shard_map/ppermute | solution.py:698
  29.6 5.8 %collective-permute-start.22 = (bf16[1088,256]{1,0:T(8,128)(2,1)S(1)}, bf16[1088,256]{1,0:T(8,128)(2,1)S(1)}, u32[]{:S(2)}, u32[]{:S(2)}) collective-permute-start(bf16[1088,256]{1,0:T(8,128)(2,1)S(1)} %get-tuple-element.93), channel_id=1, source_target_pairs={{0,16},{16,0},{1,17},{17,1},{2,18},{18,2},{3,19},{19,3},{4,20},{20... | collective-permute-start | bytes 1671176 | tf_op jit(solution)/shard_map/ppermute | solution.py:698
  30.7 9.5 %collective-permute-start.7 = (bf16[2,2,128,256]{3,2,1,0:T(8,128)(2,1)S(1)}, bf16[2,2,128,256]{3,2,1,0:T(8,128)(2,1)S(1)}, u32[]{:S(2)}, u32[]{:S(2)}) collective-permute-start(bf16[2,2,128,256]{3,2,1,0:T(8,128)(2,1)S(1)} %bitcast.152), channel_id=1, source_target_pairs={{0,1},{1,0},{2,3},{3,2},{4,5},{5,4},{6,7},{7,6},{8,9},{9,8},{10,11... | collective-permute-start | bytes 786440 | tf_op jit(solution)/shard_map/ppermute | solution.py:710
  33.8 8.3 %collective-permute-start.15 = (bf16[2,2,128,256]{3,2,1,0:T(8,128)(2,1)S(1)}, bf16[2,2,128,256]{3,2,1,0:T(8,128)(2,1)S(1)}, u32[]{:S(2)}, u32[]{:S(2)}) collective-permute-start(bf16[2,2,128,256]{3,2,1,0:T(8,128)(2,1)S(1)} %bitcast.153), channel_id=1, source_target_pairs={{0,2},{1,3},{2,0},{3,1},{4,6},{5,7},{6,4},{7,5},{8,10},{9,11},{10,... | collective-permute-start | bytes 786440 | tf_op jit(solution)/shard_map/ppermute | solution.py:710
  35.6 8.3 %collective-permute-start.23 = (bf16[2,2,136,256]{3,2,1,0:T(8,128)(2,1)S(1)}, bf16[2,2,136,256]{3,2,1,0:T(8,128)(2,1)S(1)}, u32[]{:S(2)}, u32[]{:S(2)}) collective-permute-start(bf16[2,2,136,256]{3,2,1,0:T(8,128)(2,1)S(1)} %bitcast.151), channel_id=1, source_target_pairs={{0,4},{1,5},{2,6},{3,7},{4,0},{5,1},{6,2},{7,3},{8,12},{9,13},{10,... | collective-permute-start | bytes 835592 | tf_op jit(solution)/shard_map/ppermute | solution.py:710
  40.3 5.2 %collective-permute-start.8 = (bf16[2,128,256]{2,1,0:T(8,128)(2,1)S(1)}, bf16[2,128,256]{2,1,0:T(8,128)(2,1)S(1)}, u32[]{:S(2)}, u32[]{:S(2)}) collective-permute-start(bf16[2,128,256]{2,1,0:T(8,128)(2,1)S(1)} %select_bitcast_fusion.14), channel_id=1, source_target_pairs={{0,2},{1,3},{2,0},{3,1},{4,6},{5,7},{6,4},{7,5},{8,10},{9,11},{10,... | collective-permute-start | bytes 393224 | tf_op jit(solution)/shard_map/ppermute | solution.py:710
  42.2 5.5 %collective-permute-start.16 = (bf16[2,128,256]{2,1,0:T(8,128)(2,1)S(1)}, bf16[2,128,256]{2,1,0:T(8,128)(2,1)S(1)}, u32[]{:S(2)}, u32[]{:S(2)}) collective-permute-start(bf16[2,128,256]{2,1,0:T(8,128)(2,1)S(1)} %select_bitcast_fusion.11), channel_id=1, source_target_pairs={{0,4},{1,5},{2,6},{3,7},{4,0},{5,1},{6,2},{7,3},{8,12},{9,13},{10,... | collective-permute-start | bytes 393224 | tf_op jit(solution)/shard_map/ppermute | solution.py:710
  44.0 5.8 %collective-permute-start.24 = (bf16[2,136,256]{2,1,0:T(8,128)(2,1)S(1)}, bf16[2,136,256]{2,1,0:T(8,128)(2,1)S(1)}, u32[]{:S(2)}, u32[]{:S(2)}) collective-permute-start(bf16[2,136,256]{2,1,0:T(8,128)(2,1)S(1)} %select_bitcast_fusion.8), channel_id=1, source_target_pairs={{0,1},{1,0},{2,3},{3,2},{4,5},{5,4},{6,7},{7,6},{8,9},{9,8},{10,11... | collective-permute-start | bytes 417800 | tf_op jit(solution)/shard_map/ppermute | solution.py:710
  45.6 5.7 %collective-permute-start.9 = (bf16[128,256]{1,0:T(8,128)(2,1)S(1)}, bf16[128,256]{1,0:T(8,128)(2,1)S(1)}, u32[]{:S(2)}, u32[]{:S(2)}) collective-permute-start(bf16[128,256]{1,0:T(8,128)(2,1)S(1)} %select_bitcast_fusion.23), channel_id=1, source_target_pairs={{0,4},{1,5},{2,6},{3,7},{4,0},{5,1},{6,2},{7,3},{8,12},{9,13},{10,... | collective-permute-start | bytes 196616 | tf_op jit(solution)/shard_map/ppermute | solution.py:710
  47.8 6.2 %collective-permute-start.17 = (bf16[128,256]{1,0:T(8,128)(2,1)S(1)}, bf16[128,256]{1,0:T(8,128)(2,1)S(1)}, u32[]{:S(2)}, u32[]{:S(2)}) collective-permute-start(bf16[128,256]{1,0:T(8,128)(2,1)S(1)} %select_bitcast_fusion.20), channel_id=1, source_target_pairs={{0,1},{1,0},{2,3},{3,2},{4,5},{5,4},{6,7},{7,6},{8,9},{9,8},{10,11... | collective-permute-start | bytes 196616 | tf_op jit(solution)/shard_map/ppermute | solution.py:710
  49.9 5.0 %collective-permute-start.25 = (bf16[136,256]{1,0:T(8,128)(2,1)S(1)}, bf16[136,256]{1,0:T(8,128)(2,1)S(1)}, u32[]{:S(2)}, u32[]{:S(2)}) collective-permute-start(bf16[136,256]{1,0:T(8,128)(2,1)S(1)} %select_bitcast_fusion.17), channel_id=1, source_target_pairs={{0,2},{1,3},{2,0},{3,1},{4,6},{5,7},{6,4},{7,5},{8,10},{9,11},{10,... | collective-permute-start | bytes 208904 | tf_op jit(solution)/shard_map/ppermute | solution.py:710
  51.3 7.5 %collective-permute-start.10 = (bf16[128,256]{1,0:T(8,128)(2,1)S(1)}, bf16[128,256]{1,0:T(8,128)(2,1)S(1)}, u32[]{:S(2)}, u32[]{:S(2)}) collective-permute-start(bf16[128,256]{1,0:T(8,128)(2,1)S(1)} %fusion.8), channel_id=1, source_target_pairs={{0,8},{1,9},{2,10},{3,11},{4,12},{5,13},{6,14},{7,15},{8,0},{9,1},... | collective-permute-start | bytes 196616 | tf_op jit(solution)/shard_map/ppermute | solution.py:710
  54.0 6.3 %collective-permute-start.18 = (bf16[128,256]{1,0:T(8,128)(2,1)S(1)}, bf16[128,256]{1,0:T(8,128)(2,1)S(1)}, u32[]{:S(2)}, u32[]{:S(2)}) collective-permute-start(bf16[128,256]{1,0:T(8,128)(2,1)S(1)} %fusion.7), channel_id=1, source_target_pairs={{0,8},{1,9},{2,10},{3,11},{4,12},{5,13},{6,14},{7,15},{8,0},{9,1},... | collective-permute-start | bytes 196616 | tf_op jit(solution)/shard_map/ppermute | solution.py:710
  54.9 6.8 %collective-permute-start.26 = (bf16[136,256]{1,0:T(8,128)(2,1)S(1)}, bf16[136,256]{1,0:T(8,128)(2,1)S(1)}, u32[]{:S(2)}, u32[]{:S(2)}) collective-permute-start(bf16[136,256]{1,0:T(8,128)(2,1)S(1)} %fusion.6), channel_id=1, source_target_pairs={{0,8},{1,9},{2,10},{3,11},{4,12},{5,13},{6,14},{7,15},{8,0},{9,1},... | collective-permute-start | bytes 208904 | tf_op jit(solution)/shard_map/ppermute | solution.py:710
  58.9 4.4 %collective-permute-start.11 = (bf16[128,256]{1,0:T(8,128)(2,1)S(1)}, bf16[128,256]{1,0:T(8,128)(2,1)S(1)}, u32[]{:S(2)}, u32[]{:S(2)}) collective-permute-start(bf16[128,256]{1,0:T(8,128)(2,1)S(1)} %add_convert_fusion.5), channel_id=1, source_target_pairs={{0,4},{1,5},{2,6},{3,7},{4,0},{5,1},{6,2},{7,3},{8,12},{9,13},{10,... | collective-permute-start | bytes 196616 | tf_op jit(solution)/shard_map/ppermute | solution.py:710
  60.3 4.3 %collective-permute-start.19 = (bf16[128,256]{1,0:T(8,128)(2,1)S(1)}, bf16[128,256]{1,0:T(8,128)(2,1)S(1)}, u32[]{:S(2)}, u32[]{:S(2)}) collective-permute-start(bf16[128,256]{1,0:T(8,128)(2,1)S(1)} %add_convert_fusion.4), channel_id=1, source_target_pairs={{0,1},{1,0},{2,3},{3,2},{4,5},{5,4},{6,7},{7,6},{8,9},{9,8},{10,11... | collective-permute-start | bytes 196616 | tf_op jit(solution)/shard_map/ppermute | solution.py:710
  61.8 4.4 %collective-permute-start.27 = (bf16[136,256]{1,0:T(8,128)(2,1)S(1)}, bf16[136,256]{1,0:T(8,128)(2,1)S(1)}, u32[]{:S(2)}, u32[]{:S(2)}) collective-permute-start(bf16[136,256]{1,0:T(8,128)(2,1)S(1)} %add_convert_fusion.3), channel_id=1, source_target_pairs={{0,2},{1,3},{2,0},{3,1},{4,6},{5,7},{6,4},{7,5},{8,10},{9,11},{10,... | collective-permute-start | bytes 208904 | tf_op jit(solution)/shard_map/ppermute | solution.py:710
  63.3 5.8 %collective-permute-start.12 = (bf16[2,128,256]{2,1,0:T(8,128)(2,1)S(1)}, bf16[2,128,256]{2,1,0:T(8,128)(2,1)S(1)}, u32[]{:S(2)}, u32[]{:S(2)}) collective-permute-start(bf16[2,128,256]{2,1,0:T(8,128)(2,1)S(1)} %pad_maximum_fusion.7), channel_id=1, source_target_pairs={{0,2},{1,3},{2,0},{3,1},{4,6},{5,7},{6,4},{7,5},{8,10},{9,11},{10,... | collective-permute-start | bytes 393224 | tf_op jit(solution)/shard_map/ppermute | solution.py:710
  64.7 5.7 %collective-permute-start.20 = (bf16[2,128,256]{2,1,0:T(8,128)(2,1)S(1)}, bf16[2,128,256]{2,1,0:T(8,128)(2,1)S(1)}, u32[]{:S(2)}, u32[]{:S(2)}) collective-permute-start(bf16[2,128,256]{2,1,0:T(8,128)(2,1)S(1)} %pad_maximum_fusion.8), channel_id=1, source_target_pairs={{0,4},{1,5},{2,6},{3,7},{4,0},{5,1},{6,2},{7,3},{8,12},{9,13},{10,... | collective-permute-start | bytes 393224 | tf_op jit(solution)/shard_map/ppermute | solution.py:710
  66.2 5.1 %collective-permute-start.28 = (bf16[2,136,256]{2,1,0:T(8,128)(2,1)S(1)}, bf16[2,136,256]{2,1,0:T(8,128)(2,1)S(1)}, u32[]{:S(2)}, u32[]{:S(2)}) collective-permute-start(bf16[2,136,256]{2,1,0:T(8,128)(2,1)S(1)} %pad_maximum_fusion.6), channel_id=1, source_target_pairs={{0,1},{1,0},{2,3},{3,2},{4,5},{5,4},{6,7},{7,6},{8,9},{9,8},{10,11... | collective-permute-start | bytes 417800 | tf_op jit(solution)/shard_map/ppermute | solution.py:710
  69.1 6.4 %collective-permute-start.13 = (bf16[2,2,128,256]{3,2,1,0:T(8,128)(2,1)S(1)}, bf16[2,2,128,256]{3,2,1,0:T(8,128)(2,1)S(1)}, u32[]{:S(2)}, u32[]{:S(2)}) collective-permute-start(bf16[2,2,128,256]{3,2,1,0:T(8,128)(2,1)S(1)} %pad_maximum_fusion.4), channel_id=1, source_target_pairs={{0,1},{1,0},{2,3},{3,2},{4,5},{5,4},{6,7},{7,6},{8,9},{9,8},{10,11... | collective-permute-start | bytes 786440 | tf_op jit(solution)/shard_map/ppermute | solution.py:710
  70.4 9.2 %copy-start.11 = (f32[1,256,256]{2,1,0:T(8,128)S(1)}, f32[1,256,256]{2,1,0:T(8,128)}, u32[]{:S(2)}) copy-start(f32[1,256,256]{2,1,0:T(8,128)} %param.44) | copy-start | bytes 786436
  70.5 9.2 %copy-start.15 = (f32[1,9,256]{2,0,1:T(1,128)S(1)}, f32[1,9,256]{2,0,1:T(1,128)}, u32[]{:S(2)}) copy-start(f32[1,9,256]{2,0,1:T(1,128)} %param.30) | copy-start | bytes 27652
  70.5 9.2 %copy-start.16 = (f32[1,3328]{1,0:T(1,128)S(1)}, f32[1,3328]{1,0:T(1,128)}, u32[]{:S(2)}) copy-start(f32[1,3328]{1,0:T(1,128)} %refs_15_.2) | copy-start | bytes 39940
  70.5 9.2 %copy-start.17 = (f32[1,3328]{1,0:T(1,128)S(1)}, f32[1,3328]{1,0:T(1,128)}, u32[]{:S(2)}) copy-start(f32[1,3328]{1,0:T(1,128)} %refs_21_.1) | copy-start | bytes 39940
  70.5 9.2 %copy-start.18 = (f32[1,9,256]{2,0,1:T(1,128)S(1)}, f32[1,9,256]{2,0,1:T(1,128)}, u32[]{:S(2)}) copy-start(f32[1,9,256]{2,0,1:T(1,128)} %param.36) | copy-start | bytes 27652
  70.5 9.2 %copy-start.19 = (f32[1,9,256]{2,0,1:T(1,128)S(1)}, f32[1,9,256]{2,0,1:T(1,128)}, u32[]{:S(2)}) copy-start(f32[1,9,256]{2,0,1:T(1,128)} %param.42) | copy-start | bytes 27652
  70.6 6.4 %collective-permute-start.21 = (bf16[2,2,128,256]{3,2,1,0:T(8,128)(2,1)S(1)}, bf16[2,2,128,256]{3,2,1,0:T(8,128)(2,1)S(1)}, u32[]{:S(2)}, u32[]{:S(2)}) collective-permute-start(bf16[2,2,128,256]{3,2,1,0:T(8,128)(2,1)S(1)} %pad_maximum_fusion.5), channel_id=1, source_target_pairs={{0,2},{1,3},{2,0},{3,1},{4,6},{5,7},{6,4},{7,5},{8,10},{9,11},{10,... | collective-permute-start | bytes 786440 | tf_op jit(solution)/shard_map/ppermute | solution.py:710
  71.3 8.4 %copy-start.9 = (f32[1,256,768]{2,1,0:T(8,128)S(1)}, f32[1,256,768]{2,1,0:T(8,128)}, u32[]{:S(2)}) copy-start(f32[1,256,768]{2,1,0:T(8,128)} %param.43) | copy-start | bytes 2359300
  71.4 8.3 %copy-start.8 = (f32[1,256,768]{2,1,0:T(8,128)S(1)}, f32[1,256,768]{2,1,0:T(8,128)}, u32[]{:S(2)}) copy-start(f32[1,256,768]{2,1,0:T(8,128)} %param.37) | copy-start | bytes 2359300
  71.4 6.6 %collective-permute-start.29 = (bf16[2,2,136,256]{3,2,1,0:T(8,128)(2,1)S(1)}, bf16[2,2,136,256]{3,2,1,0:T(8,128)(2,1)S(1)}, u32[]{:S(2)}, u32[]{:S(2)}) collective-permute-start(bf16[2,2,136,256]{3,2,1,0:T(8,128)(2,1)S(1)} %pad_maximum_fusion.3), channel_id=1, source_target_pairs={{0,4},{1,5},{2,6},{3,7},{4,0},{5,1},{6,2},{7,3},{8,12},{9,13},{10,... | collective-permute-start | bytes 835592 | tf_op jit(solution)/shard_map/ppermute | solution.py:710
  75.6 4.1 %copy-start.6 = (f32[1,1024,256]{2,1,0:T(8,128)S(1)}, f32[1,1024,256]{2,1,0:T(8,128)}, u32[]{:S(2)}) copy-start(f32[1,1024,256]{2,1,0:T(8,128)} %param.46) | copy-start | bytes 3145732
  77.0 2.7 %copy-start.5 = (f32[1,256,1024]{2,1,0:T(8,128)S(1)}, f32[1,256,1024]{2,1,0:T(8,128)}, u32[]{:S(2)}) copy-start(f32[1,256,1024]{2,1,0:T(8,128)} %param.45) | copy-start | bytes 3145732
  77.0 2.7 %copy-start.4 = (f32[1,1024,256]{2,1,0:T(8,128)S(1)}, f32[1,1024,256]{2,1,0:T(8,128)}, u32[]{:S(2)}) copy-start(f32[1,1024,256]{2,1,0:T(8,128)} %param.40) | copy-start | bytes 3145732
  77.1 2.6 %copy-start.3 = (f32[1,256,1024]{2,1,0:T(8,128)S(1)}, f32[1,256,1024]{2,1,0:T(8,128)}, u32[]{:S(2)}) copy-start(f32[1,256,1024]{2,1,0:T(8,128)} %param.39) | copy-start | bytes 3145732
  78.0 1.7 %copy-start.2 = (f32[1,256,768]{2,1,0:T(8,128)S(1)}, f32[1,256,768]{2,1,0:T(8,128)}, u32[]{:S(2)}) copy-start(f32[1,256,768]{2,1,0:T(8,128)} %param.31) | copy-start | bytes 2359300
  78.1 1.7 %copy-start.1 = (f32[1,1024,256]{2,1,0:T(8,128)S(1)}, f32[1,1024,256]{2,1,0:T(8,128)}, u32[]{:S(2)}) copy-start(f32[1,1024,256]{2,1,0:T(8,128)} %param.34) | copy-start | bytes 3145732
  78.1 1.8 %copy-start = (f32[1,256,1024]{2,1,0:T(8,128)S(1)}, f32[1,256,1024]{2,1,0:T(8,128)}, u32[]{:S(2)}) copy-start(f32[1,256,1024]{2,1,0:T(8,128)} %param.33) | copy-start | bytes 3145732
  78.2 1.8 %copy-start.7 = (f32[1,256,256]{2,1,0:T(8,128)S(1)}, f32[1,256,256]{2,1,0:T(8,128)}, u32[]{:S(2)}) copy-start(f32[1,256,256]{2,1,0:T(8,128)} %param.32) | copy-start | bytes 786436
  78.2 1.9 %copy-start.10 = (f32[1,256,256]{2,1,0:T(8,128)S(1)}, f32[1,256,256]{2,1,0:T(8,128)}, u32[]{:S(2)}) copy-start(f32[1,256,256]{2,1,0:T(8,128)} %param.38) | copy-start | bytes 786436
  78.2 1.9 %copy-start.13 = (f32[1,3328]{1,0:T(1,128)S(1)}, f32[1,3328]{1,0:T(1,128)}, u32[]{:S(2)}) copy-start(f32[1,3328]{1,0:T(1,128)} %refs_9_.1) | copy-start | bytes 39940
  78.5 1.2 %collective-permute-start.30 = (f32[8,128]{1,0:T(8,128)S(1)}, f32[8,128]{1,0:T(8,128)S(1)}, u32[]{:S(2)}, u32[]{:S(2)}) collective-permute-start(f32[8,128]{1,0:T(8,128)S(1)} %squares.1.refs_4_), channel_id=1, source_target_pairs={{0,16},{16,0},{1,17},{17,1},{2,18},{18,2},{3,19},{19,3},{4,20},{20... | collective-permute-start | bytes 12296 | tf_op jit(solution)/shard_map/ppermute | solution.py:698

commit v3 on v2

--- a/solution.py
+++ b/solution.py
@@ -29,10 +29,9 @@
 BF16 = jnp.bfloat16
 
 GROUP = 128
-GROUPS = ((0, 112), (112, 84), (196, 108))
-KINDS = (0, 0, 1)
-NGROUP = len(GROUPS)
-ATT = NGROUP * GROUP
+WINDOWS = ((0, BIG_SIDE, 0, 112), (112, BIG_SIDE, 0, 84), (192, SMALL_SIDE, 4, 108))
+NGROUP = len(WINDOWS)
+LONG_TOK = 320
 SCALE = HEAD ** -0.5
 LOG2E = 1.4426950408889634
 EXP_SCALE = SCALE * LOG2E
@@ -41,41 +40,37 @@
 PARTS = (1024, 1024, 1088)
 
 
-def placement_tables():
-    plain = np.zeros((ATT, MB_TOK), np.float32)
-    turned = np.zeros((ATT, MB_TOK), np.float32)
-    transposed = []
+def turned_table():
+    turned = np.zeros((MB_TOK, MB_TOK), np.float32)
     base = 0
     for side, count in ((BIG_SIDE, BIG_MB), (SMALL_SIDE, SMALL_MB)):
         for _ in range(count):
             for row in range(side):
                 for col in range(side):
-                    transposed.append(base + col * side + row)
+                    turned[base + row * side + col, base + col * side + row] = 1.0
             base += side * side
-    for group, (first, size) in enumerate(GROUPS):
+    return turned
+
+
+def stripe_tables():
+    shifts = np.zeros((NGROUP, 5 * GROUP, GROUP), np.float32)
+    fence = np.full((NGROUP, GROUP, GROUP), OFF, np.float32)
+    lower = np.zeros((NGROUP, GROUP, HALF), np.float32)
+    for kind, (_, side, first, size) in enumerate(WINDOWS):
+        stripe = 2 * side
+        number = (np.arange(GROUP) - first) // stripe
+        number[:first] = -1
+        number[first + size :] = GROUP
+        fence[kind][number[:, None] == number[None, :]] = 0.0
         for at in range(size):
-            plain[group * GROUP + at, first + at] = 1.0
-            turned[group * GROUP + at, transposed[first + at]] = 1.0
-    return plain, turned
-
-
-def stripe_tables():
-    shifts = np.zeros((2, 5 * GROUP, GROUP), np.float32)
-    fence = np.full((2, GROUP, GROUP), OFF, np.float32)
-    lower = np.zeros((2, GROUP, HALF), np.float32)
-    for kind, (side, sizes) in enumerate(((BIG_SIDE, 112), (SMALL_SIDE, 108))):
-        stripe = 2 * side
-        for at in range(GROUP):
-            own = at // stripe
-            fence[kind, at, own * stripe : (own + 1) * stripe] = 0.0
-        for at in range(sizes):
             own, inner = divmod(at, stripe)
             row, col = divmod(inner, side)
-            lower[kind, at, :] = float(row)
+            lower[kind, first + at, :] = float(row)
             moves = ((row, col - 1), (row, col + 1), (1 - row, col - 1), (1 - row, col), (1 - row, col + 1))
             for move, (to_row, to_col) in enumerate(moves):
                 if 0 <= to_col < side:
-                    shifts[kind, move * GROUP + at, own * stripe + to_row * side + to_col] = 1.0
+                    target = first + own * stripe + to_row * side + to_col
+                    shifts[kind, move * GROUP + first + at, target] = 1.0
     return shifts, fence, lower
 
 
@@ -144,15 +139,30 @@
     return jnp.sum(x.astype(F32), axis=0, keepdims=True)
 
 
+def window(group):
+    return pl.ds(WINDOWS[group][0], GROUP)
+
+
+def put_window(ref, group, value):
+    if group == 0:
+        ref[0:112, :] = value[0:112].astype(BF16)
+    elif group == 1:
+        ref[112:208, :] = value[0:96].astype(BF16)
+    else:
+        before = lax.broadcasted_iota(jnp.int32, (16, value.shape[1]), 0) < 4
+        ref[192:208, :] = jnp.where(before, ref[192:208, :].astype(F32), value[0:16]).astype(BF16)
+        ref[208:304, :] = value[16:112].astype(BF16)
+
+
 def vec_at(vec, index, width=1):
     return vec[:, index * D : (index + width) * D]
 
 
 def forward_block(x_ref, out_ref, vec_ref, taps_ref, w, saved, tables, work, need):
     wq, wp, w1, w2 = w
-    (hat1, scale1, normed, qkv, probs, mixed, hat2, scale2, normed2, slope, activ) = saved
-    plain, turned, plain_t, turned_t, shifts, fence, lower = tables
-    normed_nat, mixed_att, middle, hidden = work
+    (hat1, scale1, normed, qkv, probs, probs_low, mixed, hat2, scale2, normed2, slope, activ) = saved
+    turned, shifts, fence, lower = tables
+    mixed_att, middle, hidden, flipped, local = work
     need("x", "vec")
     vec = vec_ref[...]
     for start, size in ROWS:
@@ -160,52 +170,55 @@
         hat, scale, y = norm_forward(x_ref[rows, :].astype(F32), vec_at(vec, 0), vec_at(vec, 2))
         hat1[rows, :] = hat
         scale1[rows, :] = jnp.broadcast_to(scale, (size, HALF))
-        normed_nat[rows, :] = y.astype(BF16)
+        normed[0, rows, :] = y.astype(BF16)
     need("place", "wide")
-    base = normed_nat[...]
+    normed[1] = dot(turned[...], normed[0]).astype(BF16)
     biases = (vec_at(vec, 4), None, vec_at(vec, 5))
-    for half, table in enumerate((plain, turned)):
-        placed = dot(table[...], base).astype(BF16)
-        normed[half] = placed
+    for half in range(2):
         lanes = slice(half * HALF, (half + 1) * HALF)
         for part in range(3):
-            got = dot(placed, wq[:, part * D + half * HALF : part * D + (half + 1) * HALF])
+            got = dot(normed[half], wq[:, part * D + half * HALF : part * D + (half + 1) * HALF])
             if biases[part] is not None:
                 got = got + biases[part][:, lanes]
-            qkv[part, :, lanes] = got.astype(BF16)
+            qkv[part, 0:MB_TOK, lanes] = got.astype(BF16)
     masks = head_masks()
     need("stripe")
     taps9 = turned_taps(taps_ref[...])
     bias = vec_at(vec, 7)
+    units = [(group, half) for group in range(NGROUP) for half in range(2)]
+    for unit, (group, half) in enumerate(units):
+        rows = window(group)
+        lanes = slice(half * HALF, (half + 1) * HALF)
+        probs[unit] = dot_nt(qkv[1, rows, lanes], stacked_heads(qkv[0, rows, lanes], masks))
+        flipped[unit] = qkv[2, rows, lanes].T
+    for unit, (group, half) in enumerate(units):
+        fenced = fence[group]
+        for head in range(HEADS // 2):
+            cols = slice(head * GROUP, (head + 1) * GROUP)
+            s = probs[unit, :, cols] + fenced
+            p = jnp.exp2((s - jnp.max(s, axis=0, keepdims=True)) * EXP_SCALE)
+            p = p * (1.0 / jnp.sum(p, axis=0, keepdims=True))
+            probs[unit, :, cols] = p
+            probs_low[unit, :, cols] = p.astype(BF16)
     for group in range(NGROUP):
-        kind = KINDS[group]
-        rows = pl.ds(group * GROUP, GROUP)
+        rows = window(group)
         v = qkv[2, rows, :]
-        moved = dot(shifts[kind], v)
-        low_row = lower[kind] > 0.5
+        moved = dot(shifts[group], v)
+        low_row = lower[group] > 0.5
         low_row = jnp.concatenate([low_row, low_row], axis=1)
         lepe = bias + taps9[4] * v.astype(F32)
         lepe = lepe + taps9[3] * moved[0:GROUP] + taps9[5] * moved[GROUP : 2 * GROUP]
         for step in range(3):
             tap = jnp.where(low_row, taps9[step], taps9[6 + step])
             lepe = lepe + tap * moved[(2 + step) * GROUP : (3 + step) * GROUP]
-        fenced = fence[kind]
-        for half in range(2):
-            lanes = slice(half * HALF, (half + 1) * HALF)
-            q_stack = stacked_heads(qkv[0, rows, lanes], masks)
-            scores = dot_nt(qkv[1, rows, lanes], q_stack)
-            low = []
-            for head in range(HEADS // 2):
-                s = scores[:, head * GROUP : (head + 1) * GROUP] + fenced
-                p = jnp.exp2((s - jnp.max(s, axis=0, keepdims=True)) * EXP_SCALE)
-                p = p * (1.0 / jnp.sum(p, axis=0, keepdims=True))
-                probs[group * 2 + half, :, head * GROUP : (head + 1) * GROUP] = p
-                low.append(p.astype(BF16))
-            attended = picked_heads(dot(v[:, lanes].T, jnp.concatenate(low, axis=1))).T
-            mixed_att[rows, lanes] = (attended + lepe[:, lanes]).astype(BF16)
-    need("place_t")
-    mixed[:, :HALF] = dot(plain_t[...], mixed_att[:, :HALF]).astype(BF16)
-    mixed[:, HALF:] = dot(turned_t[...], mixed_att[:, HALF:]).astype(BF16)
+        local[group] = lepe
+    for unit, (group, half) in enumerate(units):
+        rows = window(group)
+        lanes = slice(half * HALF, (half + 1) * HALF)
+        attended = picked_heads(dot(flipped[unit], probs_low[unit])).T
+        put_window(mixed_att.at[half], group, attended + local[group, :, lanes])
+    mixed[:, :HALF] = mixed_att[0]
+    mixed[:, HALF:] = dot(turned[...], mixed_att[1]).astype(BF16)
     middle[...] = dot(mixed[...], wp[...])
     for start, size in ROWS:
         rows = pl.ds(start, size)
@@ -234,9 +247,9 @@
 
 def backward_block(up_ref, grad_ref, vec_ref, taps_ref, w, saved, tables, work, sums, small):
     wq, wp, w1, w2 = w
-    (hat1, scale1, normed, qkv, probs, mixed, hat2, scale2, normed2, slope, activ) = saved
-    plain, turned, plain_t, turned_t, shifts, fence, lower = tables
-    branch, gact, ghid, gmid, gmix, dqkv, dnat, gnorm = work
+    (hat1, scale1, normed, qkv, probs, probs_low, mixed, hat2, scale2, normed2, slope, activ) = saved
+    turned, shifts, fence, lower = tables
+    branch, gact, ghid, gmid, gmix, dqkv, dnat, gnorm, gprobs, gscores, flipped, local = work
     early, inner, outer = sums
     vec = vec_ref[...]
     branch[...] = up_ref[...].astype(BF16)
@@ -278,25 +291,36 @@
     small[6:7, :] = outs
     early[3 * D : 4 * D, :] = dot_tn(mixed[...], branch[...]).astype(BF16)
     low = dot_nt(branch[...], wp[...]).astype(BF16)
-    gmix[0:MB_TOK, :] = low
     small[7:8, :] = column_sum(low)
-    place_h = dot(plain[...], low[:, :HALF]).astype(BF16)
-    place_v = dot(turned[...], low[:, HALF:]).astype(BF16)
-    gmix[:, :HALF] = place_h
-    gmix[:, HALF:] = place_v
+    gmix[0:MB_TOK, :HALF] = low[:, :HALF]
+    gmix[0:MB_TOK, HALF:] = dot(turned[...], low[:, HALF:]).astype(BF16)
     masks = head_masks()
     taps9 = turned_taps(taps_ref[...])
     tap_sums = [jnp.zeros((1, D), F32) for _ in range(9)]
+    for start, size in ROWS:
+        rows = pl.ds(start, size)
+        tap_sums[4] = tap_sums[4] + column_sum(qkv[2, rows, :].astype(F32) * gmix[rows, :].astype(F32))
+    units = [(group, half) for group in range(NGROUP) for half in range(2)]
+    for unit, (group, half) in enumerate(units):
+        rows = window(group)
+        lanes = slice(half * HALF, (half + 1) * HALF)
+        gprobs[unit] = dot_nt(qkv[2, rows, lanes], stacked_heads(gmix[rows, lanes], masks))
+        flipped[unit] = qkv[1, rows, lanes].T
+    for unit in range(len(units)):
+        for head in range(HEADS // 2):
+            cols = slice(head * GROUP, (head + 1) * GROUP)
+            p = probs[unit, :, cols]
+            gp = gprobs[unit, :, cols]
+            down = jnp.sum(gp * p, axis=0, keepdims=True)
+            gscores[unit, :, cols] = (p * (gp - down)).astype(BF16)
     for group in range(NGROUP):
-        kind = KINDS[group]
-        rows = pl.ds(group * GROUP, GROUP)
+        rows = window(group)
         g_low = gmix[rows, :]
-        moved = dot(shifts[kind], g_low)
-        low_row = lower[kind] > 0.5
+        moved = dot(shifts[group], g_low)
+        low_row = lower[group] > 0.5
         low_row = jnp.concatenate([low_row, low_row], axis=1)
         v32 = qkv[2, rows, :].astype(F32)
         g32 = g_low.astype(F32)
-        tap_sums[4] = tap_sums[4] + column_sum(v32 * g32)
         left, right = moved[0:GROUP], moved[GROUP : 2 * GROUP]
         lepe = taps9[4] * g32 + taps9[3] * right + taps9[5] * left
         tap_sums[3] = tap_sums[3] + column_sum(v32 * right)
@@ -307,36 +331,22 @@
             product = v32 * at
             tap_sums[6 + step] = tap_sums[6 + step] + column_sum(jnp.where(low_row, product, 0.0))
             tap_sums[step] = tap_sums[step] + column_sum(jnp.where(low_row, 0.0, product))
-        for half in range(2):
-            lanes = slice(half * HALF, (half + 1) * HALF)
-            unit = group * 2 + half
-            g_stack = stacked_heads(gmix[rows, lanes], masks)
-            q_stack = stacked_heads(qkv[0, rows, lanes], masks)
-            k = qkv[1, rows, lanes]
-            gprobs = dot_nt(qkv[2, rows, lanes], g_stack)
-            low_p, low_s = [], []
-            for head in range(HEADS // 2):
-                cols = slice(head * GROUP, (head + 1) * GROUP)
-                p = probs[unit, :, cols]
-                gp = gprobs[:, cols]
-                down = jnp.sum(gp * p, axis=0, keepdims=True)
-                low_s.append((p * (gp - down)).astype(BF16))
-                low_p.append(p.astype(BF16))
-            low_p = jnp.concatenate(low_p, axis=1)
-            low_s = jnp.concatenate(low_s, axis=1)
-            grad_v = dot(low_p, g_stack) + lepe[:, lanes]
-            grad_k = dot(low_s, q_stack) * SCALE
-            grad_q = picked_heads(dot(k.T, low_s)).T * SCALE
-            dqkv[half, rows, 0:HALF] = grad_q.astype(BF16)
-            dqkv[half, rows, HALF:D] = grad_k.astype(BF16)
-            dqkv[half, rows, D : 3 * HALF] = grad_v.astype(BF16)
+        local[group] = lepe
+    for unit, (group, half) in enumerate(units):
+        rows = window(group)
+        lanes = slice(half * HALF, (half + 1) * HALF)
+        low_s = gscores[unit]
+        grad_v = dot(probs_low[unit], stacked_heads(gmix[rows, lanes], masks)) + local[group, :, lanes]
+        grad_k = dot(low_s, stacked_heads(qkv[0, rows, lanes], masks)) * SCALE
+        grad_q = picked_heads(dot(flipped[unit], low_s)).T * SCALE
+        put_window(dqkv.at[half], group, jnp.concatenate([grad_q, grad_k, grad_v], axis=1))
     for index in range(9):
         tap = index
         turned_index = 3 * (index % 3) + index // 3
         small[13 + index : 14 + index, :] = jnp.concatenate(
             [tap_sums[tap][:, :HALF], tap_sums[turned_index][:, HALF:]], axis=1
         )
-    for half, table_t in enumerate((plain_t, turned_t)):
+    for half in range(2):
         lanes = slice(half * HALF, (half + 1) * HALF)
         both = dqkv[half]
         small[4:5, lanes] = column_sum(both[:, 0:HALF])
@@ -344,7 +354,7 @@
         grads = dot_tn(normed[half], both)
         for part in range(3):
             early[part * D : (part + 1) * D, lanes] = grads[:, part * HALF : (part + 1) * HALF].astype(BF16)
-        natural = dot(table_t[...], both).astype(BF16)
+        natural = both if half == 0 else dot(turned[...], both).astype(BF16)
         for part in range(3):
             dnat[:, part * D + half * HALF : part * D + (half + 1) * HALF] = natural[
                 :, part * HALF : (part + 1) * HALF
@@ -368,9 +378,10 @@
 SAVED = [
     ((MB_TOK, D), F32),
     ((MB_TOK, HALF), F32),
-    ((2, ATT, D), BF16),
-    ((3, ATT, D), BF16),
+    ((2, MB_TOK, D), BF16),
+    ((3, LONG_TOK, D), BF16),
     ((2 * NGROUP, GROUP, 4 * GROUP), F32),
+    ((2 * NGROUP, GROUP, 4 * GROUP), BF16),
     ((MB_TOK, D), BF16),
     ((MB_TOK, D), F32),
     ((MB_TOK, HALF), F32),
@@ -378,16 +389,26 @@
     ((MB_TOK, FF), F32),
     ((MB_TOK, FF), BF16),
 ]
-FORWARD_WORK = [((MB_TOK, D), BF16), ((ATT, D), BF16), ((MB_TOK, D), F32), ((MB_TOK, FF), F32)]
+FORWARD_WORK = [
+    ((2, MB_TOK, HALF), BF16),
+    ((MB_TOK, D), F32),
+    ((MB_TOK, FF), F32),
+    ((2 * NGROUP, GROUP, GROUP), BF16),
+    ((NGROUP, GROUP, D), F32),
+]
 BACKWARD_WORK = [
     ((MB_TOK, D), BF16),
     ((MB_TOK, FF), F32),
     ((MB_TOK, FF), BF16),
     ((MB_TOK, D), F32),
-    ((ATT, D), BF16),
-    ((2, ATT, 3 * HALF), BF16),
+    ((LONG_TOK, D), BF16),
+    ((2, MB_TOK, 3 * HALF), BF16),
     ((MB_TOK, 3 * D), BF16),
     ((MB_TOK, D), F32),
+    ((2 * NGROUP, GROUP, 4 * GROUP), F32),
+    ((2 * NGROUP, GROUP, 4 * GROUP), BF16),
+    ((2 * NGROUP, GROUP, GROUP), BF16),
+    ((NGROUP, GROUP, D), F32),
 ]
 
 
@@ -398,13 +419,10 @@
     ((2, 1, 9 * D), F32),
     ((2, D, 8 * D), BF16),
     ((2, FF, D), BF16),
-    ((ATT, MB_TOK), BF16),
-    ((ATT, MB_TOK), BF16),
-    ((MB_TOK, ATT), BF16),
-    ((MB_TOK, ATT), BF16),
-    ((2, 5 * GROUP, GROUP), BF16),
-    ((2, GROUP, GROUP), F32),
-    ((2, GROUP, HALF), F32),
+    ((MB_TOK, MB_TOK), BF16),
+    ((NGROUP, 5 * GROUP, GROUP), BF16),
+    ((NGROUP, GROUP, GROUP), F32),
+    ((NGROUP, GROUP, HALF), F32),
 ]
 RESULTS = [((2, MB_TOK, D), F32), ((2, MB_TOK, D), F32)] + [((2, rows, D), BF16) for rows in PARTS]
 OTHER_WORK = [((MB_TOK, D), BF16), ((32, D), F32)]
@@ -417,7 +435,7 @@
         return taken
 
     x_in, c_in, vec_own, vec_other, ker_own, ker_other, wide_own, wide_other, deep_own, deep_other = take(10)
-    table_in = take(7)
+    table_in = take(4)
     sent = [take(2) for _ in RESULTS]
     held = take(len(INPUTS))
     results = take(len(RESULTS))
@@ -434,16 +452,13 @@
         ("vec", vec_own, vecs.at[sec]),
         ("vec", vec_other, vecs.at[1 - sec]),
         ("place", table_in[0], tables[0]),
-        ("place", table_in[1], tables[1]),
         ("wide", wide_own, wide.at[sec]),
         ("wide", wide_other, wide.at[1 - sec]),
-        ("stripe", table_in[4], tables[4]),
-        ("stripe", table_in[5], tables[5]),
-        ("stripe", table_in[6], tables[6]),
+        ("stripe", table_in[1], tables[1]),
+        ("stripe", table_in[2], tables[2]),
+        ("stripe", table_in[3], tables[3]),
         ("stripe", ker_own, taps.at[sec]),
         ("stripe", ker_other, taps.at[1 - sec]),
-        ("place_t", table_in[2], tables[2]),
-        ("place_t", table_in[3], tables[3]),
         ("deep", deep_own, deep.at[sec]),
         ("deep", deep_other, deep.at[1 - sec]),
         ("c", c_in.at[pl.ds(at, MB_TOK)], c),
@@ -469,6 +484,9 @@
 
     outs, grads, early, inner, outer = results
     small[...] = jnp.zeros_like(small)
+    for b in range(2):
+        kept[b][3][:, MB_TOK:, :] = jnp.zeros((3, LONG_TOK - MB_TOK, D), BF16)
+    backward_work[4][MB_TOK:, :] = jnp.zeros((LONG_TOK - MB_TOK, D), BF16)
     for part, rows in zip((early, inner, outer), PARTS):
         if rows > FF:
             part[:, FF:, :] = jnp.zeros((2, rows - FF, D), BF16)
@@ -503,18 +521,14 @@
 
 
 def run_blocks(sec, *arrays):
-    plain, turned = placement_tables()
     shifts, fence, lower = stripe_tables()
     tables = (
-        jnp.asarray(plain, BF16),
-        jnp.asarray(turned, BF16),
-        jnp.asarray(plain.T, BF16),
-        jnp.asarray(turned.T, BF16),
+        jnp.asarray(turned_table(), BF16),
         jnp.asarray(shifts, BF16),
         jnp.asarray(fence, F32),
         jnp.asarray(lower, F32),
     )
-    spaces = [pltpu.HBM] * 3 + [pltpu.VMEM, pltpu.HBM] * 3 + [pltpu.VMEM] + [pltpu.HBM] * 7
+    spaces = [pltpu.HBM] * 3 + [pltpu.VMEM, pltpu.HBM] + [pltpu.VMEM] * 5 + [pltpu.HBM] * 4
     smem = pl.BlockSpec(memory_space=pltpu.SMEM)
     scratch = INPUTS + RESULTS + SAVED + SAVED + FORWARD_WORK + BACKWARD_WORK + OTHER_WORK
     out_shape = [pltpu.VMEM(shape[1:], kind) for shape, kind in RESULTS for _ in range(2)]
@@ -524,7 +538,7 @@
         in_specs=[smem] + [pl.BlockSpec(memory_space=space) for space in spaces],
         out_specs=[pl.BlockSpec(memory_space=pl.ANY)] * len(out_shape),
         scratch_shapes=[pltpu.VMEM(shape, kind) for shape, kind in scratch]
-        + [pltpu.SemaphoreType.DMA((17,)), pltpu.SemaphoreType.DMA((2 * len(RESULTS),))],
+        + [pltpu.SemaphoreType.DMA((14,)), pltpu.SemaphoreType.DMA((2 * len(RESULTS),))],
         compiler_params=pltpu.CompilerParams(vmem_limit_bytes=34 << 20),
         name="blocks",
     )(sec, *kept_in(arrays + tables, spaces))
@@ -534,38 +548,26 @@
 
 
 def narrowed(*refs):
-    sources, (wide_out, deep_out), held, made, (in_sems, out_sems) = (
-        refs[:4],
-        refs[4:6],
-        refs[6:10],
-        refs[10:14],
-        refs[14:],
-    )
-    coming = [pltpu.make_async_copy(sources[k], held[k], in_sems.at[k]) for k in range(4)]
+    sources, (wide, deep), held, (sems,) = refs[:4], refs[4:6], refs[6:10], refs[10:]
+    coming = [pltpu.make_async_copy(sources[k], held[k], sems.at[k]) for k in range(4)]
     for copy in coming:
         copy.start()
-    going = []
     for k, (shape, first) in enumerate(NARROW):
         coming[k].wait()
-        made[k][...] = held[k][...].astype(BF16)
-        target = deep_out if first is None else wide_out.at[:, pl.ds(first, shape[1])]
-        copy = pltpu.make_async_copy(made[k], target, out_sems.at[k])
-        copy.start()
-        going.append(copy)
-    for copy in going:
-        copy.wait()
+        if first is None:
+            deep[...] = held[k][...].astype(BF16)
+        else:
+            wide[:, first : first + shape[1]] = held[k][...].astype(BF16)
 
 
 def run_narrowed(*weights):
-    hbm = pl.BlockSpec(memory_space=pltpu.HBM)
+    vmem = pl.BlockSpec(memory_space=pltpu.VMEM)
     return pl.pallas_call(
         narrowed,
-        out_shape=[pltpu.HBM((D, 8 * D), BF16), pltpu.HBM((FF, D), BF16)],
-        in_specs=[hbm] * 4,
-        out_specs=[hbm] * 2,
-        scratch_shapes=[pltpu.VMEM(shape, F32) for shape, _ in NARROW]
-        + [pltpu.VMEM(shape, BF16) for shape, _ in NARROW]
-        + [pltpu.SemaphoreType.DMA((4,)), pltpu.SemaphoreType.DMA((4,))],
+        out_shape=[pltpu.VMEM((D, 8 * D), BF16), pltpu.VMEM((FF, D), BF16)],
+        in_specs=[pl.BlockSpec(memory_space=pltpu.HBM)] * 4,
+        out_specs=[vmem] * 2,
+        scratch_shapes=[pltpu.VMEM(shape, F32) for shape, _ in NARROW] + [pltpu.SemaphoreType.DMA((4,))],
         compiler_params=pltpu.CompilerParams(vmem_limit_bytes=8 << 20),
         name="narrowed",
     )(*kept_in(weights, [pltpu.HBM] * 4))

time: 86.8 us -> 83.5 us (0.962)
  Pallas kernels: 30.7 us -> 27.7 us
    pallas_call x1, Pallas kernels: 21.2 us -> 19 us  [run_blocks(): pl.pallas_call(section_step, out_shape=out_shape, in_specs=[smem] + [pl.B...]
  transfers between devices with their start and end apart: 31 -> 31, of which waited for: 18 -> 17; matrix products, arithmetic and copies ran while one was open for 2% -> 2% of each run, Pallas kernels for 0% -> 0%
where the time goes in v3:
time: 83.5 us; the launch traced here: 83.4 us
  starting transfers between devices  32.9 us (39%)
  Pallas kernels  27.7 us (33%)
  waiting for transfers between devices  19.4 us (23%)
  other arithmetic  1.62 us (2%)
  between operations  1.37 us (2%)
    ppermute x21, starting transfers between devices, exchanged(): lax.ppermute(value, 'dp', [(index, index ^ 1 << bit) for index in range(s...  30.3 us
    pallas_call x1, Pallas kernels, run_blocks(): pl.pallas_call(section_step, out_shape=out_shape, in_specs=[smem] + [pl.B...  19 us
    ppermute x21, waiting for transfers between devices, exchanged(): lax.ppermute(value, 'dp', [(index, index ^ 1 << bit) for index in range(s...  15.3 us
    pallas_call x1, Pallas kernels, run_optimizer(): pl.pallas_call(optimizer_step, out_shape=[pltpu.HBM(shape, kind) for shap...  6.42 us
    ppermute x10, waiting for transfers between devices, swapped(): return lax.ppermute(value, 'section', [(0, 1), (1, 0)])  4.14 us
    ppermute x10, starting transfers between devices, swapped(): return lax.ppermute(value, 'section', [(0, 1), (1, 0)])  2.58 us
    pallas_call x1, Pallas kernels, run_narrowed(): pl.pallas_call(narrowed, out_shape=[pltpu.VMEM((D, 8 * D), BF16), pltpu.V...  1.95 us
  transfers between devices with their start and end apart: 31, of which 17 were waited for; matrix products, arithmetic and copies ran while one was open for 2% of the time, Pallas kernels for 0%

profile of v3, /device:TPU:0, one launch (start us, length us, event | category | flops | bytes accessed | tf_op | source)
XLA Modules:
  0.0 83.4 jit_solution(10917682152949696639)
XLA Ops:
  0.7 2.0 %narrowed.1 = (bf16[256,2048]{1,0:T(8,128)(2,1)S(1)}, bf16[1024,256]{1,0:T(8,128)(2,1)S(1)}) custom-call(f32[256,768]{1,0:T(8,128)} %bitcast.131, f32[256,256]{1,0:T(8,128)} %bitcast.137, f32[256,1024]{1,0:T(8,128)} %bitcast.127, f32[1024,256]{1,0:T(8,128)} %bitcast.129), custom_call_target="tpu_custom_call" | custom-call | tf_op jit(solution)/shard_map/narrowed/pallas_call | solution.py:565
  2.7 0.5 collective-permute-start.2
  3.2 0.1 collective-permute-start.3
  3.3 0.4 collective-permute-start
  3.7 0.1 collective-permute-start.1
  3.8 2.5 %collective-permute-done.1.refs_5_ = f32[1,2304]{1,0:T(1,128)S(1)} collective-permute-done((f32[1,2304]{1,0:T(1,128)S(1)}, f32[1,2304]{1,0:T(1,128)S(1)}, u32[]{:S(2)}, u32[]{:S(2)}) %collective-permute-start.1) | collective-permute-done | bytes 9248 | tf_op jit(solution)/shard_map/ppermute | solution.py:700
  6.3 19.0 %blocks.1 = (f32[304,256]{1,0:T(8,128)S(1)}, f32[304,256]{1,0:T(8,128)S(1)}, f32[304,256]{1,0:T(8,128)S(1)}, f32[304,256]{1,0:T(8,128)S(1)}, bf16[1024,256]{1,0:...) custom-call(s32[1]{0:T(128)} %bitcast.sec_ref, ...), custom_call_target="tpu_custom_call" | custom-call | tf_op jit(solution)/shard_map/blocks/pallas_call | solution.py:535
  25.2 0.4 collective-permute-start.6
  25.7 0.1 collective-permute-start.14
  25.8 0.4 collective-permute-start.4
  26.2 0.1 collective-permute-start.5
  26.3 0.4 collective-permute-start.22
  26.7 0.5 collective-permute-done.6
  27.2 0.1 add_convert_fusion.2
  27.4 2.9 %collective-permute-start.7 = (bf16[2,2,128,256]{3,2,1,0:T(8,128)(2,1)S(1)}, bf16[2,2,128,256]{3,2,1,0:T(8,128)(2,1)S(1)}, u32[]{:S(2)}, u32[]{:S(2)}) collective-permute-start(bf16[2,2,128,256]{3,2,1,0:T(8,128)(2,1)S(1)} %bitcast.152), channel_id=1, source_target_pairs={{0,1},{1,0},{2,3},{3,2},{4,5},{5,4},{6,7},{7,6},{8,9},{9,8},{10,11... | collective-permute-start | bytes 786440 | tf_op jit(solution)/shard_map/ppermute | solution.py:712
  30.3 0.1 add_convert_fusion.1
  30.5 1.6 %collective-permute-start.15 = (bf16[2,2,128,256]{3,2,1,0:T(8,128)(2,1)S(1)}, bf16[2,2,128,256]{3,2,1,0:T(8,128)(2,1)S(1)}, u32[]{:S(2)}, u32[]{:S(2)}) collective-permute-start(bf16[2,2,128,256]{3,2,1,0:T(8,128)(2,1)S(1)} %bitcast.153), channel_id=1, source_target_pairs={{0,2},{1,3},{2,0},{3,1},{4,6},{5,7},{6,4},{7,5},{8,10},{9,11},{10,... | collective-permute-start | bytes 786440 | tf_op jit(solution)/shard_map/ppermute | solution.py:712
  32.1 0.1 add_convert_fusion
  32.3 1.7 %collective-permute-start.23 = (bf16[2,2,136,256]{3,2,1,0:T(8,128)(2,1)S(1)}, bf16[2,2,136,256]{3,2,1,0:T(8,128)(2,1)S(1)}, u32[]{:S(2)}, u32[]{:S(2)}) collective-permute-start(bf16[2,2,136,256]{3,2,1,0:T(8,128)(2,1)S(1)} %bitcast.151), channel_id=1, source_target_pairs={{0,4},{1,5},{2,6},{3,7},{4,0},{5,1},{6,2},{7,3},{8,12},{9,13},{10,... | collective-permute-start | bytes 835592 | tf_op jit(solution)/shard_map/ppermute | solution.py:712
  33.9 3.0 %collective-permute-done.7 = bf16[2,2,128,256]{3,2,1,0:T(8,128)(2,1)S(1)} collective-permute-done((bf16[2,2,128,256]{3,2,1,0:T(8,128)(2,1)S(1)}, bf16[2,2,128,256]{3,2,1,0:T(8,128)(2,1)S(1)}, u32[]{:S(2)}, u32[]{:S(2)}) %collective-permute-start.7) | collective-permute-done | bytes 262176 | tf_op jit(solution)/shard_map/ppermute | solution.py:712
  36.9 0.1 fusion.2
  37.0 1.8 %collective-permute-start.8 = (bf16[2,128,256]{2,1,0:T(8,128)(2,1)S(1)}, bf16[2,128,256]{2,1,0:T(8,128)(2,1)S(1)}, u32[]{:S(2)}, u32[]{:S(2)}) collective-permute-start(bf16[2,128,256]{2,1,0:T(8,128)(2,1)S(1)} %select_bitcast_fusion.14), channel_id=1, source_target_pairs={{0,2},{1,3},{2,0},{3,1},{4,6},{5,7},{6,4},{7,5},{8,10},{9,11},{10,... | collective-permute-start | bytes 393224 | tf_op jit(solution)/shard_map/ppermute | solution.py:712
  38.9 0.1 fusion.1
  39.0 1.6 %collective-permute-start.16 = (bf16[2,128,256]{2,1,0:T(8,128)(2,1)S(1)}, bf16[2,128,256]{2,1,0:T(8,128)(2,1)S(1)}, u32[]{:S(2)}, u32[]{:S(2)}) collective-permute-start(bf16[2,128,256]{2,1,0:T(8,128)(2,1)S(1)} %select_bitcast_fusion.11), channel_id=1, source_target_pairs={{0,4},{1,5},{2,6},{3,7},{4,0},{5,1},{6,2},{7,3},{8,12},{9,13},{10,... | collective-permute-start | bytes 393224 | tf_op jit(solution)/shard_map/ppermute | solution.py:712
  40.6 0.1 fusion
  40.7 1.6 %collective-permute-start.24 = (bf16[2,136,256]{2,1,0:T(8,128)(2,1)S(1)}, bf16[2,136,256]{2,1,0:T(8,128)(2,1)S(1)}, u32[]{:S(2)}, u32[]{:S(2)}) collective-permute-start(bf16[2,136,256]{2,1,0:T(8,128)(2,1)S(1)} %select_bitcast_fusion.8), channel_id=1, source_target_pairs={{0,1},{1,0},{2,3},{3,2},{4,5},{5,4},{6,7},{7,6},{8,9},{9,8},{10,11... | collective-permute-start | bytes 417800 | tf_op jit(solution)/shard_map/ppermute | solution.py:712
  42.3 0.1 fusion.5
  42.3 1.7 %collective-permute-start.9 = (bf16[128,256]{1,0:T(8,128)(2,1)S(1)}, bf16[128,256]{1,0:T(8,128)(2,1)S(1)}, u32[]{:S(2)}, u32[]{:S(2)}) collective-permute-start(bf16[128,256]{1,0:T(8,128)(2,1)S(1)} %select_bitcast_fusion.23), channel_id=1, source_target_pairs={{0,4},{1,5},{2,6},{3,7},{4,0},{5,1},{6,2},{7,3},{8,12},{9,13},{10,... | collective-permute-start | bytes 196616 | tf_op jit(solution)/shard_map/ppermute | solution.py:712
  44.0 0.4 collective-permute-done.16
  44.5 1.8 %collective-permute-start.17 = (bf16[128,256]{1,0:T(8,128)(2,1)S(1)}, bf16[128,256]{1,0:T(8,128)(2,1)S(1)}, u32[]{:S(2)}, u32[]{:S(2)}) collective-permute-start(bf16[128,256]{1,0:T(8,128)(2,1)S(1)} %select_bitcast_fusion.20), channel_id=1, source_target_pairs={{0,1},{1,0},{2,3},{3,2},{4,5},{5,4},{6,7},{7,6},{8,9},{9,8},{10,11... | collective-permute-start | bytes 196616 | tf_op jit(solution)/shard_map/ppermute | solution.py:712
  46.3 0.2 collective-permute-done.24
  46.5 0.1 fusion.3
  46.6 1.4 %collective-permute-start.25 = (bf16[136,256]{1,0:T(8,128)(2,1)S(1)}, bf16[136,256]{1,0:T(8,128)(2,1)S(1)}, u32[]{:S(2)}, u32[]{:S(2)}) collective-permute-start(bf16[136,256]{1,0:T(8,128)(2,1)S(1)} %select_bitcast_fusion.17), channel_id=1, source_target_pairs={{0,2},{1,3},{2,0},{3,1},{4,6},{5,7},{6,4},{7,5},{8,10},{9,11},{10,... | collective-permute-start | bytes 208904 | tf_op jit(solution)/shard_map/ppermute | solution.py:712
  48.0 2.6 %collective-permute-start.10 = (bf16[128,256]{1,0:T(8,128)(2,1)S(1)}, bf16[128,256]{1,0:T(8,128)(2,1)S(1)}, u32[]{:S(2)}, u32[]{:S(2)}) collective-permute-start(bf16[128,256]{1,0:T(8,128)(2,1)S(1)} %fusion.8), channel_id=1, source_target_pairs={{0,8},{1,9},{2,10},{3,11},{4,12},{5,13},{6,14},{7,15},{8,0},{9,1},... | collective-permute-start | bytes 196616 | tf_op jit(solution)/shard_map/ppermute | solution.py:712
  50.7 0.9 %collective-permute-start.18 = (bf16[128,256]{1,0:T(8,128)(2,1)S(1)}, bf16[128,256]{1,0:T(8,128)(2,1)S(1)}, u32[]{:S(2)}, u32[]{:S(2)}) collective-permute-start(bf16[128,256]{1,0:T(8,128)(2,1)S(1)} %fusion.7), channel_id=1, source_target_pairs={{0,8},{1,9},{2,10},{3,11},{4,12},{5,13},{6,14},{7,15},{8,0},{9,1},... | collective-permute-start | bytes 196616 | tf_op jit(solution)/shard_map/ppermute | solution.py:712
  51.7 2.1 %collective-permute-start.26 = (bf16[136,256]{1,0:T(8,128)(2,1)S(1)}, bf16[136,256]{1,0:T(8,128)(2,1)S(1)}, u32[]{:S(2)}, u32[]{:S(2)}) collective-permute-start(bf16[136,256]{1,0:T(8,128)(2,1)S(1)} %fusion.6), channel_id=1, source_target_pairs={{0,8},{1,9},{2,10},{3,11},{4,12},{5,13},{6,14},{7,15},{8,0},{9,1},... | collective-permute-start | bytes 208904 | tf_op jit(solution)/shard_map/ppermute | solution.py:712
  53.8 1.8 %collective-permute-done.10 = bf16[128,256]{1,0:T(8,128)(2,1)S(1)} collective-permute-done((bf16[128,256]{1,0:T(8,128)(2,1)S(1)}, bf16[128,256]{1,0:T(8,128)(2,1)S(1)}, u32[]{:S(2)}, u32[]{:S(2)}) %collective-permute-start.10) | collective-permute-done | bytes 65568 | tf_op jit(solution)/shard_map/ppermute | solution.py:712
  55.6 0.2 collective-permute-start.11
  55.7 1.2 %collective-permute-done.18 = bf16[128,256]{1,0:T(8,128)(2,1)S(1)} collective-permute-done((bf16[128,256]{1,0:T(8,128)(2,1)S(1)}, bf16[128,256]{1,0:T(8,128)(2,1)S(1)}, u32[]{:S(2)}, u32[]{:S(2)}) %collective-permute-start.18) | collective-permute-done | bytes 65568 | tf_op jit(solution)/shard_map/ppermute | solution.py:712
  57.0 1.3 %collective-permute-start.19 = (bf16[128,256]{1,0:T(8,128)(2,1)S(1)}, bf16[128,256]{1,0:T(8,128)(2,1)S(1)}, u32[]{:S(2)}, u32[]{:S(2)}) collective-permute-start(bf16[128,256]{1,0:T(8,128)(2,1)S(1)} %add_convert_fusion.4), channel_id=1, source_target_pairs={{0,1},{1,0},{2,3},{3,2},{4,5},{5,4},{6,7},{7,6},{8,9},{9,8},{10,11... | collective-permute-start | bytes 196616 | tf_op jit(solution)/shard_map/ppermute | solution.py:712
  58.3 0.1 collective-permute-done.26
  58.5 1.5 %collective-permute-start.27 = (bf16[136,256]{1,0:T(8,128)(2,1)S(1)}, bf16[136,256]{1,0:T(8,128)(2,1)S(1)}, u32[]{:S(2)}, u32[]{:S(2)}) collective-permute-start(bf16[136,256]{1,0:T(8,128)(2,1)S(1)} %add_convert_fusion.3), channel_id=1, source_target_pairs={{0,2},{1,3},{2,0},{3,1},{4,6},{5,7},{6,4},{7,5},{8,10},{9,11},{10,... | collective-permute-start | bytes 208904 | tf_op jit(solution)/shard_map/ppermute | solution.py:712
  60.0 1.1 %collective-permute-start.12 = (bf16[2,128,256]{2,1,0:T(8,128)(2,1)S(1)}, bf16[2,128,256]{2,1,0:T(8,128)(2,1)S(1)}, u32[]{:S(2)}, u32[]{:S(2)}) collective-permute-start(bf16[2,128,256]{2,1,0:T(8,128)(2,1)S(1)} %pad_maximum_fusion.7), channel_id=1, source_target_pairs={{0,2},{1,3},{2,0},{3,1},{4,6},{5,7},{6,4},{7,5},{8,10},{9,11},{10,... | collective-permute-start | bytes 393224 | tf_op jit(solution)/shard_map/ppermute | solution.py:712
  61.1 0.3 collective-permute-done.19
  61.4 0.9 %collective-permute-start.20 = (bf16[2,128,256]{2,1,0:T(8,128)(2,1)S(1)}, bf16[2,128,256]{2,1,0:T(8,128)(2,1)S(1)}, u32[]{:S(2)}, u32[]{:S(2)}) collective-permute-start(bf16[2,128,256]{2,1,0:T(8,128)(2,1)S(1)} %pad_maximum_fusion.8), channel_id=1, source_target_pairs={{0,4},{1,5},{2,6},{3,7},{4,0},{5,1},{6,2},{7,3},{8,12},{9,13},{10,... | collective-permute-start | bytes 393224 | tf_op jit(solution)/shard_map/ppermute | solution.py:712
  62.2 0.6 collective-permute-done.27
  62.9 1.3 %collective-permute-start.28 = (bf16[2,136,256]{2,1,0:T(8,128)(2,1)S(1)}, bf16[2,136,256]{2,1,0:T(8,128)(2,1)S(1)}, u32[]{:S(2)}, u32[]{:S(2)}) collective-permute-start(bf16[2,136,256]{2,1,0:T(8,128)(2,1)S(1)} %pad_maximum_fusion.6), channel_id=1, source_target_pairs={{0,1},{1,0},{2,3},{3,2},{4,5},{5,4},{6,7},{7,6},{8,9},{9,8},{10,11... | collective-permute-start | bytes 417800 | tf_op jit(solution)/shard_map/ppermute | solution.py:712
  64.3 1.6 %collective-permute-done.12 = bf16[2,128,256]{2,1,0:T(8,128)(2,1)S(1)} collective-permute-done((bf16[2,128,256]{2,1,0:T(8,128)(2,1)S(1)}, bf16[2,128,256]{2,1,0:T(8,128)(2,1)S(1)}, u32[]{:S(2)}, u32[]{:S(2)}) %collective-permute-start.12) | collective-permute-done | bytes 131104 | tf_op jit(solution)/shard_map/ppermute | solution.py:712
  65.9 1.0 %collective-permute-start.13 = (bf16[2,2,128,256]{3,2,1,0:T(8,128)(2,1)S(1)}, bf16[2,2,128,256]{3,2,1,0:T(8,128)(2,1)S(1)}, u32[]{:S(2)}, u32[]{:S(2)}) collective-permute-start(bf16[2,2,128,256]{3,2,1,0:T(8,128)(2,1)S(1)} %pad_maximum_fusion.4), channel_id=1, source_target_pairs={{0,1},{1,0},{2,3},{3,2},{4,5},{5,4},{6,7},{7,6},{8,9},{9,8},{10,11... | collective-permute-start | bytes 786440 | tf_op jit(solution)/shard_map/ppermute | solution.py:712
  66.9 0.2 collective-permute-done.20
  67.3 0.5 collective-permute-start.21
  67.8 0.3 collective-permute-done.28
  68.1 0.8 collective-permute-start.29
  68.9 3.4 %collective-permute-done.13 = bf16[2,2,128,256]{3,2,1,0:T(8,128)(2,1)S(1)} collective-permute-done((bf16[2,2,128,256]{3,2,1,0:T(8,128)(2,1)S(1)}, bf16[2,2,128,256]{3,2,1,0:T(8,128)(2,1)S(1)}, u32[]{:S(2)}, u32[]{:S(2)}) %collective-permute-start.13) | collective-permute-done | bytes 262176 | tf_op jit(solution)/shard_map/ppermute | solution.py:712
  72.4 1.3 %collective-permute-done.21 = bf16[2,2,128,256]{3,2,1,0:T(8,128)(2,1)S(1)} collective-permute-done((bf16[2,2,128,256]{3,2,1,0:T(8,128)(2,1)S(1)}, bf16[2,2,128,256]{3,2,1,0:T(8,128)(2,1)S(1)}, u32[]{:S(2)}, u32[]{:S(2)}) %collective-permute-start.21) | collective-permute-done | bytes 262176 | tf_op jit(solution)/shard_map/ppermute | solution.py:712
  73.8 0.1 pad_maximum_fusion.1
  73.8 0.1 pad_maximum_fusion.2
  73.9 0.8 %collective-permute-done.29 = bf16[2,2,136,256]{3,2,1,0:T(8,128)(2,1)S(1)} collective-permute-done((bf16[2,2,136,256]{3,2,1,0:T(8,128)(2,1)S(1)}, bf16[2,2,136,256]{3,2,1,0:T(8,128)(2,1)S(1)}, u32[]{:S(2)}, u32[]{:S(2)}) %collective-permute-start.29) | collective-permute-done | bytes 278560 | tf_op jit(solution)/shard_map/ppermute | solution.py:712
  74.8 0.1 pad_maximum_fusion
  74.9 0.3 squares.1.refs_4_
  75.2 1.1 %collective-permute-done.30.refs_5_ = f32[8,128]{1,0:T(8,128)S(1)} collective-permute-done((f32[8,128]{1,0:T(8,128)S(1)}, f32[8,128]{1,0:T(8,128)S(1)}, u32[]{:S(2)}, u32[]{:S(2)}) %collective-permute-start.30) | collective-permute-done | bytes 4128 | tf_op jit(solution)/shard_map/ppermute | solution.py:700
  76.5 0.2 copy-done
  76.7 0.1 copy-done.10
  76.8 6.4 %optimizer.1 = (f32[1,3328]{1,0:T(1,128)}, f32[1,2304]{1,0:T(1,128)}, f32[256,768]{1,0:T(8,128)}, f32[256,256]{1,0:T(8,128)}, f32[256,1024]{1,0:T(8,128)}, /*ind...) custom-call(s32[1]{0:T(128)} %bitcast.sec_ref, ...), custom_call_target="tpu_custom_call" | custom-call | tf_op jit(solution)/shard_map/optimizer/pallas_call | solution.py:686
  (84 shorter events, 0.9 us)
Async XLA Ops:
  0.7 2.6 %copy-start.12 = (f32[1,3328]{1,0:T(1,128)S(1)}, f32[1,3328]{1,0:T(1,128)}, u32[]{:S(2)}) copy-start(f32[1,3328]{1,0:T(1,128)} %refs_9_.1) | copy-start | bytes 39940
  0.7 3.0 %copy-start.14 = (f32[1,9,256]{2,0,1:T(1,128)S(1)}, f32[1,9,256]{2,0,1:T(1,128)}, u32[]{:S(2)}) copy-start(f32[1,9,256]{2,0,1:T(1,128)} %param.27) | copy-start | bytes 27652
  2.7 3.6 %collective-permute-start.2 = (bf16[256,2048]{1,0:T(8,128)(2,1)S(1)}, bf16[256,2048]{1,0:T(8,128)(2,1)S(1)}, u32[]{:S(2)}, u32[]{:S(2)}) collective-permute-start(bf16[256,2048]{1,0:T(8,128)(2,1)S(1)} %get-tuple-element.79.refs_6_), channel_id=1, source_target_pairs={{0,16},{16,0},{1,17},{17,1},{2,18},{18,2},{3,19},{19,3},{4,20},{20... | collective-permute-start | bytes 3145736 | tf_op jit(solution)/shard_map/ppermute | solution.py:700
  3.2 3.1 %collective-permute-start.3 = (bf16[1024,256]{1,0:T(8,128)(2,1)S(1)}, bf16[1024,256]{1,0:T(8,128)(2,1)S(1)}, u32[]{:S(2)}, u32[]{:S(2)}) collective-permute-start(bf16[1024,256]{1,0:T(8,128)(2,1)S(1)} %get-tuple-element.80.refs_8_), channel_id=1, source_target_pairs={{0,16},{16,0},{1,17},{17,1},{2,18},{18,2},{3,19},{19,3},{4,20},{20... | collective-permute-start | bytes 1572872 | tf_op jit(solution)/shard_map/ppermute | solution.py:700
  3.3 3.0 %collective-permute-start = (f32[1,3328]{1,0:T(1,128)S(1)}, f32[1,3328]{1,0:T(1,128)S(1)}, u32[]{:S(2)}, u32[]{:S(2)}) collective-permute-start(f32[1,3328]{1,0:T(1,128)S(1)} %copy-done.12), channel_id=1, source_target_pairs={{0,16},{16,0},{1,17},{17,1},{2,18},{18,2},{3,19},{19,3},{4,20},{20... | collective-permute-start | bytes 39944 | tf_op jit(solution)/shard_map/ppermute | solution.py:700
  3.7 2.6 %collective-permute-start.1 = (f32[1,2304]{1,0:T(1,128)S(1)}, f32[1,2304]{1,0:T(1,128)S(1)}, u32[]{:S(2)}, u32[]{:S(2)}) collective-permute-start(f32[1,2304]{1,0:T(1,128)S(1)} %bitcast.144), channel_id=1, source_target_pairs={{0,16},{16,0},{1,17},{17,1},{2,18},{18,2},{3,19},{19,3},{4,20},{20... | collective-permute-start | bytes 27656 | tf_op jit(solution)/shard_map/ppermute | solution.py:700
  25.2 2.0 %collective-permute-start.6 = (bf16[1024,256]{1,0:T(8,128)(2,1)S(1)}, bf16[1024,256]{1,0:T(8,128)(2,1)S(1)}, u32[]{:S(2)}, u32[]{:S(2)}) collective-permute-start(bf16[1024,256]{1,0:T(8,128)(2,1)S(1)} %get-tuple-element.89), channel_id=1, source_target_pairs={{0,16},{16,0},{1,17},{17,1},{2,18},{18,2},{3,19},{19,3},{4,20},{20... | collective-permute-start | bytes 1572872 | tf_op jit(solution)/shard_map/ppermute | solution.py:700
  25.7 4.6 %collective-permute-start.14 = (bf16[1024,256]{1,0:T(8,128)(2,1)S(1)}, bf16[1024,256]{1,0:T(8,128)(2,1)S(1)}, u32[]{:S(2)}, u32[]{:S(2)}) collective-permute-start(bf16[1024,256]{1,0:T(8,128)(2,1)S(1)} %get-tuple-element.91), channel_id=1, source_target_pairs={{0,16},{16,0},{1,17},{17,1},{2,18},{18,2},{3,19},{19,3},{4,20},{20... | collective-permute-start | bytes 1572872 | tf_op jit(solution)/shard_map/ppermute | solution.py:700
  25.8 49.4 %collective-permute-start.4 = (f32[304,256]{1,0:T(8,128)S(1)}, f32[304,256]{1,0:T(8,128)S(1)}, u32[]{:S(2)}, u32[]{:S(2)}) collective-permute-start(f32[304,256]{1,0:T(8,128)S(1)} %get-tuple-element.82), channel_id=1, source_target_pairs={{0,16},{16,0},{1,17},{17,1},{2,18},{18,2},{3,19},{19,3},{4,20},{20... | collective-permute-start | bytes 933896 | tf_op jit(solution)/shard_map/ppermute | solution.py:700
  26.2 49.0 %collective-permute-start.5 = (f32[304,256]{1,0:T(8,128)S(1)}, f32[304,256]{1,0:T(8,128)S(1)}, u32[]{:S(2)}, u32[]{:S(2)}) collective-permute-start(f32[304,256]{1,0:T(8,128)S(1)} %get-tuple-element.84), channel_id=1, source_target_pairs={{0,16},{16,0},{1,17},{17,1},{2,18},{18,2},{3,19},{19,3},{4,20},{20... | collective-permute-start | bytes 933896 | tf_op jit(solution)/shard_map/ppermute | solution.py:700
  26.3 5.8 %collective-permute-start.22 = (bf16[1088,256]{1,0:T(8,128)(2,1)S(1)}, bf16[1088,256]{1,0:T(8,128)(2,1)S(1)}, u32[]{:S(2)}, u32[]{:S(2)}) collective-permute-start(bf16[1088,256]{1,0:T(8,128)(2,1)S(1)} %get-tuple-element.93), channel_id=1, source_target_pairs={{0,16},{16,0},{1,17},{17,1},{2,18},{18,2},{3,19},{19,3},{4,20},{20... | collective-permute-start | bytes 1671176 | tf_op jit(solution)/shard_map/ppermute | solution.py:700
  27.4 9.5 %collective-permute-start.7 = (bf16[2,2,128,256]{3,2,1,0:T(8,128)(2,1)S(1)}, bf16[2,2,128,256]{3,2,1,0:T(8,128)(2,1)S(1)}, u32[]{:S(2)}, u32[]{:S(2)}) collective-permute-start(bf16[2,2,128,256]{3,2,1,0:T(8,128)(2,1)S(1)} %bitcast.152), channel_id=1, source_target_pairs={{0,1},{1,0},{2,3},{3,2},{4,5},{5,4},{6,7},{7,6},{8,9},{9,8},{10,11... | collective-permute-start | bytes 786440 | tf_op jit(solution)/shard_map/ppermute | solution.py:712
  30.5 8.4 %collective-permute-start.15 = (bf16[2,2,128,256]{3,2,1,0:T(8,128)(2,1)S(1)}, bf16[2,2,128,256]{3,2,1,0:T(8,128)(2,1)S(1)}, u32[]{:S(2)}, u32[]{:S(2)}) collective-permute-start(bf16[2,2,128,256]{3,2,1,0:T(8,128)(2,1)S(1)} %bitcast.153), channel_id=1, source_target_pairs={{0,2},{1,3},{2,0},{3,1},{4,6},{5,7},{6,4},{7,5},{8,10},{9,11},{10,... | collective-permute-start | bytes 786440 | tf_op jit(solution)/shard_map/ppermute | solution.py:712
  32.3 8.3 %collective-permute-start.23 = (bf16[2,2,136,256]{3,2,1,0:T(8,128)(2,1)S(1)}, bf16[2,2,136,256]{3,2,1,0:T(8,128)(2,1)S(1)}, u32[]{:S(2)}, u32[]{:S(2)}) collective-permute-start(bf16[2,2,136,256]{3,2,1,0:T(8,128)(2,1)S(1)} %bitcast.151), channel_id=1, source_target_pairs={{0,4},{1,5},{2,6},{3,7},{4,0},{5,1},{6,2},{7,3},{8,12},{9,13},{10,... | collective-permute-start | bytes 835592 | tf_op jit(solution)/shard_map/ppermute | solution.py:712
  37.0 5.2 %collective-permute-start.8 = (bf16[2,128,256]{2,1,0:T(8,128)(2,1)S(1)}, bf16[2,128,256]{2,1,0:T(8,128)(2,1)S(1)}, u32[]{:S(2)}, u32[]{:S(2)}) collective-permute-start(bf16[2,128,256]{2,1,0:T(8,128)(2,1)S(1)} %select_bitcast_fusion.14), channel_id=1, source_target_pairs={{0,2},{1,3},{2,0},{3,1},{4,6},{5,7},{6,4},{7,5},{8,10},{9,11},{10,... | collective-permute-start | bytes 393224 | tf_op jit(solution)/shard_map/ppermute | solution.py:712
  39.0 5.4 %collective-permute-start.16 = (bf16[2,128,256]{2,1,0:T(8,128)(2,1)S(1)}, bf16[2,128,256]{2,1,0:T(8,128)(2,1)S(1)}, u32[]{:S(2)}, u32[]{:S(2)}) collective-permute-start(bf16[2,128,256]{2,1,0:T(8,128)(2,1)S(1)} %select_bitcast_fusion.11), channel_id=1, source_target_pairs={{0,4},{1,5},{2,6},{3,7},{4,0},{5,1},{6,2},{7,3},{8,12},{9,13},{10,... | collective-permute-start | bytes 393224 | tf_op jit(solution)/shard_map/ppermute | solution.py:712
  40.7 5.8 %collective-permute-start.24 = (bf16[2,136,256]{2,1,0:T(8,128)(2,1)S(1)}, bf16[2,136,256]{2,1,0:T(8,128)(2,1)S(1)}, u32[]{:S(2)}, u32[]{:S(2)}) collective-permute-start(bf16[2,136,256]{2,1,0:T(8,128)(2,1)S(1)} %select_bitcast_fusion.8), channel_id=1, source_target_pairs={{0,1},{1,0},{2,3},{3,2},{4,5},{5,4},{6,7},{7,6},{8,9},{9,8},{10,11... | collective-permute-start | bytes 417800 | tf_op jit(solution)/shard_map/ppermute | solution.py:712
  42.3 5.6 %collective-permute-start.9 = (bf16[128,256]{1,0:T(8,128)(2,1)S(1)}, bf16[128,256]{1,0:T(8,128)(2,1)S(1)}, u32[]{:S(2)}, u32[]{:S(2)}) collective-permute-start(bf16[128,256]{1,0:T(8,128)(2,1)S(1)} %select_bitcast_fusion.23), channel_id=1, source_target_pairs={{0,4},{1,5},{2,6},{3,7},{4,0},{5,1},{6,2},{7,3},{8,12},{9,13},{10,... | collective-permute-start | bytes 196616 | tf_op jit(solution)/shard_map/ppermute | solution.py:712
  44.5 6.2 %collective-permute-start.17 = (bf16[128,256]{1,0:T(8,128)(2,1)S(1)}, bf16[128,256]{1,0:T(8,128)(2,1)S(1)}, u32[]{:S(2)}, u32[]{:S(2)}) collective-permute-start(bf16[128,256]{1,0:T(8,128)(2,1)S(1)} %select_bitcast_fusion.20), channel_id=1, source_target_pairs={{0,1},{1,0},{2,3},{3,2},{4,5},{5,4},{6,7},{7,6},{8,9},{9,8},{10,11... | collective-permute-start | bytes 196616 | tf_op jit(solution)/shard_map/ppermute | solution.py:712
  46.6 5.0 %collective-permute-start.25 = (bf16[136,256]{1,0:T(8,128)(2,1)S(1)}, bf16[136,256]{1,0:T(8,128)(2,1)S(1)}, u32[]{:S(2)}, u32[]{:S(2)}) collective-permute-start(bf16[136,256]{1,0:T(8,128)(2,1)S(1)} %select_bitcast_fusion.17), channel_id=1, source_target_pairs={{0,2},{1,3},{2,0},{3,1},{4,6},{5,7},{6,4},{7,5},{8,10},{9,11},{10,... | collective-permute-start | bytes 208904 | tf_op jit(solution)/shard_map/ppermute | solution.py:712
  48.0 7.5 %collective-permute-start.10 = (bf16[128,256]{1,0:T(8,128)(2,1)S(1)}, bf16[128,256]{1,0:T(8,128)(2,1)S(1)}, u32[]{:S(2)}, u32[]{:S(2)}) collective-permute-start(bf16[128,256]{1,0:T(8,128)(2,1)S(1)} %fusion.8), channel_id=1, source_target_pairs={{0,8},{1,9},{2,10},{3,11},{4,12},{5,13},{6,14},{7,15},{8,0},{9,1},... | collective-permute-start | bytes 196616 | tf_op jit(solution)/shard_map/ppermute | solution.py:712
  50.7 6.3 %collective-permute-start.18 = (bf16[128,256]{1,0:T(8,128)(2,1)S(1)}, bf16[128,256]{1,0:T(8,128)(2,1)S(1)}, u32[]{:S(2)}, u32[]{:S(2)}) collective-permute-start(bf16[128,256]{1,0:T(8,128)(2,1)S(1)} %fusion.7), channel_id=1, source_target_pairs={{0,8},{1,9},{2,10},{3,11},{4,12},{5,13},{6,14},{7,15},{8,0},{9,1},... | collective-permute-start | bytes 196616 | tf_op jit(solution)/shard_map/ppermute | solution.py:712
  51.7 6.8 %collective-permute-start.26 = (bf16[136,256]{1,0:T(8,128)(2,1)S(1)}, bf16[136,256]{1,0:T(8,128)(2,1)S(1)}, u32[]{:S(2)}, u32[]{:S(2)}) collective-permute-start(bf16[136,256]{1,0:T(8,128)(2,1)S(1)} %fusion.6), channel_id=1, source_target_pairs={{0,8},{1,9},{2,10},{3,11},{4,12},{5,13},{6,14},{7,15},{8,0},{9,1},... | collective-permute-start | bytes 208904 | tf_op jit(solution)/shard_map/ppermute | solution.py:712
  55.6 4.4 %collective-permute-start.11 = (bf16[128,256]{1,0:T(8,128)(2,1)S(1)}, bf16[128,256]{1,0:T(8,128)(2,1)S(1)}, u32[]{:S(2)}, u32[]{:S(2)}) collective-permute-start(bf16[128,256]{1,0:T(8,128)(2,1)S(1)} %add_convert_fusion.5), channel_id=1, source_target_pairs={{0,4},{1,5},{2,6},{3,7},{4,0},{5,1},{6,2},{7,3},{8,12},{9,13},{10,... | collective-permute-start | bytes 196616 | tf_op jit(solution)/shard_map/ppermute | solution.py:712
  57.0 4.3 %collective-permute-start.19 = (bf16[128,256]{1,0:T(8,128)(2,1)S(1)}, bf16[128,256]{1,0:T(8,128)(2,1)S(1)}, u32[]{:S(2)}, u32[]{:S(2)}) collective-permute-start(bf16[128,256]{1,0:T(8,128)(2,1)S(1)} %add_convert_fusion.4), channel_id=1, source_target_pairs={{0,1},{1,0},{2,3},{3,2},{4,5},{5,4},{6,7},{7,6},{8,9},{9,8},{10,11... | collective-permute-start | bytes 196616 | tf_op jit(solution)/shard_map/ppermute | solution.py:712
  58.5 4.4 %collective-permute-start.27 = (bf16[136,256]{1,0:T(8,128)(2,1)S(1)}, bf16[136,256]{1,0:T(8,128)(2,1)S(1)}, u32[]{:S(2)}, u32[]{:S(2)}) collective-permute-start(bf16[136,256]{1,0:T(8,128)(2,1)S(1)} %add_convert_fusion.3), channel_id=1, source_target_pairs={{0,2},{1,3},{2,0},{3,1},{4,6},{5,7},{6,4},{7,5},{8,10},{9,11},{10,... | collective-permute-start | bytes 208904 | tf_op jit(solution)/shard_map/ppermute | solution.py:712
  60.0 5.8 %collective-permute-start.12 = (bf16[2,128,256]{2,1,0:T(8,128)(2,1)S(1)}, bf16[2,128,256]{2,1,0:T(8,128)(2,1)S(1)}, u32[]{:S(2)}, u32[]{:S(2)}) collective-permute-start(bf16[2,128,256]{2,1,0:T(8,128)(2,1)S(1)} %pad_maximum_fusion.7), channel_id=1, source_target_pairs={{0,2},{1,3},{2,0},{3,1},{4,6},{5,7},{6,4},{7,5},{8,10},{9,11},{10,... | collective-permute-start | bytes 393224 | tf_op jit(solution)/shard_map/ppermute | solution.py:712
  61.4 5.7 %collective-permute-start.20 = (bf16[2,128,256]{2,1,0:T(8,128)(2,1)S(1)}, bf16[2,128,256]{2,1,0:T(8,128)(2,1)S(1)}, u32[]{:S(2)}, u32[]{:S(2)}) collective-permute-start(bf16[2,128,256]{2,1,0:T(8,128)(2,1)S(1)} %pad_maximum_fusion.8), channel_id=1, source_target_pairs={{0,4},{1,5},{2,6},{3,7},{4,0},{5,1},{6,2},{7,3},{8,12},{9,13},{10,... | collective-permute-start | bytes 393224 | tf_op jit(solution)/shard_map/ppermute | solution.py:712
  62.9 5.1 %collective-permute-start.28 = (bf16[2,136,256]{2,1,0:T(8,128)(2,1)S(1)}, bf16[2,136,256]{2,1,0:T(8,128)(2,1)S(1)}, u32[]{:S(2)}, u32[]{:S(2)}) collective-permute-start(bf16[2,136,256]{2,1,0:T(8,128)(2,1)S(1)} %pad_maximum_fusion.6), channel_id=1, source_target_pairs={{0,1},{1,0},{2,3},{3,2},{4,5},{5,4},{6,7},{7,6},{8,9},{9,8},{10,11... | collective-permute-start | bytes 417800 | tf_op jit(solution)/shard_map/ppermute | solution.py:712
  65.9 6.4 %collective-permute-start.13 = (bf16[2,2,128,256]{3,2,1,0:T(8,128)(2,1)S(1)}, bf16[2,2,128,256]{3,2,1,0:T(8,128)(2,1)S(1)}, u32[]{:S(2)}, u32[]{:S(2)}) collective-permute-start(bf16[2,2,128,256]{3,2,1,0:T(8,128)(2,1)S(1)} %pad_maximum_fusion.4), channel_id=1, source_target_pairs={{0,1},{1,0},{2,3},{3,2},{4,5},{5,4},{6,7},{7,6},{8,9},{9,8},{10,11... | collective-permute-start | bytes 786440 | tf_op jit(solution)/shard_map/ppermute | solution.py:712
  67.2 9.2 %copy-start.11 = (f32[1,256,256]{2,1,0:T(8,128)S(1)}, f32[1,256,256]{2,1,0:T(8,128)}, u32[]{:S(2)}) copy-start(f32[1,256,256]{2,1,0:T(8,128)} %param.41) | copy-start | bytes 786436
  67.2 9.2 %copy-start.15 = (f32[1,9,256]{2,0,1:T(1,128)S(1)}, f32[1,9,256]{2,0,1:T(1,128)}, u32[]{:S(2)}) copy-start(f32[1,9,256]{2,0,1:T(1,128)} %param.27) | copy-start | bytes 27652
  67.2 9.2 %copy-start.16 = (f32[1,3328]{1,0:T(1,128)S(1)}, f32[1,3328]{1,0:T(1,128)}, u32[]{:S(2)}) copy-start(f32[1,3328]{1,0:T(1,128)} %refs_15_.1) | copy-start | bytes 39940
  67.2 9.2 %copy-start.17 = (f32[1,3328]{1,0:T(1,128)S(1)}, f32[1,3328]{1,0:T(1,128)}, u32[]{:S(2)}) copy-start(f32[1,3328]{1,0:T(1,128)} %refs_21_.1) | copy-start | bytes 39940
  67.2 9.2 %copy-start.18 = (f32[1,9,256]{2,0,1:T(1,128)S(1)}, f32[1,9,256]{2,0,1:T(1,128)}, u32[]{:S(2)}) copy-start(f32[1,9,256]{2,0,1:T(1,128)} %param.33) | copy-start | bytes 27652
  67.2 9.2 %copy-start.19 = (f32[1,9,256]{2,0,1:T(1,128)S(1)}, f32[1,9,256]{2,0,1:T(1,128)}, u32[]{:S(2)}) copy-start(f32[1,9,256]{2,0,1:T(1,128)} %param.39) | copy-start | bytes 27652
  67.3 6.4 %collective-permute-start.21 = (bf16[2,2,128,256]{3,2,1,0:T(8,128)(2,1)S(1)}, bf16[2,2,128,256]{3,2,1,0:T(8,128)(2,1)S(1)}, u32[]{:S(2)}, u32[]{:S(2)}) collective-permute-start(bf16[2,2,128,256]{3,2,1,0:T(8,128)(2,1)S(1)} %pad_maximum_fusion.5), channel_id=1, source_target_pairs={{0,2},{1,3},{2,0},{3,1},{4,6},{5,7},{6,4},{7,5},{8,10},{9,11},{10,... | collective-permute-start | bytes 786440 | tf_op jit(solution)/shard_map/ppermute | solution.py:712
  68.0 8.4 %copy-start.9 = (f32[1,256,768]{2,1,0:T(8,128)S(1)}, f32[1,256,768]{2,1,0:T(8,128)}, u32[]{:S(2)}) copy-start(f32[1,256,768]{2,1,0:T(8,128)} %param.40) | copy-start | bytes 2359300
  68.1 8.3 %copy-start.8 = (f32[1,256,768]{2,1,0:T(8,128)S(1)}, f32[1,256,768]{2,1,0:T(8,128)}, u32[]{:S(2)}) copy-start(f32[1,256,768]{2,1,0:T(8,128)} %param.34) | copy-start | bytes 2359300
  68.1 6.6 %collective-permute-start.29 = (bf16[2,2,136,256]{3,2,1,0:T(8,128)(2,1)S(1)}, bf16[2,2,136,256]{3,2,1,0:T(8,128)(2,1)S(1)}, u32[]{:S(2)}, u32[]{:S(2)}) collective-permute-start(bf16[2,2,136,256]{3,2,1,0:T(8,128)(2,1)S(1)} %pad_maximum_fusion.3), channel_id=1, source_target_pairs={{0,4},{1,5},{2,6},{3,7},{4,0},{5,1},{6,2},{7,3},{8,12},{9,13},{10,... | collective-permute-start | bytes 835592 | tf_op jit(solution)/shard_map/ppermute | solution.py:712
  72.3 4.1 %copy-start.6 = (f32[1,1024,256]{2,1,0:T(8,128)S(1)}, f32[1,1024,256]{2,1,0:T(8,128)}, u32[]{:S(2)}) copy-start(f32[1,1024,256]{2,1,0:T(8,128)} %param.43) | copy-start | bytes 3145732
  73.7 2.7 %copy-start.5 = (f32[1,256,1024]{2,1,0:T(8,128)S(1)}, f32[1,256,1024]{2,1,0:T(8,128)}, u32[]{:S(2)}) copy-start(f32[1,256,1024]{2,1,0:T(8,128)} %param.42) | copy-start | bytes 3145732
  73.7 2.7 %copy-start.4 = (f32[1,1024,256]{2,1,0:T(8,128)S(1)}, f32[1,1024,256]{2,1,0:T(8,128)}, u32[]{:S(2)}) copy-start(f32[1,1024,256]{2,1,0:T(8,128)} %param.37) | copy-start | bytes 3145732
  73.8 2.6 %copy-start.3 = (f32[1,256,1024]{2,1,0:T(8,128)S(1)}, f32[1,256,1024]{2,1,0:T(8,128)}, u32[]{:S(2)}) copy-start(f32[1,256,1024]{2,1,0:T(8,128)} %param.36) | copy-start | bytes 3145732
  74.7 1.7 %copy-start.2 = (f32[1,256,768]{2,1,0:T(8,128)S(1)}, f32[1,256,768]{2,1,0:T(8,128)}, u32[]{:S(2)}) copy-start(f32[1,256,768]{2,1,0:T(8,128)} %param.28) | copy-start | bytes 2359300
  74.8 1.7 %copy-start.1 = (f32[1,1024,256]{2,1,0:T(8,128)S(1)}, f32[1,1024,256]{2,1,0:T(8,128)}, u32[]{:S(2)}) copy-start(f32[1,1024,256]{2,1,0:T(8,128)} %param.31) | copy-start | bytes 3145732
  74.9 1.8 %copy-start = (f32[1,256,1024]{2,1,0:T(8,128)S(1)}, f32[1,256,1024]{2,1,0:T(8,128)}, u32[]{:S(2)}) copy-start(f32[1,256,1024]{2,1,0:T(8,128)} %param.30) | copy-start | bytes 3145732
  74.9 1.8 %copy-start.7 = (f32[1,256,256]{2,1,0:T(8,128)S(1)}, f32[1,256,256]{2,1,0:T(8,128)}, u32[]{:S(2)}) copy-start(f32[1,256,256]{2,1,0:T(8,128)} %param.29) | copy-start | bytes 786436
  74.9 1.9 %copy-start.10 = (f32[1,256,256]{2,1,0:T(8,128)S(1)}, f32[1,256,256]{2,1,0:T(8,128)}, u32[]{:S(2)}) copy-start(f32[1,256,256]{2,1,0:T(8,128)} %param.35) | copy-start | bytes 786436
  74.9 1.9 %copy-start.13 = (f32[1,3328]{1,0:T(1,128)S(1)}, f32[1,3328]{1,0:T(1,128)}, u32[]{:S(2)}) copy-start(f32[1,3328]{1,0:T(1,128)} %refs_9_.1) | copy-start | bytes 39940
  75.2 1.2 %collective-permute-start.30 = (f32[8,128]{1,0:T(8,128)S(1)}, f32[8,128]{1,0:T(8,128)S(1)}, u32[]{:S(2)}, u32[]{:S(2)}) collective-permute-start(f32[8,128]{1,0:T(8,128)S(1)} %squares.1.refs_4_), channel_id=1, source_target_pairs={{0,16},{16,0},{1,17},{17,1},{2,18},{18,2},{3,19},{19,3},{4,20},{20... | collective-permute-start | bytes 12296 | tf_op jit(solution)/shard_map/ppermute | solution.py:700

commit v4 on v3

--- a/solution.py
+++ b/solution.py
@@ -191,16 +191,16 @@
         lanes = slice(half * HALF, (half + 1) * HALF)
         probs[unit] = dot_nt(qkv[1, rows, lanes], stacked_heads(qkv[0, rows, lanes], masks))
         flipped[unit] = qkv[2, rows, lanes].T
-    for unit, (group, half) in enumerate(units):
+    for group in range(NGROUP):
         fenced = fence[group]
-        for head in range(HEADS // 2):
-            cols = slice(head * GROUP, (head + 1) * GROUP)
-            s = probs[unit, :, cols] + fenced
-            p = jnp.exp2((s - jnp.max(s, axis=0, keepdims=True)) * EXP_SCALE)
-            p = p * (1.0 / jnp.sum(p, axis=0, keepdims=True))
-            probs[unit, :, cols] = p
-            probs_low[unit, :, cols] = p.astype(BF16)
-    for group in range(NGROUP):
+        for unit in (2 * group, 2 * group + 1):
+            for head in range(HEADS // 2):
+                cols = slice(head * GROUP, (head + 1) * GROUP)
+                s = probs[unit, :, cols] + fenced
+                p = jnp.exp2((s - jnp.max(s, axis=0, keepdims=True)) * EXP_SCALE)
+                p = p * (1.0 / jnp.sum(p, axis=0, keepdims=True))
+                probs[unit, :, cols] = p
+                probs_low[unit, :, cols] = p.astype(BF16)
         rows = window(group)
         v = qkv[2, rows, :]
         moved = dot(shifts[group], v)
@@ -220,29 +220,29 @@
     mixed[:, :HALF] = mixed_att[0]
     mixed[:, HALF:] = dot(turned[...], mixed_att[1]).astype(BF16)
     middle[...] = dot(mixed[...], wp[...])
-    for start, size in ROWS:
-        rows = pl.ds(start, size)
-        mid = x_ref[rows, :].astype(F32) + middle[rows, :] + vec_at(vec, 6)
-        middle[rows, :] = mid
-        hat, scale, y = norm_forward(mid, vec_at(vec, 1), vec_at(vec, 3))
-        hat2[rows, :] = hat
-        scale2[rows, :] = jnp.broadcast_to(scale, (size, HALF))
-        normed2[rows, :] = y.astype(BF16)
-    hidden[...] = dot(normed2[...], w1[...])
-    for start, size in ROWS:
-        rows = pl.ds(start, size)
-        for part in range(4):
-            cols = slice(part * D, (part + 1) * D)
-            h = hidden[rows, cols] + vec_at(vec, 9 + part)
-            cdf = 0.5 * (1.0 + lax.erf(h * 0.7071067811865476))
-            pdf = 0.3989422804014327 * jnp.exp(-0.5 * h * h)
-            activ[rows, cols] = (h * cdf).astype(BF16)
-            slope[rows, cols] = cdf + h * pdf
     need("deep")
-    out_ref[...] = dot(activ[...], w2[...])
-    for start, size in ROWS:
-        rows = pl.ds(start, size)
-        out_ref[rows, :] = out_ref[rows, :] + middle[rows, :] + vec_at(vec, 8)
+    sides = ((slice(0, 160), ROWS[:2]), (slice(160, MB_TOK), ROWS[2:]))
+    for side, chunks in sides:
+        for start, size in chunks:
+            rows = pl.ds(start, size)
+            mid = x_ref[rows, :].astype(F32) + middle[rows, :] + vec_at(vec, 6)
+            middle[rows, :] = mid
+            hat, scale, y = norm_forward(mid, vec_at(vec, 1), vec_at(vec, 3))
+            hat2[rows, :] = hat
+            scale2[rows, :] = jnp.broadcast_to(scale, (size, HALF))
+            normed2[rows, :] = y.astype(BF16)
+        hidden[side, :] = dot(normed2[side, :], w1[...])
+    for side, chunks in sides:
+        for start, size in chunks:
+            rows = pl.ds(start, size)
+            for part in range(4):
+                cols = slice(part * D, (part + 1) * D)
+                h = hidden[rows, cols] + vec_at(vec, 9 + part)
+                cdf = 0.5 * (1.0 + lax.erf(h * 0.7071067811865476))
+                pdf = 0.3989422804014327 * jnp.exp(-0.5 * h * h)
+                activ[rows, cols] = (h * cdf).astype(BF16)
+                slope[rows, cols] = cdf + h * pdf
+        out_ref[side, :] = dot(activ[side, :], w2[...]) + middle[side, :] + vec_at(vec, 8)
 
 
 def backward_block(up_ref, grad_ref, vec_ref, taps_ref, w, saved, tables, work, sums, small):
@@ -253,13 +253,13 @@
     early, inner, outer = sums
     vec = vec_ref[...]
     branch[...] = up_ref[...].astype(BF16)
-    outer[0:FF, :] = dot_tn(activ[...], branch[...]).astype(BF16)
     sums = column_sum(branch[...])
     small[8:9, :] = sums
     gact[...] = dot_nt(branch[...], w2[...])
     parts = [jnp.zeros((1, D), F32) for _ in range(4)]
-    for start, size in ROWS:
+    for turn, (start, size) in enumerate(ROWS):
         rows = pl.ds(start, size)
+        outer[turn * D : (turn + 1) * D, :] = dot_tn(activ[:, turn * D : (turn + 1) * D], branch[...]).astype(BF16)
         for part in range(4):
             cols = slice(part * D, (part + 1) * D)
             low = (gact[rows, cols] * slope[rows, cols]).astype(BF16)
@@ -267,14 +267,11 @@
             parts[part] = parts[part] + column_sum(low)
     for part in range(4):
         small[9 + part : 10 + part, :] = parts[part]
-    for part in range(4):
-        inner[part * D : (part + 1) * D, :] = dot_tn(
-            normed2[...], ghid[:, part * D : (part + 1) * D]
-        ).astype(BF16)
     gnorm[...] = dot_nt(ghid[...], w1[...])
     gains, offsets, outs = (jnp.zeros((1, D), F32) for _ in range(3))
-    for start, size in ROWS:
+    for turn, (start, size) in enumerate(ROWS):
         rows = pl.ds(start, size)
+        inner[turn * D : (turn + 1) * D, :] = dot_tn(normed2[...], ghid[:, turn * D : (turn + 1) * D]).astype(BF16)
         g = gnorm[rows, :]
         hat = hat2[rows, :]
         scale = scale2[rows, :]
@@ -289,7 +286,6 @@
     small[1:2, :] = gains
     small[3:4, :] = offsets
     small[6:7, :] = outs
-    early[3 * D : 4 * D, :] = dot_tn(mixed[...], branch[...]).astype(BF16)
     low = dot_nt(branch[...], wp[...]).astype(BF16)
     small[7:8, :] = column_sum(low)
     gmix[0:MB_TOK, :HALF] = low[:, :HALF]
@@ -306,14 +302,17 @@
         lanes = slice(half * HALF, (half + 1) * HALF)
         gprobs[unit] = dot_nt(qkv[2, rows, lanes], stacked_heads(gmix[rows, lanes], masks))
         flipped[unit] = qkv[1, rows, lanes].T
-    for unit in range(len(units)):
-        for head in range(HEADS // 2):
-            cols = slice(head * GROUP, (head + 1) * GROUP)
-            p = probs[unit, :, cols]
-            gp = gprobs[unit, :, cols]
-            down = jnp.sum(gp * p, axis=0, keepdims=True)
-            gscores[unit, :, cols] = (p * (gp - down)).astype(BF16)
     for group in range(NGROUP):
+        if group < 2:
+            lanes = slice(group * HALF, (group + 1) * HALF)
+            early[3 * D + group * HALF : 3 * D + (group + 1) * HALF, :] = dot_tn(mixed[:, lanes], branch[...]).astype(BF16)
+        for unit in (2 * group, 2 * group + 1):
+            for head in range(HEADS // 2):
+                cols = slice(head * GROUP, (head + 1) * GROUP)
+                p = probs[unit, :, cols]
+                gp = gprobs[unit, :, cols]
+                down = jnp.sum(gp * p, axis=0, keepdims=True)
+                gscores[unit, :, cols] = (p * (gp - down)).astype(BF16)
         rows = window(group)
         g_low = gmix[rows, :]
         moved = dot(shifts[group], g_low)
@@ -347,13 +346,7 @@
             [tap_sums[tap][:, :HALF], tap_sums[turned_index][:, HALF:]], axis=1
         )
     for half in range(2):
-        lanes = slice(half * HALF, (half + 1) * HALF)
         both = dqkv[half]
-        small[4:5, lanes] = column_sum(both[:, 0:HALF])
-        small[5:6, lanes] = column_sum(both[:, D : 3 * HALF])
-        grads = dot_tn(normed[half], both)
-        for part in range(3):
-            early[part * D : (part + 1) * D, lanes] = grads[:, part * HALF : (part + 1) * HALF].astype(BF16)
         natural = both if half == 0 else dot(turned[...], both).astype(BF16)
         for part in range(3):
             dnat[:, part * D + half * HALF : part * D + (half + 1) * HALF] = natural[
@@ -361,8 +354,16 @@
             ]
     gnorm[...] = dot_nt(dnat[...], wq[...])
     gains, offsets = (jnp.zeros((1, D), F32) for _ in range(2))
-    for start, size in ROWS:
+    for turn, (start, size) in enumerate(ROWS):
         rows = pl.ds(start, size)
+        if turn < 2:
+            both = dqkv[turn]
+            lanes = slice(turn * HALF, (turn + 1) * HALF)
+            small[4:5, lanes] = column_sum(both[:, 0:HALF])
+            small[5:6, lanes] = column_sum(both[:, D : 3 * HALF])
+            grads = dot_tn(normed[turn], both)
+            for part in range(3):
+                early[part * D : (part + 1) * D, lanes] = grads[:, part * HALF : (part + 1) * HALF].astype(BF16)
         g = gnorm[rows, :]
         hat = hat1[rows, :]
         scale = scale1[rows, :]

time: 83.5 us -> 81.7 us (0.978)
  Pallas kernels: 27.7 us -> 25.9 us
    pallas_call x1, Pallas kernels: 19 us -> 17.2 us  [run_blocks(): pl.pallas_call(section_step, out_shape=out_shape, in_specs=[smem] + [pl.B...]
where the time goes in v4:
time: 81.7 us; the launch traced here: 81.6 us
  starting transfers between devices  32.9 us (40%)
  Pallas kernels  25.9 us (32%)
  waiting for transfers between devices  19.4 us (24%)
  other arithmetic  1.62 us (2%)
  between operations  1.37 us (2%)
    ppermute x21, starting transfers between devices, exchanged(): lax.ppermute(value, 'dp', [(index, index ^ 1 << bit) for index in range(s...  30.3 us
    pallas_call x1, Pallas kernels, run_blocks(): pl.pallas_call(section_step, out_shape=out_shape, in_specs=[smem] + [pl.B...  17.2 us
    ppermute x21, waiting for transfers between devices, exchanged(): lax.ppermute(value, 'dp', [(index, index ^ 1 << bit) for index in range(s...  15.3 us
    pallas_call x1, Pallas kernels, run_optimizer(): pl.pallas_call(optimizer_step, out_shape=[pltpu.HBM(shape, kind) for shap...  6.42 us
    ppermute x10, waiting for transfers between devices, swapped(): return lax.ppermute(value, 'section', [(0, 1), (1, 0)])  4.14 us
    ppermute x10, starting transfers between devices, swapped(): return lax.ppermute(value, 'section', [(0, 1), (1, 0)])  2.57 us
    pallas_call x1, Pallas kernels, run_narrowed(): pl.pallas_call(narrowed, out_shape=[pltpu.VMEM((D, 8 * D), BF16), pltpu.V...  1.95 us
  transfers between devices with their start and end apart: 31, of which 17 were waited for; matrix products, arithmetic and copies ran while one was open for 2% of the time, Pallas kernels for 0%

profile of v4, /device:TPU:0, one launch (start us, length us, event | category | flops | bytes accessed | tf_op | source)
XLA Modules:
  0.0 81.6 jit_solution(15050672633075252392)
XLA Ops:
  0.7 2.0 %narrowed.1 = (bf16[256,2048]{1,0:T(8,128)(2,1)S(1)}, bf16[1024,256]{1,0:T(8,128)(2,1)S(1)}) custom-call(f32[256,768]{1,0:T(8,128)} %bitcast.131, f32[256,256]{1,0:T(8,128)} %bitcast.137, f32[256,1024]{1,0:T(8,128)} %bitcast.127, f32[1024,256]{1,0:T(8,128)} %bitcast.129), custom_call_target="tpu_custom_call" | custom-call | tf_op jit(solution)/shard_map/narrowed/pallas_call | solution.py:566
  2.7 0.5 collective-permute-start.2
  3.2 0.1 collective-permute-start.3
  3.3 0.4 collective-permute-start
  3.7 0.1 collective-permute-start.1
  3.8 2.5 %collective-permute-done.1.refs_5_ = f32[1,2304]{1,0:T(1,128)S(1)} collective-permute-done((f32[1,2304]{1,0:T(1,128)S(1)}, f32[1,2304]{1,0:T(1,128)S(1)}, u32[]{:S(2)}, u32[]{:S(2)}) %collective-permute-start.1) | collective-permute-done | bytes 9248 | tf_op jit(solution)/shard_map/ppermute | solution.py:701
  6.3 17.2 %blocks.1 = (f32[304,256]{1,0:T(8,128)S(1)}, f32[304,256]{1,0:T(8,128)S(1)}, f32[304,256]{1,0:T(8,128)S(1)}, f32[304,256]{1,0:T(8,128)S(1)}, bf16[1024,256]{1,0:...) custom-call(s32[1]{0:T(128)} %bitcast.sec_ref, ...), custom_call_target="tpu_custom_call" | custom-call | tf_op jit(solution)/shard_map/blocks/pallas_call | solution.py:536
  23.4 0.4 collective-permute-start.6
  23.9 0.1 collective-permute-start.14
  24.0 0.4 collective-permute-start.4
  24.4 0.1 collective-permute-start.5
  24.5 0.4 collective-permute-start.22
  24.9 0.5 collective-permute-done.6
  25.4 0.1 add_convert_fusion.2
  25.6 2.9 %collective-permute-start.7 = (bf16[2,2,128,256]{3,2,1,0:T(8,128)(2,1)S(1)}, bf16[2,2,128,256]{3,2,1,0:T(8,128)(2,1)S(1)}, u32[]{:S(2)}, u32[]{:S(2)}) collective-permute-start(bf16[2,2,128,256]{3,2,1,0:T(8,128)(2,1)S(1)} %bitcast.152), channel_id=1, source_target_pairs={{0,1},{1,0},{2,3},{3,2},{4,5},{5,4},{6,7},{7,6},{8,9},{9,8},{10,11... | collective-permute-start | bytes 786440 | tf_op jit(solution)/shard_map/ppermute | solution.py:713
  28.5 0.1 add_convert_fusion.1
  28.7 1.6 %collective-permute-start.15 = (bf16[2,2,128,256]{3,2,1,0:T(8,128)(2,1)S(1)}, bf16[2,2,128,256]{3,2,1,0:T(8,128)(2,1)S(1)}, u32[]{:S(2)}, u32[]{:S(2)}) collective-permute-start(bf16[2,2,128,256]{3,2,1,0:T(8,128)(2,1)S(1)} %bitcast.153), channel_id=1, source_target_pairs={{0,2},{1,3},{2,0},{3,1},{4,6},{5,7},{6,4},{7,5},{8,10},{9,11},{10,... | collective-permute-start | bytes 786440 | tf_op jit(solution)/shard_map/ppermute | solution.py:713
  30.3 0.1 add_convert_fusion
  30.5 1.6 %collective-permute-start.23 = (bf16[2,2,136,256]{3,2,1,0:T(8,128)(2,1)S(1)}, bf16[2,2,136,256]{3,2,1,0:T(8,128)(2,1)S(1)}, u32[]{:S(2)}, u32[]{:S(2)}) collective-permute-start(bf16[2,2,136,256]{3,2,1,0:T(8,128)(2,1)S(1)} %bitcast.151), channel_id=1, source_target_pairs={{0,4},{1,5},{2,6},{3,7},{4,0},{5,1},{6,2},{7,3},{8,12},{9,13},{10,... | collective-permute-start | bytes 835592 | tf_op jit(solution)/shard_map/ppermute | solution.py:713
  32.1 3.0 %collective-permute-done.7 = bf16[2,2,128,256]{3,2,1,0:T(8,128)(2,1)S(1)} collective-permute-done((bf16[2,2,128,256]{3,2,1,0:T(8,128)(2,1)S(1)}, bf16[2,2,128,256]{3,2,1,0:T(8,128)(2,1)S(1)}, u32[]{:S(2)}, u32[]{:S(2)}) %collective-permute-start.7) | collective-permute-done | bytes 262176 | tf_op jit(solution)/shard_map/ppermute | solution.py:713
  35.1 0.1 fusion.2
  35.2 1.8 %collective-permute-start.8 = (bf16[2,128,256]{2,1,0:T(8,128)(2,1)S(1)}, bf16[2,128,256]{2,1,0:T(8,128)(2,1)S(1)}, u32[]{:S(2)}, u32[]{:S(2)}) collective-permute-start(bf16[2,128,256]{2,1,0:T(8,128)(2,1)S(1)} %select_bitcast_fusion.14), channel_id=1, source_target_pairs={{0,2},{1,3},{2,0},{3,1},{4,6},{5,7},{6,4},{7,5},{8,10},{9,11},{10,... | collective-permute-start | bytes 393224 | tf_op jit(solution)/shard_map/ppermute | solution.py:713
  37.1 0.1 fusion.1
  37.2 1.6 %collective-permute-start.16 = (bf16[2,128,256]{2,1,0:T(8,128)(2,1)S(1)}, bf16[2,128,256]{2,1,0:T(8,128)(2,1)S(1)}, u32[]{:S(2)}, u32[]{:S(2)}) collective-permute-start(bf16[2,128,256]{2,1,0:T(8,128)(2,1)S(1)} %select_bitcast_fusion.11), channel_id=1, source_target_pairs={{0,4},{1,5},{2,6},{3,7},{4,0},{5,1},{6,2},{7,3},{8,12},{9,13},{10,... | collective-permute-start | bytes 393224 | tf_op jit(solution)/shard_map/ppermute | solution.py:713
  38.8 0.1 fusion
  38.9 1.6 %collective-permute-start.24 = (bf16[2,136,256]{2,1,0:T(8,128)(2,1)S(1)}, bf16[2,136,256]{2,1,0:T(8,128)(2,1)S(1)}, u32[]{:S(2)}, u32[]{:S(2)}) collective-permute-start(bf16[2,136,256]{2,1,0:T(8,128)(2,1)S(1)} %select_bitcast_fusion.8), channel_id=1, source_target_pairs={{0,1},{1,0},{2,3},{3,2},{4,5},{5,4},{6,7},{7,6},{8,9},{9,8},{10,11... | collective-permute-start | bytes 417800 | tf_op jit(solution)/shard_map/ppermute | solution.py:713
  40.5 0.1 fusion.5
  40.5 1.7 %collective-permute-start.9 = (bf16[128,256]{1,0:T(8,128)(2,1)S(1)}, bf16[128,256]{1,0:T(8,128)(2,1)S(1)}, u32[]{:S(2)}, u32[]{:S(2)}) collective-permute-start(bf16[128,256]{1,0:T(8,128)(2,1)S(1)} %select_bitcast_fusion.23), channel_id=1, source_target_pairs={{0,4},{1,5},{2,6},{3,7},{4,0},{5,1},{6,2},{7,3},{8,12},{9,13},{10,... | collective-permute-start | bytes 196616 | tf_op jit(solution)/shard_map/ppermute | solution.py:713
  42.2 0.4 collective-permute-done.16
  42.7 1.8 %collective-permute-start.17 = (bf16[128,256]{1,0:T(8,128)(2,1)S(1)}, bf16[128,256]{1,0:T(8,128)(2,1)S(1)}, u32[]{:S(2)}, u32[]{:S(2)}) collective-permute-start(bf16[128,256]{1,0:T(8,128)(2,1)S(1)} %select_bitcast_fusion.20), channel_id=1, source_target_pairs={{0,1},{1,0},{2,3},{3,2},{4,5},{5,4},{6,7},{7,6},{8,9},{9,8},{10,11... | collective-permute-start | bytes 196616 | tf_op jit(solution)/shard_map/ppermute | solution.py:713
  44.5 0.2 collective-permute-done.24
  44.7 0.1 fusion.3
  44.8 1.4 %collective-permute-start.25 = (bf16[136,256]{1,0:T(8,128)(2,1)S(1)}, bf16[136,256]{1,0:T(8,128)(2,1)S(1)}, u32[]{:S(2)}, u32[]{:S(2)}) collective-permute-start(bf16[136,256]{1,0:T(8,128)(2,1)S(1)} %select_bitcast_fusion.17), channel_id=1, source_target_pairs={{0,2},{1,3},{2,0},{3,1},{4,6},{5,7},{6,4},{7,5},{8,10},{9,11},{10,... | collective-permute-start | bytes 208904 | tf_op jit(solution)/shard_map/ppermute | solution.py:713
  46.2 2.7 %collective-permute-start.10 = (bf16[128,256]{1,0:T(8,128)(2,1)S(1)}, bf16[128,256]{1,0:T(8,128)(2,1)S(1)}, u32[]{:S(2)}, u32[]{:S(2)}) collective-permute-start(bf16[128,256]{1,0:T(8,128)(2,1)S(1)} %fusion.8), channel_id=1, source_target_pairs={{0,8},{1,9},{2,10},{3,11},{4,12},{5,13},{6,14},{7,15},{8,0},{9,1},... | collective-permute-start | bytes 196616 | tf_op jit(solution)/shard_map/ppermute | solution.py:713
  48.9 0.9 %collective-permute-start.18 = (bf16[128,256]{1,0:T(8,128)(2,1)S(1)}, bf16[128,256]{1,0:T(8,128)(2,1)S(1)}, u32[]{:S(2)}, u32[]{:S(2)}) collective-permute-start(bf16[128,256]{1,0:T(8,128)(2,1)S(1)} %fusion.7), channel_id=1, source_target_pairs={{0,8},{1,9},{2,10},{3,11},{4,12},{5,13},{6,14},{7,15},{8,0},{9,1},... | collective-permute-start | bytes 196616 | tf_op jit(solution)/shard_map/ppermute | solution.py:713
  49.9 2.1 %collective-permute-start.26 = (bf16[136,256]{1,0:T(8,128)(2,1)S(1)}, bf16[136,256]{1,0:T(8,128)(2,1)S(1)}, u32[]{:S(2)}, u32[]{:S(2)}) collective-permute-start(bf16[136,256]{1,0:T(8,128)(2,1)S(1)} %fusion.6), channel_id=1, source_target_pairs={{0,8},{1,9},{2,10},{3,11},{4,12},{5,13},{6,14},{7,15},{8,0},{9,1},... | collective-permute-start | bytes 208904 | tf_op jit(solution)/shard_map/ppermute | solution.py:713
  52.0 1.8 %collective-permute-done.10 = bf16[128,256]{1,0:T(8,128)(2,1)S(1)} collective-permute-done((bf16[128,256]{1,0:T(8,128)(2,1)S(1)}, bf16[128,256]{1,0:T(8,128)(2,1)S(1)}, u32[]{:S(2)}, u32[]{:S(2)}) %collective-permute-start.10) | collective-permute-done | bytes 65568 | tf_op jit(solution)/shard_map/ppermute | solution.py:713
  53.8 0.2 collective-permute-start.11
  53.9 1.2 %collective-permute-done.18 = bf16[128,256]{1,0:T(8,128)(2,1)S(1)} collective-permute-done((bf16[128,256]{1,0:T(8,128)(2,1)S(1)}, bf16[128,256]{1,0:T(8,128)(2,1)S(1)}, u32[]{:S(2)}, u32[]{:S(2)}) %collective-permute-start.18) | collective-permute-done | bytes 65568 | tf_op jit(solution)/shard_map/ppermute | solution.py:713
  55.2 1.3 %collective-permute-start.19 = (bf16[128,256]{1,0:T(8,128)(2,1)S(1)}, bf16[128,256]{1,0:T(8,128)(2,1)S(1)}, u32[]{:S(2)}, u32[]{:S(2)}) collective-permute-start(bf16[128,256]{1,0:T(8,128)(2,1)S(1)} %add_convert_fusion.4), channel_id=1, source_target_pairs={{0,1},{1,0},{2,3},{3,2},{4,5},{5,4},{6,7},{7,6},{8,9},{9,8},{10,11... | collective-permute-start | bytes 196616 | tf_op jit(solution)/shard_map/ppermute | solution.py:713
  56.5 0.1 collective-permute-done.26
  56.7 1.5 %collective-permute-start.27 = (bf16[136,256]{1,0:T(8,128)(2,1)S(1)}, bf16[136,256]{1,0:T(8,128)(2,1)S(1)}, u32[]{:S(2)}, u32[]{:S(2)}) collective-permute-start(bf16[136,256]{1,0:T(8,128)(2,1)S(1)} %add_convert_fusion.3), channel_id=1, source_target_pairs={{0,2},{1,3},{2,0},{3,1},{4,6},{5,7},{6,4},{7,5},{8,10},{9,11},{10,... | collective-permute-start | bytes 208904 | tf_op jit(solution)/shard_map/ppermute | solution.py:713
  58.2 1.1 %collective-permute-start.12 = (bf16[2,128,256]{2,1,0:T(8,128)(2,1)S(1)}, bf16[2,128,256]{2,1,0:T(8,128)(2,1)S(1)}, u32[]{:S(2)}, u32[]{:S(2)}) collective-permute-start(bf16[2,128,256]{2,1,0:T(8,128)(2,1)S(1)} %pad_maximum_fusion.7), channel_id=1, source_target_pairs={{0,2},{1,3},{2,0},{3,1},{4,6},{5,7},{6,4},{7,5},{8,10},{9,11},{10,... | collective-permute-start | bytes 393224 | tf_op jit(solution)/shard_map/ppermute | solution.py:713
  59.3 0.3 collective-permute-done.19
  59.6 0.9 %collective-permute-start.20 = (bf16[2,128,256]{2,1,0:T(8,128)(2,1)S(1)}, bf16[2,128,256]{2,1,0:T(8,128)(2,1)S(1)}, u32[]{:S(2)}, u32[]{:S(2)}) collective-permute-start(bf16[2,128,256]{2,1,0:T(8,128)(2,1)S(1)} %pad_maximum_fusion.8), channel_id=1, source_target_pairs={{0,4},{1,5},{2,6},{3,7},{4,0},{5,1},{6,2},{7,3},{8,12},{9,13},{10,... | collective-permute-start | bytes 393224 | tf_op jit(solution)/shard_map/ppermute | solution.py:713
  60.4 0.6 collective-permute-done.27
  61.1 1.3 %collective-permute-start.28 = (bf16[2,136,256]{2,1,0:T(8,128)(2,1)S(1)}, bf16[2,136,256]{2,1,0:T(8,128)(2,1)S(1)}, u32[]{:S(2)}, u32[]{:S(2)}) collective-permute-start(bf16[2,136,256]{2,1,0:T(8,128)(2,1)S(1)} %pad_maximum_fusion.6), channel_id=1, source_target_pairs={{0,1},{1,0},{2,3},{3,2},{4,5},{5,4},{6,7},{7,6},{8,9},{9,8},{10,11... | collective-permute-start | bytes 417800 | tf_op jit(solution)/shard_map/ppermute | solution.py:713
  62.5 1.6 %collective-permute-done.12 = bf16[2,128,256]{2,1,0:T(8,128)(2,1)S(1)} collective-permute-done((bf16[2,128,256]{2,1,0:T(8,128)(2,1)S(1)}, bf16[2,128,256]{2,1,0:T(8,128)(2,1)S(1)}, u32[]{:S(2)}, u32[]{:S(2)}) %collective-permute-start.12) | collective-permute-done | bytes 131104 | tf_op jit(solution)/shard_map/ppermute | solution.py:713
  64.1 1.1 %collective-permute-start.13 = (bf16[2,2,128,256]{3,2,1,0:T(8,128)(2,1)S(1)}, bf16[2,2,128,256]{3,2,1,0:T(8,128)(2,1)S(1)}, u32[]{:S(2)}, u32[]{:S(2)}) collective-permute-start(bf16[2,2,128,256]{3,2,1,0:T(8,128)(2,1)S(1)} %pad_maximum_fusion.4), channel_id=1, source_target_pairs={{0,1},{1,0},{2,3},{3,2},{4,5},{5,4},{6,7},{7,6},{8,9},{9,8},{10,11... | collective-permute-start | bytes 786440 | tf_op jit(solution)/shard_map/ppermute | solution.py:713
  65.1 0.2 collective-permute-done.20
  65.5 0.5 collective-permute-start.21
  66.0 0.3 collective-permute-done.28
  66.3 0.8 collective-permute-start.29
  67.1 3.4 %collective-permute-done.13 = bf16[2,2,128,256]{3,2,1,0:T(8,128)(2,1)S(1)} collective-permute-done((bf16[2,2,128,256]{3,2,1,0:T(8,128)(2,1)S(1)}, bf16[2,2,128,256]{3,2,1,0:T(8,128)(2,1)S(1)}, u32[]{:S(2)}, u32[]{:S(2)}) %collective-permute-start.13) | collective-permute-done | bytes 262176 | tf_op jit(solution)/shard_map/ppermute | solution.py:713
  70.6 1.3 %collective-permute-done.21 = bf16[2,2,128,256]{3,2,1,0:T(8,128)(2,1)S(1)} collective-permute-done((bf16[2,2,128,256]{3,2,1,0:T(8,128)(2,1)S(1)}, bf16[2,2,128,256]{3,2,1,0:T(8,128)(2,1)S(1)}, u32[]{:S(2)}, u32[]{:S(2)}) %collective-permute-start.21) | collective-permute-done | bytes 262176 | tf_op jit(solution)/shard_map/ppermute | solution.py:713
  72.0 0.1 pad_maximum_fusion.1
  72.0 0.1 pad_maximum_fusion.2
  72.1 0.8 %collective-permute-done.29 = bf16[2,2,136,256]{3,2,1,0:T(8,128)(2,1)S(1)} collective-permute-done((bf16[2,2,136,256]{3,2,1,0:T(8,128)(2,1)S(1)}, bf16[2,2,136,256]{3,2,1,0:T(8,128)(2,1)S(1)}, u32[]{:S(2)}, u32[]{:S(2)}) %collective-permute-start.29) | collective-permute-done | bytes 278560 | tf_op jit(solution)/shard_map/ppermute | solution.py:713
  73.0 0.1 pad_maximum_fusion
  73.1 0.3 squares.1.refs_4_
  73.4 1.1 %collective-permute-done.30.refs_5_ = f32[8,128]{1,0:T(8,128)S(1)} collective-permute-done((f32[8,128]{1,0:T(8,128)S(1)}, f32[8,128]{1,0:T(8,128)S(1)}, u32[]{:S(2)}, u32[]{:S(2)}) %collective-permute-start.30) | collective-permute-done | bytes 4128 | tf_op jit(solution)/shard_map/ppermute | solution.py:701
  74.7 0.2 copy-done
  74.9 0.1 copy-done.10
  75.0 6.4 %optimizer.1 = (f32[1,3328]{1,0:T(1,128)}, f32[1,2304]{1,0:T(1,128)}, f32[256,768]{1,0:T(8,128)}, f32[256,256]{1,0:T(8,128)}, f32[256,1024]{1,0:T(8,128)}, /*ind...) custom-call(s32[1]{0:T(128)} %bitcast.sec_ref, ...), custom_call_target="tpu_custom_call" | custom-call | tf_op jit(solution)/shard_map/optimizer/pallas_call | solution.py:687
  (84 shorter events, 0.9 us)
Async XLA Ops:
  0.7 2.6 %copy-start.12 = (f32[1,3328]{1,0:T(1,128)S(1)}, f32[1,3328]{1,0:T(1,128)}, u32[]{:S(2)}) copy-start(f32[1,3328]{1,0:T(1,128)} %refs_9_.1) | copy-start | bytes 39940
  0.7 3.0 %copy-start.14 = (f32[1,9,256]{2,0,1:T(1,128)S(1)}, f32[1,9,256]{2,0,1:T(1,128)}, u32[]{:S(2)}) copy-start(f32[1,9,256]{2,0,1:T(1,128)} %param.27) | copy-start | bytes 27652
  2.7 3.6 %collective-permute-start.2 = (bf16[256,2048]{1,0:T(8,128)(2,1)S(1)}, bf16[256,2048]{1,0:T(8,128)(2,1)S(1)}, u32[]{:S(2)}, u32[]{:S(2)}) collective-permute-start(bf16[256,2048]{1,0:T(8,128)(2,1)S(1)} %get-tuple-element.79.refs_6_), channel_id=1, source_target_pairs={{0,16},{16,0},{1,17},{17,1},{2,18},{18,2},{3,19},{19,3},{4,20},{20... | collective-permute-start | bytes 3145736 | tf_op jit(solution)/shard_map/ppermute | solution.py:701
  3.2 3.1 %collective-permute-start.3 = (bf16[1024,256]{1,0:T(8,128)(2,1)S(1)}, bf16[1024,256]{1,0:T(8,128)(2,1)S(1)}, u32[]{:S(2)}, u32[]{:S(2)}) collective-permute-start(bf16[1024,256]{1,0:T(8,128)(2,1)S(1)} %get-tuple-element.80.refs_8_), channel_id=1, source_target_pairs={{0,16},{16,0},{1,17},{17,1},{2,18},{18,2},{3,19},{19,3},{4,20},{20... | collective-permute-start | bytes 1572872 | tf_op jit(solution)/shard_map/ppermute | solution.py:701
  3.3 3.0 %collective-permute-start = (f32[1,3328]{1,0:T(1,128)S(1)}, f32[1,3328]{1,0:T(1,128)S(1)}, u32[]{:S(2)}, u32[]{:S(2)}) collective-permute-start(f32[1,3328]{1,0:T(1,128)S(1)} %copy-done.12), channel_id=1, source_target_pairs={{0,16},{16,0},{1,17},{17,1},{2,18},{18,2},{3,19},{19,3},{4,20},{20... | collective-permute-start | bytes 39944 | tf_op jit(solution)/shard_map/ppermute | solution.py:701
  3.7 2.6 %collective-permute-start.1 = (f32[1,2304]{1,0:T(1,128)S(1)}, f32[1,2304]{1,0:T(1,128)S(1)}, u32[]{:S(2)}, u32[]{:S(2)}) collective-permute-start(f32[1,2304]{1,0:T(1,128)S(1)} %bitcast.144), channel_id=1, source_target_pairs={{0,16},{16,0},{1,17},{17,1},{2,18},{18,2},{3,19},{19,3},{4,20},{20... | collective-permute-start | bytes 27656 | tf_op jit(solution)/shard_map/ppermute | solution.py:701
  23.4 2.0 %collective-permute-start.6 = (bf16[1024,256]{1,0:T(8,128)(2,1)S(1)}, bf16[1024,256]{1,0:T(8,128)(2,1)S(1)}, u32[]{:S(2)}, u32[]{:S(2)}) collective-permute-start(bf16[1024,256]{1,0:T(8,128)(2,1)S(1)} %get-tuple-element.89), channel_id=1, source_target_pairs={{0,16},{16,0},{1,17},{17,1},{2,18},{18,2},{3,19},{19,3},{4,20},{20... | collective-permute-start | bytes 1572872 | tf_op jit(solution)/shard_map/ppermute | solution.py:701
  23.9 4.6 %collective-permute-start.14 = (bf16[1024,256]{1,0:T(8,128)(2,1)S(1)}, bf16[1024,256]{1,0:T(8,128)(2,1)S(1)}, u32[]{:S(2)}, u32[]{:S(2)}) collective-permute-start(bf16[1024,256]{1,0:T(8,128)(2,1)S(1)} %get-tuple-element.91), channel_id=1, source_target_pairs={{0,16},{16,0},{1,17},{17,1},{2,18},{18,2},{3,19},{19,3},{4,20},{20... | collective-permute-start | bytes 1572872 | tf_op jit(solution)/shard_map/ppermute | solution.py:701
  24.0 49.4 %collective-permute-start.4 = (f32[304,256]{1,0:T(8,128)S(1)}, f32[304,256]{1,0:T(8,128)S(1)}, u32[]{:S(2)}, u32[]{:S(2)}) collective-permute-start(f32[304,256]{1,0:T(8,128)S(1)} %get-tuple-element.82), channel_id=1, source_target_pairs={{0,16},{16,0},{1,17},{17,1},{2,18},{18,2},{3,19},{19,3},{4,20},{20... | collective-permute-start | bytes 933896 | tf_op jit(solution)/shard_map/ppermute | solution.py:701
  24.4 49.0 %collective-permute-start.5 = (f32[304,256]{1,0:T(8,128)S(1)}, f32[304,256]{1,0:T(8,128)S(1)}, u32[]{:S(2)}, u32[]{:S(2)}) collective-permute-start(f32[304,256]{1,0:T(8,128)S(1)} %get-tuple-element.84), channel_id=1, source_target_pairs={{0,16},{16,0},{1,17},{17,1},{2,18},{18,2},{3,19},{19,3},{4,20},{20... | collective-permute-start | bytes 933896 | tf_op jit(solution)/shard_map/ppermute | solution.py:701
  24.5 5.8 %collective-permute-start.22 = (bf16[1088,256]{1,0:T(8,128)(2,1)S(1)}, bf16[1088,256]{1,0:T(8,128)(2,1)S(1)}, u32[]{:S(2)}, u32[]{:S(2)}) collective-permute-start(bf16[1088,256]{1,0:T(8,128)(2,1)S(1)} %get-tuple-element.93), channel_id=1, source_target_pairs={{0,16},{16,0},{1,17},{17,1},{2,18},{18,2},{3,19},{19,3},{4,20},{20... | collective-permute-start | bytes 1671176 | tf_op jit(solution)/shard_map/ppermute | solution.py:701
  25.6 9.5 %collective-permute-start.7 = (bf16[2,2,128,256]{3,2,1,0:T(8,128)(2,1)S(1)}, bf16[2,2,128,256]{3,2,1,0:T(8,128)(2,1)S(1)}, u32[]{:S(2)}, u32[]{:S(2)}) collective-permute-start(bf16[2,2,128,256]{3,2,1,0:T(8,128)(2,1)S(1)} %bitcast.152), channel_id=1, source_target_pairs={{0,1},{1,0},{2,3},{3,2},{4,5},{5,4},{6,7},{7,6},{8,9},{9,8},{10,11... | collective-permute-start | bytes 786440 | tf_op jit(solution)/shard_map/ppermute | solution.py:713
  28.7 8.4 %collective-permute-start.15 = (bf16[2,2,128,256]{3,2,1,0:T(8,128)(2,1)S(1)}, bf16[2,2,128,256]{3,2,1,0:T(8,128)(2,1)S(1)}, u32[]{:S(2)}, u32[]{:S(2)}) collective-permute-start(bf16[2,2,128,256]{3,2,1,0:T(8,128)(2,1)S(1)} %bitcast.153), channel_id=1, source_target_pairs={{0,2},{1,3},{2,0},{3,1},{4,6},{5,7},{6,4},{7,5},{8,10},{9,11},{10,... | collective-permute-start | bytes 786440 | tf_op jit(solution)/shard_map/ppermute | solution.py:713
  30.5 8.3 %collective-permute-start.23 = (bf16[2,2,136,256]{3,2,1,0:T(8,128)(2,1)S(1)}, bf16[2,2,136,256]{3,2,1,0:T(8,128)(2,1)S(1)}, u32[]{:S(2)}, u32[]{:S(2)}) collective-permute-start(bf16[2,2,136,256]{3,2,1,0:T(8,128)(2,1)S(1)} %bitcast.151), channel_id=1, source_target_pairs={{0,4},{1,5},{2,6},{3,7},{4,0},{5,1},{6,2},{7,3},{8,12},{9,13},{10,... | collective-permute-start | bytes 835592 | tf_op jit(solution)/shard_map/ppermute | solution.py:713
  35.2 5.2 %collective-permute-start.8 = (bf16[2,128,256]{2,1,0:T(8,128)(2,1)S(1)}, bf16[2,128,256]{2,1,0:T(8,128)(2,1)S(1)}, u32[]{:S(2)}, u32[]{:S(2)}) collective-permute-start(bf16[2,128,256]{2,1,0:T(8,128)(2,1)S(1)} %select_bitcast_fusion.14), channel_id=1, source_target_pairs={{0,2},{1,3},{2,0},{3,1},{4,6},{5,7},{6,4},{7,5},{8,10},{9,11},{10,... | collective-permute-start | bytes 393224 | tf_op jit(solution)/shard_map/ppermute | solution.py:713
  37.2 5.5 %collective-permute-start.16 = (bf16[2,128,256]{2,1,0:T(8,128)(2,1)S(1)}, bf16[2,128,256]{2,1,0:T(8,128)(2,1)S(1)}, u32[]{:S(2)}, u32[]{:S(2)}) collective-permute-start(bf16[2,128,256]{2,1,0:T(8,128)(2,1)S(1)} %select_bitcast_fusion.11), channel_id=1, source_target_pairs={{0,4},{1,5},{2,6},{3,7},{4,0},{5,1},{6,2},{7,3},{8,12},{9,13},{10,... | collective-permute-start | bytes 393224 | tf_op jit(solution)/shard_map/ppermute | solution.py:713
  38.9 5.8 %collective-permute-start.24 = (bf16[2,136,256]{2,1,0:T(8,128)(2,1)S(1)}, bf16[2,136,256]{2,1,0:T(8,128)(2,1)S(1)}, u32[]{:S(2)}, u32[]{:S(2)}) collective-permute-start(bf16[2,136,256]{2,1,0:T(8,128)(2,1)S(1)} %select_bitcast_fusion.8), channel_id=1, source_target_pairs={{0,1},{1,0},{2,3},{3,2},{4,5},{5,4},{6,7},{7,6},{8,9},{9,8},{10,11... | collective-permute-start | bytes 417800 | tf_op jit(solution)/shard_map/ppermute | solution.py:713
  40.5 5.6 %collective-permute-start.9 = (bf16[128,256]{1,0:T(8,128)(2,1)S(1)}, bf16[128,256]{1,0:T(8,128)(2,1)S(1)}, u32[]{:S(2)}, u32[]{:S(2)}) collective-permute-start(bf16[128,256]{1,0:T(8,128)(2,1)S(1)} %select_bitcast_fusion.23), channel_id=1, source_target_pairs={{0,4},{1,5},{2,6},{3,7},{4,0},{5,1},{6,2},{7,3},{8,12},{9,13},{10,... | collective-permute-start | bytes 196616 | tf_op jit(solution)/shard_map/ppermute | solution.py:713
  42.7 6.2 %collective-permute-start.17 = (bf16[128,256]{1,0:T(8,128)(2,1)S(1)}, bf16[128,256]{1,0:T(8,128)(2,1)S(1)}, u32[]{:S(2)}, u32[]{:S(2)}) collective-permute-start(bf16[128,256]{1,0:T(8,128)(2,1)S(1)} %select_bitcast_fusion.20), channel_id=1, source_target_pairs={{0,1},{1,0},{2,3},{3,2},{4,5},{5,4},{6,7},{7,6},{8,9},{9,8},{10,11... | collective-permute-start | bytes 196616 | tf_op jit(solution)/shard_map/ppermute | solution.py:713
  44.8 5.0 %collective-permute-start.25 = (bf16[136,256]{1,0:T(8,128)(2,1)S(1)}, bf16[136,256]{1,0:T(8,128)(2,1)S(1)}, u32[]{:S(2)}, u32[]{:S(2)}) collective-permute-start(bf16[136,256]{1,0:T(8,128)(2,1)S(1)} %select_bitcast_fusion.17), channel_id=1, source_target_pairs={{0,2},{1,3},{2,0},{3,1},{4,6},{5,7},{6,4},{7,5},{8,10},{9,11},{10,... | collective-permute-start | bytes 208904 | tf_op jit(solution)/shard_map/ppermute | solution.py:713
  46.2 7.5 %collective-permute-start.10 = (bf16[128,256]{1,0:T(8,128)(2,1)S(1)}, bf16[128,256]{1,0:T(8,128)(2,1)S(1)}, u32[]{:S(2)}, u32[]{:S(2)}) collective-permute-start(bf16[128,256]{1,0:T(8,128)(2,1)S(1)} %fusion.8), channel_id=1, source_target_pairs={{0,8},{1,9},{2,10},{3,11},{4,12},{5,13},{6,14},{7,15},{8,0},{9,1},... | collective-permute-start | bytes 196616 | tf_op jit(solution)/shard_map/ppermute | solution.py:713
  48.9 6.3 %collective-permute-start.18 = (bf16[128,256]{1,0:T(8,128)(2,1)S(1)}, bf16[128,256]{1,0:T(8,128)(2,1)S(1)}, u32[]{:S(2)}, u32[]{:S(2)}) collective-permute-start(bf16[128,256]{1,0:T(8,128)(2,1)S(1)} %fusion.7), channel_id=1, source_target_pairs={{0,8},{1,9},{2,10},{3,11},{4,12},{5,13},{6,14},{7,15},{8,0},{9,1},... | collective-permute-start | bytes 196616 | tf_op jit(solution)/shard_map/ppermute | solution.py:713
  49.9 6.8 %collective-permute-start.26 = (bf16[136,256]{1,0:T(8,128)(2,1)S(1)}, bf16[136,256]{1,0:T(8,128)(2,1)S(1)}, u32[]{:S(2)}, u32[]{:S(2)}) collective-permute-start(bf16[136,256]{1,0:T(8,128)(2,1)S(1)} %fusion.6), channel_id=1, source_target_pairs={{0,8},{1,9},{2,10},{3,11},{4,12},{5,13},{6,14},{7,15},{8,0},{9,1},... | collective-permute-start | bytes 208904 | tf_op jit(solution)/shard_map/ppermute | solution.py:713
  53.8 4.4 %collective-permute-start.11 = (bf16[128,256]{1,0:T(8,128)(2,1)S(1)}, bf16[128,256]{1,0:T(8,128)(2,1)S(1)}, u32[]{:S(2)}, u32[]{:S(2)}) collective-permute-start(bf16[128,256]{1,0:T(8,128)(2,1)S(1)} %add_convert_fusion.5), channel_id=1, source_target_pairs={{0,4},{1,5},{2,6},{3,7},{4,0},{5,1},{6,2},{7,3},{8,12},{9,13},{10,... | collective-permute-start | bytes 196616 | tf_op jit(solution)/shard_map/ppermute | solution.py:713
  55.2 4.3 %collective-permute-start.19 = (bf16[128,256]{1,0:T(8,128)(2,1)S(1)}, bf16[128,256]{1,0:T(8,128)(2,1)S(1)}, u32[]{:S(2)}, u32[]{:S(2)}) collective-permute-start(bf16[128,256]{1,0:T(8,128)(2,1)S(1)} %add_convert_fusion.4), channel_id=1, source_target_pairs={{0,1},{1,0},{2,3},{3,2},{4,5},{5,4},{6,7},{7,6},{8,9},{9,8},{10,11... | collective-permute-start | bytes 196616 | tf_op jit(solution)/shard_map/ppermute | solution.py:713
  56.7 4.4 %collective-permute-start.27 = (bf16[136,256]{1,0:T(8,128)(2,1)S(1)}, bf16[136,256]{1,0:T(8,128)(2,1)S(1)}, u32[]{:S(2)}, u32[]{:S(2)}) collective-permute-start(bf16[136,256]{1,0:T(8,128)(2,1)S(1)} %add_convert_fusion.3), channel_id=1, source_target_pairs={{0,2},{1,3},{2,0},{3,1},{4,6},{5,7},{6,4},{7,5},{8,10},{9,11},{10,... | collective-permute-start | bytes 208904 | tf_op jit(solution)/shard_map/ppermute | solution.py:713
  58.2 5.8 %collective-permute-start.12 = (bf16[2,128,256]{2,1,0:T(8,128)(2,1)S(1)}, bf16[2,128,256]{2,1,0:T(8,128)(2,1)S(1)}, u32[]{:S(2)}, u32[]{:S(2)}) collective-permute-start(bf16[2,128,256]{2,1,0:T(8,128)(2,1)S(1)} %pad_maximum_fusion.7), channel_id=1, source_target_pairs={{0,2},{1,3},{2,0},{3,1},{4,6},{5,7},{6,4},{7,5},{8,10},{9,11},{10,... | collective-permute-start | bytes 393224 | tf_op jit(solution)/shard_map/ppermute | solution.py:713
  59.6 5.7 %collective-permute-start.20 = (bf16[2,128,256]{2,1,0:T(8,128)(2,1)S(1)}, bf16[2,128,256]{2,1,0:T(8,128)(2,1)S(1)}, u32[]{:S(2)}, u32[]{:S(2)}) collective-permute-start(bf16[2,128,256]{2,1,0:T(8,128)(2,1)S(1)} %pad_maximum_fusion.8), channel_id=1, source_target_pairs={{0,4},{1,5},{2,6},{3,7},{4,0},{5,1},{6,2},{7,3},{8,12},{9,13},{10,... | collective-permute-start | bytes 393224 | tf_op jit(solution)/shard_map/ppermute | solution.py:713
  61.1 5.1 %collective-permute-start.28 = (bf16[2,136,256]{2,1,0:T(8,128)(2,1)S(1)}, bf16[2,136,256]{2,1,0:T(8,128)(2,1)S(1)}, u32[]{:S(2)}, u32[]{:S(2)}) collective-permute-start(bf16[2,136,256]{2,1,0:T(8,128)(2,1)S(1)} %pad_maximum_fusion.6), channel_id=1, source_target_pairs={{0,1},{1,0},{2,3},{3,2},{4,5},{5,4},{6,7},{7,6},{8,9},{9,8},{10,11... | collective-permute-start | bytes 417800 | tf_op jit(solution)/shard_map/ppermute | solution.py:713
  64.1 6.4 %collective-permute-start.13 = (bf16[2,2,128,256]{3,2,1,0:T(8,128)(2,1)S(1)}, bf16[2,2,128,256]{3,2,1,0:T(8,128)(2,1)S(1)}, u32[]{:S(2)}, u32[]{:S(2)}) collective-permute-start(bf16[2,2,128,256]{3,2,1,0:T(8,128)(2,1)S(1)} %pad_maximum_fusion.4), channel_id=1, source_target_pairs={{0,1},{1,0},{2,3},{3,2},{4,5},{5,4},{6,7},{7,6},{8,9},{9,8},{10,11... | collective-permute-start | bytes 786440 | tf_op jit(solution)/shard_map/ppermute | solution.py:713
  65.4 9.2 %copy-start.11 = (f32[1,256,256]{2,1,0:T(8,128)S(1)}, f32[1,256,256]{2,1,0:T(8,128)}, u32[]{:S(2)}) copy-start(f32[1,256,256]{2,1,0:T(8,128)} %param.41) | copy-start | bytes 786436
  65.4 9.2 %copy-start.15 = (f32[1,9,256]{2,0,1:T(1,128)S(1)}, f32[1,9,256]{2,0,1:T(1,128)}, u32[]{:S(2)}) copy-start(f32[1,9,256]{2,0,1:T(1,128)} %param.27) | copy-start | bytes 27652
  65.4 9.2 %copy-start.16 = (f32[1,3328]{1,0:T(1,128)S(1)}, f32[1,3328]{1,0:T(1,128)}, u32[]{:S(2)}) copy-start(f32[1,3328]{1,0:T(1,128)} %refs_15_.1) | copy-start | bytes 39940
  65.4 9.2 %copy-start.17 = (f32[1,3328]{1,0:T(1,128)S(1)}, f32[1,3328]{1,0:T(1,128)}, u32[]{:S(2)}) copy-start(f32[1,3328]{1,0:T(1,128)} %refs_21_.1) | copy-start | bytes 39940
  65.4 9.2 %copy-start.18 = (f32[1,9,256]{2,0,1:T(1,128)S(1)}, f32[1,9,256]{2,0,1:T(1,128)}, u32[]{:S(2)}) copy-start(f32[1,9,256]{2,0,1:T(1,128)} %param.33) | copy-start | bytes 27652
  65.4 9.2 %copy-start.19 = (f32[1,9,256]{2,0,1:T(1,128)S(1)}, f32[1,9,256]{2,0,1:T(1,128)}, u32[]{:S(2)}) copy-start(f32[1,9,256]{2,0,1:T(1,128)} %param.39) | copy-start | bytes 27652
  65.5 6.4 %collective-permute-start.21 = (bf16[2,2,128,256]{3,2,1,0:T(8,128)(2,1)S(1)}, bf16[2,2,128,256]{3,2,1,0:T(8,128)(2,1)S(1)}, u32[]{:S(2)}, u32[]{:S(2)}) collective-permute-start(bf16[2,2,128,256]{3,2,1,0:T(8,128)(2,1)S(1)} %pad_maximum_fusion.5), channel_id=1, source_target_pairs={{0,2},{1,3},{2,0},{3,1},{4,6},{5,7},{6,4},{7,5},{8,10},{9,11},{10,... | collective-permute-start | bytes 786440 | tf_op jit(solution)/shard_map/ppermute | solution.py:713
  66.2 8.4 %copy-start.9 = (f32[1,256,768]{2,1,0:T(8,128)S(1)}, f32[1,256,768]{2,1,0:T(8,128)}, u32[]{:S(2)}) copy-start(f32[1,256,768]{2,1,0:T(8,128)} %param.40) | copy-start | bytes 2359300
  66.3 8.3 %copy-start.8 = (f32[1,256,768]{2,1,0:T(8,128)S(1)}, f32[1,256,768]{2,1,0:T(8,128)}, u32[]{:S(2)}) copy-start(f32[1,256,768]{2,1,0:T(8,128)} %param.34) | copy-start | bytes 2359300
  66.3 6.6 %collective-permute-start.29 = (bf16[2,2,136,256]{3,2,1,0:T(8,128)(2,1)S(1)}, bf16[2,2,136,256]{3,2,1,0:T(8,128)(2,1)S(1)}, u32[]{:S(2)}, u32[]{:S(2)}) collective-permute-start(bf16[2,2,136,256]{3,2,1,0:T(8,128)(2,1)S(1)} %pad_maximum_fusion.3), channel_id=1, source_target_pairs={{0,4},{1,5},{2,6},{3,7},{4,0},{5,1},{6,2},{7,3},{8,12},{9,13},{10,... | collective-permute-start | bytes 835592 | tf_op jit(solution)/shard_map/ppermute | solution.py:713
  70.5 4.1 %copy-start.6 = (f32[1,1024,256]{2,1,0:T(8,128)S(1)}, f32[1,1024,256]{2,1,0:T(8,128)}, u32[]{:S(2)}) copy-start(f32[1,1024,256]{2,1,0:T(8,128)} %param.43) | copy-start | bytes 3145732
  71.9 2.7 %copy-start.5 = (f32[1,256,1024]{2,1,0:T(8,128)S(1)}, f32[1,256,1024]{2,1,0:T(8,128)}, u32[]{:S(2)}) copy-start(f32[1,256,1024]{2,1,0:T(8,128)} %param.42) | copy-start | bytes 3145732
  71.9 2.7 %copy-start.4 = (f32[1,1024,256]{2,1,0:T(8,128)S(1)}, f32[1,1024,256]{2,1,0:T(8,128)}, u32[]{:S(2)}) copy-start(f32[1,1024,256]{2,1,0:T(8,128)} %param.37) | copy-start | bytes 3145732
  72.0 2.6 %copy-start.3 = (f32[1,256,1024]{2,1,0:T(8,128)S(1)}, f32[1,256,1024]{2,1,0:T(8,128)}, u32[]{:S(2)}) copy-start(f32[1,256,1024]{2,1,0:T(8,128)} %param.36) | copy-start | bytes 3145732
  72.9 1.7 %copy-start.2 = (f32[1,256,768]{2,1,0:T(8,128)S(1)}, f32[1,256,768]{2,1,0:T(8,128)}, u32[]{:S(2)}) copy-start(f32[1,256,768]{2,1,0:T(8,128)} %param.28) | copy-start | bytes 2359300
  73.0 1.7 %copy-start.1 = (f32[1,1024,256]{2,1,0:T(8,128)S(1)}, f32[1,1024,256]{2,1,0:T(8,128)}, u32[]{:S(2)}) copy-start(f32[1,1024,256]{2,1,0:T(8,128)} %param.31) | copy-start | bytes 3145732
  73.1 1.8 %copy-start = (f32[1,256,1024]{2,1,0:T(8,128)S(1)}, f32[1,256,1024]{2,1,0:T(8,128)}, u32[]{:S(2)}) copy-start(f32[1,256,1024]{2,1,0:T(8,128)} %param.30) | copy-start | bytes 3145732
  73.1 1.8 %copy-start.7 = (f32[1,256,256]{2,1,0:T(8,128)S(1)}, f32[1,256,256]{2,1,0:T(8,128)}, u32[]{:S(2)}) copy-start(f32[1,256,256]{2,1,0:T(8,128)} %param.29) | copy-start | bytes 786436
  73.1 1.9 %copy-start.10 = (f32[1,256,256]{2,1,0:T(8,128)S(1)}, f32[1,256,256]{2,1,0:T(8,128)}, u32[]{:S(2)}) copy-start(f32[1,256,256]{2,1,0:T(8,128)} %param.35) | copy-start | bytes 786436
  73.1 1.9 %copy-start.13 = (f32[1,3328]{1,0:T(1,128)S(1)}, f32[1,3328]{1,0:T(1,128)}, u32[]{:S(2)}) copy-start(f32[1,3328]{1,0:T(1,128)} %refs_9_.1) | copy-start | bytes 39940
  73.4 1.2 %collective-permute-start.30 = (f32[8,128]{1,0:T(8,128)S(1)}, f32[8,128]{1,0:T(8,128)S(1)}, u32[]{:S(2)}, u32[]{:S(2)}) collective-permute-start(f32[8,128]{1,0:T(8,128)S(1)} %squares.1.refs_4_), channel_id=1, source_target_pairs={{0,16},{16,0},{1,17},{17,1},{2,18},{18,2},{3,19},{19,3},{4,20},{20... | collective-permute-start | bytes 12296 | tf_op jit(solution)/shard_map/ppermute | solution.py:701

commit v5 on v4

--- a/solution.py
+++ b/solution.py
@@ -171,7 +171,7 @@
         hat1[rows, :] = hat
         scale1[rows, :] = jnp.broadcast_to(scale, (size, HALF))
         normed[0, rows, :] = y.astype(BF16)
-    need("place", "wide")
+    need("rest")
     normed[1] = dot(turned[...], normed[0]).astype(BF16)
     biases = (vec_at(vec, 4), None, vec_at(vec, 5))
     for half in range(2):
@@ -182,7 +182,6 @@
                 got = got + biases[part][:, lanes]
             qkv[part, 0:MB_TOK, lanes] = got.astype(BF16)
     masks = head_masks()
-    need("stripe")
     taps9 = turned_taps(taps_ref[...])
     bias = vec_at(vec, 7)
     units = [(group, half) for group in range(NGROUP) for half in range(2)]
@@ -220,7 +219,6 @@
     mixed[:, :HALF] = mixed_att[0]
     mixed[:, HALF:] = dot(turned[...], mixed_att[1]).astype(BF16)
     middle[...] = dot(mixed[...], wp[...])
-    need("deep")
     sides = ((slice(0, 160), ROWS[:2]), (slice(160, MB_TOK), ROWS[2:]))
     for side, chunks in sides:
         for start, size in chunks:
@@ -437,7 +435,7 @@
 
     x_in, c_in, vec_own, vec_other, ker_own, ker_other, wide_own, wide_other, deep_own, deep_other = take(10)
     table_in = take(4)
-    sent = [take(2) for _ in RESULTS]
+    rows_out, (rows_sent,), sent = take(2), take(1), [take(2) for _ in PARTS]
     held = take(len(INPUTS))
     results = take(len(RESULTS))
     kept = (take(len(SAVED)), take(len(SAVED)))
@@ -452,17 +450,17 @@
         ("x", x_in.at[pl.ds(at, MB_TOK)], x),
         ("vec", vec_own, vecs.at[sec]),
         ("vec", vec_other, vecs.at[1 - sec]),
-        ("place", table_in[0], tables[0]),
-        ("wide", wide_own, wide.at[sec]),
-        ("wide", wide_other, wide.at[1 - sec]),
-        ("stripe", table_in[1], tables[1]),
-        ("stripe", table_in[2], tables[2]),
-        ("stripe", table_in[3], tables[3]),
-        ("stripe", ker_own, taps.at[sec]),
-        ("stripe", ker_other, taps.at[1 - sec]),
-        ("deep", deep_own, deep.at[sec]),
-        ("deep", deep_other, deep.at[1 - sec]),
-        ("c", c_in.at[pl.ds(at, MB_TOK)], c),
+        ("rest", table_in[0], tables[0]),
+        ("rest", wide_own, wide.at[sec]),
+        ("rest", wide_other, wide.at[1 - sec]),
+        ("rest", table_in[1], tables[1]),
+        ("rest", table_in[2], tables[2]),
+        ("rest", table_in[3], tables[3]),
+        ("rest", ker_own, taps.at[sec]),
+        ("rest", ker_other, taps.at[1 - sec]),
+        ("rest", deep_own, deep.at[sec]),
+        ("rest", deep_other, deep.at[1 - sec]),
+        ("rest", c_in.at[pl.ds(at, MB_TOK)], c),
     ]
     pending = {}
     for index, (name, source, target) in enumerate(moves):
@@ -478,8 +476,9 @@
     leaving = []
 
     def leave(index):
+        targets = (rows_out[index].at[pl.ds(at, MB_TOK)], rows_sent.at[index]) if index < 2 else sent[index - 2]
         for which, slot in enumerate((sec, 1 - sec)):
-            copy = pltpu.make_async_copy(results[index].at[slot], sent[index][which], out_sems.at[2 * index + which])
+            copy = pltpu.make_async_copy(results[index].at[slot], targets[which], out_sems.at[2 * index + which])
             copy.start()
             leaving.append(copy)
 
@@ -510,12 +509,10 @@
     forward(0, x)
     feed[...] = outs[0].astype(BF16)
     forward(1, feed)
-    leave(0)
-    need("c")
     backward(1, c)
     feed[...] = grads[1].astype(BF16)
     backward(0, feed)
-    for index in range(1, len(RESULTS)):
+    for index in range(len(RESULTS)):
         leave(index)
     for copy in leaving:
         copy.wait()
@@ -532,12 +529,13 @@
     spaces = [pltpu.HBM] * 3 + [pltpu.VMEM, pltpu.HBM] + [pltpu.VMEM] * 5 + [pltpu.HBM] * 4
     smem = pl.BlockSpec(memory_space=pltpu.SMEM)
     scratch = INPUTS + RESULTS + SAVED + SAVED + FORWARD_WORK + BACKWARD_WORK + OTHER_WORK
-    out_shape = [pltpu.VMEM(shape[1:], kind) for shape, kind in RESULTS for _ in range(2)]
+    out_shape = [pltpu.HBM((2 * MB_TOK, D), F32)] * 2 + [pltpu.VMEM((2, MB_TOK, D), F32)]
+    out_shape += [pltpu.VMEM((rows, D), BF16) for rows in PARTS for _ in range(2)]
     return pl.pallas_call(
         section_step,
         out_shape=out_shape,
         in_specs=[smem] + [pl.BlockSpec(memory_space=space) for space in spaces],
-        out_specs=[pl.BlockSpec(memory_space=pl.ANY)] * len(out_shape),
+        out_specs=[pl.BlockSpec(memory_space=pltpu.HBM)] * 2 + [pl.BlockSpec(memory_space=pl.ANY)] * 7,
         scratch_shapes=[pltpu.VMEM(shape, kind) for shape, kind in scratch]
         + [pltpu.SemaphoreType.DMA((14,)), pltpu.SemaphoreType.DMA((2 * len(RESULTS),))],
         compiler_params=pltpu.CompilerParams(vmem_limit_bytes=34 << 20),
@@ -610,20 +608,9 @@
 
 
 SHAPES = ((1, VEC), (1, 9 * D), (D, 3 * D), (D, D), (D, FF), (FF, D))
-PIECES = (
-    (3, 0, 128),
-    (3, 128, 128),
-    (2, 0, 128),
-    (2, 128, 128),
-    (4, 0, 128),
-    (4, 128, 128),
-    (5, 0, 256),
-    (5, 256, 256),
-    (5, 512, 256),
-    (5, 768, 256),
-)
+PIECES = ((3, 0, D), (2, 0, D), (4, 0, D), (5, 0, FF))
 OUT_SHAPES = [(shape, F32) for shape in SHAPES] * 4 + [(shape, BF16) for shape in SHAPES[2:]]
-MOVES = 4 + 4 * 2 + 5 * len(PIECES)
+MOVES = 2 + 4 * 2 + 5 * len(PIECES)
 
 
 def optimizer_step(sec_ref, *refs):
@@ -632,7 +619,7 @@
         taken, refs = refs[:count], refs[count:]
         return taken
 
-    rows_in, (own, other), (a, b, c), states = take(4), take(2), take(3), take(18)
+    (_, _, came), (own, other), (a, b, c), states = take(3), take(2), take(3), take(18)
     outs, (norm_ref,), rows_out, made, (sems,) = take(28), take(1), take(2), take(28), take(1)
     sec = sec_ref[0]
     moves = []
@@ -642,9 +629,9 @@
         move.start()
         moves.append(move)
 
-    for index in range(4):
-        first = pl.multiple_of((sec if index % 2 == 0 else 1 - sec) * MB_TOK, 8)
-        leave(rows_in[index], rows_out[index // 2].at[pl.ds(first, MB_TOK)])
+    first = pl.multiple_of((1 - sec) * MB_TOK, 8)
+    for index in range(2):
+        leave(came.at[index], rows_out[index].at[pl.ds(first, MB_TOK)])
     norm = jnp.sqrt(own[0:1, 0:1] + other[0:1, 0:1])
     factor = jnp.minimum(1.0, CLIP_LIMIT / (norm + 1e-06))
     norm_ref[...] = norm
@@ -681,7 +668,7 @@
         move.wait()
 
 
-def run_optimizer(sec, rows_in, own, other, a, b, c, states):
+def run_optimizer(sec, rows, came, own, other, a, b, c, states):
     vmem = pl.BlockSpec(memory_space=pltpu.VMEM)
     hbm = pl.BlockSpec(memory_space=pltpu.HBM)
     return pl.pallas_call(
@@ -689,12 +676,13 @@
         out_shape=[pltpu.HBM(shape, kind) for shape, kind in OUT_SHAPES]
         + [jax.ShapeDtypeStruct((1, 1), F32)]
         + [pltpu.HBM((2 * MB_TOK, D), F32)] * 2,
-        in_specs=[pl.BlockSpec(memory_space=pltpu.SMEM)] + [vmem] * (4 + 2 + 3 + 18),
+        in_specs=[pl.BlockSpec(memory_space=pltpu.SMEM)] + [hbm] * 2 + [vmem] * (1 + 2 + 3 + 18),
         out_specs=[hbm] * 28 + [vmem] + [hbm] * 2,
         scratch_shapes=[pltpu.VMEM(shape, kind) for shape, kind in OUT_SHAPES] + [pltpu.SemaphoreType.DMA((MOVES,))],
         compiler_params=pltpu.CompilerParams(vmem_limit_bytes=20 << 20),
+        input_output_aliases={1: 29, 2: 30},
         name="optimizer",
-    )(sec, *kept_in((*rows_in, own, other, a, b, c, *states), [pltpu.VMEM] * 27))
+    )(sec, *kept_in((*rows, came, own, other, a, b, c, *states), [pltpu.HBM] * 2 + [pltpu.VMEM] * 24))
 
 
 def swapped(value):
@@ -769,12 +757,11 @@
     )
     totals = [
         (own.astype(F32) + swapped(other).astype(F32)).astype(BF16)
-        for own, other in zip(results[4::2], results[5::2])
+        for own, other in zip(results[3::2], results[4::2])
     ]
     a, b, c = summed_over_dp(totals, clear)
     squares = run_square_sum(a, b, c)
-    rows_in = (results[0], swapped(results[1]), results[2], swapped(results[3]))
-    new = run_optimizer(section, rows_in, squares, swapped(squares), a, b, c, states)
+    new = run_optimizer(section, results[:2], swapped(results[2]), squares, swapped(squares), a, b, c, states)
 
     def whole(arrays):
         return [

time: 81.7 us -> 80.6 us (0.987)
  Pallas kernels: 25.9 us -> 24.5 us
  waiting for transfers between devices: 19.4 us -> 20.3 us
    pallas_call x1, Pallas kernels: 17.2 us -> 16.3 us  [run_blocks(): pl.pallas_call(section_step, out_shape=out_shape, in_specs=[smem] + [pl.B...]
    ppermute x10 -> x9, waiting for transfers between devices: 4.14 us -> 4.53 us  [swapped(): return lax.ppermute(value, 'section', [(0, 1), (1, 0)])]
    ppermute x10 -> x9, starting transfers between devices: 2.57 us -> 2.19 us  [swapped(): return lax.ppermute(value, 'section', [(0, 1), (1, 0)])]
  transfers between devices with their start and end apart: 31 -> 30, of which waited for: 17 -> 16; matrix products, arithmetic and copies ran while one was open for 2% -> 2% of each run, Pallas kernels for 0% -> 0%
where the time goes in v5:
time: 80.6 us; the launch traced here: 80.4 us
  starting transfers between devices  32.3 us (40%)
  Pallas kernels  24.5 us (30%)
  waiting for transfers between devices  20.3 us (25%)
  other arithmetic  1.63 us (2%)
  between operations  1.36 us (2%)
    ppermute x21, starting transfers between devices, exchanged(): lax.ppermute(value, 'dp', [(index, index ^ 1 << bit) for index in range(s...  30.1 us
    pallas_call x1, Pallas kernels, run_blocks(): pl.pallas_call(section_step, out_shape=out_shape, in_specs=[smem] + [pl.B...  16.3 us
    ppermute x21, waiting for transfers between devices, exchanged(): lax.ppermute(value, 'dp', [(index, index ^ 1 << bit) for index in range(s...  15.7 us
    pallas_call x1, Pallas kernels, run_optimizer(): pl.pallas_call(optimizer_step, out_shape=[pltpu.HBM(shape, kind) for shap...  6.01 us
    ppermute x9, waiting for transfers between devices, swapped(): return lax.ppermute(value, 'section', [(0, 1), (1, 0)])  4.53 us
    ppermute x9, starting transfers between devices, swapped(): return lax.ppermute(value, 'section', [(0, 1), (1, 0)])  2.19 us
    pallas_call x1, Pallas kernels, run_narrowed(): pl.pallas_call(narrowed, out_shape=[pltpu.VMEM((D, 8 * D), BF16), pltpu.V...  1.95 us
  transfers between devices with their start and end apart: 30, of which 16 were waited for; matrix products, arithmetic and copies ran while one was open for 2% of the time, Pallas kernels for 0%

profile of v5, /device:TPU:0, one launch (start us, length us, event | category | flops | bytes accessed | tf_op | source)
XLA Modules:
  0.0 80.4 jit_solution(13053639322536240503)
XLA Ops:
  0.7 2.0 %narrowed.1 = (bf16[256,2048]{1,0:T(8,128)(2,1)S(1)}, bf16[1024,256]{1,0:T(8,128)(2,1)S(1)}) custom-call(f32[256,768]{1,0:T(8,128)} %bitcast.131, f32[256,256]{1,0:T(8,128)} %bitcast.137, f32[256,1024]{1,0:T(8,128)} %bitcast.127, f32[1024,256]{1,0:T(8,128)} %bitcast.129), custom_call_target="tpu_custom_call" | custom-call | tf_op jit(solution)/shard_map/narrowed/pallas_call | solution.py:564
  2.7 0.5 collective-permute-start.2
  3.2 0.1 collective-permute-start.3
  3.3 0.4 collective-permute-start
  3.7 0.1 collective-permute-start.1
  3.8 2.5 %collective-permute-done.1.refs_5_ = f32[1,2304]{1,0:T(1,128)S(1)} collective-permute-done((f32[1,2304]{1,0:T(1,128)S(1)}, f32[1,2304]{1,0:T(1,128)S(1)}, u32[]{:S(2)}, u32[]{:S(2)}) %collective-permute-start.1) | collective-permute-done | bytes 9248 | tf_op jit(solution)/shard_map/ppermute | solution.py:689
  6.3 16.3 %blocks.1 = (f32[608,256]{1,0:T(8,128)}, f32[608,256]{1,0:T(8,128)}, f32[2,304,256]{2,1,0:T(8,128)S(1)}, bf16[1024,256]{1,0:T(8,128)(2,1)S(1)}, bf16[1024,256]{1...) custom-call(s32[1]{0:T(128)} %bitcast.sec_ref, ...), custom_call_target="tpu_custom_call" | custom-call | tf_op jit(solution)/shard_map/blocks/pallas_call | solution.py:534
  22.5 0.4 collective-permute-start.5
  23.0 0.1 collective-permute-start.13
  23.1 0.4 collective-permute-start.21
  23.5 0.1 collective-permute-start.4
  23.6 0.9 %collective-permute-done.5 = bf16[1024,256]{1,0:T(8,128)(2,1)S(1)} collective-permute-done((bf16[1024,256]{1,0:T(8,128)(2,1)S(1)}, bf16[1024,256]{1,0:T(8,128)(2,1)S(1)}, u32[]{:S(2)}, u32[]{:S(2)}) %collective-permute-start.5) | collective-permute-done | bytes 524320 | tf_op jit(solution)/shard_map/ppermute | solution.py:689
  24.5 0.1 add_convert_fusion.2
  24.7 2.9 %collective-permute-start.6 = (bf16[2,2,128,256]{3,2,1,0:T(8,128)(2,1)S(1)}, bf16[2,2,128,256]{3,2,1,0:T(8,128)(2,1)S(1)}, u32[]{:S(2)}, u32[]{:S(2)}) collective-permute-start(bf16[2,2,128,256]{3,2,1,0:T(8,128)(2,1)S(1)} %bitcast.154), channel_id=1, source_target_pairs={{0,1},{1,0},{2,3},{3,2},{4,5},{5,4},{6,7},{7,6},{8,9},{9,8},{10,11... | collective-permute-start | bytes 786440 | tf_op jit(solution)/shard_map/ppermute | solution.py:701
  27.6 0.1 add_convert_fusion.1
  27.8 1.6 %collective-permute-start.14 = (bf16[2,2,128,256]{3,2,1,0:T(8,128)(2,1)S(1)}, bf16[2,2,128,256]{3,2,1,0:T(8,128)(2,1)S(1)}, u32[]{:S(2)}, u32[]{:S(2)}) collective-permute-start(bf16[2,2,128,256]{3,2,1,0:T(8,128)(2,1)S(1)} %bitcast.155), channel_id=1, source_target_pairs={{0,2},{1,3},{2,0},{3,1},{4,6},{5,7},{6,4},{7,5},{8,10},{9,11},{10,... | collective-permute-start | bytes 786440 | tf_op jit(solution)/shard_map/ppermute | solution.py:701
  29.4 0.1 add_convert_fusion
  29.6 1.6 %collective-permute-start.22 = (bf16[2,2,136,256]{3,2,1,0:T(8,128)(2,1)S(1)}, bf16[2,2,136,256]{3,2,1,0:T(8,128)(2,1)S(1)}, u32[]{:S(2)}, u32[]{:S(2)}) collective-permute-start(bf16[2,2,136,256]{3,2,1,0:T(8,128)(2,1)S(1)} %bitcast.153), channel_id=1, source_target_pairs={{0,4},{1,5},{2,6},{3,7},{4,0},{5,1},{6,2},{7,3},{8,12},{9,13},{10,... | collective-permute-start | bytes 835592 | tf_op jit(solution)/shard_map/ppermute | solution.py:701
  31.2 3.0 %collective-permute-done.6 = bf16[2,2,128,256]{3,2,1,0:T(8,128)(2,1)S(1)} collective-permute-done((bf16[2,2,128,256]{3,2,1,0:T(8,128)(2,1)S(1)}, bf16[2,2,128,256]{3,2,1,0:T(8,128)(2,1)S(1)}, u32[]{:S(2)}, u32[]{:S(2)}) %collective-permute-start.6) | collective-permute-done | bytes 262176 | tf_op jit(solution)/shard_map/ppermute | solution.py:701
  34.2 0.1 fusion.2
  34.3 1.8 %collective-permute-start.7 = (bf16[2,128,256]{2,1,0:T(8,128)(2,1)S(1)}, bf16[2,128,256]{2,1,0:T(8,128)(2,1)S(1)}, u32[]{:S(2)}, u32[]{:S(2)}) collective-permute-start(bf16[2,128,256]{2,1,0:T(8,128)(2,1)S(1)} %select_bitcast_fusion.14), channel_id=1, source_target_pairs={{0,2},{1,3},{2,0},{3,1},{4,6},{5,7},{6,4},{7,5},{8,10},{9,11},{10,... | collective-permute-start | bytes 393224 | tf_op jit(solution)/shard_map/ppermute | solution.py:701
  36.2 0.1 fusion.1
  36.3 1.6 %collective-permute-start.15 = (bf16[2,128,256]{2,1,0:T(8,128)(2,1)S(1)}, bf16[2,128,256]{2,1,0:T(8,128)(2,1)S(1)}, u32[]{:S(2)}, u32[]{:S(2)}) collective-permute-start(bf16[2,128,256]{2,1,0:T(8,128)(2,1)S(1)} %select_bitcast_fusion.11), channel_id=1, source_target_pairs={{0,4},{1,5},{2,6},{3,7},{4,0},{5,1},{6,2},{7,3},{8,12},{9,13},{10,... | collective-permute-start | bytes 393224 | tf_op jit(solution)/shard_map/ppermute | solution.py:701
  37.9 0.1 fusion
  38.0 1.6 %collective-permute-start.23 = (bf16[2,136,256]{2,1,0:T(8,128)(2,1)S(1)}, bf16[2,136,256]{2,1,0:T(8,128)(2,1)S(1)}, u32[]{:S(2)}, u32[]{:S(2)}) collective-permute-start(bf16[2,136,256]{2,1,0:T(8,128)(2,1)S(1)} %select_bitcast_fusion.8), channel_id=1, source_target_pairs={{0,1},{1,0},{2,3},{3,2},{4,5},{5,4},{6,7},{7,6},{8,9},{9,8},{10,11... | collective-permute-start | bytes 417800 | tf_op jit(solution)/shard_map/ppermute | solution.py:701
  39.6 0.1 fusion.5
  39.6 1.7 %collective-permute-start.8 = (bf16[128,256]{1,0:T(8,128)(2,1)S(1)}, bf16[128,256]{1,0:T(8,128)(2,1)S(1)}, u32[]{:S(2)}, u32[]{:S(2)}) collective-permute-start(bf16[128,256]{1,0:T(8,128)(2,1)S(1)} %select_bitcast_fusion.23), channel_id=1, source_target_pairs={{0,4},{1,5},{2,6},{3,7},{4,0},{5,1},{6,2},{7,3},{8,12},{9,13},{10,... | collective-permute-start | bytes 196616 | tf_op jit(solution)/shard_map/ppermute | solution.py:701
  41.3 0.4 collective-permute-done.15
  41.7 0.1 fusion.4
  41.8 1.9 %collective-permute-start.16 = (bf16[128,256]{1,0:T(8,128)(2,1)S(1)}, bf16[128,256]{1,0:T(8,128)(2,1)S(1)}, u32[]{:S(2)}, u32[]{:S(2)}) collective-permute-start(bf16[128,256]{1,0:T(8,128)(2,1)S(1)} %select_bitcast_fusion.20), channel_id=1, source_target_pairs={{0,1},{1,0},{2,3},{3,2},{4,5},{5,4},{6,7},{7,6},{8,9},{9,8},{10,11... | collective-permute-start | bytes 196616 | tf_op jit(solution)/shard_map/ppermute | solution.py:701
  43.6 0.2 collective-permute-done.23
  43.8 0.1 fusion.3
  43.9 1.4 %collective-permute-start.24 = (bf16[136,256]{1,0:T(8,128)(2,1)S(1)}, bf16[136,256]{1,0:T(8,128)(2,1)S(1)}, u32[]{:S(2)}, u32[]{:S(2)}) collective-permute-start(bf16[136,256]{1,0:T(8,128)(2,1)S(1)} %select_bitcast_fusion.17), channel_id=1, source_target_pairs={{0,2},{1,3},{2,0},{3,1},{4,6},{5,7},{6,4},{7,5},{8,10},{9,11},{10,... | collective-permute-start | bytes 208904 | tf_op jit(solution)/shard_map/ppermute | solution.py:701
  45.3 2.7 %collective-permute-start.9 = (bf16[128,256]{1,0:T(8,128)(2,1)S(1)}, bf16[128,256]{1,0:T(8,128)(2,1)S(1)}, u32[]{:S(2)}, u32[]{:S(2)}) collective-permute-start(bf16[128,256]{1,0:T(8,128)(2,1)S(1)} %fusion.8), channel_id=1, source_target_pairs={{0,8},{1,9},{2,10},{3,11},{4,12},{5,13},{6,14},{7,15},{8,0},{9,1},... | collective-permute-start | bytes 196616 | tf_op jit(solution)/shard_map/ppermute | solution.py:701
  48.0 0.9 %collective-permute-start.17 = (bf16[128,256]{1,0:T(8,128)(2,1)S(1)}, bf16[128,256]{1,0:T(8,128)(2,1)S(1)}, u32[]{:S(2)}, u32[]{:S(2)}) collective-permute-start(bf16[128,256]{1,0:T(8,128)(2,1)S(1)} %fusion.7), channel_id=1, source_target_pairs={{0,8},{1,9},{2,10},{3,11},{4,12},{5,13},{6,14},{7,15},{8,0},{9,1},... | collective-permute-start | bytes 196616 | tf_op jit(solution)/shard_map/ppermute | solution.py:701
  49.0 2.1 %collective-permute-start.25 = (bf16[136,256]{1,0:T(8,128)(2,1)S(1)}, bf16[136,256]{1,0:T(8,128)(2,1)S(1)}, u32[]{:S(2)}, u32[]{:S(2)}) collective-permute-start(bf16[136,256]{1,0:T(8,128)(2,1)S(1)} %fusion.6), channel_id=1, source_target_pairs={{0,8},{1,9},{2,10},{3,11},{4,12},{5,13},{6,14},{7,15},{8,0},{9,1},... | collective-permute-start | bytes 208904 | tf_op jit(solution)/shard_map/ppermute | solution.py:701
  51.1 2.3 %collective-permute-done.9 = bf16[128,256]{1,0:T(8,128)(2,1)S(1)} collective-permute-done((bf16[128,256]{1,0:T(8,128)(2,1)S(1)}, bf16[128,256]{1,0:T(8,128)(2,1)S(1)}, u32[]{:S(2)}, u32[]{:S(2)}) %collective-permute-start.9) | collective-permute-done | bytes 65568 | tf_op jit(solution)/shard_map/ppermute | solution.py:701
  53.4 0.1 collective-permute-start.10
  53.5 0.6 collective-permute-done.17
  54.1 1.1 %collective-permute-start.18 = (bf16[128,256]{1,0:T(8,128)(2,1)S(1)}, bf16[128,256]{1,0:T(8,128)(2,1)S(1)}, u32[]{:S(2)}, u32[]{:S(2)}) collective-permute-start(bf16[128,256]{1,0:T(8,128)(2,1)S(1)} %add_convert_fusion.4), channel_id=1, source_target_pairs={{0,1},{1,0},{2,3},{3,2},{4,5},{5,4},{6,7},{7,6},{8,9},{9,8},{10,11... | collective-permute-start | bytes 196616 | tf_op jit(solution)/shard_map/ppermute | solution.py:701
  55.2 0.4 collective-permute-done.25
  55.6 1.6 %collective-permute-start.26 = (bf16[136,256]{1,0:T(8,128)(2,1)S(1)}, bf16[136,256]{1,0:T(8,128)(2,1)S(1)}, u32[]{:S(2)}, u32[]{:S(2)}) collective-permute-start(bf16[136,256]{1,0:T(8,128)(2,1)S(1)} %add_convert_fusion.3), channel_id=1, source_target_pairs={{0,2},{1,3},{2,0},{3,1},{4,6},{5,7},{6,4},{7,5},{8,10},{9,11},{10,... | collective-permute-start | bytes 208904 | tf_op jit(solution)/shard_map/ppermute | solution.py:701
  57.3 0.5 collective-permute-done.10
  57.8 0.6 collective-permute-start.11
  58.4 0.1 collective-permute-done.18
  58.5 1.6 %collective-permute-start.19 = (bf16[2,128,256]{2,1,0:T(8,128)(2,1)S(1)}, bf16[2,128,256]{2,1,0:T(8,128)(2,1)S(1)}, u32[]{:S(2)}, u32[]{:S(2)}) collective-permute-start(bf16[2,128,256]{2,1,0:T(8,128)(2,1)S(1)} %pad_maximum_fusion.8), channel_id=1, source_target_pairs={{0,4},{1,5},{2,6},{3,7},{4,0},{5,1},{6,2},{7,3},{8,12},{9,13},{10,... | collective-permute-start | bytes 393224 | tf_op jit(solution)/shard_map/ppermute | solution.py:701
  60.1 0.6 collective-permute-start.27
  60.7 2.6 %collective-permute-done.11 = bf16[2,128,256]{2,1,0:T(8,128)(2,1)S(1)} collective-permute-done((bf16[2,128,256]{2,1,0:T(8,128)(2,1)S(1)}, bf16[2,128,256]{2,1,0:T(8,128)(2,1)S(1)}, u32[]{:S(2)}, u32[]{:S(2)}) %collective-permute-start.11) | collective-permute-done | bytes 131104 | tf_op jit(solution)/shard_map/ppermute | solution.py:701
  63.4 0.1 collective-permute-start.12
  63.5 0.2 collective-permute-done.19
  63.8 1.8 %collective-permute-start.20 = (bf16[2,2,128,256]{3,2,1,0:T(8,128)(2,1)S(1)}, bf16[2,2,128,256]{3,2,1,0:T(8,128)(2,1)S(1)}, u32[]{:S(2)}, u32[]{:S(2)}) collective-permute-start(bf16[2,2,128,256]{3,2,1,0:T(8,128)(2,1)S(1)} %pad_maximum_fusion.5), channel_id=1, source_target_pairs={{0,2},{1,3},{2,0},{3,1},{4,6},{5,7},{6,4},{7,5},{8,10},{9,11},{10,... | collective-permute-start | bytes 786440 | tf_op jit(solution)/shard_map/ppermute | solution.py:701
  65.7 0.9 %collective-permute-start.28 = (bf16[2,2,136,256]{3,2,1,0:T(8,128)(2,1)S(1)}, bf16[2,2,136,256]{3,2,1,0:T(8,128)(2,1)S(1)}, u32[]{:S(2)}, u32[]{:S(2)}) collective-permute-start(bf16[2,2,136,256]{3,2,1,0:T(8,128)(2,1)S(1)} %pad_maximum_fusion.3), channel_id=1, source_target_pairs={{0,4},{1,5},{2,6},{3,7},{4,0},{5,1},{6,2},{7,3},{8,12},{9,13},{10,... | collective-permute-start | bytes 835592 | tf_op jit(solution)/shard_map/ppermute | solution.py:701
  66.6 3.2 %collective-permute-done.12 = bf16[2,2,128,256]{3,2,1,0:T(8,128)(2,1)S(1)} collective-permute-done((bf16[2,2,128,256]{3,2,1,0:T(8,128)(2,1)S(1)}, bf16[2,2,128,256]{3,2,1,0:T(8,128)(2,1)S(1)}, u32[]{:S(2)}, u32[]{:S(2)}) %collective-permute-start.12) | collective-permute-done | bytes 262176 | tf_op jit(solution)/shard_map/ppermute | solution.py:701
  69.9 0.4 collective-permute-done.20
  70.3 0.1 pad_maximum_fusion.1
  70.4 0.1 pad_maximum_fusion.2
  70.5 1.8 %collective-permute-done.28 = bf16[2,2,136,256]{3,2,1,0:T(8,128)(2,1)S(1)} collective-permute-done((bf16[2,2,136,256]{3,2,1,0:T(8,128)(2,1)S(1)}, bf16[2,2,136,256]{3,2,1,0:T(8,128)(2,1)S(1)}, u32[]{:S(2)}, u32[]{:S(2)}) %collective-permute-start.28) | collective-permute-done | bytes 278560 | tf_op jit(solution)/shard_map/ppermute | solution.py:701
  72.4 0.1 pad_maximum_fusion
  72.5 0.3 squares.1.refs_3_
  72.8 1.1 %collective-permute-done.29.refs_4_ = f32[8,128]{1,0:T(8,128)S(1)} collective-permute-done((f32[8,128]{1,0:T(8,128)S(1)}, f32[8,128]{1,0:T(8,128)S(1)}, u32[]{:S(2)}, u32[]{:S(2)}) %collective-permute-start.29) | collective-permute-done | bytes 4128 | tf_op jit(solution)/shard_map/ppermute | solution.py:689
  74.1 0.1 copy-done
  74.1 0.0 copy-done.7
  74.1 0.1 copy-done.10
  74.2 6.0 %optimizer.1 = (f32[1,3328]{1,0:T(1,128)}, f32[1,2304]{1,0:T(1,128)}, f32[256,768]{1,0:T(8,128)}, f32[256,256]{1,0:T(8,128)}, f32[256,1024]{1,0:T(8,128)}, /*ind...) custom-call(s32[1]{0:T(128)} %bitcast.sec_ref, ...), custom_call_target="tpu_custom_call", output_to_operand_aliasing={{29}: (1, {}), {30}: (2, {})} | custom-call | tf_op jit(solution)/shard_map/optimizer/pallas_call | solution.py:674
  (82 shorter events, 0.9 us)
Async XLA Ops:
  0.7 2.6 %copy-start.12 = (f32[1,3328]{1,0:T(1,128)S(1)}, f32[1,3328]{1,0:T(1,128)}, u32[]{:S(2)}) copy-start(f32[1,3328]{1,0:T(1,128)} %refs_8_.1) | copy-start | bytes 39940
  0.7 3.0 %copy-start.14 = (f32[1,9,256]{2,0,1:T(1,128)S(1)}, f32[1,9,256]{2,0,1:T(1,128)}, u32[]{:S(2)}) copy-start(f32[1,9,256]{2,0,1:T(1,128)} %param.27) | copy-start | bytes 27652
  2.7 3.6 %collective-permute-start.2 = (bf16[256,2048]{1,0:T(8,128)(2,1)S(1)}, bf16[256,2048]{1,0:T(8,128)(2,1)S(1)}, u32[]{:S(2)}, u32[]{:S(2)}) collective-permute-start(bf16[256,2048]{1,0:T(8,128)(2,1)S(1)} %get-tuple-element.78.refs_6_), channel_id=1, source_target_pairs={{0,16},{16,0},{1,17},{17,1},{2,18},{18,2},{3,19},{19,3},{4,20},{20... | collective-permute-start | bytes 3145736 | tf_op jit(solution)/shard_map/ppermute | solution.py:689
  3.2 3.1 %collective-permute-start.3 = (bf16[1024,256]{1,0:T(8,128)(2,1)S(1)}, bf16[1024,256]{1,0:T(8,128)(2,1)S(1)}, u32[]{:S(2)}, u32[]{:S(2)}) collective-permute-start(bf16[1024,256]{1,0:T(8,128)(2,1)S(1)} %get-tuple-element.79.refs_8_), channel_id=1, source_target_pairs={{0,16},{16,0},{1,17},{17,1},{2,18},{18,2},{3,19},{19,3},{4,20},{20... | collective-permute-start | bytes 1572872 | tf_op jit(solution)/shard_map/ppermute | solution.py:689
  3.3 3.0 %collective-permute-start = (f32[1,3328]{1,0:T(1,128)S(1)}, f32[1,3328]{1,0:T(1,128)S(1)}, u32[]{:S(2)}, u32[]{:S(2)}) collective-permute-start(f32[1,3328]{1,0:T(1,128)S(1)} %copy-done.12), channel_id=1, source_target_pairs={{0,16},{16,0},{1,17},{17,1},{2,18},{18,2},{3,19},{19,3},{4,20},{20... | collective-permute-start | bytes 39944 | tf_op jit(solution)/shard_map/ppermute | solution.py:689
  3.7 2.6 %collective-permute-start.1 = (f32[1,2304]{1,0:T(1,128)S(1)}, f32[1,2304]{1,0:T(1,128)S(1)}, u32[]{:S(2)}, u32[]{:S(2)}) collective-permute-start(f32[1,2304]{1,0:T(1,128)S(1)} %bitcast.144), channel_id=1, source_target_pairs={{0,16},{16,0},{1,17},{17,1},{2,18},{18,2},{3,19},{19,3},{4,20},{20... | collective-permute-start | bytes 27656 | tf_op jit(solution)/shard_map/ppermute | solution.py:689
  22.5 2.0 %collective-permute-start.5 = (bf16[1024,256]{1,0:T(8,128)(2,1)S(1)}, bf16[1024,256]{1,0:T(8,128)(2,1)S(1)}, u32[]{:S(2)}, u32[]{:S(2)}) collective-permute-start(bf16[1024,256]{1,0:T(8,128)(2,1)S(1)} %get-tuple-element.87), channel_id=1, source_target_pairs={{0,16},{16,0},{1,17},{17,1},{2,18},{18,2},{3,19},{19,3},{4,20},{20... | collective-permute-start | bytes 1572872 | tf_op jit(solution)/shard_map/ppermute | solution.py:689
  23.0 4.6 %collective-permute-start.13 = (bf16[1024,256]{1,0:T(8,128)(2,1)S(1)}, bf16[1024,256]{1,0:T(8,128)(2,1)S(1)}, u32[]{:S(2)}, u32[]{:S(2)}) collective-permute-start(bf16[1024,256]{1,0:T(8,128)(2,1)S(1)} %get-tuple-element.89), channel_id=1, source_target_pairs={{0,16},{16,0},{1,17},{17,1},{2,18},{18,2},{3,19},{19,3},{4,20},{20... | collective-permute-start | bytes 1572872 | tf_op jit(solution)/shard_map/ppermute | solution.py:689
  23.1 6.3 %collective-permute-start.21 = (bf16[1088,256]{1,0:T(8,128)(2,1)S(1)}, bf16[1088,256]{1,0:T(8,128)(2,1)S(1)}, u32[]{:S(2)}, u32[]{:S(2)}) collective-permute-start(bf16[1088,256]{1,0:T(8,128)(2,1)S(1)} %get-tuple-element.91), channel_id=1, source_target_pairs={{0,16},{16,0},{1,17},{17,1},{2,18},{18,2},{3,19},{19,3},{4,20},{20... | collective-permute-start | bytes 1671176 | tf_op jit(solution)/shard_map/ppermute | solution.py:689
  23.5 49.3 %collective-permute-start.4 = (f32[2,304,256]{2,1,0:T(8,128)S(1)}, f32[2,304,256]{2,1,0:T(8,128)S(1)}, u32[]{:S(2)}, u32[]{:S(2)}) collective-permute-start(f32[2,304,256]{2,1,0:T(8,128)S(1)} %get-tuple-element.82), channel_id=1, source_target_pairs={{0,16},{16,0},{1,17},{17,1},{2,18},{18,2},{3,19},{19,3},{4,20},{20... | collective-permute-start | bytes 1867784 | tf_op jit(solution)/shard_map/ppermute | solution.py:689
  24.7 9.5 %collective-permute-start.6 = (bf16[2,2,128,256]{3,2,1,0:T(8,128)(2,1)S(1)}, bf16[2,2,128,256]{3,2,1,0:T(8,128)(2,1)S(1)}, u32[]{:S(2)}, u32[]{:S(2)}) collective-permute-start(bf16[2,2,128,256]{3,2,1,0:T(8,128)(2,1)S(1)} %bitcast.154), channel_id=1, source_target_pairs={{0,1},{1,0},{2,3},{3,2},{4,5},{5,4},{6,7},{7,6},{8,9},{9,8},{10,11... | collective-permute-start | bytes 786440 | tf_op jit(solution)/shard_map/ppermute | solution.py:701
  27.8 8.4 %collective-permute-start.14 = (bf16[2,2,128,256]{3,2,1,0:T(8,128)(2,1)S(1)}, bf16[2,2,128,256]{3,2,1,0:T(8,128)(2,1)S(1)}, u32[]{:S(2)}, u32[]{:S(2)}) collective-permute-start(bf16[2,2,128,256]{3,2,1,0:T(8,128)(2,1)S(1)} %bitcast.155), channel_id=1, source_target_pairs={{0,2},{1,3},{2,0},{3,1},{4,6},{5,7},{6,4},{7,5},{8,10},{9,11},{10,... | collective-permute-start | bytes 786440 | tf_op jit(solution)/shard_map/ppermute | solution.py:701
  29.6 8.3 %collective-permute-start.22 = (bf16[2,2,136,256]{3,2,1,0:T(8,128)(2,1)S(1)}, bf16[2,2,136,256]{3,2,1,0:T(8,128)(2,1)S(1)}, u32[]{:S(2)}, u32[]{:S(2)}) collective-permute-start(bf16[2,2,136,256]{3,2,1,0:T(8,128)(2,1)S(1)} %bitcast.153), channel_id=1, source_target_pairs={{0,4},{1,5},{2,6},{3,7},{4,0},{5,1},{6,2},{7,3},{8,12},{9,13},{10,... | collective-permute-start | bytes 835592 | tf_op jit(solution)/shard_map/ppermute | solution.py:701
  34.3 5.2 %collective-permute-start.7 = (bf16[2,128,256]{2,1,0:T(8,128)(2,1)S(1)}, bf16[2,128,256]{2,1,0:T(8,128)(2,1)S(1)}, u32[]{:S(2)}, u32[]{:S(2)}) collective-permute-start(bf16[2,128,256]{2,1,0:T(8,128)(2,1)S(1)} %select_bitcast_fusion.14), channel_id=1, source_target_pairs={{0,2},{1,3},{2,0},{3,1},{4,6},{5,7},{6,4},{7,5},{8,10},{9,11},{10,... | collective-permute-start | bytes 393224 | tf_op jit(solution)/shard_map/ppermute | solution.py:701
  36.3 5.4 %collective-permute-start.15 = (bf16[2,128,256]{2,1,0:T(8,128)(2,1)S(1)}, bf16[2,128,256]{2,1,0:T(8,128)(2,1)S(1)}, u32[]{:S(2)}, u32[]{:S(2)}) collective-permute-start(bf16[2,128,256]{2,1,0:T(8,128)(2,1)S(1)} %select_bitcast_fusion.11), channel_id=1, source_target_pairs={{0,4},{1,5},{2,6},{3,7},{4,0},{5,1},{6,2},{7,3},{8,12},{9,13},{10,... | collective-permute-start | bytes 393224 | tf_op jit(solution)/shard_map/ppermute | solution.py:701
  38.0 5.8 %collective-permute-start.23 = (bf16[2,136,256]{2,1,0:T(8,128)(2,1)S(1)}, bf16[2,136,256]{2,1,0:T(8,128)(2,1)S(1)}, u32[]{:S(2)}, u32[]{:S(2)}) collective-permute-start(bf16[2,136,256]{2,1,0:T(8,128)(2,1)S(1)} %select_bitcast_fusion.8), channel_id=1, source_target_pairs={{0,1},{1,0},{2,3},{3,2},{4,5},{5,4},{6,7},{7,6},{8,9},{9,8},{10,11... | collective-permute-start | bytes 417800 | tf_op jit(solution)/shard_map/ppermute | solution.py:701
  39.6 5.6 %collective-permute-start.8 = (bf16[128,256]{1,0:T(8,128)(2,1)S(1)}, bf16[128,256]{1,0:T(8,128)(2,1)S(1)}, u32[]{:S(2)}, u32[]{:S(2)}) collective-permute-start(bf16[128,256]{1,0:T(8,128)(2,1)S(1)} %select_bitcast_fusion.23), channel_id=1, source_target_pairs={{0,4},{1,5},{2,6},{3,7},{4,0},{5,1},{6,2},{7,3},{8,12},{9,13},{10,... | collective-permute-start | bytes 196616 | tf_op jit(solution)/shard_map/ppermute | solution.py:701
  41.8 6.2 %collective-permute-start.16 = (bf16[128,256]{1,0:T(8,128)(2,1)S(1)}, bf16[128,256]{1,0:T(8,128)(2,1)S(1)}, u32[]{:S(2)}, u32[]{:S(2)}) collective-permute-start(bf16[128,256]{1,0:T(8,128)(2,1)S(1)} %select_bitcast_fusion.20), channel_id=1, source_target_pairs={{0,1},{1,0},{2,3},{3,2},{4,5},{5,4},{6,7},{7,6},{8,9},{9,8},{10,11... | collective-permute-start | bytes 196616 | tf_op jit(solution)/shard_map/ppermute | solution.py:701
  43.9 5.0 %collective-permute-start.24 = (bf16[136,256]{1,0:T(8,128)(2,1)S(1)}, bf16[136,256]{1,0:T(8,128)(2,1)S(1)}, u32[]{:S(2)}, u32[]{:S(2)}) collective-permute-start(bf16[136,256]{1,0:T(8,128)(2,1)S(1)} %select_bitcast_fusion.17), channel_id=1, source_target_pairs={{0,2},{1,3},{2,0},{3,1},{4,6},{5,7},{6,4},{7,5},{8,10},{9,11},{10,... | collective-permute-start | bytes 208904 | tf_op jit(solution)/shard_map/ppermute | solution.py:701
  45.3 8.1 %collective-permute-start.9 = (bf16[128,256]{1,0:T(8,128)(2,1)S(1)}, bf16[128,256]{1,0:T(8,128)(2,1)S(1)}, u32[]{:S(2)}, u32[]{:S(2)}) collective-permute-start(bf16[128,256]{1,0:T(8,128)(2,1)S(1)} %fusion.8), channel_id=1, source_target_pairs={{0,8},{1,9},{2,10},{3,11},{4,12},{5,13},{6,14},{7,15},{8,0},{9,1},... | collective-permute-start | bytes 196616 | tf_op jit(solution)/shard_map/ppermute | solution.py:701
  48.0 6.1 %collective-permute-start.17 = (bf16[128,256]{1,0:T(8,128)(2,1)S(1)}, bf16[128,256]{1,0:T(8,128)(2,1)S(1)}, u32[]{:S(2)}, u32[]{:S(2)}) collective-permute-start(bf16[128,256]{1,0:T(8,128)(2,1)S(1)} %fusion.7), channel_id=1, source_target_pairs={{0,8},{1,9},{2,10},{3,11},{4,12},{5,13},{6,14},{7,15},{8,0},{9,1},... | collective-permute-start | bytes 196616 | tf_op jit(solution)/shard_map/ppermute | solution.py:701
  49.0 6.7 %collective-permute-start.25 = (bf16[136,256]{1,0:T(8,128)(2,1)S(1)}, bf16[136,256]{1,0:T(8,128)(2,1)S(1)}, u32[]{:S(2)}, u32[]{:S(2)}) collective-permute-start(bf16[136,256]{1,0:T(8,128)(2,1)S(1)} %fusion.6), channel_id=1, source_target_pairs={{0,8},{1,9},{2,10},{3,11},{4,12},{5,13},{6,14},{7,15},{8,0},{9,1},... | collective-permute-start | bytes 208904 | tf_op jit(solution)/shard_map/ppermute | solution.py:701
  53.4 4.3 %collective-permute-start.10 = (bf16[128,256]{1,0:T(8,128)(2,1)S(1)}, bf16[128,256]{1,0:T(8,128)(2,1)S(1)}, u32[]{:S(2)}, u32[]{:S(2)}) collective-permute-start(bf16[128,256]{1,0:T(8,128)(2,1)S(1)} %add_convert_fusion.5), channel_id=1, source_target_pairs={{0,4},{1,5},{2,6},{3,7},{4,0},{5,1},{6,2},{7,3},{8,12},{9,13},{10,... | collective-permute-start | bytes 196616 | tf_op jit(solution)/shard_map/ppermute | solution.py:701
  54.1 4.3 %collective-permute-start.18 = (bf16[128,256]{1,0:T(8,128)(2,1)S(1)}, bf16[128,256]{1,0:T(8,128)(2,1)S(1)}, u32[]{:S(2)}, u32[]{:S(2)}) collective-permute-start(bf16[128,256]{1,0:T(8,128)(2,1)S(1)} %add_convert_fusion.4), channel_id=1, source_target_pairs={{0,1},{1,0},{2,3},{3,2},{4,5},{5,4},{6,7},{7,6},{8,9},{9,8},{10,11... | collective-permute-start | bytes 196616 | tf_op jit(solution)/shard_map/ppermute | solution.py:701
  55.6 4.5 %collective-permute-start.26 = (bf16[136,256]{1,0:T(8,128)(2,1)S(1)}, bf16[136,256]{1,0:T(8,128)(2,1)S(1)}, u32[]{:S(2)}, u32[]{:S(2)}) collective-permute-start(bf16[136,256]{1,0:T(8,128)(2,1)S(1)} %add_convert_fusion.3), channel_id=1, source_target_pairs={{0,2},{1,3},{2,0},{3,1},{4,6},{5,7},{6,4},{7,5},{8,10},{9,11},{10,... | collective-permute-start | bytes 208904 | tf_op jit(solution)/shard_map/ppermute | solution.py:701
  57.8 5.5 %collective-permute-start.11 = (bf16[2,128,256]{2,1,0:T(8,128)(2,1)S(1)}, bf16[2,128,256]{2,1,0:T(8,128)(2,1)S(1)}, u32[]{:S(2)}, u32[]{:S(2)}) collective-permute-start(bf16[2,128,256]{2,1,0:T(8,128)(2,1)S(1)} %pad_maximum_fusion.7), channel_id=1, source_target_pairs={{0,2},{1,3},{2,0},{3,1},{4,6},{5,7},{6,4},{7,5},{8,10},{9,11},{10,... | collective-permute-start | bytes 393224 | tf_op jit(solution)/shard_map/ppermute | solution.py:701
  58.5 5.2 %collective-permute-start.19 = (bf16[2,128,256]{2,1,0:T(8,128)(2,1)S(1)}, bf16[2,128,256]{2,1,0:T(8,128)(2,1)S(1)}, u32[]{:S(2)}, u32[]{:S(2)}) collective-permute-start(bf16[2,128,256]{2,1,0:T(8,128)(2,1)S(1)} %pad_maximum_fusion.8), channel_id=1, source_target_pairs={{0,4},{1,5},{2,6},{3,7},{4,0},{5,1},{6,2},{7,3},{8,12},{9,13},{10,... | collective-permute-start | bytes 393224 | tf_op jit(solution)/shard_map/ppermute | solution.py:701
  60.1 5.5 %collective-permute-start.27 = (bf16[2,136,256]{2,1,0:T(8,128)(2,1)S(1)}, bf16[2,136,256]{2,1,0:T(8,128)(2,1)S(1)}, u32[]{:S(2)}, u32[]{:S(2)}) collective-permute-start(bf16[2,136,256]{2,1,0:T(8,128)(2,1)S(1)} %pad_maximum_fusion.6), channel_id=1, source_target_pairs={{0,1},{1,0},{2,3},{3,2},{4,5},{5,4},{6,7},{7,6},{8,9},{9,8},{10,11... | collective-permute-start | bytes 417800 | tf_op jit(solution)/shard_map/ppermute | solution.py:701
  63.4 6.4 %collective-permute-start.12 = (bf16[2,2,128,256]{3,2,1,0:T(8,128)(2,1)S(1)}, bf16[2,2,128,256]{3,2,1,0:T(8,128)(2,1)S(1)}, u32[]{:S(2)}, u32[]{:S(2)}) collective-permute-start(bf16[2,2,128,256]{3,2,1,0:T(8,128)(2,1)S(1)} %pad_maximum_fusion.4), channel_id=1, source_target_pairs={{0,1},{1,0},{2,3},{3,2},{4,5},{5,4},{6,7},{7,6},{8,9},{9,8},{10,11... | collective-permute-start | bytes 786440 | tf_op jit(solution)/shard_map/ppermute | solution.py:701
  63.7 10.2 %copy-start.11 = (f32[1,256,256]{2,1,0:T(8,128)S(1)}, f32[1,256,256]{2,1,0:T(8,128)}, u32[]{:S(2)}) copy-start(f32[1,256,256]{2,1,0:T(8,128)} %param.41) | copy-start | bytes 786436
  63.8 10.2 %copy-start.15 = (f32[1,9,256]{2,0,1:T(1,128)S(1)}, f32[1,9,256]{2,0,1:T(1,128)}, u32[]{:S(2)}) copy-start(f32[1,9,256]{2,0,1:T(1,128)} %param.27) | copy-start | bytes 27652
  63.8 10.2 %copy-start.16 = (f32[1,3328]{1,0:T(1,128)S(1)}, f32[1,3328]{1,0:T(1,128)}, u32[]{:S(2)}) copy-start(f32[1,3328]{1,0:T(1,128)} %refs_14_.1) | copy-start | bytes 39940
  63.8 10.2 %copy-start.17 = (f32[1,3328]{1,0:T(1,128)S(1)}, f32[1,3328]{1,0:T(1,128)}, u32[]{:S(2)}) copy-start(f32[1,3328]{1,0:T(1,128)} %refs_20_.1) | copy-start | bytes 39940
  63.8 10.2 %copy-start.18 = (f32[1,9,256]{2,0,1:T(1,128)S(1)}, f32[1,9,256]{2,0,1:T(1,128)}, u32[]{:S(2)}) copy-start(f32[1,9,256]{2,0,1:T(1,128)} %param.33) | copy-start | bytes 27652
  63.8 10.2 %copy-start.19 = (f32[1,9,256]{2,0,1:T(1,128)S(1)}, f32[1,9,256]{2,0,1:T(1,128)}, u32[]{:S(2)}) copy-start(f32[1,9,256]{2,0,1:T(1,128)} %param.39) | copy-start | bytes 27652
  63.8 6.4 %collective-permute-start.20 = (bf16[2,2,128,256]{3,2,1,0:T(8,128)(2,1)S(1)}, bf16[2,2,128,256]{3,2,1,0:T(8,128)(2,1)S(1)}, u32[]{:S(2)}, u32[]{:S(2)}) collective-permute-start(bf16[2,2,128,256]{3,2,1,0:T(8,128)(2,1)S(1)} %pad_maximum_fusion.5), channel_id=1, source_target_pairs={{0,2},{1,3},{2,0},{3,1},{4,6},{5,7},{6,4},{7,5},{8,10},{9,11},{10,... | collective-permute-start | bytes 786440 | tf_op jit(solution)/shard_map/ppermute | solution.py:701
  65.6 8.4 %copy-start.9 = (f32[1,256,768]{2,1,0:T(8,128)S(1)}, f32[1,256,768]{2,1,0:T(8,128)}, u32[]{:S(2)}) copy-start(f32[1,256,768]{2,1,0:T(8,128)} %param.40) | copy-start | bytes 2359300
  65.6 8.3 %copy-start.8 = (f32[1,256,768]{2,1,0:T(8,128)S(1)}, f32[1,256,768]{2,1,0:T(8,128)}, u32[]{:S(2)}) copy-start(f32[1,256,768]{2,1,0:T(8,128)} %param.34) | copy-start | bytes 2359300
  65.7 6.6 %collective-permute-start.28 = (bf16[2,2,136,256]{3,2,1,0:T(8,128)(2,1)S(1)}, bf16[2,2,136,256]{3,2,1,0:T(8,128)(2,1)S(1)}, u32[]{:S(2)}, u32[]{:S(2)}) collective-permute-start(bf16[2,2,136,256]{3,2,1,0:T(8,128)(2,1)S(1)} %pad_maximum_fusion.3), channel_id=1, source_target_pairs={{0,4},{1,5},{2,6},{3,7},{4,0},{5,1},{6,2},{7,3},{8,12},{9,13},{10,... | collective-permute-start | bytes 835592 | tf_op jit(solution)/shard_map/ppermute | solution.py:701
  69.8 4.2 %copy-start.6 = (f32[1,1024,256]{2,1,0:T(8,128)S(1)}, f32[1,1024,256]{2,1,0:T(8,128)}, u32[]{:S(2)}) copy-start(f32[1,1024,256]{2,1,0:T(8,128)} %param.43) | copy-start | bytes 3145732
  70.3 3.7 %copy-start.5 = (f32[1,256,1024]{2,1,0:T(8,128)S(1)}, f32[1,256,1024]{2,1,0:T(8,128)}, u32[]{:S(2)}) copy-start(f32[1,256,1024]{2,1,0:T(8,128)} %param.42) | copy-start | bytes 3145732
  70.3 3.7 %copy-start.4 = (f32[1,1024,256]{2,1,0:T(8,128)S(1)}, f32[1,1024,256]{2,1,0:T(8,128)}, u32[]{:S(2)}) copy-start(f32[1,1024,256]{2,1,0:T(8,128)} %param.37) | copy-start | bytes 3145732
  70.4 3.6 %copy-start.3 = (f32[1,256,1024]{2,1,0:T(8,128)S(1)}, f32[1,256,1024]{2,1,0:T(8,128)}, u32[]{:S(2)}) copy-start(f32[1,256,1024]{2,1,0:T(8,128)} %param.36) | copy-start | bytes 3145732
  72.3 1.7 %copy-start.2 = (f32[1,256,768]{2,1,0:T(8,128)S(1)}, f32[1,256,768]{2,1,0:T(8,128)}, u32[]{:S(2)}) copy-start(f32[1,256,768]{2,1,0:T(8,128)} %param.28) | copy-start | bytes 2359300
  72.3 1.7 %copy-start.1 = (f32[1,1024,256]{2,1,0:T(8,128)S(1)}, f32[1,1024,256]{2,1,0:T(8,128)}, u32[]{:S(2)}) copy-start(f32[1,1024,256]{2,1,0:T(8,128)} %param.31) | copy-start | bytes 3145732
  72.4 1.7 %copy-start = (f32[1,256,1024]{2,1,0:T(8,128)S(1)}, f32[1,256,1024]{2,1,0:T(8,128)}, u32[]{:S(2)}) copy-start(f32[1,256,1024]{2,1,0:T(8,128)} %param.30) | copy-start | bytes 3145732
  72.4 1.7 %copy-start.7 = (f32[1,256,256]{2,1,0:T(8,128)S(1)}, f32[1,256,256]{2,1,0:T(8,128)}, u32[]{:S(2)}) copy-start(f32[1,256,256]{2,1,0:T(8,128)} %param.29) | copy-start | bytes 786436
  72.4 1.8 %copy-start.10 = (f32[1,256,256]{2,1,0:T(8,128)S(1)}, f32[1,256,256]{2,1,0:T(8,128)}, u32[]{:S(2)}) copy-start(f32[1,256,256]{2,1,0:T(8,128)} %param.35) | copy-start | bytes 786436
  72.5 1.8 %copy-start.13 = (f32[1,3328]{1,0:T(1,128)S(1)}, f32[1,3328]{1,0:T(1,128)}, u32[]{:S(2)}) copy-start(f32[1,3328]{1,0:T(1,128)} %refs_8_.1) | copy-start | bytes 39940
  72.8 1.2 %collective-permute-start.29 = (f32[8,128]{1,0:T(8,128)S(1)}, f32[8,128]{1,0:T(8,128)S(1)}, u32[]{:S(2)}, u32[]{:S(2)}) collective-permute-start(f32[8,128]{1,0:T(8,128)S(1)} %squares.1.refs_3_), channel_id=1, source_target_pairs={{0,16},{16,0},{1,17},{17,1},{2,18},{18,2},{3,19},{19,3},{4,20},{20... | collective-permute-start | bytes 12296 | tf_op jit(solution)/shard_map/ppermute | solution.py:689

commit v6 on v5

--- a/solution.py
+++ b/solution.py
@@ -691,7 +691,7 @@
 
 def exchange_orders(bits):
     if bits == 4:
-        return ((0, 1, 2, 3), (1, 2, 0, 3), (2, 0, 1, 3))
+        return ((1, 2, 0, 3), (2, 0, 1, 3), (0, 1, 2, 3))
     turn = max(1, bits // 3)
     every = tuple(range(bits))
     return tuple(every[turn * part :] + every[: turn * part] for part in range(3))

time: 80.6 us -> 80.4 us (level)
  waiting for transfers between devices: 20.3 us -> 18.3 us
  starting transfers between devices: 32.3 us -> 34.1 us
    ppermute x21, waiting for transfers between devices: 15.7 us -> 13.8 us  [exchanged(): lax.ppermute(value, 'dp', [(index, index ^ 1 << bit) for index in range(s...]
    ppermute x21, starting transfers between devices: 30.1 us -> 31.9 us  [exchanged(): lax.ppermute(value, 'dp', [(index, index ^ 1 << bit) for index in range(s...]
  transfers between devices with their start and end apart: 30 -> 30, of which waited for: 16 -> 18; matrix products, arithmetic and copies ran while one was open for 2% -> 2% of each run, Pallas kernels for 0% -> 0%
where the time goes in v6:
time: 80.4 us; the launch traced here: 80.2 us
  starting transfers between devices  34.1 us (42%)
  Pallas kernels  24.5 us (30%)
  waiting for transfers between devices  18.3 us (23%)
  other arithmetic  1.63 us (2%)
  between operations  1.34 us (2%)
    ppermute x21, starting transfers between devices, exchanged(): lax.ppermute(value, 'dp', [(index, index ^ 1 << bit) for index in range(s...  31.9 us
    pallas_call x1, Pallas kernels, run_blocks(): pl.pallas_call(section_step, out_shape=out_shape, in_specs=[smem] + [pl.B...  16.3 us
    ppermute x21, waiting for transfers between devices, exchanged(): lax.ppermute(value, 'dp', [(index, index ^ 1 << bit) for index in range(s...  13.8 us
    pallas_call x1, Pallas kernels, run_optimizer(): pl.pallas_call(optimizer_step, out_shape=[pltpu.HBM(shape, kind) for shap...  6.01 us
    ppermute x9, waiting for transfers between devices, swapped(): return lax.ppermute(value, 'section', [(0, 1), (1, 0)])  4.53 us
    ppermute x9, starting transfers between devices, swapped(): return lax.ppermute(value, 'section', [(0, 1), (1, 0)])  2.19 us
    pallas_call x1, Pallas kernels, run_narrowed(): pl.pallas_call(narrowed, out_shape=[pltpu.VMEM((D, 8 * D), BF16), pltpu.V...  1.95 us
  transfers between devices with their start and end apart: 30, of which 18 were waited for; matrix products, arithmetic and copies ran while one was open for 2% of the time, Pallas kernels for 0%

profile of v6, /device:TPU:0, one launch (start us, length us, event | category | flops | bytes accessed | tf_op | source)
XLA Modules:
  0.0 80.2 jit_solution(17963880637737167696)
XLA Ops:
  0.7 2.0 %narrowed.1 = (bf16[256,2048]{1,0:T(8,128)(2,1)S(1)}, bf16[1024,256]{1,0:T(8,128)(2,1)S(1)}) custom-call(f32[256,768]{1,0:T(8,128)} %bitcast.131, f32[256,256]{1,0:T(8,128)} %bitcast.137, f32[256,1024]{1,0:T(8,128)} %bitcast.127, f32[1024,256]{1,0:T(8,128)} %bitcast.129), custom_call_target="tpu_custom_call" | custom-call | tf_op jit(solution)/shard_map/narrowed/pallas_call | solution.py:564
  2.7 0.5 collective-permute-start.2
  3.2 0.1 collective-permute-start.3
  3.3 0.4 collective-permute-start
  3.7 0.1 collective-permute-start.1
  3.8 2.5 %collective-permute-done.1.refs_5_ = f32[1,2304]{1,0:T(1,128)S(1)} collective-permute-done((f32[1,2304]{1,0:T(1,128)S(1)}, f32[1,2304]{1,0:T(1,128)S(1)}, u32[]{:S(2)}, u32[]{:S(2)}) %collective-permute-start.1) | collective-permute-done | bytes 9248 | tf_op jit(solution)/shard_map/ppermute | solution.py:689
  6.3 16.3 %blocks.1 = (f32[608,256]{1,0:T(8,128)}, f32[608,256]{1,0:T(8,128)}, f32[2,304,256]{2,1,0:T(8,128)S(1)}, bf16[1024,256]{1,0:T(8,128)(2,1)S(1)}, bf16[1024,256]{1...) custom-call(s32[1]{0:T(128)} %bitcast.sec_ref, ...), custom_call_target="tpu_custom_call" | custom-call | tf_op jit(solution)/shard_map/blocks/pallas_call | solution.py:534
  22.5 0.4 collective-permute-start.5
  23.0 0.1 collective-permute-start.13
  23.1 0.4 collective-permute-start.21
  23.5 0.1 collective-permute-start.4
  23.6 0.9 %collective-permute-done.5 = bf16[1024,256]{1,0:T(8,128)(2,1)S(1)} collective-permute-done((bf16[1024,256]{1,0:T(8,128)(2,1)S(1)}, bf16[1024,256]{1,0:T(8,128)(2,1)S(1)}, u32[]{:S(2)}, u32[]{:S(2)}) %collective-permute-start.5) | collective-permute-done | bytes 524320 | tf_op jit(solution)/shard_map/ppermute | solution.py:689
  24.5 0.1 add_convert_fusion.2
  24.7 3.0 %collective-permute-start.6 = (bf16[2,2,128,256]{3,2,1,0:T(8,128)(2,1)S(1)}, bf16[2,2,128,256]{3,2,1,0:T(8,128)(2,1)S(1)}, u32[]{:S(2)}, u32[]{:S(2)}) collective-permute-start(bf16[2,2,128,256]{3,2,1,0:T(8,128)(2,1)S(1)} %bitcast.154), channel_id=1, source_target_pairs={{0,2},{1,3},{2,0},{3,1},{4,6},{5,7},{6,4},{7,5},{8,10},{9,11},{10,... | collective-permute-start | bytes 786440 | tf_op jit(solution)/shard_map/ppermute | solution.py:701
  27.7 0.1 add_convert_fusion.1
  27.8 1.7 %collective-permute-start.14 = (bf16[2,2,128,256]{3,2,1,0:T(8,128)(2,1)S(1)}, bf16[2,2,128,256]{3,2,1,0:T(8,128)(2,1)S(1)}, u32[]{:S(2)}, u32[]{:S(2)}) collective-permute-start(bf16[2,2,128,256]{3,2,1,0:T(8,128)(2,1)S(1)} %bitcast.155), channel_id=1, source_target_pairs={{0,4},{1,5},{2,6},{3,7},{4,0},{5,1},{6,2},{7,3},{8,12},{9,13},{10,... | collective-permute-start | bytes 786440 | tf_op jit(solution)/shard_map/ppermute | solution.py:701
  29.5 0.1 add_convert_fusion
  29.7 1.5 %collective-permute-start.22 = (bf16[2,2,136,256]{3,2,1,0:T(8,128)(2,1)S(1)}, bf16[2,2,136,256]{3,2,1,0:T(8,128)(2,1)S(1)}, u32[]{:S(2)}, u32[]{:S(2)}) collective-permute-start(bf16[2,2,136,256]{3,2,1,0:T(8,128)(2,1)S(1)} %bitcast.153), channel_id=1, source_target_pairs={{0,1},{1,0},{2,3},{3,2},{4,5},{5,4},{6,7},{7,6},{8,9},{9,8},{10,11... | collective-permute-start | bytes 835592 | tf_op jit(solution)/shard_map/ppermute | solution.py:701
  31.2 3.0 %collective-permute-done.6 = bf16[2,2,128,256]{3,2,1,0:T(8,128)(2,1)S(1)} collective-permute-done((bf16[2,2,128,256]{3,2,1,0:T(8,128)(2,1)S(1)}, bf16[2,2,128,256]{3,2,1,0:T(8,128)(2,1)S(1)}, u32[]{:S(2)}, u32[]{:S(2)}) %collective-permute-start.6) | collective-permute-done | bytes 262176 | tf_op jit(solution)/shard_map/ppermute | solution.py:701
  34.3 0.1 fusion.2
  34.4 1.9 %collective-permute-start.7 = (bf16[2,128,256]{2,1,0:T(8,128)(2,1)S(1)}, bf16[2,128,256]{2,1,0:T(8,128)(2,1)S(1)}, u32[]{:S(2)}, u32[]{:S(2)}) collective-permute-start(bf16[2,128,256]{2,1,0:T(8,128)(2,1)S(1)} %select_bitcast_fusion.14), channel_id=1, source_target_pairs={{0,4},{1,5},{2,6},{3,7},{4,0},{5,1},{6,2},{7,3},{8,12},{9,13},{10,... | collective-permute-start | bytes 393224 | tf_op jit(solution)/shard_map/ppermute | solution.py:701
  36.2 0.1 fusion.1
  36.3 1.6 %collective-permute-start.15 = (bf16[2,128,256]{2,1,0:T(8,128)(2,1)S(1)}, bf16[2,128,256]{2,1,0:T(8,128)(2,1)S(1)}, u32[]{:S(2)}, u32[]{:S(2)}) collective-permute-start(bf16[2,128,256]{2,1,0:T(8,128)(2,1)S(1)} %select_bitcast_fusion.11), channel_id=1, source_target_pairs={{0,1},{1,0},{2,3},{3,2},{4,5},{5,4},{6,7},{7,6},{8,9},{9,8},{10,11... | collective-permute-start | bytes 393224 | tf_op jit(solution)/shard_map/ppermute | solution.py:701
  37.9 0.1 fusion
  38.0 1.6 %collective-permute-start.23 = (bf16[2,136,256]{2,1,0:T(8,128)(2,1)S(1)}, bf16[2,136,256]{2,1,0:T(8,128)(2,1)S(1)}, u32[]{:S(2)}, u32[]{:S(2)}) collective-permute-start(bf16[2,136,256]{2,1,0:T(8,128)(2,1)S(1)} %select_bitcast_fusion.8), channel_id=1, source_target_pairs={{0,2},{1,3},{2,0},{3,1},{4,6},{5,7},{6,4},{7,5},{8,10},{9,11},{10,... | collective-permute-start | bytes 417800 | tf_op jit(solution)/shard_map/ppermute | solution.py:701
  39.6 0.1 fusion.5
  39.6 1.6 %collective-permute-start.8 = (bf16[128,256]{1,0:T(8,128)(2,1)S(1)}, bf16[128,256]{1,0:T(8,128)(2,1)S(1)}, u32[]{:S(2)}, u32[]{:S(2)}) collective-permute-start(bf16[128,256]{1,0:T(8,128)(2,1)S(1)} %select_bitcast_fusion.23), channel_id=1, source_target_pairs={{0,1},{1,0},{2,3},{3,2},{4,5},{5,4},{6,7},{7,6},{8,9},{9,8},{10,11... | collective-permute-start | bytes 196616 | tf_op jit(solution)/shard_map/ppermute | solution.py:701
  41.2 0.5 collective-permute-done.15
  41.8 1.9 %collective-permute-start.16 = (bf16[128,256]{1,0:T(8,128)(2,1)S(1)}, bf16[128,256]{1,0:T(8,128)(2,1)S(1)}, u32[]{:S(2)}, u32[]{:S(2)}) collective-permute-start(bf16[128,256]{1,0:T(8,128)(2,1)S(1)} %select_bitcast_fusion.20), channel_id=1, source_target_pairs={{0,2},{1,3},{2,0},{3,1},{4,6},{5,7},{6,4},{7,5},{8,10},{9,11},{10,... | collective-permute-start | bytes 196616 | tf_op jit(solution)/shard_map/ppermute | solution.py:701
  43.7 0.1 collective-permute-done.23
  43.8 0.1 fusion.3
  43.9 1.4 %collective-permute-start.24 = (bf16[136,256]{1,0:T(8,128)(2,1)S(1)}, bf16[136,256]{1,0:T(8,128)(2,1)S(1)}, u32[]{:S(2)}, u32[]{:S(2)}) collective-permute-start(bf16[136,256]{1,0:T(8,128)(2,1)S(1)} %select_bitcast_fusion.17), channel_id=1, source_target_pairs={{0,4},{1,5},{2,6},{3,7},{4,0},{5,1},{6,2},{7,3},{8,12},{9,13},{10,... | collective-permute-start | bytes 208904 | tf_op jit(solution)/shard_map/ppermute | solution.py:701
  45.3 2.7 %collective-permute-start.9 = (bf16[128,256]{1,0:T(8,128)(2,1)S(1)}, bf16[128,256]{1,0:T(8,128)(2,1)S(1)}, u32[]{:S(2)}, u32[]{:S(2)}) collective-permute-start(bf16[128,256]{1,0:T(8,128)(2,1)S(1)} %fusion.8), channel_id=1, source_target_pairs={{0,8},{1,9},{2,10},{3,11},{4,12},{5,13},{6,14},{7,15},{8,0},{9,1},... | collective-permute-start | bytes 196616 | tf_op jit(solution)/shard_map/ppermute | solution.py:701
  48.0 1.0 %collective-permute-start.17 = (bf16[128,256]{1,0:T(8,128)(2,1)S(1)}, bf16[128,256]{1,0:T(8,128)(2,1)S(1)}, u32[]{:S(2)}, u32[]{:S(2)}) collective-permute-start(bf16[128,256]{1,0:T(8,128)(2,1)S(1)} %fusion.7), channel_id=1, source_target_pairs={{0,8},{1,9},{2,10},{3,11},{4,12},{5,13},{6,14},{7,15},{8,0},{9,1},... | collective-permute-start | bytes 196616 | tf_op jit(solution)/shard_map/ppermute | solution.py:701
  49.1 2.0 %collective-permute-start.25 = (bf16[136,256]{1,0:T(8,128)(2,1)S(1)}, bf16[136,256]{1,0:T(8,128)(2,1)S(1)}, u32[]{:S(2)}, u32[]{:S(2)}) collective-permute-start(bf16[136,256]{1,0:T(8,128)(2,1)S(1)} %fusion.6), channel_id=1, source_target_pairs={{0,8},{1,9},{2,10},{3,11},{4,12},{5,13},{6,14},{7,15},{8,0},{9,1},... | collective-permute-start | bytes 208904 | tf_op jit(solution)/shard_map/ppermute | solution.py:701
  51.1 1.5 %collective-permute-done.9 = bf16[128,256]{1,0:T(8,128)(2,1)S(1)} collective-permute-done((bf16[128,256]{1,0:T(8,128)(2,1)S(1)}, bf16[128,256]{1,0:T(8,128)(2,1)S(1)}, u32[]{:S(2)}, u32[]{:S(2)}) %collective-permute-start.9) | collective-permute-done | bytes 65568 | tf_op jit(solution)/shard_map/ppermute | solution.py:701
  52.7 1.0 %collective-permute-start.10 = (bf16[128,256]{1,0:T(8,128)(2,1)S(1)}, bf16[128,256]{1,0:T(8,128)(2,1)S(1)}, u32[]{:S(2)}, u32[]{:S(2)}) collective-permute-start(bf16[128,256]{1,0:T(8,128)(2,1)S(1)} %add_convert_fusion.5), channel_id=1, source_target_pairs={{0,1},{1,0},{2,3},{3,2},{4,5},{5,4},{6,7},{7,6},{8,9},{9,8},{10,11... | collective-permute-start | bytes 196616 | tf_op jit(solution)/shard_map/ppermute | solution.py:701
  53.6 0.4 collective-permute-done.17
  54.1 1.2 %collective-permute-start.18 = (bf16[128,256]{1,0:T(8,128)(2,1)S(1)}, bf16[128,256]{1,0:T(8,128)(2,1)S(1)}, u32[]{:S(2)}, u32[]{:S(2)}) collective-permute-start(bf16[128,256]{1,0:T(8,128)(2,1)S(1)} %add_convert_fusion.4), channel_id=1, source_target_pairs={{0,2},{1,3},{2,0},{3,1},{4,6},{5,7},{6,4},{7,5},{8,10},{9,11},{10,... | collective-permute-start | bytes 196616 | tf_op jit(solution)/shard_map/ppermute | solution.py:701
  55.3 0.3 collective-permute-done.25
  55.6 0.3 collective-permute-start.26
  55.9 1.1 %collective-permute-done.10 = bf16[128,256]{1,0:T(8,128)(2,1)S(1)} collective-permute-done((bf16[128,256]{1,0:T(8,128)(2,1)S(1)}, bf16[128,256]{1,0:T(8,128)(2,1)S(1)}, u32[]{:S(2)}, u32[]{:S(2)}) %collective-permute-start.10) | collective-permute-done | bytes 65568 | tf_op jit(solution)/shard_map/ppermute | solution.py:701
  57.0 0.7 collective-permute-start.11
  57.8 0.6 collective-permute-done.18
  58.4 1.4 %collective-permute-start.19 = (bf16[2,128,256]{2,1,0:T(8,128)(2,1)S(1)}, bf16[2,128,256]{2,1,0:T(8,128)(2,1)S(1)}, u32[]{:S(2)}, u32[]{:S(2)}) collective-permute-start(bf16[2,128,256]{2,1,0:T(8,128)(2,1)S(1)} %pad_maximum_fusion.8), channel_id=1, source_target_pairs={{0,1},{1,0},{2,3},{3,2},{4,5},{5,4},{6,7},{7,6},{8,9},{9,8},{10,11... | collective-permute-start | bytes 393224 | tf_op jit(solution)/shard_map/ppermute | solution.py:701
  59.9 0.1 collective-permute-done.26
  60.0 2.0 %collective-permute-start.27 = (bf16[2,136,256]{2,1,0:T(8,128)(2,1)S(1)}, bf16[2,136,256]{2,1,0:T(8,128)(2,1)S(1)}, u32[]{:S(2)}, u32[]{:S(2)}) collective-permute-start(bf16[2,136,256]{2,1,0:T(8,128)(2,1)S(1)} %pad_maximum_fusion.6), channel_id=1, source_target_pairs={{0,2},{1,3},{2,0},{3,1},{4,6},{5,7},{6,4},{7,5},{8,10},{9,11},{10,... | collective-permute-start | bytes 417800 | tf_op jit(solution)/shard_map/ppermute | solution.py:701
  62.0 0.1 collective-permute-done.11
  62.1 0.8 %collective-permute-start.12 = (bf16[2,2,128,256]{3,2,1,0:T(8,128)(2,1)S(1)}, bf16[2,2,128,256]{3,2,1,0:T(8,128)(2,1)S(1)}, u32[]{:S(2)}, u32[]{:S(2)}) collective-permute-start(bf16[2,2,128,256]{3,2,1,0:T(8,128)(2,1)S(1)} %pad_maximum_fusion.4), channel_id=1, source_target_pairs={{0,2},{1,3},{2,0},{3,1},{4,6},{5,7},{6,4},{7,5},{8,10},{9,11},{10,... | collective-permute-start | bytes 786440 | tf_op jit(solution)/shard_map/ppermute | solution.py:701
  62.9 0.5 collective-permute-done.19
  63.6 0.8 collective-permute-start.20
  64.4 1.0 %collective-permute-done.27 = bf16[2,136,256]{2,1,0:T(8,128)(2,1)S(1)} collective-permute-done((bf16[2,136,256]{2,1,0:T(8,128)(2,1)S(1)}, bf16[2,136,256]{2,1,0:T(8,128)(2,1)S(1)}, u32[]{:S(2)}, u32[]{:S(2)}) %collective-permute-start.27) | collective-permute-done | bytes 139296 | tf_op jit(solution)/shard_map/ppermute | solution.py:701
  65.5 2.0 %collective-permute-start.28 = (bf16[2,2,136,256]{3,2,1,0:T(8,128)(2,1)S(1)}, bf16[2,2,136,256]{3,2,1,0:T(8,128)(2,1)S(1)}, u32[]{:S(2)}, u32[]{:S(2)}) collective-permute-start(bf16[2,2,136,256]{3,2,1,0:T(8,128)(2,1)S(1)} %pad_maximum_fusion.3), channel_id=1, source_target_pairs={{0,1},{1,0},{2,3},{3,2},{4,5},{5,4},{6,7},{7,6},{8,9},{9,8},{10,11... | collective-permute-start | bytes 835592 | tf_op jit(solution)/shard_map/ppermute | solution.py:701
  67.5 1.1 %collective-permute-done.12 = bf16[2,2,128,256]{3,2,1,0:T(8,128)(2,1)S(1)} collective-permute-done((bf16[2,2,128,256]{3,2,1,0:T(8,128)(2,1)S(1)}, bf16[2,2,128,256]{3,2,1,0:T(8,128)(2,1)S(1)}, u32[]{:S(2)}, u32[]{:S(2)}) %collective-permute-start.12) | collective-permute-done | bytes 262176 | tf_op jit(solution)/shard_map/ppermute | solution.py:701
  68.6 1.4 %collective-permute-done.20 = bf16[2,2,128,256]{3,2,1,0:T(8,128)(2,1)S(1)} collective-permute-done((bf16[2,2,128,256]{3,2,1,0:T(8,128)(2,1)S(1)}, bf16[2,2,128,256]{3,2,1,0:T(8,128)(2,1)S(1)}, u32[]{:S(2)}, u32[]{:S(2)}) %collective-permute-start.20) | collective-permute-done | bytes 262176 | tf_op jit(solution)/shard_map/ppermute | solution.py:701
  70.1 0.1 pad_maximum_fusion.1
  70.2 0.1 pad_maximum_fusion.2
  70.2 1.9 %collective-permute-done.28 = bf16[2,2,136,256]{3,2,1,0:T(8,128)(2,1)S(1)} collective-permute-done((bf16[2,2,136,256]{3,2,1,0:T(8,128)(2,1)S(1)}, bf16[2,2,136,256]{3,2,1,0:T(8,128)(2,1)S(1)}, u32[]{:S(2)}, u32[]{:S(2)}) %collective-permute-start.28) | collective-permute-done | bytes 278560 | tf_op jit(solution)/shard_map/ppermute | solution.py:701
  72.2 0.1 pad_maximum_fusion
  72.3 0.3 squares.1.refs_3_
  72.6 1.1 %collective-permute-done.29.refs_4_ = f32[8,128]{1,0:T(8,128)S(1)} collective-permute-done((f32[8,128]{1,0:T(8,128)S(1)}, f32[8,128]{1,0:T(8,128)S(1)}, u32[]{:S(2)}, u32[]{:S(2)}) %collective-permute-start.29) | collective-permute-done | bytes 4128 | tf_op jit(solution)/shard_map/ppermute | solution.py:689
  73.9 0.1 copy-done
  74.0 0.1 copy-done.10
  74.1 6.0 %optimizer.1 = (f32[1,3328]{1,0:T(1,128)}, f32[1,2304]{1,0:T(1,128)}, f32[256,768]{1,0:T(8,128)}, f32[256,256]{1,0:T(8,128)}, f32[256,1024]{1,0:T(8,128)}, /*ind...) custom-call(s32[1]{0:T(128)} %bitcast.sec_ref, ...), custom_call_target="tpu_custom_call", output_to_operand_aliasing={{29}: (1, {}), {30}: (2, {})} | custom-call | tf_op jit(solution)/shard_map/optimizer/pallas_call | solution.py:674
  (82 shorter events, 1.0 us)
Async XLA Ops:
  0.7 2.6 %copy-start.12 = (f32[1,3328]{1,0:T(1,128)S(1)}, f32[1,3328]{1,0:T(1,128)}, u32[]{:S(2)}) copy-start(f32[1,3328]{1,0:T(1,128)} %refs_8_.1) | copy-start | bytes 39940
  0.7 3.0 %copy-start.14 = (f32[1,9,256]{2,0,1:T(1,128)S(1)}, f32[1,9,256]{2,0,1:T(1,128)}, u32[]{:S(2)}) copy-start(f32[1,9,256]{2,0,1:T(1,128)} %param.27) | copy-start | bytes 27652
  2.7 3.6 %collective-permute-start.2 = (bf16[256,2048]{1,0:T(8,128)(2,1)S(1)}, bf16[256,2048]{1,0:T(8,128)(2,1)S(1)}, u32[]{:S(2)}, u32[]{:S(2)}) collective-permute-start(bf16[256,2048]{1,0:T(8,128)(2,1)S(1)} %get-tuple-element.78.refs_6_), channel_id=1, source_target_pairs={{0,16},{16,0},{1,17},{17,1},{2,18},{18,2},{3,19},{19,3},{4,20},{20... | collective-permute-start | bytes 3145736 | tf_op jit(solution)/shard_map/ppermute | solution.py:689
  3.2 3.1 %collective-permute-start.3 = (bf16[1024,256]{1,0:T(8,128)(2,1)S(1)}, bf16[1024,256]{1,0:T(8,128)(2,1)S(1)}, u32[]{:S(2)}, u32[]{:S(2)}) collective-permute-start(bf16[1024,256]{1,0:T(8,128)(2,1)S(1)} %get-tuple-element.79.refs_8_), channel_id=1, source_target_pairs={{0,16},{16,0},{1,17},{17,1},{2,18},{18,2},{3,19},{19,3},{4,20},{20... | collective-permute-start | bytes 1572872 | tf_op jit(solution)/shard_map/ppermute | solution.py:689
  3.3 3.0 %collective-permute-start = (f32[1,3328]{1,0:T(1,128)S(1)}, f32[1,3328]{1,0:T(1,128)S(1)}, u32[]{:S(2)}, u32[]{:S(2)}) collective-permute-start(f32[1,3328]{1,0:T(1,128)S(1)} %copy-done.12), channel_id=1, source_target_pairs={{0,16},{16,0},{1,17},{17,1},{2,18},{18,2},{3,19},{19,3},{4,20},{20... | collective-permute-start | bytes 39944 | tf_op jit(solution)/shard_map/ppermute | solution.py:689
  3.7 2.6 %collective-permute-start.1 = (f32[1,2304]{1,0:T(1,128)S(1)}, f32[1,2304]{1,0:T(1,128)S(1)}, u32[]{:S(2)}, u32[]{:S(2)}) collective-permute-start(f32[1,2304]{1,0:T(1,128)S(1)} %bitcast.144), channel_id=1, source_target_pairs={{0,16},{16,0},{1,17},{17,1},{2,18},{18,2},{3,19},{19,3},{4,20},{20... | collective-permute-start | bytes 27656 | tf_op jit(solution)/shard_map/ppermute | solution.py:689
  22.5 2.0 %collective-permute-start.5 = (bf16[1024,256]{1,0:T(8,128)(2,1)S(1)}, bf16[1024,256]{1,0:T(8,128)(2,1)S(1)}, u32[]{:S(2)}, u32[]{:S(2)}) collective-permute-start(bf16[1024,256]{1,0:T(8,128)(2,1)S(1)} %get-tuple-element.87), channel_id=1, source_target_pairs={{0,16},{16,0},{1,17},{17,1},{2,18},{18,2},{3,19},{19,3},{4,20},{20... | collective-permute-start | bytes 1572872 | tf_op jit(solution)/shard_map/ppermute | solution.py:689
  23.0 4.7 %collective-permute-start.13 = (bf16[1024,256]{1,0:T(8,128)(2,1)S(1)}, bf16[1024,256]{1,0:T(8,128)(2,1)S(1)}, u32[]{:S(2)}, u32[]{:S(2)}) collective-permute-start(bf16[1024,256]{1,0:T(8,128)(2,1)S(1)} %get-tuple-element.89), channel_id=1, source_target_pairs={{0,16},{16,0},{1,17},{17,1},{2,18},{18,2},{3,19},{19,3},{4,20},{20... | collective-permute-start | bytes 1572872 | tf_op jit(solution)/shard_map/ppermute | solution.py:689
  23.1 6.4 %collective-permute-start.21 = (bf16[1088,256]{1,0:T(8,128)(2,1)S(1)}, bf16[1088,256]{1,0:T(8,128)(2,1)S(1)}, u32[]{:S(2)}, u32[]{:S(2)}) collective-permute-start(bf16[1088,256]{1,0:T(8,128)(2,1)S(1)} %get-tuple-element.91), channel_id=1, source_target_pairs={{0,16},{16,0},{1,17},{17,1},{2,18},{18,2},{3,19},{19,3},{4,20},{20... | collective-permute-start | bytes 1671176 | tf_op jit(solution)/shard_map/ppermute | solution.py:689
  23.5 49.1 %collective-permute-start.4 = (f32[2,304,256]{2,1,0:T(8,128)S(1)}, f32[2,304,256]{2,1,0:T(8,128)S(1)}, u32[]{:S(2)}, u32[]{:S(2)}) collective-permute-start(f32[2,304,256]{2,1,0:T(8,128)S(1)} %get-tuple-element.82), channel_id=1, source_target_pairs={{0,16},{16,0},{1,17},{17,1},{2,18},{18,2},{3,19},{19,3},{4,20},{20... | collective-permute-start | bytes 1867784 | tf_op jit(solution)/shard_map/ppermute | solution.py:689
  24.7 9.6 %collective-permute-start.6 = (bf16[2,2,128,256]{3,2,1,0:T(8,128)(2,1)S(1)}, bf16[2,2,128,256]{3,2,1,0:T(8,128)(2,1)S(1)}, u32[]{:S(2)}, u32[]{:S(2)}) collective-permute-start(bf16[2,2,128,256]{3,2,1,0:T(8,128)(2,1)S(1)} %bitcast.154), channel_id=1, source_target_pairs={{0,2},{1,3},{2,0},{3,1},{4,6},{5,7},{6,4},{7,5},{8,10},{9,11},{10,... | collective-permute-start | bytes 786440 | tf_op jit(solution)/shard_map/ppermute | solution.py:701
  27.8 8.4 %collective-permute-start.14 = (bf16[2,2,128,256]{3,2,1,0:T(8,128)(2,1)S(1)}, bf16[2,2,128,256]{3,2,1,0:T(8,128)(2,1)S(1)}, u32[]{:S(2)}, u32[]{:S(2)}) collective-permute-start(bf16[2,2,128,256]{3,2,1,0:T(8,128)(2,1)S(1)} %bitcast.155), channel_id=1, source_target_pairs={{0,4},{1,5},{2,6},{3,7},{4,0},{5,1},{6,2},{7,3},{8,12},{9,13},{10,... | collective-permute-start | bytes 786440 | tf_op jit(solution)/shard_map/ppermute | solution.py:701
  29.7 8.2 %collective-permute-start.22 = (bf16[2,2,136,256]{3,2,1,0:T(8,128)(2,1)S(1)}, bf16[2,2,136,256]{3,2,1,0:T(8,128)(2,1)S(1)}, u32[]{:S(2)}, u32[]{:S(2)}) collective-permute-start(bf16[2,2,136,256]{3,2,1,0:T(8,128)(2,1)S(1)} %bitcast.153), channel_id=1, source_target_pairs={{0,1},{1,0},{2,3},{3,2},{4,5},{5,4},{6,7},{7,6},{8,9},{9,8},{10,11... | collective-permute-start | bytes 835592 | tf_op jit(solution)/shard_map/ppermute | solution.py:701
  34.4 5.2 %collective-permute-start.7 = (bf16[2,128,256]{2,1,0:T(8,128)(2,1)S(1)}, bf16[2,128,256]{2,1,0:T(8,128)(2,1)S(1)}, u32[]{:S(2)}, u32[]{:S(2)}) collective-permute-start(bf16[2,128,256]{2,1,0:T(8,128)(2,1)S(1)} %select_bitcast_fusion.14), channel_id=1, source_target_pairs={{0,4},{1,5},{2,6},{3,7},{4,0},{5,1},{6,2},{7,3},{8,12},{9,13},{10,... | collective-permute-start | bytes 393224 | tf_op jit(solution)/shard_map/ppermute | solution.py:701
  36.3 5.5 %collective-permute-start.15 = (bf16[2,128,256]{2,1,0:T(8,128)(2,1)S(1)}, bf16[2,128,256]{2,1,0:T(8,128)(2,1)S(1)}, u32[]{:S(2)}, u32[]{:S(2)}) collective-permute-start(bf16[2,128,256]{2,1,0:T(8,128)(2,1)S(1)} %select_bitcast_fusion.11), channel_id=1, source_target_pairs={{0,1},{1,0},{2,3},{3,2},{4,5},{5,4},{6,7},{7,6},{8,9},{9,8},{10,11... | collective-permute-start | bytes 393224 | tf_op jit(solution)/shard_map/ppermute | solution.py:701
  38.0 5.8 %collective-permute-start.23 = (bf16[2,136,256]{2,1,0:T(8,128)(2,1)S(1)}, bf16[2,136,256]{2,1,0:T(8,128)(2,1)S(1)}, u32[]{:S(2)}, u32[]{:S(2)}) collective-permute-start(bf16[2,136,256]{2,1,0:T(8,128)(2,1)S(1)} %select_bitcast_fusion.8), channel_id=1, source_target_pairs={{0,2},{1,3},{2,0},{3,1},{4,6},{5,7},{6,4},{7,5},{8,10},{9,11},{10,... | collective-permute-start | bytes 417800 | tf_op jit(solution)/shard_map/ppermute | solution.py:701
  39.6 5.6 %collective-permute-start.8 = (bf16[128,256]{1,0:T(8,128)(2,1)S(1)}, bf16[128,256]{1,0:T(8,128)(2,1)S(1)}, u32[]{:S(2)}, u32[]{:S(2)}) collective-permute-start(bf16[128,256]{1,0:T(8,128)(2,1)S(1)} %select_bitcast_fusion.23), channel_id=1, source_target_pairs={{0,1},{1,0},{2,3},{3,2},{4,5},{5,4},{6,7},{7,6},{8,9},{9,8},{10,11... | collective-permute-start | bytes 196616 | tf_op jit(solution)/shard_map/ppermute | solution.py:701
  41.8 6.1 %collective-permute-start.16 = (bf16[128,256]{1,0:T(8,128)(2,1)S(1)}, bf16[128,256]{1,0:T(8,128)(2,1)S(1)}, u32[]{:S(2)}, u32[]{:S(2)}) collective-permute-start(bf16[128,256]{1,0:T(8,128)(2,1)S(1)} %select_bitcast_fusion.20), channel_id=1, source_target_pairs={{0,2},{1,3},{2,0},{3,1},{4,6},{5,7},{6,4},{7,5},{8,10},{9,11},{10,... | collective-permute-start | bytes 196616 | tf_op jit(solution)/shard_map/ppermute | solution.py:701
  43.9 5.1 %collective-permute-start.24 = (bf16[136,256]{1,0:T(8,128)(2,1)S(1)}, bf16[136,256]{1,0:T(8,128)(2,1)S(1)}, u32[]{:S(2)}, u32[]{:S(2)}) collective-permute-start(bf16[136,256]{1,0:T(8,128)(2,1)S(1)} %select_bitcast_fusion.17), channel_id=1, source_target_pairs={{0,4},{1,5},{2,6},{3,7},{4,0},{5,1},{6,2},{7,3},{8,12},{9,13},{10,... | collective-permute-start | bytes 208904 | tf_op jit(solution)/shard_map/ppermute | solution.py:701
  45.3 7.3 %collective-permute-start.9 = (bf16[128,256]{1,0:T(8,128)(2,1)S(1)}, bf16[128,256]{1,0:T(8,128)(2,1)S(1)}, u32[]{:S(2)}, u32[]{:S(2)}) collective-permute-start(bf16[128,256]{1,0:T(8,128)(2,1)S(1)} %fusion.8), channel_id=1, source_target_pairs={{0,8},{1,9},{2,10},{3,11},{4,12},{5,13},{6,14},{7,15},{8,0},{9,1},... | collective-permute-start | bytes 196616 | tf_op jit(solution)/shard_map/ppermute | solution.py:701
  48.0 6.0 %collective-permute-start.17 = (bf16[128,256]{1,0:T(8,128)(2,1)S(1)}, bf16[128,256]{1,0:T(8,128)(2,1)S(1)}, u32[]{:S(2)}, u32[]{:S(2)}) collective-permute-start(bf16[128,256]{1,0:T(8,128)(2,1)S(1)} %fusion.7), channel_id=1, source_target_pairs={{0,8},{1,9},{2,10},{3,11},{4,12},{5,13},{6,14},{7,15},{8,0},{9,1},... | collective-permute-start | bytes 196616 | tf_op jit(solution)/shard_map/ppermute | solution.py:701
  49.1 6.5 %collective-permute-start.25 = (bf16[136,256]{1,0:T(8,128)(2,1)S(1)}, bf16[136,256]{1,0:T(8,128)(2,1)S(1)}, u32[]{:S(2)}, u32[]{:S(2)}) collective-permute-start(bf16[136,256]{1,0:T(8,128)(2,1)S(1)} %fusion.6), channel_id=1, source_target_pairs={{0,8},{1,9},{2,10},{3,11},{4,12},{5,13},{6,14},{7,15},{8,0},{9,1},... | collective-permute-start | bytes 208904 | tf_op jit(solution)/shard_map/ppermute | solution.py:701
  52.7 4.3 %collective-permute-start.10 = (bf16[128,256]{1,0:T(8,128)(2,1)S(1)}, bf16[128,256]{1,0:T(8,128)(2,1)S(1)}, u32[]{:S(2)}, u32[]{:S(2)}) collective-permute-start(bf16[128,256]{1,0:T(8,128)(2,1)S(1)} %add_convert_fusion.5), channel_id=1, source_target_pairs={{0,1},{1,0},{2,3},{3,2},{4,5},{5,4},{6,7},{7,6},{8,9},{9,8},{10,11... | collective-permute-start | bytes 196616 | tf_op jit(solution)/shard_map/ppermute | solution.py:701
  54.1 4.3 %collective-permute-start.18 = (bf16[128,256]{1,0:T(8,128)(2,1)S(1)}, bf16[128,256]{1,0:T(8,128)(2,1)S(1)}, u32[]{:S(2)}, u32[]{:S(2)}) collective-permute-start(bf16[128,256]{1,0:T(8,128)(2,1)S(1)} %add_convert_fusion.4), channel_id=1, source_target_pairs={{0,2},{1,3},{2,0},{3,1},{4,6},{5,7},{6,4},{7,5},{8,10},{9,11},{10,... | collective-permute-start | bytes 196616 | tf_op jit(solution)/shard_map/ppermute | solution.py:701
  55.6 4.4 %collective-permute-start.26 = (bf16[136,256]{1,0:T(8,128)(2,1)S(1)}, bf16[136,256]{1,0:T(8,128)(2,1)S(1)}, u32[]{:S(2)}, u32[]{:S(2)}) collective-permute-start(bf16[136,256]{1,0:T(8,128)(2,1)S(1)} %add_convert_fusion.3), channel_id=1, source_target_pairs={{0,4},{1,5},{2,6},{3,7},{4,0},{5,1},{6,2},{7,3},{8,12},{9,13},{10,... | collective-permute-start | bytes 208904 | tf_op jit(solution)/shard_map/ppermute | solution.py:701
  57.0 5.0 %collective-permute-start.11 = (bf16[2,128,256]{2,1,0:T(8,128)(2,1)S(1)}, bf16[2,128,256]{2,1,0:T(8,128)(2,1)S(1)}, u32[]{:S(2)}, u32[]{:S(2)}) collective-permute-start(bf16[2,128,256]{2,1,0:T(8,128)(2,1)S(1)} %pad_maximum_fusion.7), channel_id=1, source_target_pairs={{0,4},{1,5},{2,6},{3,7},{4,0},{5,1},{6,2},{7,3},{8,12},{9,13},{10,... | collective-permute-start | bytes 393224 | tf_op jit(solution)/shard_map/ppermute | solution.py:701
  58.4 5.0 %collective-permute-start.19 = (bf16[2,128,256]{2,1,0:T(8,128)(2,1)S(1)}, bf16[2,128,256]{2,1,0:T(8,128)(2,1)S(1)}, u32[]{:S(2)}, u32[]{:S(2)}) collective-permute-start(bf16[2,128,256]{2,1,0:T(8,128)(2,1)S(1)} %pad_maximum_fusion.8), channel_id=1, source_target_pairs={{0,1},{1,0},{2,3},{3,2},{4,5},{5,4},{6,7},{7,6},{8,9},{9,8},{10,11... | collective-permute-start | bytes 393224 | tf_op jit(solution)/shard_map/ppermute | solution.py:701
  60.0 5.5 %collective-permute-start.27 = (bf16[2,136,256]{2,1,0:T(8,128)(2,1)S(1)}, bf16[2,136,256]{2,1,0:T(8,128)(2,1)S(1)}, u32[]{:S(2)}, u32[]{:S(2)}) collective-permute-start(bf16[2,136,256]{2,1,0:T(8,128)(2,1)S(1)} %pad_maximum_fusion.6), channel_id=1, source_target_pairs={{0,2},{1,3},{2,0},{3,1},{4,6},{5,7},{6,4},{7,5},{8,10},{9,11},{10,... | collective-permute-start | bytes 417800 | tf_op jit(solution)/shard_map/ppermute | solution.py:701
  62.1 6.4 %collective-permute-start.12 = (bf16[2,2,128,256]{3,2,1,0:T(8,128)(2,1)S(1)}, bf16[2,2,128,256]{3,2,1,0:T(8,128)(2,1)S(1)}, u32[]{:S(2)}, u32[]{:S(2)}) collective-permute-start(bf16[2,2,128,256]{3,2,1,0:T(8,128)(2,1)S(1)} %pad_maximum_fusion.4), channel_id=1, source_target_pairs={{0,2},{1,3},{2,0},{3,1},{4,6},{5,7},{6,4},{7,5},{8,10},{9,11},{10,... | collective-permute-start | bytes 786440 | tf_op jit(solution)/shard_map/ppermute | solution.py:701
  63.5 10.3 %copy-start.11 = (f32[1,256,256]{2,1,0:T(8,128)S(1)}, f32[1,256,256]{2,1,0:T(8,128)}, u32[]{:S(2)}) copy-start(f32[1,256,256]{2,1,0:T(8,128)} %param.41) | copy-start | bytes 786436
  63.5 10.3 %copy-start.15 = (f32[1,9,256]{2,0,1:T(1,128)S(1)}, f32[1,9,256]{2,0,1:T(1,128)}, u32[]{:S(2)}) copy-start(f32[1,9,256]{2,0,1:T(1,128)} %param.27) | copy-start | bytes 27652
  63.5 10.3 %copy-start.16 = (f32[1,3328]{1,0:T(1,128)S(1)}, f32[1,3328]{1,0:T(1,128)}, u32[]{:S(2)}) copy-start(f32[1,3328]{1,0:T(1,128)} %refs_14_.1) | copy-start | bytes 39940
  63.5 10.2 %copy-start.17 = (f32[1,3328]{1,0:T(1,128)S(1)}, f32[1,3328]{1,0:T(1,128)}, u32[]{:S(2)}) copy-start(f32[1,3328]{1,0:T(1,128)} %refs_20_.1) | copy-start | bytes 39940
  63.5 10.2 %copy-start.18 = (f32[1,9,256]{2,0,1:T(1,128)S(1)}, f32[1,9,256]{2,0,1:T(1,128)}, u32[]{:S(2)}) copy-start(f32[1,9,256]{2,0,1:T(1,128)} %param.33) | copy-start | bytes 27652
  63.6 10.2 %copy-start.19 = (f32[1,9,256]{2,0,1:T(1,128)S(1)}, f32[1,9,256]{2,0,1:T(1,128)}, u32[]{:S(2)}) copy-start(f32[1,9,256]{2,0,1:T(1,128)} %param.39) | copy-start | bytes 27652
  63.6 6.4 %collective-permute-start.20 = (bf16[2,2,128,256]{3,2,1,0:T(8,128)(2,1)S(1)}, bf16[2,2,128,256]{3,2,1,0:T(8,128)(2,1)S(1)}, u32[]{:S(2)}, u32[]{:S(2)}) collective-permute-start(bf16[2,2,128,256]{3,2,1,0:T(8,128)(2,1)S(1)} %pad_maximum_fusion.5), channel_id=1, source_target_pairs={{0,4},{1,5},{2,6},{3,7},{4,0},{5,1},{6,2},{7,3},{8,12},{9,13},{10,... | collective-permute-start | bytes 786440 | tf_op jit(solution)/shard_map/ppermute | solution.py:701
  65.4 8.4 %copy-start.9 = (f32[1,256,768]{2,1,0:T(8,128)S(1)}, f32[1,256,768]{2,1,0:T(8,128)}, u32[]{:S(2)}) copy-start(f32[1,256,768]{2,1,0:T(8,128)} %param.40) | copy-start | bytes 2359300
  65.5 8.3 %copy-start.8 = (f32[1,256,768]{2,1,0:T(8,128)S(1)}, f32[1,256,768]{2,1,0:T(8,128)}, u32[]{:S(2)}) copy-start(f32[1,256,768]{2,1,0:T(8,128)} %param.34) | copy-start | bytes 2359300
  65.5 6.6 %collective-permute-start.28 = (bf16[2,2,136,256]{3,2,1,0:T(8,128)(2,1)S(1)}, bf16[2,2,136,256]{3,2,1,0:T(8,128)(2,1)S(1)}, u32[]{:S(2)}, u32[]{:S(2)}) collective-permute-start(bf16[2,2,136,256]{3,2,1,0:T(8,128)(2,1)S(1)} %pad_maximum_fusion.3), channel_id=1, source_target_pairs={{0,1},{1,0},{2,3},{3,2},{4,5},{5,4},{6,7},{7,6},{8,9},{9,8},{10,11... | collective-permute-start | bytes 835592 | tf_op jit(solution)/shard_map/ppermute | solution.py:701
  68.6 5.3 %copy-start.6 = (f32[1,1024,256]{2,1,0:T(8,128)S(1)}, f32[1,1024,256]{2,1,0:T(8,128)}, u32[]{:S(2)}) copy-start(f32[1,1024,256]{2,1,0:T(8,128)} %param.43) | copy-start | bytes 3145732
  70.0 3.8 %copy-start.5 = (f32[1,256,1024]{2,1,0:T(8,128)S(1)}, f32[1,256,1024]{2,1,0:T(8,128)}, u32[]{:S(2)}) copy-start(f32[1,256,1024]{2,1,0:T(8,128)} %param.42) | copy-start | bytes 3145732
  70.1 3.8 %copy-start.4 = (f32[1,1024,256]{2,1,0:T(8,128)S(1)}, f32[1,1024,256]{2,1,0:T(8,128)}, u32[]{:S(2)}) copy-start(f32[1,1024,256]{2,1,0:T(8,128)} %param.37) | copy-start | bytes 3145732
  70.2 3.7 %copy-start.3 = (f32[1,256,1024]{2,1,0:T(8,128)S(1)}, f32[1,256,1024]{2,1,0:T(8,128)}, u32[]{:S(2)}) copy-start(f32[1,256,1024]{2,1,0:T(8,128)} %param.36) | copy-start | bytes 3145732
  72.1 1.7 %copy-start.2 = (f32[1,256,768]{2,1,0:T(8,128)S(1)}, f32[1,256,768]{2,1,0:T(8,128)}, u32[]{:S(2)}) copy-start(f32[1,256,768]{2,1,0:T(8,128)} %param.28) | copy-start | bytes 2359300
  72.2 1.7 %copy-start.1 = (f32[1,1024,256]{2,1,0:T(8,128)S(1)}, f32[1,1024,256]{2,1,0:T(8,128)}, u32[]{:S(2)}) copy-start(f32[1,1024,256]{2,1,0:T(8,128)} %param.31) | copy-start | bytes 3145732
  72.3 1.7 %copy-start = (f32[1,256,1024]{2,1,0:T(8,128)S(1)}, f32[1,256,1024]{2,1,0:T(8,128)}, u32[]{:S(2)}) copy-start(f32[1,256,1024]{2,1,0:T(8,128)} %param.30) | copy-start | bytes 3145732
  72.3 1.7 %copy-start.7 = (f32[1,256,256]{2,1,0:T(8,128)S(1)}, f32[1,256,256]{2,1,0:T(8,128)}, u32[]{:S(2)}) copy-start(f32[1,256,256]{2,1,0:T(8,128)} %param.29) | copy-start | bytes 786436
  72.3 1.8 %copy-start.10 = (f32[1,256,256]{2,1,0:T(8,128)S(1)}, f32[1,256,256]{2,1,0:T(8,128)}, u32[]{:S(2)}) copy-start(f32[1,256,256]{2,1,0:T(8,128)} %param.35) | copy-start | bytes 786436
  72.3 1.8 %copy-start.13 = (f32[1,3328]{1,0:T(1,128)S(1)}, f32[1,3328]{1,0:T(1,128)}, u32[]{:S(2)}) copy-start(f32[1,3328]{1,0:T(1,128)} %refs_8_.1) | copy-start | bytes 39940
  72.6 1.2 %collective-permute-start.29 = (f32[8,128]{1,0:T(8,128)S(1)}, f32[8,128]{1,0:T(8,128)S(1)}, u32[]{:S(2)}, u32[]{:S(2)}) collective-permute-start(f32[8,128]{1,0:T(8,128)S(1)} %squares.1.refs_3_), channel_id=1, source_target_pairs={{0,16},{16,0},{1,17},{17,1},{2,18},{18,2},{3,19},{19,3},{4,20},{20... | collective-permute-start | bytes 12296 | tf_op jit(solution)/shard_map/ppermute | solution.py:689
